TPU v7x, 32 devices: a whole 2x2x4 slice. The times are simulated.
32 devices in a mesh: seq: 8 (over y, x, core), wt: 4 (over z).
Axes of the slice: x: 2, y: 2, z: 4, core: 2. Of those that a mesh axis runs over, the one named last changes fastest.
Arguments:
- inputs: bfloat16 [8, 1024, 1024], P('wt', 'seq'), may hold values from -5 to 5
- cotangent: bfloat16 [8, 1024, 1024], P('wt', 'seq'), may hold values from -6 to 6
- decay: float32 [8, 1024, 8], P('wt', 'seq'), may hold values from 0.3 to 1
- w_query: bfloat16 [1024, 1024], P('wt'), may hold values from -0.1875 to 0.1875
- w_key: bfloat16 [1024, 1024], P('wt'), may hold values from -0.1875 to 0.1875
- w_value: bfloat16 [1024, 2048], P('wt'), may hold values from -0.1875 to 0.1875
- w_gate_out: bfloat16 [1024, 2048], P('wt'), may hold values from -0.1875 to 0.1875
- w_out: bfloat16 [1024, 2048], P('wt'), may hold values from -0.125 to 0.125
- w_ffn_gate: bfloat16 [1024, 2816], P('wt'), may hold values from -0.1875 to 0.1875
- w_ffn_up: bfloat16 [1024, 2816], P('wt'), may hold values from -0.1875 to 0.1875
- w_ffn_down: bfloat16 [1024, 2816], P('wt'), may hold values from -0.109375 to 0.109375
- w_beta: bfloat16 [1024, 8], replicated, may hold values from -1 to 1
- conv_weight: float32 [4, 4096], replicated, may hold values from -3 to 3
- norm_in: float32 [1024], replicated, may hold values from 0.5 to 1.5
- norm_mid: float32 [1024], replicated, may hold values from 0.5 to 1.5
- norm_head: float32 [256], replicated, may hold values from 0.5 to 1.5
Outputs:
- layer_out: bfloat16 [8, 1024, 1024], P('wt', 'seq')
- grad_input: float32 [8, 1024, 1024], P('wt', 'seq')
- grad_query: float32 [1024, 1024], P('wt')
- grad_key: float32 [1024, 1024], P('wt')
- grad_value: float32 [1024, 2048], P('wt')
- grad_gate_out: float32 [1024, 2048], P('wt')
- grad_out: float32 [1024, 2048], P('wt')
- slope_feedforward_switch: float32 [1024, 2816], P('wt')
- grad_ffn_up: float32 [1024, 2816], P('wt')
- grad_ffn_down: float32 [1024, 2816], P('wt')
- grad_beta: float32 [1024, 8], replicated
- grad_conv: float32 [4, 4096], replicated
- grad_norm_in: float32 [1024], replicated
- grad_norm_mid: float32 [1024], replicated
- grad_norm_head: float32 [256], replicated
All inputs are finite; a program needn't handle non-finite values.
Results may differ from a plain program's by a relative error of at most 0.0095.
The roundings to bfloat16 on the way count: a program that leaves them out, or rounds other values in their place, can miss the bound.
Values may be sent and summed in bfloat16 or wider, within the bound.
No kernel may reach another device: no remote copies, remote signals or barrier semaphores. Data moves between devices by JAX's collectives and lax.ppermute only.
A program may use at most 320 MiB of HBM per device.

v0:
```python
import jax
import jax.numpy as jnp
from jax import lax
from jax.sharding import PartitionSpec as P

H = 8
DK = 128
DV = 256
FF = 2816
CONV = 4
GROUP = 64


highest = lax.Precision.HIGHEST


def passed_along(array, axis, by):
    peers = lax.axis_size(axis)
    pairs = [(i, i + by) for i in range(peers) if 0 <= i + by < peers]
    return lax.ppermute(array, axis, pairs)


def product(left, right):
    return jnp.dot(left, right, preferred_element_type=jnp.float32)


def contract_rows(left, right):
    return lax.dot_general(
        left, right, (((0,), (0,)), ((), ())), preferred_element_type=jnp.float32
    )


def contract_cols(left, right):
    return lax.dot_general(
        left, right, (((1,), (1,)), ((), ())), preferred_element_type=jnp.float32
    )


def rms_norm(values, scaling):
    return values * lax.rsqrt(jnp.mean(values * values, axis=-1, keepdims=True) + 1e-05) * scaling


def head_norm(mixed, out_gate, scaling):
    multiplier_coefficient = lax.rsqrt(jnp.mean(mixed * mixed, axis=-1, keepdims=True) + 1e-05)
    gate_heads = out_gate.reshape(mixed.shape)
    return (mixed * multiplier_coefficient * scaling * jax.nn.silu(gate_heads)).reshape(
        out_gate.shape
    )


def pre_mix(padded, conv_weight, beta_logit):
    length = padded.shape[1] - (CONV - 1)
    summed = padded[:, 0:length] * conv_weight[0]
    for tap_index in range(1, CONV):
        summed = summed + padded[:, tap_index : tap_index + length] * conv_weight[tap_index]
    active = jax.nn.silu(summed)
    leading = active.shape[:2]
    queries = active[..., : H * DK].reshape(leading + (H, DK))
    keys_raw = active[..., H * DK : 2 * H * DK].reshape(leading + (H, DK))
    keys_unit = keys_raw * lax.rsqrt(jnp.sum(keys_raw * keys_raw, axis=-1, keepdims=True) + 1e-06)
    values = active[..., 2 * H * DK :].reshape(leading + (H, DV))
    return (queries, keys_unit, values, jax.nn.sigmoid(beta_logit))


def group_step(state, pieces):
    queries, keys_unit, values, betas, log_decay = pieces
    length = queries.shape[1]
    row_ids = lax.broadcasted_iota(jnp.int32, (length, length), 0)
    col_ids = lax.broadcasted_iota(jnp.int32, (length, length), 1)
    causal = row_ids >= col_ids
    strict = row_ids > col_ids
    running = jnp.cumsum(log_decay, axis=1)
    value_spread = jnp.where(causal, running[:, :, None] - running[:, None, :], 0.0)
    decay_mat = jnp.where(causal, jnp.exp(value_spread), 0.0)
    key_gram = jnp.einsum("hid,hjd->hij", keys_unit, keys_unit, precision=highest)
    system = jnp.eye(length, dtype=state.dtype) + jnp.where(
        strict, betas[:, :, None] * key_gram * decay_mat, 0.0
    )
    growth = jnp.exp(running)
    recalled = jnp.einsum("hid,hde->hie", keys_unit, state, precision=highest)
    target = betas[:, :, None] * (values - growth[:, :, None] * recalled)
    deltas = jax.scipy.linalg.solve_triangular(system, target, lower=True, unit_diagonal=True)
    scores = jnp.einsum("hid,hjd->hij", queries, keys_unit, precision=highest) * decay_mat
    read_out = growth[:, :, None] * jnp.einsum("hid,hde->hie", queries, state, precision=highest)
    read_out = read_out + jnp.einsum("hij,hje->hie", scores, deltas, precision=highest)
    final_log = running[:, -1:]
    weights_in = jnp.exp(final_log - running)
    new_state = jnp.exp(final_log)[:, :, None] * state + jnp.einsum(
        "hid,hie->hde", keys_unit * weights_in[:, :, None], deltas, precision=highest
    )
    return (new_state, read_out)


def delta_rule(state, queries, keys_unit, values, betas, log_decay):
    length = queries.shape[0]
    blocks = length // GROUP

    def arrange(array):
        return jnp.swapaxes(array.reshape((blocks, GROUP) + array.shape[1:]), 1, 2)

    final_state, read_out = lax.scan(
        jax.checkpoint(group_step),
        state,
        (arrange(queries), arrange(keys_unit), arrange(values), arrange(betas), arrange(log_decay)),
    )
    ordered = jnp.swapaxes(read_out, 1, 2)
    return (ordered.reshape((length,) + ordered.shape[2:]), final_state)


def shards(
    inputs,
    cotangent,
    decay,
    w_query,
    w_key,
    w_value,
    w_gate_out,
    w_out,
    w_ffn_gate,
    w_ffn_up,
    w_ffn_down,
    w_beta,
    conv_weight,
    norm_in,
    norm_mid,
    norm_head,
):
    seq_count, block_len, model_width = inputs.shape
    row_count = seq_count * block_len
    edge_rows = CONV - 1
    head_keys = H * DK
    head_values = H * DV
    (
        full_query,
        full_key,
        full_value,
        full_gate,
        full_out,
        full_ffn_gate,
        full_ffn_up,
        full_ffn_down,
    ) = (
        lax.all_gather(w_query, "wt", axis=0, tiled=True),
        lax.all_gather(w_key, "wt", axis=0, tiled=True),
        lax.all_gather(w_value, "wt", axis=0, tiled=True),
        lax.all_gather(w_gate_out, "wt", axis=0, tiled=True),
        lax.all_gather(w_out, "wt", axis=0, tiled=True),
        lax.all_gather(w_ffn_gate, "wt", axis=0, tiled=True),
        lax.all_gather(w_ffn_up, "wt", axis=0, tiled=True),
        lax.all_gather(w_ffn_down, "wt", axis=0, tiled=True),
    )
    flat_in = inputs.reshape(row_count, model_width).astype(jnp.float32)
    normed_first, norm_back_in = jax.vjp(rms_norm, flat_in, norm_in)
    normed_in = normed_first.astype(jnp.bfloat16)
    conv_in = jnp.concatenate(
        [
            product(normed_in, full_query),
            product(normed_in, full_key),
            product(normed_in, full_value),
        ],
        axis=1,
    ).astype(jnp.bfloat16)
    out_gate = product(normed_in, full_gate)
    beta_logit = product(normed_in, w_beta)
    conv_blocks = conv_in.reshape(seq_count, block_len, -1)
    before_rows = passed_along(conv_blocks[:, block_len - edge_rows :], "seq", 1)
    padded = jnp.concatenate([before_rows, conv_blocks], axis=1).astype(jnp.float32)
    (queries, keys_unit, values, betas), pre_back = jax.vjp(
        pre_mix, padded, conv_weight, beta_logit.reshape(seq_count, block_len, H)
    )
    log_decay = jnp.log(decay)
    eye_state = jnp.broadcast_to(jnp.eye(DK, dtype=jnp.float32), (seq_count, H, DK, DK))
    zero_state = jnp.zeros((seq_count, H, DK, DV), jnp.float32)
    run_rule = jax.vmap(delta_rule)
    transfer = run_rule(eye_state, queries, keys_unit, jnp.zeros_like(keys_unit), betas, log_decay)[
        1
    ]
    local_end = run_rule(zero_state, queries, keys_unit, values, betas, log_decay)[1]

    def forward_turn(turn_index, carried):
        moved = jnp.einsum("shij,shjk->shik", transfer, carried, precision=highest) + local_end
        return passed_along(moved, "seq", 1)

    start_state = lax.fori_loop(0, lax.axis_size("seq") - 1, forward_turn, zero_state)

    def mixer(state_in, query_in, key_in, value_in, beta_in):
        return run_rule(state_in, query_in, key_in, value_in, beta_in, log_decay)

    mixer_output, mixer_back = jax.vjp(mixer, start_state, queries, keys_unit, values, betas)
    mixed = mixer_output[0]
    headed_full, head_back = jax.vjp(
        head_norm, mixed, out_gate.reshape(seq_count, block_len, head_values), norm_head
    )
    headed = headed_full.reshape(row_count, head_values).astype(jnp.bfloat16)
    residual = flat_in + contract_cols(headed, full_out)
    normed_second, norm_back_mid = jax.vjp(rms_norm, residual, norm_mid)
    normed_mid = normed_second.astype(jnp.bfloat16)
    gate_pre = product(normed_mid, full_ffn_gate)
    up_pre = product(normed_mid, full_ffn_up)
    sigmoid_gate = jax.nn.sigmoid(gate_pre)
    swish_gate = gate_pre * sigmoid_gate
    hidden = (swish_gate * up_pre).astype(jnp.bfloat16)
    layer_out = (
        (residual + contract_cols(hidden, full_ffn_down))
        .astype(jnp.bfloat16)
        .reshape(seq_count, block_len, model_width)
    )
    upstream = cotangent.reshape(row_count, model_width)
    inner_feedforward_width = product(upstream, full_ffn_down)
    d_gate = (
        inner_feedforward_width * up_pre * sigmoid_gate * (1.0 + gate_pre * (1.0 - sigmoid_gate))
    ).astype(jnp.bfloat16)
    d_up = (inner_feedforward_width * swish_gate).astype(jnp.bfloat16)
    left_rows = normed_mid
    outer_rows = upstream
    ffn_share = lax.psum_scatter(
        jnp.concatenate(
            [
                contract_rows(left_rows, d_gate),
                contract_rows(left_rows, d_up),
                contract_rows(outer_rows, hidden),
            ],
            axis=1,
        ),
        "wt",
        scatter_dimension=0,
        tiled=True,
    )
    d_normed_mid = contract_cols(d_gate, full_ffn_gate) + contract_cols(d_up, full_ffn_up)
    d_from_mid, middle_gradient = norm_back_mid(d_normed_mid)
    d_residual = upstream.astype(jnp.float32) + d_from_mid
    d_branch = d_residual.astype(jnp.bfloat16)
    dimension_across_heads = product(d_branch, full_out)
    d_mixed, d_out_gate, grad_head = head_back(
        dimension_across_heads.reshape(seq_count, block_len, head_values)
    )
    local_start = mixer_back((d_mixed, zero_state))[0]
    transposed = jnp.swapaxes(transfer, 2, 3)

    def backward_turn(turn_index, carried):
        moved = jnp.einsum("shij,shjk->shik", transposed, carried, precision=highest) + local_start
        return passed_along(moved, "seq", -1)

    end_grad = lax.fori_loop(0, lax.axis_size("seq") - 1, backward_turn, zero_state)
    mixer_grads = mixer_back((d_mixed, end_grad))
    d_padded, grad_conv, d_beta_logit = pre_back(
        (mixer_grads[1], mixer_grads[2], mixer_grads[3], mixer_grads[4])
    )
    after_rows = passed_along(d_padded[:, :edge_rows], "seq", -1)
    d_conv_in = d_padded[:, edge_rows:] + jnp.pad(
        after_rows, ((0, 0), (block_len - edge_rows, 0), (0, 0))
    )
    d_conv_flat = d_conv_in.reshape(row_count, -1).astype(jnp.bfloat16)
    d_gate_flat = d_out_gate.reshape(row_count, head_values).astype(jnp.bfloat16)
    d_beta_flat = d_beta_logit.reshape(row_count, H).astype(jnp.bfloat16)
    left_rows = normed_in
    outer_rows = d_branch
    mixer_share = lax.psum_scatter(
        jnp.concatenate(
            [
                contract_rows(left_rows, d_conv_flat),
                contract_rows(left_rows, d_gate_flat),
                contract_rows(outer_rows, headed),
            ],
            axis=1,
        ),
        "wt",
        scatter_dimension=0,
        tiled=True,
    )
    grad_beta = contract_rows(normed_in, d_beta_flat)
    d_normed_in = contract_cols(d_conv_flat[:, :head_keys], full_query) + contract_cols(
        d_conv_flat[:, head_keys : 2 * head_keys], full_key
    )
    d_normed_in = (
        d_normed_in
        + contract_cols(d_conv_flat[:, 2 * head_keys :], full_value)
        + contract_cols(d_gate_flat, full_gate)
    )
    d_normed_in = d_normed_in + contract_cols(d_beta_flat, w_beta)
    d_from_in, grad_in = norm_back_in(d_normed_in)
    grad_input = (d_residual + d_from_in).reshape(seq_count, block_len, model_width)
    mixer_sum, ffn_sum = lax.psum((mixer_share, ffn_share), "seq")
    grad_beta, grad_conv, grad_in, middle_gradient, grad_head = lax.psum(
        (grad_beta, grad_conv, grad_in, middle_gradient, grad_head), ("seq", "wt")
    )
    value_end = 2 * head_keys + head_values
    gate_end = value_end + head_values
    return (
        layer_out,
        grad_input,
        mixer_sum[:, :head_keys],
        mixer_sum[:, head_keys : 2 * head_keys],
        mixer_sum[:, 2 * head_keys : value_end],
        mixer_sum[:, value_end:gate_end],
        mixer_sum[:, gate_end:],
        ffn_sum[:, :FF],
        ffn_sum[:, FF : 2 * FF],
        ffn_sum[:, 2 * FF :],
        grad_beta,
        grad_conv,
        grad_in,
        middle_gradient,
        grad_head,
    )


def solution(mesh):
    in_specs = (
        P("wt", "seq", None),
        P("wt", "seq", None),
        P("wt", "seq", None),
        P("wt", None),
        P("wt", None),
        P("wt", None),
        P("wt", None),
        P("wt", None),
        P("wt", None),
        P("wt", None),
        P("wt", None),
        P(),
        P(),
        P(),
        P(),
        P(),
    )
    out_specs = (
        P("wt", "seq", None),
        P("wt", "seq", None),
        P("wt", None),
        P("wt", None),
        P("wt", None),
        P("wt", None),
        P("wt", None),
        P("wt", None),
        P("wt", None),
        P("wt", None),
        P(),
        P(),
        P(),
        P(),
        P(),
    )
    return jax.shard_map(shards, mesh=mesh, in_specs=in_specs, out_specs=out_specs, check_vma=False)
```

profile of v0, /device:TPU:0, one launch (start us, length us, event | category | flops | bytes accessed | tf_op | source)
XLA Modules:
  0.0 3430.9 jit_solution(14489899089912197021)
XLA Ops:
  13.6 44.7 %all-gather.11.cloned.1.call-done = bf16[1024,1024]{1,0:T(8,128)(2,1)} async-done(((bf16[256,1024]{1,0:T(8,128)(2,1)}), bf16[1024,1024]{1,0:T(8,128)(2,1)}) %all-gather.11.cloned.1.call-update) | async-done | bytes 2097168 | tf_op jit(solution)/shard_map/all_gather | solution.py:144
  60.6 43.9 %all-gather.9.cloned.1.call-done = bf16[1024,1024]{1,0:T(8,128)(2,1)} async-done(((bf16[256,1024]{1,0:T(8,128)(2,1)}), bf16[1024,1024]{1,0:T(8,128)(2,1)}) %all-gather.9.cloned.1.call-update) | async-done | bytes 2097168 | tf_op jit(solution)/shard_map/all_gather | solution.py:143
  106.8 78.8 %all-gather.13.cloned.1.call-done = bf16[1024,2048]{1,0:T(8,128)(2,1)} async-done(((bf16[256,2048]{1,0:T(8,128)(2,1)}), bf16[1024,2048]{1,0:T(8,128)(2,1)}) %all-gather.13.cloned.1.call-update) | async-done | bytes 4194320 | tf_op jit(solution)/shard_map/all_gather | solution.py:145
  192.3 74.1 %all-gather.15.cloned.1.call-done = bf16[1024,2048]{1,0:T(8,128)(2,1)} async-done(((bf16[256,2048]{1,0:T(8,128)(2,1)}), bf16[1024,2048]{1,0:T(8,128)(2,1)}) %all-gather.15.cloned.1.call-update) | async-done | bytes 4194320 | tf_op jit(solution)/shard_map/all_gather | solution.py:146
  288.6 182.3 %while.96 = (s32[]{:T(128)}, f32[2,8,128,128]{3,2,1,0:T(8,128)}, f32[2,2,8,64]{3,2,1,0:T(8,128)S(1)}, f32[2,2,8,64,128]{4,3,2,1,0:T(8,128)S(1)}, f32[2,2,8,64]{3,2,1,0:T(8,128)S(1)}, /*index=5*/s32[]{:T(128)}, f32[]{:T(128)}) while((s32[]{:T(128)}, f32[2,8,128,128]{3,2,1,0:T(8,128)}, f32[2,2,8,64]{3,2,1,0:T(8,128)S(1)}, ...), condition=%wide.region_4.5_spmd, body=%wide.region_2.4_spmd.sunk | while | flops 605712448 | bytes 15951777 | solution.py:101
  294.3 80.0 %custom-call.36 = f32[2,8,1,64,64]{3,4,2,1,0:T(8,128)} custom-call(f32[2,8,1,64,64]{4,3,2,1,0:T(8,128)} %fusion.427), custom_call_target="InvertDiagBlocksLowerTriangular" | custom-call | tf_op jit(solution)/shard_map/vmap()/while/body/eval_jaxpr/checkpoint/jit(_solve_triangular)/vmap()/triangular_solve | solution.py:82
  385.5 80.0 %custom-call.36 = f32[2,8,1,64,64]{3,4,2,1,0:T(8,128)} custom-call(f32[2,8,1,64,64]{4,3,2,1,0:T(8,128)} %fusion.427), custom_call_target="InvertDiagBlocksLowerTriangular" | custom-call | tf_op jit(solution)/shard_map/vmap()/while/body/eval_jaxpr/checkpoint/jit(_solve_triangular)/vmap()/triangular_solve | solution.py:82
  475.4 183.1 %while.101 = (s32[]{:T(128)}, f32[2,8,128,256]{3,2,1,0:T(8,128)S(1)}, f32[2,2,8,64]{3,2,1,0:T(8,128)S(1)}, f32[2,2,8,64,128]{4,3,2,1,0:T(8,128)S(1)}, f32[2,2,8,...) while((s32[]{:T(128)}, ...), condition=%wide.region_7.9_spmd.clone, body=%wide.region_5.8_spmd.clone.sunk | while | flops 1110994944 | bytes 13856127 | solution.py:101
  481.9 80.0 %custom-call.39 = f32[2,8,1,64,64]{3,4,2,1,0:T(8,128)} custom-call(f32[2,8,1,64,64]{4,3,2,1,0:T(8,128)} %fusion.505), custom_call_target="InvertDiagBlocksLowerTriangular" | custom-call | tf_op jit(solution)/shard_map/vmap()/while/body/eval_jaxpr/checkpoint/jit(_solve_triangular)/vmap()/triangular_solve/custom-call.0 | solution.py:82
  573.4 80.0 %custom-call.39 = f32[2,8,1,64,64]{3,4,2,1,0:T(8,128)} custom-call(f32[2,8,1,64,64]{4,3,2,1,0:T(8,128)} %fusion.505), custom_call_target="InvertDiagBlocksLowerTriangular" | custom-call | tf_op jit(solution)/shard_map/vmap()/while/body/eval_jaxpr/checkpoint/jit(_solve_triangular)/vmap()/triangular_solve/custom-call.0 | solution.py:82
  662.0 206.4 %while.97 = (s32[]{:T(128)}, f32[2,8,128,256]{3,2,1,0:T(8,128)S(1)}, f32[2,8,128,128]{3,2,1,0:T(8,128)}, f32[2,8,128,256]{3,2,1,0:T(8,128)}, s32[]{:T(128)}) while((s32[]{:T(128)}, f32[2,8,128,256]{3,2,1,0:T(8,128)S(1)}, f32[2,8,128,128]{3,2,1,0:T(8,128)}, f32[2,8,128,256]{3,2,1,0:T(8,128)}, s32[]{:T(128)}) %tuple.364), condition=%wide.region_9.11_spmd, body=%wide.region_8.10_spmd.sunk | while | flops 805830656 | bytes 15728741 | solution.py:184
  870.0 200.0 %while.100 = (s32[]{:T(128)}, f32[2,8,128,256]{3,2,1,0:T(8,128)S(1)}, f32[2,2,8,64,256]{4,3,2,1,0:T(8,128)}, f32[2,2,8,128,256]{4,3,2,1,0:T(8,128)}, f32[2,2,8,6...) while((s32[]{:T(128)}, ...), condition=%wide.region_12.14_spmd.clone.clone, body=%wide.region_10.13_spmd.clone.clone.sunk | while | flops 1815367680 | bytes 56082448 | solution.py:101
  880.4 80.0 %custom-call.38 = f32[2,8,1,64,64]{3,4,2,1,0:T(8,128)} custom-call(f32[2,8,1,64,64]{4,3,2,1,0:T(8,128)} %fusion.494), custom_call_target="InvertDiagBlocksLowerTriangular" | custom-call | tf_op jit(solution)/shard_map/jvp(vmap())/while/body/eval_jaxpr/jit(_solve_triangular)/vmap()/triangular_solve/custom-call.0 | solution.py:82
  980.1 80.0 %custom-call.38 = f32[2,8,1,64,64]{3,4,2,1,0:T(8,128)} custom-call(f32[2,8,1,64,64]{4,3,2,1,0:T(8,128)} %fusion.494), custom_call_target="InvertDiagBlocksLowerTriangular" | custom-call | tf_op jit(solution)/shard_map/jvp(vmap())/while/body/eval_jaxpr/jit(_solve_triangular)/vmap()/triangular_solve/custom-call.0 | solution.py:82
  1127.6 206.5 %while.102 = (s32[]{:T(128)}, f32[2,8,128,256]{3,2,1,0:T(8,128)}, f32[2,2,8,64,128]{4,3,2,1,0:T(8,128)}, f32[2,2,8,64,128]{4,3,2,1,0:T(8,128)S(1)}, f32[2,2,8,64...) while((s32[]{:T(128)}, f32[2,8,128,256]{3,2,1,0:T(8,128)}, ...), condition=%wide.region_19.22_spmd.clone, body=%wide.region_17.21_spmd.clone.sunk | while | flops 1816424448 | bytes 58881144 | solution.py:101
  1144.3 80.0 %custom-call.40 = f32[2,8,1,64,64]{3,4,2,1,0:T(8,128)} custom-call(f32[2,8,1,64,64]{4,3,2,1,0:T(8,128)} %fusion.524), custom_call_target="InvertDiagBlocksLowerTriangular" | custom-call | tf_op jit(solution)/shard_map/transpose(jvp(vmap()))/while/body/eval_jaxpr/checkpoint/jit(_solve_triangular)/vmap()/triangular_solve/custom-call.2 | solution.py:82
  1247.9 80.0 %custom-call.40 = f32[2,8,1,64,64]{3,4,2,1,0:T(8,128)} custom-call(f32[2,8,1,64,64]{4,3,2,1,0:T(8,128)} %fusion.524), custom_call_target="InvertDiagBlocksLowerTriangular" | custom-call | tf_op jit(solution)/shard_map/transpose(jvp(vmap()))/while/body/eval_jaxpr/checkpoint/jit(_solve_triangular)/vmap()/triangular_solve/custom-call.2 | solution.py:82
  1334.4 229.7 %while.98 = (s32[]{:T(128)}, f32[2,8,128,256]{3,2,1,0:T(8,128)S(1)}, f32[2,8,128,128]{3,2,1,0:T(8,128)}, f32[2,8,128,256]{3,2,1,0:T(8,128)}, s32[]{:T(128)}) while((s32[]{:T(128)}, f32[2,8,128,256]{3,2,1,0:T(8,128)S(1)}, f32[2,8,128,128]{3,2,1,0:T(8,128)}, f32[2,8,128,256]{3,2,1,0:T(8,128)}, s32[]{:T(128)}) %tuple.370), condition=%wide.region_21.24_spmd, body=%wide.region_20.23_spmd.sunk | while | flops 805830656 | bytes 15728741 | solution.py:244
  1373.8 26.9 collective-permute-done.1
  1407.1 26.3 collective-permute-done.1
  1439.8 26.3 collective-permute-done.1
  1472.5 26.3 collective-permute-done.1
  1505.1 26.3 collective-permute-done.1
  1537.8 26.3 collective-permute-done.1
  1567.8 256.0 %while.99 = (s32[]{:T(128)}, f32[2,8,128,256]{3,2,1,0:T(8,128)S(1)}, f32[2,2,8,64,128]{4,3,2,1,0:T(8,128)}, f32[2,2,8,64,128]{4,2,3,0,1:T(8,128)}, f32[2,2,8,64,...) while((s32[]{:T(128)}, ...), condition=%wide.region_26.29_spmd, body=%wide.region_22.28_spmd.sunk | while | flops 4487867392 | bytes 149161456 | solution.py:101
  1582.7 80.0 %custom-call.37 = f32[2,8,1,64,64]{3,4,2,1,0:T(8,128)} custom-call(f32[2,8,1,64,64]{4,3,2,1,0:T(8,128)} %add_bitcast_fusion.2), custom_call_target="InvertDiagBlocksLowerTriangular" | custom-call | tf_op jit(solution)/shard_map/transpose(jvp(vmap()))/while/body/eval_jaxpr/checkpoint/jit(_solve_triangular)/vmap()/triangular_solve/custom-call.2 | solution.py:82
  1706.7 80.0 %custom-call.37 = f32[2,8,1,64,64]{3,4,2,1,0:T(8,128)} custom-call(f32[2,8,1,64,64]{4,3,2,1,0:T(8,128)} %add_bitcast_fusion.2), custom_call_target="InvertDiagBlocksLowerTriangular" | custom-call | tf_op jit(solution)/shard_map/transpose(jvp(vmap()))/while/body/eval_jaxpr/checkpoint/jit(_solve_triangular)/vmap()/triangular_solve/custom-call.2 | solution.py:82
  1975.2 522.9 %reduce-scatter.3.cloned.1.call-done = f32[256,8192]{1,0:T(8,128)} async-done(((f32[1024,8192]{1,0:T(8,128)}), f32[256,8192]{1,0:T(8,128)}) %reduce-scatter.3.cloned.1.call-update) | async-done | bytes 8388624 | tf_op jit(solution)/shard_map/reduce_scatter | solution.py:258
  2498.1 571.9 %reduce-scatter.5.cloned.1.call-done = f32[256,8448]{1,0:T(8,128)} async-done(((f32[1024,8448]{1,0:T(8,128)}), f32[256,8448]{1,0:T(8,128)}) %reduce-scatter.5.cloned.1.call-update) | async-done | bytes 8650768 | tf_op jit(solution)/shard_map/reduce_scatter | solution.py:216
  3087.1 43.1 %all-reduce.12 = (f32[1024,8]{0,1:T(8,128)}, f32[1024]{0:T(1024)}, f32[1024]{0:T(1024)}, f32[256]{0:T(256)}) all-reduce(f32[1024,8]{0,1:T(8,128)S(1)} %convolution_bitcast_fusion.2, f32[1024]{0:T(1024)S(1)} %get-tuple-element.984, f32[1024]{0:T(1024)S(1)} %copy-done.88, ...), channel_id=1, replica_groups=mesh['seq'=8,'wt'=4] {'seq','wt'}, use_global_device_ids=true, to_apply=%region_33.36 | all-reduce | flops 10496 | bytes 83968 | tf_op jit(solution)/shard_map/psum | solution.py:284
  3130.2 167.5 %all-reduce.19.cloned.1.call-done = (f32[256,8192]{1,0:T(8,128)}, f32[256,8448]{1,0:T(8,128)}) async-done(((f32[256,8192]{1,0:T(8,128)}, f32[256,8448]{1,0:T(8,128)}), (f32[256,8192]{1,0:T(8,128)}, f32[256,8448]{1,0:T(8,128)})) %all-reduce.19.cloned.1.call-update) | async-done | bytes 17039376 | tf_op jit(solution)/shard_map/psum | solution.py:283
  3312.1 110.2 %all-reduce.17.cloned.1.call-done = f32[4,4096]{1,0:T(4,128)} async-done(((f32[4,4096]{1,0:T(4,128)}), f32[4,4096]{1,0:T(4,128)}) %all-reduce.17.cloned.1.call-update) | async-done | bytes 65552 | tf_op jit(solution)/shard_map/psum | solution.py:284
  (609 shorter events, 789.3 us)
Async XLA Ops:
  7.2 51.1 %all-gather.11.cloned.1.call-start = ((), (), s32[]{:S(2)}) async-start(), calls=%async_computation.3 | async-start | bytes 2621440 | tf_op jit(solution)/shard_map/all_gather | solution.py:144
  7.9 96.6 %all-gather.9.cloned.1.call-start = ((), (), s32[]{:S(2)}) async-start(), calls=%async_computation.2 | async-start | bytes 2621440 | tf_op jit(solution)/shard_map/all_gather | solution.py:143
  8.7 176.9 %all-gather.13.cloned.1.call-start = ((), (), s32[]{:S(2)}) async-start(), calls=%async_computation.4 | async-start | bytes 5242880 | tf_op jit(solution)/shard_map/all_gather | solution.py:145
  9.4 256.9 %all-gather.15.cloned.1.call-start = ((), (), s32[]{:S(2)}) async-start(), calls=%async_computation.5 | async-start | bytes 5242880 | tf_op jit(solution)/shard_map/all_gather | solution.py:146
  10.0 1073.7 %all-gather.17.cloned.1.call-start = ((), (), s32[]{:S(2)}) async-start(), calls=%async_computation.6 | async-start | bytes 5242880 | tf_op jit(solution)/shard_map/all_gather | solution.py:147
  10.6 1079.0 %all-gather.19.cloned.1.call-start = ((), (), s32[]{:S(2)}) async-start(), calls=%async_computation.7 | async-start | bytes 7208960 | tf_op jit(solution)/shard_map/all_gather | solution.py:148
  11.2 1084.5 %all-gather.21.cloned.1.call-start = ((), (), s32[]{:S(2)}) async-start(), calls=%async_computation.8 | async-start | bytes 7208960 | tf_op jit(solution)/shard_map/all_gather | solution.py:149
  11.9 1089.8 %all-gather.23.cloned.1.call-start = ((), (), s32[]{:S(2)}) async-start(), calls=%async_computation.9 | async-start | bytes 7208960 | tf_op jit(solution)/shard_map/all_gather | solution.py:150
  12.7 2485.4 %reduce-scatter.3.cloned.1.call-start = ((), (), s32[]{:S(2)}) async-start(), calls=%async_computation.10 | async-start | bytes 41943040 | tf_op jit(solution)/shard_map/reduce_scatter | solution.py:258
  12.8 262.0 %copy-start.67 = (f32[1,4096]{1,0:T(1,128)}, f32[1,4096]{1,0:T(1,128)S(1)}, u32[]{:S(2)}) copy-start(f32[1,4096]{1,0:T(1,128)S(1)} %get-tuple-element.1162) | copy-start | bytes 49156
  12.8 262.0 %copy-start.69 = (f32[1,4096]{1,0:T(1,128)}, f32[1,4096]{1,0:T(1,128)S(1)}, u32[]{:S(2)}) copy-start(f32[1,4096]{1,0:T(1,128)S(1)} %get-tuple-element.1163) | copy-start | bytes 49156
  12.8 262.0 %copy-start.71 = (f32[1,4096]{1,0:T(1,128)}, f32[1,4096]{1,0:T(1,128)S(1)}, u32[]{:S(2)}) copy-start(f32[1,4096]{1,0:T(1,128)S(1)} %get-tuple-element.1164) | copy-start | bytes 49156
  12.9 262.0 %copy-start.73 = (f32[1,4096]{1,0:T(1,128)}, f32[1,4096]{1,0:T(1,128)S(1)}, u32[]{:S(2)}) copy-start(f32[1,4096]{1,0:T(1,128)S(1)} %get-tuple-element.1165) | copy-start | bytes 49156
  190.1 82.8 %collective-permute-start.2 = (bf16[2,3,4096]{2,1,0:T(4,128)(2,1)S(1)}, bf16[2,3,4096]{2,1,0:T(4,128)(2,1)S(1)}, u32[]{:S(2)}, u32[]{:S(2)}) collective-permute-start(bf16[2,3,4096]{2,1,0:T(4,128)(2,1)S(1)} %pad_maximum_fusion.2), channel_id=1, source_target_pairs={{0,4},{4,8},{8,12},{12,16},{16,20},{20,24},{24,28},{1,5},{5,9},{9,... | collective-permute-start | bytes 147464 | tf_op jit(solution)/shard_map/ppermute | solution.py:20
  667.2 5.8 collective-permute-start
  678.1 26.9 collective-permute-start
  710.2 27.6 collective-permute-start
  742.8 27.6 collective-permute-start
  775.5 27.6 collective-permute-start
  808.2 27.6 collective-permute-start
  840.9 27.6 collective-permute-start
  1340.0 27.4 collective-permute-start.1
  1372.5 28.2 collective-permute-start.1
  1405.8 27.6 collective-permute-start.1
  1438.5 27.6 collective-permute-start.1
  1471.2 27.6 collective-permute-start.1
  1503.8 27.6 collective-permute-start.1
  1536.5 27.6 collective-permute-start.1
  1873.9 24.8 collective-permute-start.3
  1931.8 1138.3 %reduce-scatter.5.cloned.1.call-start = ((), (), s32[]{:S(2)}) async-start(), calls=%async_computation.11 | async-start | bytes 43253760 | tf_op jit(solution)/shard_map/reduce_scatter | solution.py:216
  1975.2 1322.6 %all-reduce.19.cloned.1.call-start = ((), (), s32[]{:S(2)}) async-start(), calls=%async_computation.13 | async-start | bytes 34078720 | tf_op jit(solution)/shard_map/psum | solution.py:283
  3070.1 352.2 %all-reduce.17.cloned.1.call-start = ((), (), s32[]{:S(2)}) async-start(), calls=%async_computation.12 | async-start | bytes 131072 | tf_op jit(solution)/shard_map/psum | solution.py:284
  (117 other events, 989.5 us)
Sparse Core Ops, SparseCore 0:
  9.6 48.6 all-gather.10
  59.8 44.6 all-gather.8
  106.1 79.4 all-gather.12
  187.0 79.2 all-gather.14
  267.8 79.3 all-gather.16
  348.6 105.3 all-gather.18
  455.6 105.3 all-gather.20
  562.6 105.0 all-gather.22
  1931.9 566.1 reduce-scatter.2
  2500.5 569.5 reduce-scatter.4
  3074.7 223.0 all-reduce.18
  3304.7 117.4 all-reduce.16
where the time goes:
time: 3440 us; the launch traced here: 3430 us
  waiting for transfers between devices  1850 us (54%)
  other arithmetic  906 us (26%)
  matrix products  336 us (10%)
  starting transfers between devices  157 us (5%)
  local copies, waits for them, and re-layouts  114 us (3%)
  blocking collectives  43.1 us (1%)
    another operation x40, other arithmetic, group_step(): jax.scipy.linalg.solve_triangular(system, target, lower=True, unit_diagon...  803 us
    reduce_scatter x1, waiting for transfers between devices, shards(): lax.psum_scatter(jnp.concatenate([contract_rows(left_rows, d_gate), contr...  572 us
    reduce_scatter x1, waiting for transfers between devices, shards(): lax.psum_scatter(jnp.concatenate([contract_rows(left_rows, d_conv_flat),...  523 us
    ppermute x16, waiting for transfers between devices, passed_along(): return lax.ppermute(array, axis, pairs)  230 us
    psum x1, waiting for transfers between devices, shards(): mixer_sum, ffn_sum = lax.psum((mixer_share, ffn_share), 'seq')  168 us
    ppermute x16, starting transfers between devices, passed_along(): return lax.ppermute(array, axis, pairs)  156 us
    psum x1, waiting for transfers between devices, shards(): lax.psum((grad_beta, grad_conv, grad_in, middle_gradient, grad_head), ('s...  110 us
    all_gather x1, waiting for transfers between devices, shards(): lax.all_gather(w_value, 'wt', axis=0, tiled=True)  78.8 us
  transfers between devices with their start and end apart: 28, of which 23 were waited for; matrix products, arithmetic and copies ran while one was open for 22% of the time, Pallas kernels for 0%

commit v1 on v0

v1 whole, which is shorter than its diff:
```python
import jax
import jax.numpy as jnp
from jax import lax
from jax.experimental import pallas as pl
from jax.experimental.pallas import tpu as pltpu
from jax.sharding import PartitionSpec as P

H = 8
DK = 128
DV = 256
CONV = 4
HALO = 16
bf16 = jnp.bfloat16
f32 = jnp.float32


def parts(values):
    high = values.astype(bf16)
    low = (values - high.astype(f32)).astype(bf16)
    return high, low


def dot(left, right, dims):
    return lax.dot_general(left, right, (dims, ((), ())), preferred_element_type=f32)


def mul(left, right):
    (lh, ll), (rh, rl) = left, right
    wide = dot(jnp.concatenate([lh, ll], 1), jnp.concatenate([rh, rh], 0), ((1,), (0,)))
    return wide + dot(lh, rl, ((1,), (0,)))


def mul_t(left, right):
    (lh, ll), (rh, rl) = left, right
    wide = dot(jnp.concatenate([lh, ll], 1), jnp.concatenate([rh, rh], 1), ((1,), (1,)))
    return wide + dot(lh, rl, ((1,), (1,)))


def cat_parts(values):
    return jnp.concatenate(parts(values), 1)


def from_cat(both):
    half = both.shape[1] // 2
    return both[:, :half], both[:, half:]


def iotas(size):
    return (
        lax.broadcasted_iota(jnp.int32, (size, size), 0),
        lax.broadcasted_iota(jnp.int32, (size, size), 1),
    )


def column(row, rows, cols):
    return jnp.sum(jnp.where(rows == cols, row, 0.0), axis=1, keepdims=True)


def unit_inverse(lower, rows, cols):
    size = lower.shape[0]
    level = 0
    inverse = jnp.where(rows == cols, 1.0, 0.0)
    while (1 << level) < size:
        pair_up = (rows >> (level + 1)) == (cols >> (level + 1))
        corner = pair_up & (((rows >> level) & 1) == 1) & (((cols >> level) & 1) == 0)
        block = jnp.where(corner, lower, 0.0)
        if level == 0:
            inverse = inverse - block
        else:
            whole = parts(inverse)
            inverse = inverse - mul(whole, parts(mul(parts(block), whole)))
        level += 1
    return inverse


def conv_rows(conv_ref, halo_ref, rows_ref, taps_ref, chunk, seq, slot):
    size = conv_ref.shape[2]
    before = conv_ref[jnp.maximum(chunk - 1, 0), seq, size - HALO :, :]
    before = jnp.where(chunk == 0, halo_ref[seq], before)
    rows_ref[slot, :HALO, :] = before.astype(f32)
    rows_ref[slot, HALO:, :] = conv_ref[chunk, seq].astype(f32)
    total = None
    for tap in range(CONV):
        start = HALO - (CONV - 1) + tap
        term = rows_ref[slot, start : start + size, :] * taps_ref[tap : tap + 1, :]
        total = term if total is None else total + term
    return total


def decays(run_ref, chunk, seq, rows, cols):
    size = rows.shape[0]
    run_row = run_ref[chunk, seq][0:1, :]
    run_col = column(run_row, rows, cols)
    spread = jnp.where(rows >= cols, run_col - run_row, 0.0)
    decay_mat = jnp.where(rows >= cols, jnp.exp(spread), 0.0)
    last = run_row[:, size - 1 : size]
    return decay_mat, jnp.exp(run_col), jnp.exp(last - run_col), jnp.exp(last)


def forward_kernel(
    conv_ref, gate_ref, run_ref, taps_ref, gain_ref, state_ref, halo_ref,
    headed_ref, mixed_ref, inverse_ref, scores_ref, delta_ref, starts_ref, end_ref,
    rows_ref, recall_ref, target_ref, query_ref, write_ref, plain_ref,
):
    chunks, seqs, size, _ = conv_ref.shape
    rows, cols = iotas(size)

    def prepare(chunk, _):
        for seq in range(seqs):
            summed = conv_rows(conv_ref, halo_ref, rows_ref, taps_ref, chunk, seq, seq)
            active = summed * jax.nn.sigmoid(summed)
            query = active[:, :DK]
            key = active[:, DK : 2 * DK]
            key = key * lax.rsqrt(jnp.sum(key * key, axis=1, keepdims=True) + 1e-06)
            value = active[:, 2 * DK :]
            beta = jax.nn.sigmoid(gate_ref[chunk, seq, :, DV : DV + 1])
            decay_mat, growth, fade, _ = decays(run_ref, chunk, seq, rows, cols)
            key_parts = parts(key)
            gram = mul_t(key_parts, key_parts)
            lower = jnp.where(rows > cols, beta * gram * decay_mat, 0.0)
            inverse = unit_inverse(lower, rows, cols)
            scores = mul_t(parts(query), key_parts) * decay_mat
            inverse_parts = parts(inverse)
            recall_ref[chunk, seq] = cat_parts(mul(inverse_parts, parts(beta * growth * key)))
            target_ref[chunk, seq] = mul(inverse_parts, parts(beta * value))
            query_ref[chunk, seq] = cat_parts(growth * query)
            write_ref[chunk, seq] = cat_parts((fade * key).T)
            plain_ref[chunk, seq] = cat_parts(scores)
            inverse_ref[chunk, seq] = cat_parts(inverse.T)
            scores_ref[chunk, seq] = cat_parts(scores.T)
        return 0

    lax.fori_loop(0, chunks, prepare, 0)

    def advance(chunk, states):
        following = []
        for seq in range(seqs):
            state = states[seq]
            starts_ref[chunk, seq] = state
            state_parts = parts(state)
            delta = target_ref[chunk, seq] - mul(from_cat(recall_ref[chunk, seq]), state_parts)
            delta_parts = parts(delta)
            read = mul(from_cat(query_ref[chunk, seq]), state_parts)
            read = read + mul(from_cat(plain_ref[chunk, seq]), delta_parts)
            total = jnp.exp(run_ref[chunk, seq][0:1, size - 1 : size])
            following.append(
                total * state + mul(from_cat(write_ref[chunk, seq]), delta_parts)
            )
            delta_ref[chunk, seq] = delta
            mixed_ref[chunk, seq] = read
            scale = lax.rsqrt(jnp.mean(read * read, axis=1, keepdims=True) + 1e-05)
            gate = gate_ref[chunk, seq, :, :DV]
            headed = read * scale * gain_ref[...] * (gate * jax.nn.sigmoid(gate))
            headed_ref[chunk, seq] = headed.astype(bf16)
        return tuple(following)

    final = lax.fori_loop(0, chunks, advance, tuple(state_ref[seq] for seq in range(seqs)))
    for seq in range(seqs):
        end_ref[seq] = final[seq]


def backward_kernel(
    conv_ref, gate_ref, run_ref, taps_ref, gain_ref, halo_ref, d_headed_ref, mixed_ref,
    inverse_ref, scores_ref, delta_ref, starts_ref, d_end_ref, d_after_ref,
    d_all_ref, grad_taps_ref, grad_gain_ref, d_start_ref, d_before_ref,
    rows_ref, d_mixed_ref, hold_ref, carry_ref, base_ref, back_ref, d_target_ref, d_state_ref,
    d_conv_ref,
):
    chunks, seqs, size, _ = conv_ref.shape
    rows, cols = iotas(size)

    def pieces(chunk, seq, slot):
        summed = conv_rows(conv_ref, halo_ref, rows_ref, taps_ref, chunk, seq, slot)
        logistic = jax.nn.sigmoid(summed)
        active = summed * logistic
        query = active[:, :DK]
        raw = active[:, DK : 2 * DK]
        shrink = lax.rsqrt(jnp.sum(raw * raw, axis=1, keepdims=True) + 1e-06)
        value = active[:, 2 * DK :]
        beta = jax.nn.sigmoid(gate_ref[chunk, seq, :, DV : DV + 1])
        slope = logistic * (1.0 + summed * (1.0 - logistic))
        return slope, query, raw * shrink, shrink, value, beta

    grad_gain_ref[...] = jnp.zeros_like(grad_gain_ref)
    grad_taps_ref[...] = jnp.zeros_like(grad_taps_ref)

    def prepare(chunk, _):
        for seq in range(seqs):
            _, query, key, _, _, beta = pieces(chunk, seq, seq)
            _, growth, fade, _ = decays(run_ref, chunk, seq, rows, cols)
            mixed = mixed_ref[chunk, seq]
            d_headed = d_headed_ref[chunk, seq]
            gate = gate_ref[chunk, seq, :, :DV]
            logistic = jax.nn.sigmoid(gate)
            scale = lax.rsqrt(jnp.mean(mixed * mixed, axis=1, keepdims=True) + 1e-05)
            normed = mixed * scale
            swish = gate * logistic
            inner = d_headed * gain_ref[...] * swish
            d_mixed = scale * (inner - normed * jnp.mean(normed * inner, axis=1, keepdims=True))
            grad_gain_ref[...] += jnp.sum(d_headed * normed * swish, axis=0, keepdims=True)
            d_gate = d_headed * gain_ref[...] * normed * logistic * (1.0 + gate * (1.0 - logistic))
            d_all_ref[chunk, seq, :, 2 * DK + DV : 2 * DK + 2 * DV] = d_gate.astype(bf16)
            d_mixed_ref[chunk, seq] = d_mixed
            d_mixed_parts = parts(d_mixed)
            inverse_parts = from_cat(inverse_ref[chunk, seq])
            scored = mul(from_cat(scores_ref[chunk, seq]), d_mixed_parts)
            base_ref[chunk, seq] = mul(inverse_parts, parts(scored))
            hold_ref[chunk, seq] = cat_parts(mul(inverse_parts, parts(fade * key)))
            back_ref[chunk, seq] = mul(parts((growth * query).T), d_mixed_parts)
            carry_ref[chunk, seq] = cat_parts((beta * growth * key).T)
        return 0

    lax.fori_loop(0, chunks, prepare, 0)

    def advance(step, d_states):
        chunk = chunks - 1 - step
        following = []
        for seq in range(seqs):
            d_state = d_states[seq]
            d_state_ref[chunk, seq] = d_state
            d_target = base_ref[chunk, seq] + mul(from_cat(hold_ref[chunk, seq]), parts(d_state))
            d_target_ref[chunk, seq] = d_target
            total = jnp.exp(run_ref[chunk, seq][0:1, size - 1 : size])
            back = mul(from_cat(carry_ref[chunk, seq]), parts(d_target))
            following.append(total * d_state + back_ref[chunk, seq] - back)
        return tuple(following)

    first = lax.fori_loop(0, chunks, advance, tuple(d_end_ref[seq] for seq in range(seqs)))
    for seq in range(seqs):
        d_start_ref[seq] = first[seq]
        d_conv_ref[seq, size:, :] = d_after_ref[seq]

    def finish(step, _):
        chunk = chunks - 1 - step
        for seq in range(seqs):
            slope, query, key, shrink, value, beta = pieces(chunk, seq, seq)
            decay_mat, growth, fade, _ = decays(run_ref, chunk, seq, rows, cols)
            key_parts = parts(key)
            query_parts = parts(query)
            gram = mul_t(key_parts, key_parts) * decay_mat
            d_target = d_target_ref[chunk, seq]
            delta_parts = parts(delta_ref[chunk, seq])
            start_parts = parts(starts_ref[chunk, seq])
            both = parts(jnp.concatenate([d_target, d_mixed_ref[chunk, seq]], 0))
            on_delta = mul_t(both, delta_parts)
            on_state = mul_t(both, start_parts)
            d_lower = jnp.where(rows > cols, -on_delta[:size], 0.0)
            d_scores = on_delta[size:] * decay_mat
            through = on_state[:size]
            d_gram = d_lower * decay_mat * beta
            d_query = growth * on_state[size:] + mul(parts(d_scores), key_parts)
            d_key = mul(parts(d_scores.T), query_parts)
            d_key = d_key + mul(parts(d_gram + d_gram.T), key_parts)
            d_key = d_key + fade * mul_t(delta_parts, parts(d_state_ref[chunk, seq]))
            d_key = d_key - (beta * growth) * through
            d_beta = (
                jnp.sum(d_target * value, axis=1, keepdims=True)
                - growth * jnp.sum(key * through, axis=1, keepdims=True)
                + jnp.sum(d_lower * gram, axis=1, keepdims=True)
            )
            d_raw = shrink * (d_key - key * jnp.sum(key * d_key, axis=1, keepdims=True))
            d_conv = jnp.concatenate([d_query, d_raw, beta * d_target], 1) * slope
            d_conv_ref[seq, :size, :] = d_conv
            d_in = None
            for tap in range(CONV):
                start = HALO - (CONV - 1) + tap
                grad_taps_ref[tap : tap + 1, :] += jnp.sum(
                    d_conv * rows_ref[seq, start : start + size, :], axis=0, keepdims=True
                )
                shift = CONV - 1 - tap
                term = d_conv_ref[seq, shift : shift + size, :] * taps_ref[tap : tap + 1, :]
                d_in = term if d_in is None else d_in + term
            d_conv_ref[seq, size:, :] = d_conv[:8, :]
            d_all_ref[chunk, seq, :, : 2 * DK + DV] = d_in.astype(bf16)
            d_logit = d_beta * beta * (1.0 - beta)
            lane = lax.broadcasted_iota(jnp.int32, (size, 128), 1)
            d_all_ref[chunk, seq, :, 2 * DK + 2 * DV :] = jnp.where(
                lane == 0, d_logit, 0.0
            ).astype(bf16)
        return 0

    lax.fori_loop(0, chunks, finish, 0)
    for seq in range(seqs):
        d_before_ref[seq] = d_conv_ref[seq, size:, :]


VMEM_LIMIT = 60 * 1024 * 1024


def whole(count):
    return [pl.BlockSpec(memory_space=pltpu.VMEM)] * count


def forward_rule(conv_in, gate_beta, run, taps, gain, state, halo):
    chunks, seqs, size, width = conv_in.shape
    lead = (chunks, seqs)
    shape = jax.ShapeDtypeStruct
    return pl.pallas_call(
        forward_kernel,
        name="delta_forward",
        out_shape=(
            shape(lead + (size, DV), bf16),
            shape(lead + (size, DV), f32),
            shape(lead + (size, 2 * size), bf16),
            shape(lead + (size, 2 * size), bf16),
            shape(lead + (size, DV), f32),
            shape(lead + (DK, DV), f32),
            shape((seqs, DK, DV), f32),
        ),
        in_specs=whole(7),
        out_specs=tuple(whole(7)),
        scratch_shapes=[
            pltpu.VMEM((seqs, HALO + size, width), f32),
            pltpu.VMEM(lead + (size, 2 * DK), bf16),
            pltpu.VMEM(lead + (size, DV), f32),
            pltpu.VMEM(lead + (size, 2 * DK), bf16),
            pltpu.VMEM(lead + (DK, 2 * size), bf16),
            pltpu.VMEM(lead + (size, 2 * size), bf16),
        ],
        compiler_params=pltpu.CompilerParams(vmem_limit_bytes=VMEM_LIMIT),
    )(conv_in, gate_beta, run, taps, gain, state, halo)


def backward_rule(conv_in, gate_beta, run, taps, gain, halo, d_headed, saved, d_end, d_after):
    chunks, seqs, size, width = conv_in.shape
    lead = (chunks, seqs)
    shape = jax.ShapeDtypeStruct
    return pl.pallas_call(
        backward_kernel,
        name="delta_backward",
        out_shape=(
            shape(lead + (size, 2 * DK + 2 * DV + 128), bf16),
            shape((8, width), f32),
            shape((1, DV), f32),
            shape((seqs, DK, DV), f32),
            shape((seqs, 8, width), f32),
        ),
        in_specs=whole(14),
        out_specs=tuple(whole(5)),
        scratch_shapes=[
            pltpu.VMEM((seqs, HALO + size, width), f32),
            pltpu.VMEM(lead + (size, DV), f32),
            pltpu.VMEM(lead + (size, 2 * DK), bf16),
            pltpu.VMEM(lead + (DK, 2 * size), bf16),
            pltpu.VMEM(lead + (size, DV), f32),
            pltpu.VMEM(lead + (DK, DV), f32),
            pltpu.VMEM(lead + (size, DV), f32),
            pltpu.VMEM(lead + (DK, DV), f32),
            pltpu.VMEM((seqs, size + 8, width), f32),
        ],
        compiler_params=pltpu.CompilerParams(vmem_limit_bytes=VMEM_LIMIT),
    )(conv_in, gate_beta, run, taps, gain, halo, d_headed, *saved, d_end, d_after)


def product(left, right):
    return jnp.dot(left, right, preferred_element_type=f32)


def contract_rows(left, right):
    return dot(left, right, ((0,), (0,)))


def contract_cols(left, right):
    return dot(left, right, ((1,), (1,)))


def passed_along(array, axis, by):
    peers = lax.axis_size(axis)
    pairs = [(i, i + by) for i in range(peers) if 0 <= i + by < peers]
    return lax.ppermute(array, axis, pairs)


def rms_scale(values):
    return lax.rsqrt(jnp.mean(values * values, axis=-1, keepdims=True) + 1e-05)


def rms_back(values, scale, gain, d_normed):
    normed = values * scale
    pulled = d_normed * gain
    d_values = scale * (pulled - normed * jnp.mean(normed * pulled, axis=-1, keepdims=True))
    return d_values, jnp.sum(d_normed * normed, axis=0)


def shards(
    inputs,
    cotangent,
    decay,
    w_query,
    w_key,
    w_value,
    w_gate_out,
    w_out,
    w_ffn_gate,
    w_ffn_up,
    w_ffn_down,
    w_beta,
    conv_weight,
    norm_in,
    norm_mid,
    norm_head,
):
    seqs, size, model = inputs.shape
    rows = seqs * size
    peers = lax.axis_size("seq")
    stages = peers // H
    groups = None
    if stages > 1:
        groups = [[stage * H + head for head in range(H)] for stage in range(stages)]
    head = lax.rem(lax.axis_index("seq"), H)
    all_rows = H * rows
    hidden_all = w_ffn_gate.shape[1]
    share = -(-hidden_all // (H * 128)) * 128

    def gather_rows(local):
        return lax.all_gather(local, "seq", axis_index_groups=groups).reshape(
            (all_rows,) + local.shape[1:]
        )

    def scatter_rows(partial):
        blocks = partial.astype(bf16).reshape(H, rows, model)
        swapped = lax.all_to_all(blocks, "seq", 0, 0, axis_index_groups=groups, tiled=True)
        return jnp.sum(swapped.astype(f32), axis=0)

    def own_columns(weight, width):
        return lax.dynamic_slice_in_dim(weight, head * width, width, axis=1)

    def own_hidden(weight):
        start = jnp.minimum(head * share, hidden_all - share)
        piece = lax.dynamic_slice_in_dim(weight, start, share, axis=1)
        lane = lax.broadcasted_iota(jnp.int32, piece.shape, 1)
        return jnp.where(lane + start >= head * share, piece, jnp.zeros_like(piece))

    def gather_weight(local):
        return lax.all_gather(local, "wt", axis=0, tiled=True)

    flat_in = inputs.reshape(rows, model).astype(f32)
    scale_in = rms_scale(flat_in)
    normed_in = gather_rows((flat_in * scale_in * norm_in).astype(bf16))

    mixer_w = gather_weight(
        jnp.concatenate(
            [
                own_columns(w_query, DK),
                own_columns(w_key, DK),
                own_columns(w_value, DV),
                own_columns(w_gate_out, DV),
            ],
            axis=1,
        )
    )
    beta_w = jnp.pad(own_columns(w_beta, 1), ((0, 0), (0, 127)))
    mixer_w = jnp.concatenate([mixer_w, beta_w], axis=1)
    full_out = gather_weight(w_out)
    ffn_w = gather_weight(
        jnp.concatenate(
            [own_hidden(w_ffn_gate), own_hidden(w_ffn_up), own_hidden(w_ffn_down)], axis=1
        )
    )
    gate_w, up_w, down_w = ffn_w[:, :share], ffn_w[:, share : 2 * share], ffn_w[:, 2 * share :]
    upstream_own = cotangent.reshape(rows, model)
    upstream = gather_rows(upstream_own)

    own_decay = lax.all_gather(decay, "seq", axis_index_groups=groups)
    own_decay = lax.dynamic_index_in_dim(own_decay, head, axis=3, keepdims=False)
    run = jnp.cumsum(jnp.log(own_decay), axis=-1)
    run = jnp.broadcast_to(run[:, :, None, :], (H, seqs, 8, size))
    taps = jnp.concatenate(
        [
            own_columns(conv_weight[:, : H * DK], DK),
            own_columns(conv_weight[:, H * DK : 2 * H * DK], DK),
            own_columns(conv_weight[:, 2 * H * DK :], DV),
        ],
        axis=1,
    )
    taps = jnp.pad(taps, ((0, 8 - CONV), (0, 0)))
    gain = norm_head[None, :]

    conv_width = 2 * DK + DV
    lead = (H, seqs, size)
    conv_in = product(normed_in, mixer_w[:, :conv_width]).astype(bf16).reshape(lead + (-1,))
    gate_beta = product(normed_in, mixer_w[:, conv_width:]).reshape(lead + (-1,))

    state = jnp.zeros((seqs, DK, DV), f32)
    halo = jnp.zeros((seqs, HALO, conv_width), bf16)
    if stages > 1:
        halo = passed_along(conv_in[H - 1, :, size - HALO :], "seq", H)
    for stage in range(stages):
        headed, *saved, ending = forward_rule(conv_in, gate_beta, run, taps, gain, state, halo)
        if stage < stages - 1:
            state = passed_along(ending, "seq", H)

    own_headed = lax.all_to_all(
        headed.reshape(H, rows, DV), "seq", 0, 0, axis_index_groups=groups, tiled=True
    )
    own_headed = jnp.swapaxes(own_headed, 0, 1).reshape(rows, H * DV)
    residual = flat_in + contract_cols(own_headed, full_out)
    scale_mid = rms_scale(residual)
    normed_mid = gather_rows((residual * scale_mid * norm_mid).astype(bf16))

    gate_pre = product(normed_mid, gate_w)
    up_pre = product(normed_mid, up_w)
    logistic = jax.nn.sigmoid(gate_pre)
    swish = gate_pre * logistic
    hidden = (swish * up_pre).astype(bf16)
    d_hidden = product(upstream, down_w)
    d_gate = (d_hidden * up_pre * logistic * (1.0 + gate_pre * (1.0 - logistic))).astype(bf16)
    d_up = (d_hidden * swish).astype(bf16)
    d_normed_mid = scatter_rows(contract_cols(d_gate, gate_w) + contract_cols(d_up, up_w))
    ffn_out = lax.psum_scatter(
        contract_cols(hidden, down_w).astype(bf16),
        "seq",
        scatter_dimension=0,
        axis_index_groups=groups,
        tiled=True,
    )
    layer_out = (residual + ffn_out.astype(f32)).astype(bf16).reshape(inputs.shape)

    d_from_mid, grad_mid = rms_back(residual, scale_mid, norm_mid, d_normed_mid)
    d_residual = upstream_own.astype(f32) + d_from_mid
    d_branch = gather_rows(d_residual.astype(bf16))
    out_w = lax.dynamic_slice_in_dim(full_out, head * DV, DV, axis=1)
    d_headed = product(d_branch, out_w).reshape(lead + (DV,))

    d_end = jnp.zeros((seqs, DK, DV), f32)
    d_after = jnp.zeros((seqs, 8, conv_width), f32)
    for stage in range(stages):
        d_all, grad_taps, grad_gain, d_start, d_before = backward_rule(
            conv_in, gate_beta, run, taps, gain, halo, d_headed, saved, d_end, d_after
        )
        if stage < stages - 1:
            d_end = passed_along(d_start, "seq", -H)
            d_after = passed_along(d_before, "seq", -H)
    d_all = d_all.reshape(all_rows, -1)

    def reduce_grads(partial):
        summed = lax.psum_scatter(
            partial.astype(bf16), "wt", scatter_dimension=0, tiled=True
        )
        spread = lax.all_gather(summed, "seq")
        spread = spread.reshape((stages, H) + summed.shape).astype(f32)
        return jnp.sum(spread, axis=0)

    def joined(spread):
        return jnp.swapaxes(spread, 0, 1).reshape(spread.shape[1], -1)

    def joined_hidden(spread):
        flat = joined(spread)
        kept = (H - 1) * share
        return jnp.concatenate([flat[:, :kept], flat[:, kept + H * share - hidden_all :]], axis=1)

    ffn_grads = reduce_grads(
        jnp.concatenate(
            [
                contract_rows(normed_mid, d_gate),
                contract_rows(normed_mid, d_up),
                contract_rows(upstream, hidden),
            ],
            axis=1,
        )
    )
    mixer_partial = contract_rows(normed_in, d_all)
    out_partial = contract_rows(d_branch, headed.reshape(all_rows, DV))
    width = conv_width + DV
    mixer_grads = reduce_grads(jnp.concatenate([mixer_partial[:, :width], out_partial], axis=1))

    d_normed_in = scatter_rows(contract_cols(d_all, mixer_w))
    d_from_in, _ = rms_back(flat_in, scale_in, norm_in, d_normed_in)
    grad_input = (d_residual + d_from_in).reshape(inputs.shape)

    grad_in_part = jnp.sum(mixer_partial * mixer_w.astype(f32), axis=1) / norm_in
    small = jnp.concatenate(
        [
            grad_taps[:CONV].reshape(-1),
            mixer_partial[:, width],
            grad_gain[0],
            grad_mid,
            grad_in_part,
        ]
    )
    small = lax.all_gather(small.reshape(-1, 128), ("seq", "wt")).reshape(
        stages, H, lax.axis_size("wt"), -1
    )
    small = jnp.sum(small, axis=(0, 2))
    bounds = [CONV * conv_width, model, DV, model, model]
    ends = []
    for bound in bounds:
        ends.append(bound + (ends[-1] if ends else 0))
    taps_part = small[:, : ends[0]].reshape(H, CONV, conv_width)
    grad_conv = jnp.concatenate(
        [
            joined(taps_part[:, :, :DK]),
            joined(taps_part[:, :, DK : 2 * DK]),
            joined(taps_part[:, :, 2 * DK :]),
        ],
        axis=1,
    )
    grad_beta = small[:, ends[0] : ends[1]].T
    shared = jnp.sum(small[:, ends[1] :], axis=0)
    grad_head, grad_mid, grad_in = (
        shared[:DV],
        shared[DV : DV + model],
        shared[DV + model :],
    )
    return (
        layer_out,
        grad_input,
        joined(mixer_grads[:, :, :DK]),
        joined(mixer_grads[:, :, DK : 2 * DK]),
        joined(mixer_grads[:, :, 2 * DK : conv_width]),
        joined(mixer_grads[:, :, conv_width:width]),
        joined(mixer_grads[:, :, width:]),
        joined_hidden(ffn_grads[:, :, :share]),
        joined_hidden(ffn_grads[:, :, share : 2 * share]),
        joined_hidden(ffn_grads[:, :, 2 * share :]),
        grad_beta,
        grad_conv,
        grad_in,
        grad_mid,
        grad_head,
    )


def solution(mesh):
    rows = P("wt", "seq", None)
    cut = P("wt", None)
    in_specs = (rows,) * 3 + (cut,) * 8 + (P(),) * 5
    out_specs = (rows,) * 2 + (cut,) * 8 + (P(),) * 5
    return jax.shard_map(shards, mesh=mesh, in_specs=in_specs, out_specs=out_specs, check_vma=False)
```

time: 3440 us -> 723 us (0.21)
  waiting for transfers between devices: 1850 us -> 260 us
  other arithmetic: 906 us -> 38.1 us
  matrix products: 336 us -> 76.6 us
  starting transfers between devices: 157 us -> 9.01 us
  blocking collectives: 43.1 us -> 151 us
  Pallas kernels: 0 us -> 93.2 us
  local copies, waits for them, and re-layouts: 114 us -> 76.6 us
    reduce_scatter x2 -> x3, waiting for transfers between devices: 1090 us -> 37.3 us  [the longest x2 37.3 us: reduce_grads(): lax.psum_scatter(partial.astype(bf16), 'wt', scatter_dimension=0, tiled=T...]
    another operation x52 -> x1, other arithmetic: 810 us -> 0.59 us  [shards(): run = jnp.cumsum(jnp.log(own_decay), axis=-1)]
    psum x2 -> x0, waiting for transfers between devices: 278 us -> none  [the longest x1 168 us: shards(): mixer_sum, ffn_sum = lax.psum((mixer_share, ffn_share), 'seq')]
    dot_general x107 -> x16, matrix products: 307 us -> 76.6 us  [the longest x10 40.4 us: dot(): lax.dot_general(left, right, (dims, ((), ())), preferred_element_type=f32)]
    ppermute x16 -> x0, waiting for transfers between devices: 230 us -> none  [passed_along(): return lax.ppermute(array, axis, pairs)]
    ppermute x16 -> x0, starting transfers between devices: 156 us -> none  [passed_along(): return lax.ppermute(array, axis, pairs)]
    pallas_call x0 -> x2, Pallas kernels: none -> 93.2 us  [the longest x1 54.4 us: forward_rule(): pl.pallas_call(forward_kernel, name='delta_forward', out_shape=(shape(lea...]
    all_gather x0 -> x2, blocking collectives: none -> 85.7 us  [the longest x1 75 us: shards(): lax.all_gather(small.reshape(-1, 128), ('seq', 'wt'))]
  transfers between devices with their start and end apart: 28 -> 14, of which waited for: 23 -> 10; matrix products, arithmetic and copies ran while one was open for 22% -> 19% of each run, Pallas kernels for 0% -> 13%
where the time goes in v1:
time: 723 us; the launch traced here: 720 us
  waiting for transfers between devices  260 us (36%)
  blocking collectives  151 us (21%)
  Pallas kernels  93.2 us (13%)
  local copies, waits for them, and re-layouts  76.6 us (11%)
  matrix products  76.6 us (11%)
  other arithmetic  38.1 us (5%)
  between operations  15.2 us (2%)
  starting transfers between devices  9.01 us (1%)
    all_gather x4, waiting for transfers between devices, gather_rows(): lax.all_gather(local, 'seq', axis_index_groups=groups)  126 us
    all_gather x1, blocking collectives, shards(): lax.all_gather(small.reshape(-1, 128), ('seq', 'wt'))  75 us
    all_gather x3, waiting for transfers between devices, gather_weight(): return lax.all_gather(local, 'wt', axis=0, tiled=True)  69.5 us
    all_to_all x1, blocking collectives, scatter_rows(): lax.all_to_all(blocks, 'seq', 0, 0, axis_index_groups=groups, tiled=True)  65.2 us
    pallas_call x1, Pallas kernels, forward_rule(): pl.pallas_call(forward_kernel, name='delta_forward', out_shape=(shape(lea...  54.4 us
    dot_general x10, matrix products, dot(): lax.dot_general(left, right, (dims, ((), ())), preferred_element_type=f32)  40.4 us
    pallas_call x1, Pallas kernels, backward_rule(): pl.pallas_call(backward_kernel, name='delta_backward', out_shape=(shape(l...  38.8 us
    reduce_scatter x2, waiting for transfers between devices, reduce_grads(): lax.psum_scatter(partial.astype(bf16), 'wt', scatter_dimension=0, tiled=T...  37.3 us
  transfers between devices with their start and end apart: 14, of which 10 were waited for; matrix products, arithmetic and copies ran while one was open for 19% of the time, Pallas kernels for 13%

profile of v1, /device:TPU:0, one launch (start us, length us, event | category | flops | bytes accessed | tf_op | source)
XLA Modules:
  0.0 719.9 jit_solution(11976804025768774216)
XLA Ops:
  16.3 10.7 %all-gather = f32[16,128,8]{1,2,0:T(8,128)S(1)} all-gather(f32[2,128,8]{1,2,0:T(8,128)S(1)} %copy-done.24), channel_id=2, replica_groups=mesh['seq'=8,'wt'=4] {'seq'}, dimensions={0}, use_global_device_ids=true | all-gather | bytes 73728 | tf_op jit(solution)/shard_map/all_gather | solution.py:463
  28.5 21.5 %all-gather.17.cloned.1.call-done = bf16[1024,768]{1,0:T(8,128)(2,1)} async-done(((bf16[256,768]{1,0:T(8,128)(2,1)}), bf16[1024,768]{1,0:T(8,128)(2,1)}) %all-gather.17.cloned.1.call-update) | async-done | bytes 1572880 | tf_op jit(solution)/shard_map/all_gather | solution.py:434
  52.8 35.3 %all-gather.15.cloned.1.call-done = bf16[8,256,1024]{2,1,0:T(8,128)(2,1)} async-done(((bf16[1,256,1024]{2,1,0:T(8,128)(2,1)}), bf16[8,256,1024]{2,1,0:T(8,128)(2,1)}) %all-gather.15.cloned.1.call-update) | async-done | bytes 4194320 | tf_op jit(solution)/shard_map/all_gather | solution.py:415
  88.1 6.5 fusion.15.gate_ref
  94.6 3.7 convolution_convert_fusion.2
  100.3 54.4 %delta_forward.1 = (bf16[8,2,128,256]{3,2,1,0:T(8,128)(2,1)}, f32[8,2,128,256]{3,2,1,0:T(8,128)}, bf16[8,2,128,256]{3,2,1,0:T(8,128)(2,1)}, bf16[8,2,128,256]{3,...) custom-call(bf16[8,2,128,512]{3,2,1,0:T(8,128)(2,1)} %bitcast.179, ...), custom_call_target="tpu_custom_call" | custom-call | tf_op jit(solution)/shard_map/delta_forward/pallas_call | solution.py:298
  160.6 9.9 %all-gather.19.cloned.1.call-done = bf16[1024,2048]{1,0:T(8,128)(2,1)} async-done(((bf16[256,2048]{1,0:T(8,128)(2,1)}), bf16[1024,2048]{1,0:T(8,128)(2,1)}) %all-gather.19.cloned.1.call-update) | async-done | bytes 4194320 | tf_op jit(solution)/shard_map/all_gather | solution.py:434
  170.5 5.4 all-to-all-done
  176.9 4.6 multiply_reduce_fusion.4
  183.4 38.1 %all-gather.21.cloned.1.call-done = bf16[1024,1152]{1,0:T(8,128)(2,1)} async-done(((bf16[256,1152]{1,0:T(8,128)(2,1)}), bf16[1024,1152]{1,0:T(8,128)(2,1)}) %all-gather.21.cloned.1.call-update) | async-done | bytes 2359312 | tf_op jit(solution)/shard_map/all_gather | solution.py:434
  221.5 37.9 %all-gather.25.cloned.1.call-done = bf16[2048,1024]{1,0:T(8,128)(2,1)} async-done(((bf16[256,1024]{1,0:T(8,128)(2,1)}), bf16[2048,1024]{1,0:T(8,128)(2,1)}) %all-gather.25.cloned.1.call-update) | async-done | bytes 4194320 | tf_op jit(solution)/shard_map/all_gather | solution.py:415
  259.4 6.7 fusion.20
  266.0 5.1 fusion.24
  271.2 26.7 %all-gather.23.cloned.1.call-done = bf16[8,256,1024]{2,1,0:T(8,128)(2,1)} async-done(((bf16[1,256,1024]{2,1,0:T(8,128)(2,1)}), bf16[8,256,1024]{2,1,0:T(8,128)(2,1)}) %all-gather.23.cloned.1.call-update) | async-done | bytes 4194320 | tf_op jit(solution)/shard_map/all_gather | solution.py:415
  297.9 9.3 %fusion.4 = (bf16[2048,384]{1,0:T(8,128)(2,1)S(1)}, bf16[2048,384]{1,0:T(8,128)(2,1)S(1)}, bf16[2048,384]{1,0:T(8,128)(2,1)}) fusion(f32[2048,384]{1,0:T(8,128)} %fusion.24, f32[2048,384]{1,0:T(8,128)} %fusion.20, bf16[2048,1024]{1,0:T(8,128)(2,1)} %bitcast.216, bf16[1024,1152]{1,0:T(8,128)(2,1)} %all-gather.21.cloned.1.call-done), kind=kOutput, calls=%fused_computation.17 | convolution fusion | flops 1622409216 | bytes 15990784 | tf_op jit(solution)/shard_map/dot_general | solution.py:356
  312.1 65.2 %all_to_all.15 = bf16[8,256,1024]{2,1,0:T(8,128)(2,1)S(1)} all-to-all(bf16[8,256,1024]{2,1,0:T(8,128)(2,1)S(1)} %bitcast.168), channel_id=1, replica_groups=mesh['seq'=8,'wt'=4] {'seq'}, dimensions={0} | all-to-all | bytes 8388608 | tf_op jit(solution)/shard_map/all_to_all | solution.py:421
  380.3 4.6 fusion.7
  390.4 25.8 %all-gather.27.cloned.1.call-done = bf16[2048,1024]{1,0:T(8,128)(2,1)} async-done(((bf16[256,1024]{1,0:T(8,128)(2,1)}), bf16[2048,1024]{1,0:T(8,128)(2,1)}) %all-gather.27.cloned.1.call-update) | async-done | bytes 4194320 | tf_op jit(solution)/shard_map/all_gather | solution.py:415
  416.2 4.9 fusion.26.d_headed_ref
  421.7 38.8 %delta_backward.1 = (bf16[8,2,128,896]{3,2,1,0:T(8,128)(2,1)}, f32[8,512]{1,0:T(8,128)}, f32[1,256]{1,0:T(1,128)}, f32[2,128,256]{2,1,0:T(8,128)}, f32[2,8,512]{2,1,0:T(8,128)}) custom-call(bf16[8,2,128,512]{3,2,1,0:T(8,128)(2,1)} %bitcast.180, f32[8,2,128,384]{3,2,1,0:T(8,128)} %fusion.15.gate_ref, f32[8,2,8,128]{3,2,1,0:T(8,128)} %broadcast_in_dim.8.run_ref, ...), custom_call_target="tpu_custom_call" | custom-call | tf_op jit(solution)/shard_map/delta_backward/pallas_call | solution.py:328
  460.5 7.1 fusion.36
  473.1 6.1 convolution_convert_fusion
  479.2 37.3 %reduce-scatter.6.cloned.1.call-done = bf16[256,1024]{0,1:T(8,128)(2,1)} async-done(((bf16[1024,1024]{0,1:T(8,128)(2,1)}), bf16[256,1024]{0,1:T(8,128)(2,1)}) %reduce-scatter.6.cloned.1.call-update) | async-done | bytes 524304 | tf_op jit(solution)/shard_map/reduce_scatter | solution.py:536
  516.5 5.0 copy.71
  521.6 8.2 %convolution_convert_fusion.1 = bf16[2048,1024]{1,0:T(8,128)(2,1)} fusion(bf16[2048,896]{1,0:T(8,128)(2,1)} %bitcast.219, bf16[1024,1]{1,0:T(8,128)(2,1)S(1)} %copy.75, bf16[1024,768]{1,0:T(8,128)(2,1)S(1)} %copy-done.11), kind=kOutput, calls=%fused_computation.4 | convolution fusion | flops 3765698560 | bytes 9439232 | tf_op jit(solution)/shard_map/dot_general | solution.py:24
  529.8 4.7 all-to-all-start.2
  537.0 75.0 %all_gather.64 = f32[32,42,128]{2,1,0:T(8,128)S(1)} all-gather(f32[1,42,128]{2,1,0:T(8,128)S(1)} %bitcast.207), channel_id=1, replica_groups=mesh['seq'=8,'wt'=4] {'seq','wt'}, dimensions={0}, use_global_device_ids=true | all-gather | bytes 709632 | tf_op jit(solution)/shard_map/all_gather | solution.py:580
  618.8 4.6 copy.83
  626.9 3.6 copy.70
  634.8 3.7 copy.69
  662.6 20.6 %all-gather.29.cloned.1.call-done = bf16[2048,1024]{0,1:T(8,128)(2,1)} async-done(((bf16[256,1024]{0,1:T(8,128)(2,1)}), bf16[2048,1024]{0,1:T(8,128)(2,1)}) %all-gather.29.cloned.1.call-update) | async-done | bytes 4194320 | tf_op jit(solution)/shard_map/all_gather | solution.py:539
  686.4 4.1 copy.77
  (188 shorter events, 109.8 us)
Async XLA Ops:
  7.2 19.8 %copy-start = (bf16[1024,8]{0,1:T(8,128)(2,1)S(1)}, bf16[1024,8]{0,1:T(8,128)(2,1)}, u32[]{:S(2)}) copy-start(bf16[1024,8]{0,1:T(8,128)(2,1)} %param.27) | copy-start | bytes 49156
  7.2 5.0 copy-start.23
  7.2 42.8 %all-gather.17.cloned.1.call-start = ((), (), s32[]{:S(2)}) async-start(), calls=%async_computation.7 | async-start | bytes 1966080 | tf_op jit(solution)/shard_map/all_gather | solution.py:434
  10.0 78.1 %all-gather.15.cloned.1.call-start = ((), (), s32[]{:S(2)}) async-start(), calls=%async_computation.6 | async-start | bytes 4718592 | tf_op jit(solution)/shard_map/all_gather | solution.py:415
  11.4 4.9 slice-start.1
  11.4 4.9 copy-start.24
  12.2 15.7 %copy-start.21 = (f32[4,4096]{1,0:T(4,128)S(1)}, f32[4,4096]{1,0:T(4,128)}, u32[]{:S(2)}) copy-start(f32[4,4096]{1,0:T(4,128)} %param.28) | copy-start | bytes 196612
  13.2 157.3 %all-gather.19.cloned.1.call-start = ((), (), s32[]{:S(2)}) async-start(), calls=%async_computation.8 | async-start | bytes 5242880 | tf_op jit(solution)/shard_map/all_gather | solution.py:434
  13.9 207.6 %all-gather.21.cloned.1.call-start = ((), (), s32[]{:S(2)}) async-start(), calls=%async_computation.9 | async-start | bytes 2949120 | tf_op jit(solution)/shard_map/all_gather | solution.py:434
  88.1 6.5 copy-start.11
  88.1 6.5 copy-start.27
  157.0 18.9 %all-to-all-start = ((bf16[8,256,256]{1,2,0:T(8,128)(2,1)}), bf16[8,256,256]{1,2,0:T(8,128)(2,1)S(1)}, u32[]{:S(2)}, u32[]{:S(2)}) async-start(bf16[8,256,256]{1,2,0:T(8,128)(2,1)} %copy.61), calls=%async_computation | async-start | bytes 2097152 | tf_op jit(solution)/shard_map/all_to_all | solution.py:492
  160.5 98.8 %all-gather.25.cloned.1.call-start = ((), (), s32[]{:S(2)}) async-start(), calls=%async_computation.14 | async-start | bytes 4718592 | tf_op jit(solution)/shard_map/all_gather | solution.py:415
  176.8 4.6 copy-start.22
  181.4 197.1 %copy-start.4 = (f32[256,1024]{1,0:T(8,128)}, f32[256,1024]{1,0:T(8,128)S(1)}, u32[]{:S(2)}) copy-start(f32[256,1024]{1,0:T(8,128)S(1)} %get-tuple-element.60) | copy-start | bytes 3145732
  182.5 115.3 %all-gather.23.cloned.1.call-start = ((), (), s32[]{:S(2)}) async-start(), calls=%async_computation.11 | async-start | bytes 4718592 | tf_op jit(solution)/shard_map/all_gather | solution.py:415
  183.1 233.1 %all-gather.27.cloned.1.call-start = ((), (), s32[]{:S(2)}) async-start(), calls=%async_computation.15 | async-start | bytes 4718592 | tf_op jit(solution)/shard_map/all_gather | solution.py:415
  259.4 6.7 copy-start.28
  297.9 9.3 %copy-start.18 = (bf16[1024,1152]{1,0:T(8,128)(2,1)S(1)}, bf16[1024,1152]{1,0:T(8,128)(2,1)}, u32[]{:S(2)}) copy-start(bf16[1024,1152]{1,0:T(8,128)(2,1)} %all-gather.21.cloned.1.call-done) | copy-start | bytes 7077892
  380.3 92.2 %reduce-scatter.8.cloned.1.call-start = ((), (), s32[]{:S(2)}) async-start(), calls=%async_computation.13 | async-start | bytes 2949120 | tf_op jit(solution)/shard_map/reduce_scatter | solution.py:536
  380.3 4.6 copy-start.17
  380.3 4.6 copy-start.29
  390.4 126.1 %reduce-scatter.6.cloned.1.call-start = ((), (), s32[]{:S(2)}) async-start(), calls=%async_computation.12 | async-start | bytes 2621440 | tf_op jit(solution)/shard_map/reduce_scatter | solution.py:536
  460.5 7.3 %copy-start.30 = (bf16[2048,1024]{1,0:T(8,128)(2,1)S(1)}, bf16[2048,1024]{1,0:T(8,128)(2,1)}, u32[]{:S(2)}) copy-start(bf16[2048,1024]{1,0:T(8,128)(2,1)} %all-gather.27.cloned.1.call-done) | copy-start | bytes 12582916
  472.4 142.8 %all-gather.31.cloned.1.call-start = ((), (), s32[]{:S(2)}) async-start(), calls=%async_computation.17 | async-start | bytes 5308416 | tf_op jit(solution)/shard_map/all_gather | solution.py:539
  473.0 186.6 %reduce-scatter.4.cloned.1.call-start = ((), (), s32[]{:S(2)}) async-start(), calls=%async_computation.10 | async-start | bytes 4718592 | tf_op jit(solution)/shard_map/reduce_scatter | solution.py:509
  479.2 204.0 %all-gather.29.cloned.1.call-start = ((), (), s32[]{:S(2)}) async-start(), calls=%async_computation.16 | async-start | bytes 4718592 | tf_op jit(solution)/shard_map/all_gather | solution.py:539
  516.5 5.0 copy-start.25
  529.7 4.7 slice-start
  529.8 4.8 copy-start.26
  529.8 126.1 %all-to-all-start.2 = ((bf16[8,256,1024]{2,1,0:T(8,128)(2,1)}), bf16[8,256,1024]{2,1,0:T(8,128)(2,1)}, u32[]{:S(2)}, u32[]{:S(2)}) async-start(bf16[8,256,1024]{2,1,0:T(8,128)(2,1)} %bitcast.186), calls=%async_computation.3 | async-start | bytes 8388608 | tf_op jit(solution)/shard_map/all_to_all | solution.py:421
  708.3 4.5 copy-start.1
  (15 other events, 36.4 us)
Sparse Core Ops, SparseCore 0:
  10.2 39.7 all-gather.16
  52.5 35.5 all-gather.14
  89.7 80.7 all-gather.18
  172.5 49.0 all-gather.20
  223.8 35.5 all-gather.24
  261.1 36.7 all-gather.22
  380.4 35.7 all-gather.26
  419.1 48.0 reduce-scatter.7
  472.5 43.8 reduce-scatter.5
  518.4 65.4 all-gather.30
  587.6 56.3 reduce-scatter.3
  645.7 37.4 all-gather.28

commit v2 on v1

v2 whole, which is shorter than its diff:
```python
import jax
import jax.numpy as jnp
from jax import lax
from jax.experimental import pallas as pl
from jax.experimental.pallas import tpu as pltpu
from jax.sharding import PartitionSpec as P

H = 8
DK = 128
DV = 256
CONV = 4
HALO = 16
WIDTH = 2 * DK + DV
VMEM_LIMIT = 60 * 1024 * 1024
bf16 = jnp.bfloat16
f32 = jnp.float32


def dot(left, right, dims):
    return lax.dot_general(left, right, (dims, ((), ())), preferred_element_type=f32)


def product(left, right):
    return dot(left, right, ((1,), (0,)))


def contract_rows(left, right):
    return dot(left, right, ((0,), (0,)))


def contract_cols(left, right):
    return dot(left, right, ((1,), (1,)))


def parts(values):
    high = values.astype(bf16)
    return high, (values - high.astype(f32)).astype(bf16)


def mul(left, right):
    (lh, ll), (rh, rl) = left, right
    wide = product(jnp.concatenate([lh, ll], 1), jnp.concatenate([rh, rh], 0))
    return wide + product(lh, rl)


def mul_t(left, right):
    (lh, ll), (rh, rl) = left, right
    wide = contract_cols(jnp.concatenate([lh, ll], 1), jnp.concatenate([rh, rh], 1))
    return wide + contract_cols(lh, rl)


def cat_parts(values):
    return jnp.concatenate(parts(values), 1)


def from_cat(both):
    half = both.shape[1] // 2
    return both[:, :half], both[:, half:]


def iotas(size):
    return (
        lax.broadcasted_iota(jnp.int32, (size, size), 0),
        lax.broadcasted_iota(jnp.int32, (size, size), 1),
    )


def unit_inverses(lowers, rows, cols):
    size = rows.shape[0]
    level = 0
    eye = jnp.where(rows == cols, 1.0, 0.0)
    inverses = [eye] * len(lowers)
    while (1 << level) < size:
        together = (rows >> (level + 1)) == (cols >> (level + 1))
        corner = together & (((rows >> level) & 1) == 1) & (((cols >> level) & 1) == 0)
        blocks = [jnp.where(corner, lower, 0.0) for lower in lowers]
        if level == 0:
            inverses = [inverse - block for inverse, block in zip(inverses, blocks)]
        else:
            wholes = [parts(inverse) for inverse in inverses]
            steps = [mul(parts(block), whole) for block, whole in zip(blocks, wholes)]
            steps = [mul(whole, parts(step)) for step, whole in zip(steps, wholes)]
            inverses = [inverse - step for inverse, step in zip(inverses, steps)]
        level += 1
    return inverses


def conv_rows(conv_ref, halo_ref, rows_ref, taps_ref, chunk, seq, slot):
    size = conv_ref.shape[2]
    before = conv_ref[jnp.maximum(chunk - 1, 0), seq, size - HALO :, :]
    before = jnp.where(chunk == 0, halo_ref[seq], before)
    rows_ref[slot, :HALO, :] = before.astype(f32)
    rows_ref[slot, HALO:, :] = conv_ref[chunk, seq].astype(f32)
    total = None
    for tap in range(CONV):
        start = HALO - (CONV - 1) + tap
        term = rows_ref[slot, start : start + size, :] * taps_ref[tap : tap + 1, :]
        total = term if total is None else total + term
    return total


def decays(run_ref, chunk, seq, rows, cols):
    size = rows.shape[0]
    run_row = run_ref[chunk, seq][0:1, :]
    run_col = jnp.sum(jnp.where(rows == cols, run_row, 0.0), axis=1, keepdims=True)
    spread = jnp.where(rows >= cols, run_col - run_row, 0.0)
    decay_mat = jnp.where(rows >= cols, jnp.exp(spread), 0.0)
    last = run_row[:, size - 1 : size]
    return decay_mat, jnp.exp(run_col), jnp.exp(last - run_col)


def units_of(first, count, seqs):
    return [(first + chunk, seq) for chunk in range(count) for seq in range(seqs)]


FORWARD_CHUNKS = 4


def forward_kernel(head_ref, *refs):
    block_refs, refs = refs[:H], refs[H:]
    (
        weight_ref, beta_ref, run_ref, taps_ref, gain_ref, state_ref, halo_ref,
        headed_ref, conv_ref, gate_ref, mixed_ref, inverse_ref, scores_ref, delta_ref, starts_ref,
        end_ref,
        rows_ref, recall_ref, target_ref, query_ref, write_ref, plain_ref,
    ) = refs
    chunks, seqs, size, _ = conv_ref.shape
    rows, cols = iotas(size)
    head = head_ref[0]

    for slot in range(H):
        chunk = slot ^ head
        block = block_refs[slot][...]
        conv = product(block, weight_ref[:, :WIDTH]).astype(bf16)
        gate = product(block, weight_ref[:, WIDTH : WIDTH + DV])
        beta = product(block, beta_ref[...])
        for seq in range(seqs):
            span = slice(seq * size, (seq + 1) * size)
            conv_ref[chunk, seq] = conv[span]
            gate_ref[chunk, seq, :, :DV] = gate[span]
            gate_ref[chunk, seq, :, DV:] = beta[span]

    def prepare(turn, _):
        units = units_of(turn * FORWARD_CHUNKS, FORWARD_CHUNKS, seqs)
        keys, betas, growths, lowers, mats = [], [], [], [], []
        for slot, (chunk, seq) in enumerate(units):
            summed = conv_rows(conv_ref, halo_ref, rows_ref, taps_ref, chunk, seq, slot)
            active = summed * jax.nn.sigmoid(summed)
            query = active[:, :DK]
            key = active[:, DK : 2 * DK]
            key = key * lax.rsqrt(jnp.sum(key * key, axis=1, keepdims=True) + 1e-06)
            beta = jax.nn.sigmoid(gate_ref[chunk, seq, :, DV : DV + 1])
            decay_mat, growth, fade = decays(run_ref, chunk, seq, rows, cols)
            target_ref[chunk, seq] = beta * active[:, 2 * DK :]
            query_ref[chunk, seq] = cat_parts(growth * query)
            write_ref[chunk, seq] = cat_parts((fade * key).T)
            recall_ref[chunk, seq] = cat_parts(beta * growth * key)
            key_parts = parts(key)
            gram = mul_t(key_parts, key_parts)
            lowers.append(jnp.where(rows > cols, beta * gram * decay_mat, 0.0))
            scores = mul_t(parts(query), key_parts) * decay_mat
            plain_ref[chunk, seq] = cat_parts(scores)
            scores_ref[chunk, seq] = cat_parts(scores.T)
        inverses = unit_inverses(lowers, rows, cols)
        for (chunk, seq), inverse in zip(units, inverses):
            inverse_parts = parts(inverse)
            recall = mul(inverse_parts, from_cat(recall_ref[chunk, seq]))
            recall_ref[chunk, seq] = cat_parts(recall)
            target_ref[chunk, seq] = mul(inverse_parts, parts(target_ref[chunk, seq]))
            inverse_ref[chunk, seq] = cat_parts(inverse.T)
        return 0

    lax.fori_loop(0, chunks // FORWARD_CHUNKS, prepare, 0)

    def advance(chunk, states):
        following = []
        for seq in range(seqs):
            state = states[seq]
            starts_ref[chunk, seq] = state
            state_parts = parts(state)
            delta = target_ref[chunk, seq] - mul(from_cat(recall_ref[chunk, seq]), state_parts)
            delta_parts = parts(delta)
            total = jnp.exp(run_ref[chunk, seq][0:1, size - 1 : size])
            following.append(
                total * state + mul(from_cat(write_ref[chunk, seq]), delta_parts)
            )
            delta_ref[chunk, seq] = delta
            read = mul(from_cat(query_ref[chunk, seq]), state_parts)
            read = read + mul(from_cat(plain_ref[chunk, seq]), delta_parts)
            mixed_ref[chunk, seq] = read
            scale = lax.rsqrt(jnp.mean(read * read, axis=1, keepdims=True) + 1e-05)
            gate = gate_ref[chunk, seq, :, :DV]
            headed = read * scale * gain_ref[...] * (gate * jax.nn.sigmoid(gate))
            headed_ref[chunk, seq] = headed.astype(bf16)
        return tuple(following)

    final = lax.fori_loop(0, chunks, advance, tuple(state_ref[seq] for seq in range(seqs)))
    for seq in range(seqs):
        end_ref[seq] = final[seq]


BACKWARD_CHUNKS = 2


def backward_kernel(
    head_ref,
    branch_ref, out_ref, conv_ref, gate_ref, run_ref, taps_ref, gain_ref, halo_ref, mixed_ref,
    inverse_ref, scores_ref, delta_ref, starts_ref, d_end_ref, d_after_ref,
    d_all_ref, grad_taps_ref, grad_gain_ref, d_start_ref, d_before_ref,
    rows_ref, d_headed_ref, hold_ref, carry_ref, base_ref, back_ref, d_target_ref, d_state_ref,
    d_conv_ref,
):
    chunks, seqs, size, _ = conv_ref.shape
    rows, cols = iotas(size)
    head = head_ref[0]

    def pieces(chunk, seq, slot):
        summed = conv_rows(conv_ref, halo_ref, rows_ref, taps_ref, chunk, seq, slot)
        logistic = jax.nn.sigmoid(summed)
        active = summed * logistic
        query = active[:, :DK]
        raw = active[:, DK : 2 * DK]
        shrink = lax.rsqrt(jnp.sum(raw * raw, axis=1, keepdims=True) + 1e-06)
        value = active[:, 2 * DK :]
        beta = jax.nn.sigmoid(gate_ref[chunk, seq, :, DV : DV + 1])
        slope = logistic * (1.0 + summed * (1.0 - logistic))
        return slope, query, raw * shrink, shrink, value, beta

    grad_gain_ref[...] = jnp.zeros_like(grad_gain_ref)
    grad_taps_ref[...] = jnp.zeros_like(grad_taps_ref)

    for chunk in range(H):
        d_headed = product(branch_ref[chunk], out_ref[...])
        for seq in range(seqs):
            d_headed_ref[chunk, seq] = d_headed[seq * size : (seq + 1) * size]

    def prepare(turn, _):
        units = units_of(turn * BACKWARD_CHUNKS, BACKWARD_CHUNKS, seqs)
        for slot, (chunk, seq) in enumerate(units):
            _, query, key, _, _, beta = pieces(chunk, seq, slot)
            _, growth, fade = decays(run_ref, chunk, seq, rows, cols)
            mixed = mixed_ref[chunk, seq]
            d_headed = d_headed_ref[chunk, seq]
            gate = gate_ref[chunk, seq, :, :DV]
            logistic = jax.nn.sigmoid(gate)
            scale = lax.rsqrt(jnp.mean(mixed * mixed, axis=1, keepdims=True) + 1e-05)
            normed = mixed * scale
            swish = gate * logistic
            inner = d_headed * gain_ref[...] * swish
            d_mixed = scale * (inner - normed * jnp.mean(normed * inner, axis=1, keepdims=True))
            grad_gain_ref[...] += jnp.sum(d_headed * normed * swish, axis=0, keepdims=True)
            d_gate = d_headed * gain_ref[...] * normed * logistic * (1.0 + gate * (1.0 - logistic))
            d_all_ref[chunk ^ head, seq, :, WIDTH : WIDTH + DV] = d_gate.astype(bf16)
            d_headed_ref[chunk, seq] = d_mixed
            d_mixed_parts = parts(d_mixed)
            inverse_parts = from_cat(inverse_ref[chunk, seq])
            scored = mul(from_cat(scores_ref[chunk, seq]), d_mixed_parts)
            base_ref[chunk, seq] = mul(inverse_parts, parts(scored))
            hold_ref[chunk, seq] = cat_parts(mul(inverse_parts, parts(fade * key)))
            back_ref[chunk, seq] = mul(parts((growth * query).T), d_mixed_parts)
            carry_ref[chunk, seq] = cat_parts((beta * growth * key).T)
        return 0

    lax.fori_loop(0, chunks // BACKWARD_CHUNKS, prepare, 0)

    def advance(step, d_states):
        chunk = chunks - 1 - step
        following = []
        for seq in range(seqs):
            d_state = d_states[seq]
            d_state_ref[chunk, seq] = d_state
            d_target = base_ref[chunk, seq] + mul(from_cat(hold_ref[chunk, seq]), parts(d_state))
            d_target_ref[chunk, seq] = d_target
            total = jnp.exp(run_ref[chunk, seq][0:1, size - 1 : size])
            back = mul(from_cat(carry_ref[chunk, seq]), parts(d_target))
            following.append(total * d_state + back_ref[chunk, seq] - back)
        return tuple(following)

    first = lax.fori_loop(0, chunks, advance, tuple(d_end_ref[seq] for seq in range(seqs)))
    for seq in range(seqs):
        d_start_ref[seq] = first[seq]
        d_conv_ref[seq, size:, :] = d_after_ref[seq]

    def finish(turn, _):
        units = [
            (chunks - 1 - turn * BACKWARD_CHUNKS - back, seq)
            for back in range(BACKWARD_CHUNKS)
            for seq in range(seqs)
        ]
        for slot, (chunk, seq) in enumerate(units):
            slope, query, key, shrink, value, beta = pieces(chunk, seq, slot)
            decay_mat, growth, fade = decays(run_ref, chunk, seq, rows, cols)
            key_parts = parts(key)
            gram = mul_t(key_parts, key_parts) * decay_mat
            d_target = d_target_ref[chunk, seq]
            delta_parts = parts(delta_ref[chunk, seq])
            start_parts = parts(starts_ref[chunk, seq])
            both = parts(jnp.concatenate([d_target, d_headed_ref[chunk, seq]], 0))
            on_delta = mul_t(both, delta_parts)
            on_state = mul_t(both, start_parts)
            d_lower = jnp.where(rows > cols, -on_delta[:size], 0.0)
            d_scores = on_delta[size:] * decay_mat
            through = on_state[:size]
            d_gram = d_lower * decay_mat * beta
            d_query = growth * on_state[size:] + mul(parts(d_scores), key_parts)
            d_key = mul(parts(d_scores.T), parts(query))
            d_key = d_key + mul(parts(d_gram + d_gram.T), key_parts)
            d_key = d_key + fade * mul_t(delta_parts, parts(d_state_ref[chunk, seq]))
            d_key = d_key - (beta * growth) * through
            d_beta = (
                jnp.sum(d_target * value, axis=1, keepdims=True)
                - growth * jnp.sum(key * through, axis=1, keepdims=True)
                + jnp.sum(d_lower * gram, axis=1, keepdims=True)
            )
            d_raw = shrink * (d_key - key * jnp.sum(key * d_key, axis=1, keepdims=True))
            d_conv = jnp.concatenate([d_query, d_raw, beta * d_target], 1) * slope
            d_conv_ref[seq, :size, :] = d_conv
            d_in = None
            for tap in range(CONV):
                start = HALO - (CONV - 1) + tap
                grad_taps_ref[tap : tap + 1, :] += jnp.sum(
                    d_conv * rows_ref[slot, start : start + size, :], axis=0, keepdims=True
                )
                shift = CONV - 1 - tap
                term = d_conv_ref[seq, shift : shift + size, :] * taps_ref[tap : tap + 1, :]
                d_in = term if d_in is None else d_in + term
            d_conv_ref[seq, size:, :] = d_conv[:8, :]
            d_all_ref[chunk ^ head, seq, :, :WIDTH] = d_in.astype(bf16)
            d_logit = d_beta * beta * (1.0 - beta)
            lane = lax.broadcasted_iota(jnp.int32, (size, 128), 1)
            d_all_ref[chunk ^ head, seq, :, WIDTH + DV :] = jnp.where(
                lane == 0, d_logit, 0.0
            ).astype(bf16)
        return 0

    lax.fori_loop(0, chunks // BACKWARD_CHUNKS, finish, 0)
    for seq in range(seqs):
        d_before_ref[seq] = d_conv_ref[seq, size:, :]


def whole(count):
    return [pl.BlockSpec(memory_space=pltpu.VMEM)] * count


def scalar():
    return [pl.BlockSpec(memory_space=pltpu.SMEM)]


shaped = jax.ShapeDtypeStruct


def kernel_params():
    return pltpu.CompilerParams(vmem_limit_bytes=VMEM_LIMIT)


def forward_rule(head, blocks, weight, beta_w, run, taps, gain, state, halo):
    chunks, seqs, _, size = run.shape
    lead = (chunks, seqs)
    return pl.pallas_call(
        forward_kernel,
        name="mixer_forward",
        out_shape=(
            shaped(lead + (size, DV), bf16),
            shaped(lead + (size, WIDTH), bf16),
            shaped(lead + (size, DV + 128), f32),
            shaped(lead + (size, DV), f32),
            shaped(lead + (size, 2 * size), bf16),
            shaped(lead + (size, 2 * size), bf16),
            shaped(lead + (size, DV), f32),
            shaped(lead + (DK, DV), f32),
            shaped((seqs, DK, DV), f32),
        ),
        in_specs=scalar() + whole(H + 7),
        out_specs=tuple(whole(9)),
        scratch_shapes=[
            pltpu.VMEM((FORWARD_CHUNKS * seqs, HALO + size, WIDTH), f32),
            pltpu.VMEM(lead + (size, 2 * DK), bf16),
            pltpu.VMEM(lead + (size, DV), f32),
            pltpu.VMEM(lead + (size, 2 * DK), bf16),
            pltpu.VMEM(lead + (DK, 2 * size), bf16),
            pltpu.VMEM(lead + (size, 2 * size), bf16),
        ],
        compiler_params=kernel_params(),
    )(head, *blocks, weight, beta_w, run, taps, gain, state, halo)


def backward_rule(head, branch, out_w, run, taps, gain, halo, saved, d_end, d_after):
    chunks, seqs, _, size = run.shape
    lead = (chunks, seqs)
    conv_in, gate_beta, mixed, inverse, scores, delta, starts = saved
    return pl.pallas_call(
        backward_kernel,
        name="mixer_backward",
        out_shape=(
            shaped(lead + (size, WIDTH + DV + 128), bf16),
            shaped((8, WIDTH), f32),
            shaped((1, DV), f32),
            shaped((seqs, DK, DV), f32),
            shaped((seqs, 8, WIDTH), f32),
        ),
        in_specs=scalar() + whole(15),
        out_specs=tuple(whole(5)),
        scratch_shapes=[
            pltpu.VMEM((BACKWARD_CHUNKS * seqs, HALO + size, WIDTH), f32),
            pltpu.VMEM(lead + (size, DV), f32),
            pltpu.VMEM(lead + (size, 2 * DK), bf16),
            pltpu.VMEM(lead + (DK, 2 * size), bf16),
            pltpu.VMEM(lead + (size, DV), f32),
            pltpu.VMEM(lead + (DK, DV), f32),
            pltpu.VMEM(lead + (size, DV), f32),
            pltpu.VMEM(lead + (DK, DV), f32),
            pltpu.VMEM((seqs, size + 8, WIDTH), f32),
        ],
        compiler_params=kernel_params(),
    )(
        head, branch, out_w, conv_in, gate_beta, run, taps, gain, halo, mixed, inverse, scores,
        delta, starts, d_end, d_after,
    )


def out_kernel(head_ref, *refs):
    block_refs, (headed_ref, inputs_ref, gain_ref, residual_ref, normed_ref) = refs[:H], refs[H:]
    head = head_ref[0]
    total = inputs_ref[...].astype(f32)
    for slot in range(H):
        total = total + contract_cols(headed_ref[slot ^ head], block_refs[slot][...])
    residual_ref[...] = total
    scale = lax.rsqrt(jnp.mean(total * total, axis=1, keepdims=True) + 1e-05)
    normed_ref[...] = (total * scale * gain_ref[...]).astype(bf16)


def out_rule(head, blocks, headed, inputs, gain):
    return pl.pallas_call(
        out_kernel,
        name="out_projection",
        out_shape=(shaped(inputs.shape, f32), shaped(inputs.shape, bf16)),
        in_specs=scalar() + whole(H + 3),
        out_specs=tuple(whole(2)),
        compiler_params=kernel_params(),
    )(head, *blocks, headed, inputs, gain)


def ffn_kernel(head_ref, normed_ref, up_ref, weight_ref, d_both_ref, hidden_ref, d_in_ref, out_ref):
    share = weight_ref.shape[1] // 3
    both = product(normed_ref[0], weight_ref[:, : 2 * share])
    d_hidden = product(up_ref[0], weight_ref[:, 2 * share :])
    gate, up = both[:, :share], both[:, share:]
    logistic = jax.nn.sigmoid(gate)
    swish = gate * logistic
    hidden = (swish * up).astype(bf16)
    hidden_ref[0] = hidden
    d_gate = (d_hidden * up * logistic * (1.0 + gate * (1.0 - logistic))).astype(bf16)
    d_up = (d_hidden * swish).astype(bf16)
    d_both = jnp.concatenate([d_gate, d_up], 1)
    d_both_ref[0] = d_both
    d_in_ref[0] = contract_cols(d_both, weight_ref[:, : 2 * share]).astype(bf16)
    out_ref[0] = contract_cols(hidden, weight_ref[:, 2 * share :]).astype(bf16)


def ffn_rule(head, normed, upstream, weight):
    count, rows, model = normed.shape
    share = weight.shape[1] // 3

    def same(step, head_ref):
        return (step, 0, 0)

    def moved(step, head_ref):
        return (step ^ head_ref[0], 0, 0)

    return pl.pallas_call(
        ffn_kernel,
        name="feed_forward",
        grid_spec=pltpu.PrefetchScalarGridSpec(
            num_scalar_prefetch=1,
            grid=(count,),
            in_specs=[
                pl.BlockSpec((1, rows, model), same),
                pl.BlockSpec((1, rows, model), moved),
                pl.BlockSpec(weight.shape, lambda step, head_ref: (0, 0)),
            ],
            out_specs=[
                pl.BlockSpec((1, rows, 2 * share), same),
                pl.BlockSpec((1, rows, share), moved),
                pl.BlockSpec((1, rows, model), moved),
                pl.BlockSpec((1, rows, model), moved),
            ],
        ),
        out_shape=(
            shaped((count, rows, 2 * share), bf16),
            shaped((count, rows, share), bf16),
            shaped((count, rows, model), bf16),
            shaped((count, rows, model), bf16),
        ),
        compiler_params=kernel_params(),
    )(head, normed, upstream, weight)


def join_kernel(spread_ref, *out_refs):
    start = 0
    for out_ref in out_refs:
        width = out_ref.shape[1]
        out_ref[...] = spread_ref[0, :, start : start + width].astype(f32)
        start += width


def join_rule(spread, widths):
    count, rows, width = spread.shape
    return pl.pallas_call(
        join_kernel,
        name="join_heads",
        grid=(count,),
        in_specs=[pl.BlockSpec((1, rows, width), lambda step: (step, 0, 0))],
        out_specs=[pl.BlockSpec((rows, width), lambda step: (0, step)) for width in widths],
        out_shape=[shaped((rows, count * width), f32) for width in widths],
        compiler_params=kernel_params(),
    )(spread)


def join_hidden_kernel(total, spread_ref, *out_refs):
    count, _, width = spread_ref.shape
    share = width // len(out_refs)
    for index, out_ref in enumerate(out_refs):
        for peer in range(count):
            start = min(peer * share, total - share)
            skip = peer * share - start
            piece = spread_ref[peer, :, index * share + skip : (index + 1) * share]
            out_ref[:, start + skip : start + share] = piece.astype(f32)


def join_hidden_rule(spread, total, pieces):
    count, rows, width = spread.shape
    return pl.pallas_call(
        lambda *refs: join_hidden_kernel(total, *refs),
        name="join_hidden",
        in_specs=whole(1),
        out_specs=whole(pieces),
        out_shape=[shaped((rows, total), f32)] * pieces,
        compiler_params=kernel_params(),
    )(spread)


def passed_along(array, axis, by):
    peers = lax.axis_size(axis)
    pairs = [(i, i + by) for i in range(peers) if 0 <= i + by < peers]
    return lax.ppermute(array, axis, pairs)


def swapped(array, axis, bits):
    return lax.ppermute(array, axis, [(i, i ^ bits) for i in range(lax.axis_size(axis))])


def gather_blocks(own):
    near, far, across = (swapped(own, "seq", bits) for bits in (2, 4, 6))
    blocks = [own, None, near, None, far, None, across, None]
    for slot in range(0, H, 2):
        blocks[slot + 1] = swapped(blocks[slot], "seq", 1)
    return blocks


def scatter_blocks(partial):
    handed = [swapped(partial[slot + 1], "seq", 1) for slot in range(0, H, 2)]
    sums = [partial[2 * i].astype(f32) + handed[i].astype(f32) for i in range(H // 2)]
    total = sums[0]
    for i in range(H // 2 - 1, 0, -1):
        total = total + swapped(sums[i].astype(bf16), "seq", 2 * i).astype(f32)
    return total


def rms_scale(values):
    return lax.rsqrt(jnp.mean(values * values, axis=-1, keepdims=True) + 1e-05)


def rms_back(values, gain, d_normed):
    scale = rms_scale(values)
    normed = values * scale
    pulled = d_normed * gain
    d_values = scale * (pulled - normed * jnp.mean(normed * pulled, axis=-1, keepdims=True))
    return d_values, jnp.sum(d_normed * normed, axis=0)


def shards(
    inputs,
    cotangent,
    decay,
    w_query,
    w_key,
    w_value,
    w_gate_out,
    w_out,
    w_ffn_gate,
    w_ffn_up,
    w_ffn_down,
    w_beta,
    conv_weight,
    norm_in,
    norm_mid,
    norm_head,
):
    seqs, size, model = inputs.shape
    rows = seqs * size
    peers = lax.axis_size("seq")
    stages = peers // H
    groups = None
    if stages > 1:
        groups = [[stage * H + head for head in range(H)] for stage in range(stages)]
    place = lax.axis_index("seq")
    head = lax.rem(place, H)
    head_arg = head.reshape(1)
    all_rows = H * rows
    hidden_all = w_ffn_gate.shape[1]
    share = -(-hidden_all // (H * 128)) * 128

    def gather_rows(local):
        return lax.all_gather(local, "seq", axis_index_groups=groups)

    def own_columns(weight, width):
        return lax.dynamic_slice_in_dim(weight, head * width, width, axis=1)

    def own_hidden(weight):
        start = jnp.minimum(head * share, hidden_all - share)
        piece = lax.dynamic_slice_in_dim(weight, start, share, axis=1)
        lane = lax.broadcasted_iota(jnp.int32, piece.shape, 1)
        return jnp.where(lane + start >= head * share, piece, jnp.zeros_like(piece))

    def gather_weight(local):
        return lax.all_gather(local, "wt", axis=0, tiled=True)

    mixer_w = gather_weight(
        jnp.concatenate(
            [
                own_columns(w_query, DK),
                own_columns(w_key, DK),
                own_columns(w_value, DV),
                own_columns(w_gate_out, DV),
                own_columns(w_out, DV),
            ],
            axis=1,
        )
    )
    ffn_w = gather_weight(
        jnp.concatenate(
            [own_hidden(w_ffn_gate), own_hidden(w_ffn_up), own_hidden(w_ffn_down)], axis=1
        )
    )
    own_in = inputs.reshape(rows, model)
    flat_in = own_in.astype(f32)
    normed_own = (flat_in * rms_scale(flat_in) * norm_in).astype(bf16)
    normed_in = gather_blocks(normed_own)
    upstream_own = cotangent.reshape(rows, model)
    upstream = jnp.stack(gather_blocks(upstream_own))
    beta_w = jnp.pad(own_columns(w_beta, 1), ((0, 0), (0, 127)))
    in_width = WIDTH + DV
    out_w = mixer_w[:, in_width:]
    out_blocks = gather_blocks(out_w)

    own_decay = gather_rows(decay)
    own_decay = lax.dynamic_index_in_dim(own_decay, head, axis=3, keepdims=False)
    run = jnp.cumsum(jnp.log(own_decay), axis=-1)
    run = jnp.broadcast_to(run[:, :, None, :], (H, seqs, 8, size))
    taps = jnp.concatenate(
        [
            own_columns(conv_weight[:, : H * DK], DK),
            own_columns(conv_weight[:, H * DK : 2 * H * DK], DK),
            own_columns(conv_weight[:, 2 * H * DK :], DV),
        ],
        axis=1,
    )
    taps = jnp.pad(taps, ((0, 8 - CONV), (0, 0)))
    gain = norm_head[None, :]

    state = jnp.zeros((seqs, DK, DV), f32)
    halo = jnp.zeros((seqs, HALO, WIDTH), bf16)
    if stages > 1:
        edges = lax.all_gather(normed_own.reshape(seqs, size, model)[:, size - HALO :], "seq")
        before = lax.dynamic_index_in_dim(edges, jnp.maximum(place - head - 1, 0), keepdims=False)
        rolled = product(before.reshape(seqs * HALO, model), mixer_w[:, :WIDTH]).astype(bf16)
        halo = jnp.where(place >= H, rolled.reshape(halo.shape), halo)
    for stage in range(stages):
        headed, *saved, ending = forward_rule(
            head_arg, normed_in, mixer_w, beta_w, run, taps, gain, state, halo
        )
        if stage < stages - 1:
            state = passed_along(ending, "seq", H)

    headed = headed.reshape(H, rows, DV)
    own_headed = lax.all_to_all(headed, "seq", 0, 0, axis_index_groups=groups, tiled=True)
    residual, normed_mid = out_rule(head_arg, out_blocks, own_headed, own_in, norm_mid[None, :])
    normed_mid = gather_rows(normed_mid)

    d_both, hidden, d_mid_blocks, ffn_blocks = ffn_rule(head_arg, normed_mid, upstream, ffn_w)
    d_normed_mid = scatter_blocks(d_mid_blocks)
    d_from_mid, grad_mid = rms_back(residual, norm_mid, d_normed_mid)
    d_residual = upstream_own.astype(f32) + d_from_mid
    branch = gather_rows(d_residual.astype(bf16))

    d_end = jnp.zeros((seqs, DK, DV), f32)
    d_after = jnp.zeros((seqs, 8, WIDTH), f32)
    for stage in range(stages):
        d_all, grad_taps, grad_gain, d_start, d_before = backward_rule(
            head_arg, branch, out_w, run, taps, gain, halo, saved, d_end, d_after
        )
        if stage < stages - 1:
            d_end = passed_along(d_start, "seq", -H)
            d_after = passed_along(d_before, "seq", -H)
    d_all = d_all.reshape(all_rows, -1)

    layer_out = (residual + scatter_blocks(ffn_blocks)).astype(bf16).reshape(inputs.shape)

    def reduce_grads(partial):
        summed = lax.psum_scatter(partial.astype(bf16), "wt", scatter_dimension=0, tiled=True)
        spread = lax.all_gather(summed, "seq")
        if stages > 1:
            spread = spread.reshape((stages, H) + summed.shape).astype(f32)
            spread = jnp.sum(spread, axis=0)
        return spread

    def flat(blocks):
        return blocks.reshape(all_rows, -1)

    ffn_partial = jnp.concatenate(
        [
            contract_rows(flat(normed_mid), flat(d_both)),
            contract_rows(flat(upstream), flat(hidden)),
        ],
        axis=1,
    )
    ffn_grads = join_hidden_rule(reduce_grads(ffn_partial), hidden_all, 3)

    mixer_partial = contract_rows(jnp.concatenate(normed_in, axis=0), d_all)
    out_partial = contract_rows(flat(branch), flat(headed))
    mixer_grads = join_rule(
        reduce_grads(jnp.concatenate([mixer_partial[:, :in_width], out_partial], axis=1)),
        [DK, DK, DV, DV, DV],
    )

    in_w = jnp.concatenate([mixer_w[:, :in_width], beta_w], axis=1)
    d_in_blocks = contract_cols(d_all, in_w).astype(bf16).reshape(H, rows, model)
    d_from_in, _ = rms_back(flat_in, norm_in, scatter_blocks(d_in_blocks))
    grad_input = (d_residual + d_from_in).reshape(inputs.shape)

    grad_in_part = jnp.sum(mixer_partial * in_w.astype(f32), axis=1) / norm_in
    small = jnp.concatenate(
        [
            grad_taps[:CONV].reshape(-1),
            mixer_partial[:, in_width],
            grad_gain[0],
            grad_mid,
            grad_in_part,
        ]
    ).reshape(-1, 128)
    step = 1
    while step < lax.axis_size("wt"):
        small = small + swapped(small, "wt", step)
        step *= 2
    step = H
    while step < peers:
        small = small + swapped(small, "seq", step)
        step *= 2
    small = small[None]
    for bits in (1, 2, 4):
        small = jnp.concatenate([small, swapped(small, "seq", bits)], axis=0)
    small = small[jnp.arange(H) ^ head].reshape(H, -1)
    ends = []
    for bound in (CONV * WIDTH, model, DV, model, model):
        ends.append(bound + (ends[-1] if ends else 0))
    taps_part = small[:, : ends[0]].reshape(H, CONV, WIDTH)

    def joined(pieces):
        return jnp.swapaxes(pieces, 0, 1).reshape(CONV, -1)

    grad_conv = jnp.concatenate(
        [
            joined(taps_part[:, :, :DK]),
            joined(taps_part[:, :, DK : 2 * DK]),
            joined(taps_part[:, :, 2 * DK :]),
        ],
        axis=1,
    )
    grad_beta = small[:, ends[0] : ends[1]].T
    shared = jnp.sum(small[:, ends[1] :], axis=0)
    return (
        layer_out,
        grad_input,
        *mixer_grads,
        *ffn_grads,
        grad_beta,
        grad_conv,
        shared[DV + model :],
        shared[DV : DV + model],
        shared[:DV],
    )


def solution(mesh):
    rows = P("wt", "seq", None)
    cut = P("wt", None)
    in_specs = (rows,) * 3 + (cut,) * 8 + (P(),) * 5
    out_specs = (rows,) * 2 + (cut,) * 8 + (P(),) * 5
    return jax.shard_map(shards, mesh=mesh, in_specs=in_specs, out_specs=out_specs, check_vma=False)
```

time: 723 us -> 504 us (0.70)
  blocking collectives: 151 us -> 27.5 us
  matrix products: 76.6 us -> 21.5 us
  waiting for transfers between devices: 260 us -> 214 us
  starting transfers between devices: 9.01 us -> 37.3 us
  local copies, waits for them, and re-layouts: 76.6 us -> 58.2 us
  other arithmetic: 38.1 us -> 24.2 us
  Pallas kernels: 93.2 us -> 102 us
    ppermute x0 -> x47, waiting for transfers between devices: none -> 99.4 us  [swapped(): lax.ppermute(array, axis, [(i, i ^ bits) for i in range(lax.axis_size(axi...]
    all_gather x4 -> x2, waiting for transfers between devices: 126 us -> 27.5 us  [gather_rows(): return lax.all_gather(local, 'seq', axis_index_groups=groups)]
    all_to_all x1 -> x0, blocking collectives: 65.2 us -> none  [scatter_rows(): lax.all_to_all(blocks, 'seq', 0, 0, axis_index_groups=groups, tiled=True)]
    all_gather x2 -> x1, blocking collectives: 85.7 us -> 27.5 us  [gather_rows(): return lax.all_gather(local, 'seq', axis_index_groups=groups)]
    all_gather x3 -> x2, waiting for transfers between devices: 69.5 us -> 12 us  [gather_weight(): return lax.all_gather(local, 'wt', axis=0, tiled=True)]
    dot_general x6 -> x0, matrix products: 36.2 us -> none  [product(): return jnp.dot(left, right, preferred_element_type=f32)]
    ppermute x0 -> x47, starting transfers between devices: none -> 32.4 us  [swapped(): lax.ppermute(array, axis, [(i, i ^ bits) for i in range(lax.axis_size(axi...]
    transpose x11 -> x0, local copies, waits for them, and re-layouts: 26.5 us -> none  [joined(): return jnp.swapaxes(spread, 0, 1).reshape(spread.shape[1], -1)]
  transfers between devices with their start and end apart: 14 -> 56, of which waited for: 10 -> 25; matrix products, arithmetic and copies ran while one was open for 19% -> 17% of each run, Pallas kernels for 13% -> 16%
where the time goes in v2:
time: 504 us; the launch traced here: 500 us
  waiting for transfers between devices  214 us (42%)
  Pallas kernels  102 us (20%)
  local copies, waits for them, and re-layouts  58.2 us (12%)
  starting transfers between devices  37.3 us (7%)
  blocking collectives  27.5 us (5%)
  other arithmetic  24.2 us (5%)
  matrix products  21.5 us (4%)
  between operations  15 us (3%)
    ppermute x47, waiting for transfers between devices, swapped(): lax.ppermute(array, axis, [(i, i ^ bits) for i in range(lax.axis_size(axi...  99.4 us
    reduce_scatter x2, waiting for transfers between devices, reduce_grads(): lax.psum_scatter(partial.astype(bf16), 'wt', scatter_dimension=0, tiled=T...  48.3 us
    pallas_call x1, Pallas kernels, backward_rule(): pl.pallas_call(backward_kernel, name='mixer_backward', out_shape=(shaped(...  37.3 us
    ppermute x47, starting transfers between devices, swapped(): lax.ppermute(array, axis, [(i, i ^ bits) for i in range(lax.axis_size(axi...  32.4 us
    pallas_call x1, Pallas kernels, forward_rule(): pl.pallas_call(forward_kernel, name='mixer_forward', out_shape=(shaped(le...  30.9 us
    all_gather x2, waiting for transfers between devices, gather_rows(): return lax.all_gather(local, 'seq', axis_index_groups=groups)  27.5 us
    all_gather x1, blocking collectives, gather_rows(): return lax.all_gather(local, 'seq', axis_index_groups=groups)  27.5 us
    unnamed x100, local copies, waits for them, and re-layouts  23.1 us
  transfers between devices with their start and end apart: 56, of which 25 were waited for; matrix products, arithmetic and copies ran while one was open for 17% of the time, Pallas kernels for 16%

profile of v2, /device:TPU:0, one launch (start us, length us, event | category | flops | bytes accessed | tf_op | source)
XLA Modules:
  0.0 500.1 jit_solution(1245691625913079122)
XLA Ops:
  16.5 3.9 collective-permute-start.12
  21.0 27.5 %all-gather = f32[16,128,8]{1,2,0:T(8,128)S(1)} all-gather(f32[2,128,8]{1,2,0:T(8,128)S(1)} %copy-done.30), channel_id=2, replica_groups=mesh['seq'=8,'wt'=4] {'seq'}, dimensions={0}, use_global_device_ids=true | all-gather | bytes 73728 | tf_op jit(solution)/shard_map/all_gather | solution.py:614
  49.5 12.0 %all-gather.12.cloned.1.call-done.refs_8_ = bf16[1024,1024]{1,0:T(8,128)(2,1)} async-done(((bf16[256,1024]{1,0:T(8,128)(2,1)}), bf16[1024,1024]{1,0:T(8,128)(2,1)}) %all-gather.12.cloned.1.call-update) | async-done | bytes 2097168 | tf_op jit(solution)/shard_map/all_gather | solution.py:626
  70.5 30.9 %mixer_forward.1 = (bf16[8,2,128,256]{3,2,1,0:T(8,128)(2,1)}, bf16[8,2,128,512]{3,2,1,0:T(8,128)(2,1)}, f32[8,2,128,384]{3,2,1,0:T(8,128)}, f32[8,2,128,256]{3,2...) custom-call(s32[1]{0:T(128)} %bitcast.head_ref, ...), custom_call_target="tpu_custom_call" | custom-call | tf_op jit(solution)/shard_map/mixer_forward/pallas_call | solution.py:359
  101.4 3.9 all-to-all-start
  107.6 13.1 %all-to-all-done.refs_8_ = bf16[8,256,256]{2,1,0:T(8,128)(2,1)S(1)} async-done(((bf16[8,256,256]{2,1,0:T(8,128)(2,1)}), bf16[8,256,256]{2,1,0:T(8,128)(2,1)S(1)}, u32[]{:S(2)}, u32[]{:S(2)}) %all-to-all-start) | async-done | bytes 1048608 | tf_op jit(solution)/shard_map/all_to_all | solution.py:686
  121.8 5.1 %out_projection.1 = (f32[256,1024]{1,0:T(8,128)}, bf16[256,1024]{1,0:T(8,128)(2,1)}) custom-call(s32[1]{0:T(128)} %bitcast.head_ref, bf16[1024,256]{1,0:T(8,128)(2,1)} %copy-done.9, bf16[1024,256]{1,0:T(8,128)(2,1)} %copy-done.23, bf16[1024,256]{1,0:T(8,128)(2,1)} %collective-permute-done.1.refs_2_, bf16[1024,256]{1,0:T(8,128)(2,1)} %collective-permute-done.2.refs_3_, ...), custom_call_target="tpu_custom_call" | custom-call | tf_op jit(solution)/shard_map/out_projection/pallas_call | solution.py:433
  130.6 17.0 %collective-permute-done.15 = bf16[256,1024]{1,0:T(8,128)(2,1)S(1)} collective-permute-done((bf16[256,1024]{1,0:T(8,128)(2,1)S(1)}, bf16[256,1024]{1,0:T(8,128)(2,1)S(1)}, u32[]{:S(2)}, u32[]{:S(2)}) %collective-permute-start.15) | collective-permute-done | bytes 524320 | tf_op jit(solution)/shard_map/ppermute | solution.py:549
  148.4 8.1 %collective-permute-done.19 = bf16[256,1024]{1,0:T(8,128)(2,1)S(1)} collective-permute-done((bf16[256,1024]{1,0:T(8,128)(2,1)S(1)}, bf16[256,1024]{1,0:T(8,128)(2,1)S(1)}, u32[]{:S(2)}, u32[]{:S(2)}) %collective-permute-start.19) | collective-permute-done | bytes 524320 | tf_op jit(solution)/shard_map/ppermute | solution.py:549
  164.0 13.4 %all-gather.16.cloned.1.call-done = bf16[2048,1024]{1,0:T(8,128)(2,1)} async-done(((bf16[256,1024]{1,0:T(8,128)(2,1)}), bf16[2048,1024]{1,0:T(8,128)(2,1)}) %all-gather.16.cloned.1.call-update) | async-done | bytes 4194320 | tf_op jit(solution)/shard_map/all_gather | solution.py:614
  177.3 15.8 %feed_forward.1 = (bf16[8,256,768]{2,1,0:T(8,128)(2,1)}, bf16[8,256,384]{2,1,0:T(8,128)(2,1)}, bf16[8,256,1024]{2,1,0:T(8,128)(2,1)}, bf16[8,256,1024]{2,1,0:T(8,128)(2,1)}) custom-call(s32[1]{0:T(128)} %bitcast.head_ref, bf16[8,256,1024]{2,1,0:T(8,128)(2,1)} %bitcast.144, bf16[8,256,1024]{2,1,0:T(8,128)(2,1)} %bitcast_dynamic-update-slice_fusion.up_ref, ...), custom_call_target="tpu_custom_call" | custom-call | tf_op jit(solution)/shard_map/feed_forward/pallas_call | solution.py:470
  205.0 9.9 %collective-permute-done.30 = bf16[256,1024]{1,0:T(8,128)(2,1)S(1)} collective-permute-done((bf16[256,1024]{1,0:T(8,128)(2,1)S(1)}, bf16[256,1024]{1,0:T(8,128)(2,1)S(1)}, u32[]{:S(2)}, u32[]{:S(2)}) %collective-permute-start.30) | collective-permute-done | bytes 524320 | tf_op jit(solution)/shard_map/ppermute | solution.py:549
  216.4 9.6 %collective-permute-done.34 = bf16[256,1024]{1,0:T(8,128)(2,1)S(1)} collective-permute-done((bf16[256,1024]{1,0:T(8,128)(2,1)S(1)}, bf16[256,1024]{1,0:T(8,128)(2,1)S(1)}, u32[]{:S(2)}, u32[]{:S(2)}) %collective-permute-start.34) | collective-permute-done | bytes 524320 | tf_op jit(solution)/shard_map/ppermute | solution.py:549
  227.4 10.0 %collective-permute-done.23 = bf16[256,1024]{1,0:T(8,128)(2,1)S(1)} collective-permute-done((bf16[256,1024]{1,0:T(8,128)(2,1)S(1)}, bf16[256,1024]{1,0:T(8,128)(2,1)S(1)}, u32[]{:S(2)}, u32[]{:S(2)}) %collective-permute-start.23) | collective-permute-done | bytes 524320 | tf_op jit(solution)/shard_map/ppermute | solution.py:549
  237.4 10.4 %collective-permute-done.27 = bf16[256,1024]{1,0:T(8,128)(2,1)S(1)} collective-permute-done((bf16[256,1024]{1,0:T(8,128)(2,1)S(1)}, bf16[256,1024]{1,0:T(8,128)(2,1)S(1)}, u32[]{:S(2)}, u32[]{:S(2)}) %collective-permute-start.27) | collective-permute-done | bytes 524320 | tf_op jit(solution)/shard_map/ppermute | solution.py:549
  249.7 4.6 bitcast_convert_fusion.1
  254.6 3.6 bitcast_convert_fusion
  272.4 14.2 %all-gather.18.cloned.1.call-done = bf16[2048,1024]{1,0:T(8,128)(2,1)} async-done(((bf16[256,1024]{1,0:T(8,128)(2,1)}), bf16[2048,1024]{1,0:T(8,128)(2,1)}) %all-gather.18.cloned.1.call-update) | async-done | bytes 4194320 | tf_op jit(solution)/shard_map/all_gather | solution.py:614
  287.2 37.3 %mixer_backward.1 = (bf16[8,2,128,896]{3,2,1,0:T(8,128)(2,1)}, f32[8,512]{1,0:T(8,128)}, f32[1,256]{1,0:T(1,128)}, f32[2,128,256]{2,1,0:T(8,128)}, f32[2,8,512]{2,1,0:T(8,128)}) custom-call(s32[1]{0:T(128)} %bitcast.head_ref, bf16[8,256,1024]{2,1,0:T(8,128)(2,1)} %bitcast.143, bf16[1024,256]{1,0:T(8,128)(2,1)} %copy-done.9, ...), custom_call_target="tpu_custom_call" | custom-call | tf_op jit(solution)/shard_map/mixer_backward/pallas_call | solution.py:391
  324.5 7.1 %fusion.22 = f32[1024,896]{0,1:T(8,128)S(1)} fusion(bf16[2048,1024]{1,0:T(8,128)(2,1)} %constant_dynamic-update-slice_fusion, bf16[2048,896]{1,0:T(8,128)(2,1)} %bitcast.166), kind=kOutput, calls=%fused_computation.121 | convolution fusion | flops 3758096384 | bytes 11534336 | tf_op jit(solution)/shard_map/dot_general | solution.py:20
  337.6 45.9 %reduce-scatter.3.cloned.1.call-done = bf16[256,1024]{0,1:T(8,128)(2,1)} async-done(((bf16[1024,1024]{0,1:T(8,128)(2,1)}), bf16[256,1024]{0,1:T(8,128)(2,1)}) %reduce-scatter.3.cloned.1.call-update) | async-done | bytes 524304 | tf_op jit(solution)/shard_map/reduce_scatter | solution.py:710
  386.2 5.1 %copy.62 = f32[1024,896]{1,0:T(8,128)} copy(f32[1024,896]{0,1:T(8,128)} %copy-done.5) | data formatting | bytes 7340032 | tf_op jit(solution)/shard_map/dot_general | solution.py:20
  391.4 3.4 multiply_reduce_fusion
  394.9 3.8 collective-permute-done.42
  406.1 4.9 convolution_convert_fusion
  427.9 10.5 %collective-permute-done.37 = bf16[256,1024]{1,0:T(8,128)(2,1)S(1)} collective-permute-done((bf16[256,1024]{1,0:T(8,128)(2,1)S(1)}, bf16[256,1024]{1,0:T(8,128)(2,1)S(1)}, u32[]{:S(2)}, u32[]{:S(2)}) %collective-permute-start.37) | collective-permute-done | bytes 524320 | tf_op jit(solution)/shard_map/ppermute | solution.py:549
  438.3 9.7 %collective-permute-done.41 = bf16[256,1024]{1,0:T(8,128)(2,1)S(1)} collective-permute-done((bf16[256,1024]{1,0:T(8,128)(2,1)S(1)}, bf16[256,1024]{1,0:T(8,128)(2,1)S(1)}, u32[]{:S(2)}, u32[]{:S(2)}) %collective-permute-start.41) | collective-permute-done | bytes 524320 | tf_op jit(solution)/shard_map/ppermute | solution.py:549
  453.1 6.7 %copy.61 = bf16[2048,1152]{1,0:T(8,128)(2,1)} copy(bf16[2048,1152]{0,1:T(8,128)(2,1)} %all-gather.22.cloned.1.call-done) | data formatting | bytes 9437184 | tf_op jit(solution)/shard_map/all_gather | solution.py:711
  459.8 6.0 %join_hidden.1 = (f32[256,2816]{1,0:T(8,128)}, f32[256,2816]{1,0:T(8,128)}, f32[256,2816]{1,0:T(8,128)}) custom-call(bf16[8,256,1152]{2,1,0:T(8,128)(2,1)} %bitcast.134), custom_call_target="tpu_custom_call" | custom-call | tf_op jit(solution)/shard_map/join_hidden/pallas_call | solution.py:532
  465.8 13.6 %all-gather.20.cloned.1.call-done = bf16[2048,1024]{0,1:T(8,128)(2,1)} async-done(((bf16[256,1024]{0,1:T(8,128)(2,1)}), bf16[2048,1024]{0,1:T(8,128)(2,1)}) %all-gather.20.cloned.1.call-update) | async-done | bytes 4194320 | tf_op jit(solution)/shard_map/all_gather | solution.py:711
  479.4 6.4 %copy.58 = bf16[2048,1024]{1,0:T(8,128)(2,1)} copy(bf16[2048,1024]{0,1:T(8,128)(2,1)} %all-gather.20.cloned.1.call-done) | data formatting | bytes 8388608 | tf_op jit(solution)/shard_map/all_gather | solution.py:711
  485.8 7.2 %join_heads.1 = (f32[256,1024]{1,0:T(8,128)}, f32[256,1024]{1,0:T(8,128)}, f32[256,2048]{1,0:T(8,128)}, f32[256,2048]{1,0:T(8,128)}, f32[256,2048]{1,0:T(8,128)}) custom-call(bf16[8,256,1024]{2,1,0:T(8,128)(2,1)} %bitcast.135), custom_call_target="tpu_custom_call" | custom-call | tf_op jit(solution)/shard_map/join_heads/pallas_call | solution.py:508
  (265 shorter events, 104.5 us)
Async XLA Ops:
  7.3 54.2 %all-gather.12.cloned.1.call-start = ((), (), s32[]{:S(2)}) async-start(), calls=%async_computation.3 | async-start | bytes 2621440 | tf_op jit(solution)/shard_map/all_gather | solution.py:626
  12.7 151.2 %all-gather.14.cloned.1.call-start = ((), (), s32[]{:S(2)}) async-start(), calls=%async_computation.4 | async-start | bytes 2949120 | tf_op jit(solution)/shard_map/all_gather | solution.py:626
  16.5 32.0 %collective-permute-start.12 = (bf16[256,1024]{1,0:T(8,128)(2,1)}, bf16[256,1024]{1,0:T(8,128)(2,1)S(1)}, u32[]{:S(2)}, u32[]{:S(2)}) collective-permute-start(bf16[256,1024]{1,0:T(8,128)(2,1)} %get-tuple-element.101.refs_0_), channel_id=1, source_target_pairs={{0,24},{4,28},{8,16},{12,20},{16,8},{20,12},{24,0},{28,4},{1,25},{... | collective-permute-start | bytes 1572872 | tf_op jit(solution)/shard_map/ppermute | solution.py:549
  20.4 28.5 %collective-permute-start.10 = (bf16[256,1024]{1,0:T(8,128)(2,1)}, bf16[256,1024]{1,0:T(8,128)(2,1)S(1)}, u32[]{:S(2)}, u32[]{:S(2)}) collective-permute-start(bf16[256,1024]{1,0:T(8,128)(2,1)} %get-tuple-element.101.refs_0_), channel_id=1, source_target_pairs={{0,16},{4,20},{8,24},{12,28},{16,0},{20,4},{24,8},{28,12},{1,17},{... | collective-permute-start | bytes 1572872 | tf_op jit(solution)/shard_map/ppermute | solution.py:549
  20.9 28.2 %collective-permute-start.8 = (bf16[256,1024]{1,0:T(8,128)(2,1)}, bf16[256,1024]{1,0:T(8,128)(2,1)S(1)}, u32[]{:S(2)}, u32[]{:S(2)}) collective-permute-start(bf16[256,1024]{1,0:T(8,128)(2,1)} %get-tuple-element.101.refs_0_), channel_id=1, source_target_pairs={{0,8},{4,12},{8,0},{12,4},{16,24},{20,28},{24,16},{28,20},{1,9},{5... | collective-permute-start | bytes 1572872 | tf_op jit(solution)/shard_map/ppermute | solution.py:549
  21.0 44.1 %collective-permute-start.7 = (bf16[256,1024]{1,0:T(8,128)(2,1)}, bf16[256,1024]{1,0:T(8,128)(2,1)S(1)}, u32[]{:S(2)}, u32[]{:S(2)}) collective-permute-start(bf16[256,1024]{1,0:T(8,128)(2,1)} %get-tuple-element.101.refs_0_), channel_id=1, source_target_pairs={{0,4},{4,0},{8,12},{12,8},{16,20},{20,16},{24,28},{28,24},{1,5},{5... | collective-permute-start | bytes 1572872 | tf_op jit(solution)/shard_map/ppermute | solution.py:549
  48.5 17.1 %collective-permute-start.13 = (bf16[256,1024]{1,0:T(8,128)(2,1)S(1)}, bf16[256,1024]{1,0:T(8,128)(2,1)}, u32[]{:S(2)}, u32[]{:S(2)}) collective-permute-start(bf16[256,1024]{1,0:T(8,128)(2,1)S(1)} %collective-permute-done.12.refs_6_), channel_id=1, source_target_pairs={{0,4},{4,0},{8,12},{12,8},{16,20},{20,16},{24,28},{28,24},{1,5},{5... | collective-permute-start | bytes 1572872 | tf_op jit(solution)/shard_map/ppermute | solution.py:549
  48.9 19.6 %collective-permute-start.11 = (bf16[256,1024]{1,0:T(8,128)(2,1)S(1)}, bf16[256,1024]{1,0:T(8,128)(2,1)}, u32[]{:S(2)}, u32[]{:S(2)}) collective-permute-start(bf16[256,1024]{1,0:T(8,128)(2,1)S(1)} %collective-permute-done.10.refs_4_), channel_id=1, source_target_pairs={{0,4},{4,0},{8,12},{12,8},{16,20},{20,16},{24,28},{28,24},{1,5},{5... | collective-permute-start | bytes 1572872 | tf_op jit(solution)/shard_map/ppermute | solution.py:549
  49.2 19.3 %collective-permute-start.9 = (bf16[256,1024]{1,0:T(8,128)(2,1)S(1)}, bf16[256,1024]{1,0:T(8,128)(2,1)}, u32[]{:S(2)}, u32[]{:S(2)}) collective-permute-start(bf16[256,1024]{1,0:T(8,128)(2,1)S(1)} %collective-permute-done.8.refs_2_), channel_id=1, source_target_pairs={{0,4},{4,0},{8,12},{12,8},{16,20},{20,16},{24,28},{28,24},{1,5},{5... | collective-permute-start | bytes 1572872 | tf_op jit(solution)/shard_map/ppermute | solution.py:549
  62.6 43.5 %collective-permute-start.5 = (bf16[1024,256]{1,0:T(8,128)(2,1)S(1)}, bf16[1024,256]{1,0:T(8,128)(2,1)}, u32[]{:S(2)}, u32[]{:S(2)}) collective-permute-start(bf16[1024,256]{1,0:T(8,128)(2,1)S(1)} %slice.175.refs_0_.out_ref), channel_id=1, source_target_pairs={{0,24},{4,28},{8,16},{12,20},{16,8},{20,12},{24,0},{28,4},{1,25},{... | collective-permute-start | bytes 1572872 | tf_op jit(solution)/shard_map/ppermute | solution.py:549
  65.0 41.1 %collective-permute-start.3 = (bf16[1024,256]{1,0:T(8,128)(2,1)S(1)}, bf16[1024,256]{1,0:T(8,128)(2,1)}, u32[]{:S(2)}, u32[]{:S(2)}) collective-permute-start(bf16[1024,256]{1,0:T(8,128)(2,1)S(1)} %slice.175.refs_0_.out_ref), channel_id=1, source_target_pairs={{0,16},{4,20},{8,24},{12,28},{16,0},{20,4},{24,8},{28,12},{1,17},{... | collective-permute-start | bytes 1572872 | tf_op jit(solution)/shard_map/ppermute | solution.py:549
  65.6 41.0 %collective-permute-start.1 = (bf16[1024,256]{1,0:T(8,128)(2,1)S(1)}, bf16[1024,256]{1,0:T(8,128)(2,1)}, u32[]{:S(2)}, u32[]{:S(2)}) collective-permute-start(bf16[1024,256]{1,0:T(8,128)(2,1)S(1)} %slice.175.refs_0_.out_ref), channel_id=1, source_target_pairs={{0,8},{4,12},{8,0},{12,4},{16,24},{20,28},{24,16},{28,20},{1,9},{5... | collective-permute-start | bytes 1572872 | tf_op jit(solution)/shard_map/ppermute | solution.py:549
  101.4 19.3 %all-to-all-start = ((bf16[8,256,256]{2,1,0:T(8,128)(2,1)}), bf16[8,256,256]{2,1,0:T(8,128)(2,1)S(1)}, u32[]{:S(2)}, u32[]{:S(2)}) async-start(bf16[8,256,256]{2,1,0:T(8,128)(2,1)} %bitcast.146), calls=%async_computation | async-start | bytes 2097152 | tf_op jit(solution)/shard_map/all_to_all | solution.py:686
  105.3 72.0 %all-gather.16.cloned.1.call-start = ((), (), s32[]{:S(2)}) async-start(), calls=%async_computation.7 | async-start | bytes 4718592 | tf_op jit(solution)/shard_map/all_gather | solution.py:614
  127.0 159.6 %all-gather.18.cloned.1.call-start = ((), (), s32[]{:S(2)}) async-start(), calls=%async_computation.8 | async-start | bytes 4718592 | tf_op jit(solution)/shard_map/all_gather | solution.py:614
  127.0 20.5 %collective-permute-start.15 = (bf16[256,1024]{1,0:T(8,128)(2,1)S(1)}, bf16[256,1024]{1,0:T(8,128)(2,1)S(1)}, u32[]{:S(2)}, u32[]{:S(2)}) collective-permute-start(bf16[256,1024]{1,0:T(8,128)(2,1)S(1)} %bitcast.138), channel_id=1, source_target_pairs={{0,8},{4,12},{8,0},{12,4},{16,24},{20,28},{24,16},{28,20},{1,9},{5... | collective-permute-start | bytes 1572872 | tf_op jit(solution)/shard_map/ppermute | solution.py:549
  127.6 28.9 %collective-permute-start.19 = (bf16[256,1024]{1,0:T(8,128)(2,1)S(1)}, bf16[256,1024]{1,0:T(8,128)(2,1)S(1)}, u32[]{:S(2)}, u32[]{:S(2)}) collective-permute-start(bf16[256,1024]{1,0:T(8,128)(2,1)S(1)} %bitcast.139), channel_id=1, source_target_pairs={{0,24},{4,28},{8,16},{12,20},{16,8},{20,12},{24,0},{28,4},{1,25},{... | collective-permute-start | bytes 1572872 | tf_op jit(solution)/shard_map/ppermute | solution.py:549
  129.1 29.0 %collective-permute-start.17 = (bf16[256,1024]{1,0:T(8,128)(2,1)S(1)}, bf16[256,1024]{1,0:T(8,128)(2,1)S(1)}, u32[]{:S(2)}, u32[]{:S(2)}) collective-permute-start(bf16[256,1024]{1,0:T(8,128)(2,1)S(1)} %bitcast.140), channel_id=1, source_target_pairs={{0,16},{4,20},{8,24},{12,28},{16,0},{20,4},{24,8},{28,12},{1,17},{... | collective-permute-start | bytes 1572872 | tf_op jit(solution)/shard_map/ppermute | solution.py:549
  130.6 27.5 %collective-permute-start.14 = (bf16[256,1024]{1,0:T(8,128)(2,1)S(1)}, bf16[256,1024]{1,0:T(8,128)(2,1)S(1)}, u32[]{:S(2)}, u32[]{:S(2)}) collective-permute-start(bf16[256,1024]{1,0:T(8,128)(2,1)S(1)} %bitcast.141), channel_id=1, source_target_pairs={{0,4},{4,0},{8,12},{12,8},{16,20},{20,16},{24,28},{28,24},{1,5},{5... | collective-permute-start | bytes 1572872 | tf_op jit(solution)/shard_map/ppermute | solution.py:549
  200.7 25.3 %collective-permute-start.34 = (bf16[256,1024]{1,0:T(8,128)(2,1)S(1)}, bf16[256,1024]{1,0:T(8,128)(2,1)S(1)}, u32[]{:S(2)}, u32[]{:S(2)}) collective-permute-start(bf16[256,1024]{1,0:T(8,128)(2,1)S(1)} %get-tuple-element.80), channel_id=1, source_target_pairs={{0,8},{4,12},{8,0},{12,4},{16,24},{20,28},{24,16},{28,20},{1,9},{5... | collective-permute-start | bytes 1572872 | tf_op jit(solution)/shard_map/ppermute | solution.py:549
  202.0 24.7 %collective-permute-start.32 = (bf16[256,1024]{1,0:T(8,128)(2,1)S(1)}, bf16[256,1024]{1,0:T(8,128)(2,1)S(1)}, u32[]{:S(2)}, u32[]{:S(2)}) collective-permute-start(bf16[256,1024]{1,0:T(8,128)(2,1)S(1)} %get-tuple-element.81), channel_id=1, source_target_pairs={{0,16},{4,20},{8,24},{12,28},{16,0},{20,4},{24,8},{28,12},{1,17},{... | collective-permute-start | bytes 1572872 | tf_op jit(solution)/shard_map/ppermute | solution.py:549
  202.7 24.7 %collective-permute-start.21 = (bf16[256,1024]{1,0:T(8,128)(2,1)S(1)}, bf16[256,1024]{1,0:T(8,128)(2,1)S(1)}, u32[]{:S(2)}, u32[]{:S(2)}) collective-permute-start(bf16[256,1024]{1,0:T(8,128)(2,1)S(1)} %get-tuple-element.82), channel_id=1, source_target_pairs={{0,4},{4,0},{8,12},{12,8},{16,20},{20,16},{24,28},{28,24},{1,5},{5... | collective-permute-start | bytes 1572872 | tf_op jit(solution)/shard_map/ppermute | solution.py:549
  203.4 34.0 %collective-permute-start.23 = (bf16[256,1024]{1,0:T(8,128)(2,1)S(1)}, bf16[256,1024]{1,0:T(8,128)(2,1)S(1)}, u32[]{:S(2)}, u32[]{:S(2)}) collective-permute-start(bf16[256,1024]{1,0:T(8,128)(2,1)S(1)} %get-tuple-element.86), channel_id=1, source_target_pairs={{0,24},{4,28},{8,16},{12,20},{16,8},{20,12},{24,0},{28,4},{1,25},{... | collective-permute-start | bytes 1572872 | tf_op jit(solution)/shard_map/ppermute | solution.py:549
  214.9 32.9 %collective-permute-start.27 = (bf16[256,1024]{1,0:T(8,128)(2,1)S(1)}, bf16[256,1024]{1,0:T(8,128)(2,1)S(1)}, u32[]{:S(2)}, u32[]{:S(2)}) collective-permute-start(bf16[256,1024]{1,0:T(8,128)(2,1)S(1)} %get-tuple-element.87), channel_id=1, source_target_pairs={{0,8},{4,12},{8,0},{12,4},{16,24},{20,28},{24,16},{28,20},{1,9},{5... | collective-permute-start | bytes 1572872 | tf_op jit(solution)/shard_map/ppermute | solution.py:549
  226.0 21.9 %collective-permute-start.25 = (bf16[256,1024]{1,0:T(8,128)(2,1)S(1)}, bf16[256,1024]{1,0:T(8,128)(2,1)S(1)}, u32[]{:S(2)}, u32[]{:S(2)}) collective-permute-start(bf16[256,1024]{1,0:T(8,128)(2,1)S(1)} %get-tuple-element.88), channel_id=1, source_target_pairs={{0,16},{4,20},{8,24},{12,28},{16,0},{20,4},{24,8},{28,12},{1,17},{... | collective-permute-start | bytes 1572872 | tf_op jit(solution)/shard_map/ppermute | solution.py:549
  249.6 87.8 %reduce-scatter.5.cloned.1.call-start = ((), (), s32[]{:S(2)}) async-start(), calls=%async_computation.6 | async-start | bytes 2949120 | tf_op jit(solution)/shard_map/reduce_scatter | solution.py:710
  259.8 123.7 %reduce-scatter.3.cloned.1.call-start = ((), (), s32[]{:S(2)}) async-start(), calls=%async_computation.5 | async-start | bytes 2621440 | tf_op jit(solution)/shard_map/reduce_scatter | solution.py:710
  334.9 118.1 %all-gather.22.cloned.1.call-start = ((), (), s32[]{:S(2)}) async-start(), calls=%async_computation.10 | async-start | bytes 5308416 | tf_op jit(solution)/shard_map/all_gather | solution.py:711
  337.4 142.0 %all-gather.20.cloned.1.call-start = ((), (), s32[]{:S(2)}) async-start(), calls=%async_computation.9 | async-start | bytes 4718592 | tf_op jit(solution)/shard_map/all_gather | solution.py:711
  422.5 15.9 %collective-permute-start.37 = (bf16[256,1024]{1,0:T(8,128)(2,1)S(1)}, bf16[256,1024]{1,0:T(8,128)(2,1)S(1)}, u32[]{:S(2)}, u32[]{:S(2)}) collective-permute-start(bf16[256,1024]{1,0:T(8,128)(2,1)S(1)} %get-tuple-element.72), channel_id=1, source_target_pairs={{0,24},{4,28},{8,16},{12,20},{16,8},{20,12},{24,0},{28,4},{1,25},{... | collective-permute-start | bytes 1572872 | tf_op jit(solution)/shard_map/ppermute | solution.py:549
  424.0 24.0 %collective-permute-start.41 = (bf16[256,1024]{1,0:T(8,128)(2,1)S(1)}, bf16[256,1024]{1,0:T(8,128)(2,1)S(1)}, u32[]{:S(2)}, u32[]{:S(2)}) collective-permute-start(bf16[256,1024]{1,0:T(8,128)(2,1)S(1)} %get-tuple-element.73), channel_id=1, source_target_pairs={{0,8},{4,12},{8,0},{12,4},{16,24},{20,28},{24,16},{28,20},{1,9},{5... | collective-permute-start | bytes 1572872 | tf_op jit(solution)/shard_map/ppermute | solution.py:549
  425.5 22.5 %collective-permute-start.39 = (bf16[256,1024]{1,0:T(8,128)(2,1)S(1)}, bf16[256,1024]{1,0:T(8,128)(2,1)S(1)}, u32[]{:S(2)}, u32[]{:S(2)}) collective-permute-start(bf16[256,1024]{1,0:T(8,128)(2,1)S(1)} %get-tuple-element.74), channel_id=1, source_target_pairs={{0,16},{4,20},{8,24},{12,28},{16,0},{20,4},{24,8},{28,12},{1,17},{... | collective-permute-start | bytes 1572872 | tf_op jit(solution)/shard_map/ppermute | solution.py:549
  (61 other events, 709.5 us)
Sparse Core Ops, SparseCore 0:
  12.8 48.6 all-gather.11
  63.0 49.2 all-gather.13
  127.1 50.1 all-gather.15
  249.7 36.7 all-gather.17
  289.3 48.0 reduce-scatter.4
  340.1 43.3 reduce-scatter.2
  385.5 41.1 all-gather.21
  428.8 50.6 all-gather.19

commit v3 on v2

--- a/solution.py
+++ b/solution.py
@@ -99,9 +99,12 @@
     return total
 
 
-def decays(run_ref, chunk, seq, rows, cols):
+def run_row_of(run_ref, chunk, seq, seqs):
+    return run_ref[pl.ds(chunk * seqs + seq, 1), :]
+
+
+def decays(run_row, rows, cols):
     size = rows.shape[0]
-    run_row = run_ref[chunk, seq][0:1, :]
     run_col = jnp.sum(jnp.where(rows == cols, run_row, 0.0), axis=1, keepdims=True)
     spread = jnp.where(rows >= cols, run_col - run_row, 0.0)
     decay_mat = jnp.where(rows >= cols, jnp.exp(spread), 0.0)
@@ -109,6 +112,17 @@
     return decay_mat, jnp.exp(run_col), jnp.exp(last - run_col)
 
 
+def running_sums(values, rows, cols):
+    upper = jnp.where(rows <= cols, 1.0, 0.0).astype(bf16)
+    total = None
+    for _ in range(3):
+        part = values.astype(bf16)
+        values = values - part.astype(f32)
+        term = product(part, upper)
+        total = term if total is None else total + term
+    return total
+
+
 def units_of(first, count, seqs):
     return [(first + chunk, seq) for chunk in range(count) for seq in range(seqs)]
 
@@ -117,22 +131,43 @@
 
 
 def forward_kernel(head_ref, *refs):
-    block_refs, refs = refs[:H], refs[H:]
+    block_refs, decay_refs, refs = refs[:H], refs[H : 2 * H], refs[2 * H :]
+    weight_in, beta_ref, taps_ref, gain_ref, state_ref, halo_ref = refs[:6]
+    outs, (run_ref, end_ref), held, refs = refs[6:14], refs[14:16], refs[16:24], refs[24:]
+    headed_ref, conv_ref, gate_ref, mixed_ref, inverse_ref, scores_ref, delta_ref, starts_ref = held
     (
-        weight_ref, beta_ref, run_ref, taps_ref, gain_ref, state_ref, halo_ref,
-        headed_ref, conv_ref, gate_ref, mixed_ref, inverse_ref, scores_ref, delta_ref, starts_ref,
-        end_ref,
-        rows_ref, recall_ref, target_ref, query_ref, write_ref, plain_ref,
+        block_ref, weight_ref, log_ref, rows_ref, recall_ref, target_ref, query_ref, write_ref,
+        plain_ref, block_sems, weight_sem, out_sems,
     ) = refs
     chunks, seqs, size, _ = conv_ref.shape
     rows, cols = iotas(size)
     head = head_ref[0]
 
+    weight_copy = pltpu.make_async_copy(
+        weight_in.at[:, pl.ds(0, WIDTH + DV)], weight_ref, weight_sem
+    )
+    weight_copy.start()
+    block_copies = [
+        pltpu.make_async_copy(block_refs[slot], block_ref.at[slot], block_sems.at[slot])
+        for slot in range(H)
+    ]
+    for copy in block_copies[:2]:
+        copy.start()
+    for slot in range(H):
+        logs = jnp.log(decay_refs[slot][pl.ds(head, 1), :])
+        for seq in range(seqs):
+            log_ref[pl.ds((slot ^ head) * seqs + seq, 1), :] = logs[:, seq * size : (seq + 1) * size]
+    run_ref[...] = running_sums(log_ref[...], rows, cols)
+
+    weight_copy.wait()
     for slot in range(H):
         chunk = slot ^ head
-        block = block_refs[slot][...]
+        if slot + 2 < H:
+            block_copies[slot + 2].start()
+        block_copies[slot].wait()
+        block = block_ref[slot]
         conv = product(block, weight_ref[:, :WIDTH]).astype(bf16)
-        gate = product(block, weight_ref[:, WIDTH : WIDTH + DV])
+        gate = product(block, weight_ref[:, WIDTH:])
         beta = product(block, beta_ref[...])
         for seq in range(seqs):
             span = slice(seq * size, (seq + 1) * size)
@@ -140,9 +175,21 @@
             gate_ref[chunk, seq, :, :DV] = gate[span]
             gate_ref[chunk, seq, :, DV:] = beta[span]
 
+    def send(index, first, count):
+        span = pl.ds(first, count)
+        pltpu.make_async_copy(
+            held[index].at[span], outs[index].at[span], out_sems.at[index]
+        ).start()
+
     def prepare(turn, _):
         units = units_of(turn * FORWARD_CHUNKS, FORWARD_CHUNKS, seqs)
-        keys, betas, growths, lowers, mats = [], [], [], [], []
+        lowers = []
+
+        @pl.when(turn > 0)
+        def _():
+            for index in (1, 2, 4, 5):
+                send(index, (turn - 1) * FORWARD_CHUNKS, FORWARD_CHUNKS)
+
         for slot, (chunk, seq) in enumerate(units):
             summed = conv_rows(conv_ref, halo_ref, rows_ref, taps_ref, chunk, seq, slot)
             active = summed * jax.nn.sigmoid(summed)
@@ -150,7 +197,7 @@
             key = active[:, DK : 2 * DK]
             key = key * lax.rsqrt(jnp.sum(key * key, axis=1, keepdims=True) + 1e-06)
             beta = jax.nn.sigmoid(gate_ref[chunk, seq, :, DV : DV + 1])
-            decay_mat, growth, fade = decays(run_ref, chunk, seq, rows, cols)
+            decay_mat, growth, fade = decays(run_row_of(run_ref, chunk, seq, seqs), rows, cols)
             target_ref[chunk, seq] = beta * active[:, 2 * DK :]
             query_ref[chunk, seq] = cat_parts(growth * query)
             write_ref[chunk, seq] = cat_parts((fade * key).T)
@@ -174,13 +221,24 @@
 
     def advance(chunk, states):
         following = []
+
+        @pl.when(chunk == 0)
+        def _():
+            for index in (1, 2, 4, 5):
+                send(index, chunks - FORWARD_CHUNKS, FORWARD_CHUNKS)
+
+        @pl.when(chunk > 0)
+        def _():
+            for index in (0, 3, 6, 7):
+                send(index, chunk - 1, 1)
+
         for seq in range(seqs):
             state = states[seq]
             starts_ref[chunk, seq] = state
             state_parts = parts(state)
             delta = target_ref[chunk, seq] - mul(from_cat(recall_ref[chunk, seq]), state_parts)
             delta_parts = parts(delta)
-            total = jnp.exp(run_ref[chunk, seq][0:1, size - 1 : size])
+            total = jnp.exp(run_row_of(run_ref, chunk, seq, seqs)[:, size - 1 : size])
             following.append(
                 total * state + mul(from_cat(write_ref[chunk, seq]), delta_parts)
             )
@@ -197,48 +255,83 @@
     final = lax.fori_loop(0, chunks, advance, tuple(state_ref[seq] for seq in range(seqs)))
     for seq in range(seqs):
         end_ref[seq] = final[seq]
+    for index in (0, 3, 6, 7):
+        send(index, chunks - 1, 1)
+    for index in range(len(held)):
+        pltpu.make_async_copy(held[index], outs[index], out_sems.at[index]).wait()
 
 
 BACKWARD_CHUNKS = 2
 
 
-def backward_kernel(
-    head_ref,
-    branch_ref, out_ref, conv_ref, gate_ref, run_ref, taps_ref, gain_ref, halo_ref, mixed_ref,
-    inverse_ref, scores_ref, delta_ref, starts_ref, d_end_ref, d_after_ref,
-    d_all_ref, grad_taps_ref, grad_gain_ref, d_start_ref, d_before_ref,
-    rows_ref, d_headed_ref, hold_ref, carry_ref, base_ref, back_ref, d_target_ref, d_state_ref,
-    d_conv_ref,
-):
+def backward_kernel(head_ref, *refs):
+    branch_refs, weight_in, refs = refs[:H], refs[H], refs[H + 1 :]
+    saved, refs = refs[:7], refs[7:]
+    run_ref, taps_ref, gain_ref, halo_ref, d_end_ref, d_after_ref = refs[:6]
+    d_all_out, grad_taps_ref, grad_gain_ref, d_start_ref, d_before_ref = refs[6:11]
+    branch_ref, weight_ref, held, refs = refs[11], refs[12], refs[13:20], refs[20:]
+    conv_ref, gate_ref, mixed_ref, inverse_ref, scores_ref, delta_ref, starts_ref = held
+    (
+        rows_ref, d_headed_ref, hold_ref, carry_ref, base_ref, back_ref, d_target_ref, d_state_ref,
+        d_conv_ref, d_all_ref, slope_ref, active_ref, column_ref,
+        block_sems, weight_sem, saved_sems, out_sem,
+    ) = refs
     chunks, seqs, size, _ = conv_ref.shape
     rows, cols = iotas(size)
     head = head_ref[0]
 
-    def pieces(chunk, seq, slot):
-        summed = conv_rows(conv_ref, halo_ref, rows_ref, taps_ref, chunk, seq, slot)
-        logistic = jax.nn.sigmoid(summed)
-        active = summed * logistic
-        query = active[:, :DK]
-        raw = active[:, DK : 2 * DK]
-        shrink = lax.rsqrt(jnp.sum(raw * raw, axis=1, keepdims=True) + 1e-06)
-        value = active[:, 2 * DK :]
-        beta = jax.nn.sigmoid(gate_ref[chunk, seq, :, DV : DV + 1])
-        slope = logistic * (1.0 + summed * (1.0 - logistic))
-        return slope, query, raw * shrink, shrink, value, beta
-
+    weight_copy = pltpu.make_async_copy(
+        weight_in.at[:, pl.ds(WIDTH + DV, DV)], weight_ref, weight_sem
+    )
+    weight_copy.start()
+    block_copies = [
+        pltpu.make_async_copy(branch_refs[slot], branch_ref.at[slot], block_sems.at[slot])
+        for slot in range(H)
+    ]
+    for copy in block_copies[:2]:
+        copy.start()
+    saved_copies = [
+        pltpu.make_async_copy(saved[index], held[index], saved_sems.at[index])
+        for index in range(len(saved))
+    ]
+
+    lane = lax.broadcasted_iota(jnp.int32, (size, 128), 1)
     grad_gain_ref[...] = jnp.zeros_like(grad_gain_ref)
     grad_taps_ref[...] = jnp.zeros_like(grad_taps_ref)
 
-    for chunk in range(H):
-        d_headed = product(branch_ref[chunk], out_ref[...])
+    weight_copy.wait()
+    for slot in range(H):
+        if slot + 2 < H:
+            block_copies[slot + 2].start()
+        if 1 < slot < len(saved_copies):
+            saved_copies[slot - 2].start()
+        block_copies[slot].wait()
+        d_headed = product(branch_ref[slot], weight_ref[...])
         for seq in range(seqs):
-            d_headed_ref[chunk, seq] = d_headed[seq * size : (seq + 1) * size]
+            d_headed_ref[slot ^ head, seq] = d_headed[seq * size : (seq + 1) * size]
+    for copy in saved_copies[:5]:
+        copy.wait()
+    for copy in saved_copies[5:]:
+        copy.start()
 
     def prepare(turn, _):
         units = units_of(turn * BACKWARD_CHUNKS, BACKWARD_CHUNKS, seqs)
-        for slot, (chunk, seq) in enumerate(units):
-            _, query, key, _, _, beta = pieces(chunk, seq, slot)
-            _, growth, fade = decays(run_ref, chunk, seq, rows, cols)
+        for chunk, seq in units:
+            unit = chunk * seqs + seq
+            summed = conv_rows(conv_ref, halo_ref, rows_ref, taps_ref, chunk, seq, unit)
+            logistic = jax.nn.sigmoid(summed)
+            active = summed * logistic
+            slope_ref[unit] = logistic * (1.0 + summed * (1.0 - logistic))
+            query = active[:, :DK]
+            raw = active[:, DK : 2 * DK]
+            shrink = lax.rsqrt(jnp.sum(raw * raw, axis=1, keepdims=True) + 1e-06)
+            key = raw * shrink
+            active_ref[unit, :, :DK] = query
+            active_ref[unit, :, DK : 2 * DK] = key
+            active_ref[unit, :, 2 * DK :] = active[:, 2 * DK :]
+            beta = jax.nn.sigmoid(gate_ref[chunk, seq, :, DV : DV + 1])
+            column_ref[unit] = jnp.where(lane == 0, shrink, beta)
+            _, growth, fade = decays(run_row_of(run_ref, chunk, seq, seqs), rows, cols)
             mixed = mixed_ref[chunk, seq]
             d_headed = d_headed_ref[chunk, seq]
             gate = gate_ref[chunk, seq, :, :DV]
@@ -271,7 +364,7 @@
             d_state_ref[chunk, seq] = d_state
             d_target = base_ref[chunk, seq] + mul(from_cat(hold_ref[chunk, seq]), parts(d_state))
             d_target_ref[chunk, seq] = d_target
-            total = jnp.exp(run_ref[chunk, seq][0:1, size - 1 : size])
+            total = jnp.exp(run_row_of(run_ref, chunk, seq, seqs)[:, size - 1 : size])
             back = mul(from_cat(carry_ref[chunk, seq]), parts(d_target))
             following.append(total * d_state + back_ref[chunk, seq] - back)
         return tuple(following)
@@ -280,6 +373,12 @@
     for seq in range(seqs):
         d_start_ref[seq] = first[seq]
         d_conv_ref[seq, size:, :] = d_after_ref[seq]
+    for copy in saved_copies[5:]:
+        copy.wait()
+
+    def send(chunk):
+        slot = chunk ^ head
+        pltpu.make_async_copy(d_all_ref.at[slot], d_all_out.at[slot], out_sem).start()
 
     def finish(turn, _):
         units = [
@@ -287,9 +386,21 @@
             for back in range(BACKWARD_CHUNKS)
             for seq in range(seqs)
         ]
-        for slot, (chunk, seq) in enumerate(units):
-            slope, query, key, shrink, value, beta = pieces(chunk, seq, slot)
-            decay_mat, growth, fade = decays(run_ref, chunk, seq, rows, cols)
+
+        @pl.when(turn > 0)
+        def _():
+            for back in range(BACKWARD_CHUNKS):
+                send(chunks - 1 - (turn - 1) * BACKWARD_CHUNKS - back)
+
+        for chunk, seq in units:
+            unit = chunk * seqs + seq
+            slope = slope_ref[unit]
+            query = active_ref[unit, :, :DK]
+            key = active_ref[unit, :, DK : 2 * DK]
+            value = active_ref[unit, :, 2 * DK :]
+            shrink = column_ref[unit, :, 0:1]
+            beta = column_ref[unit, :, 1:2]
+            decay_mat, growth, fade = decays(run_row_of(run_ref, chunk, seq, seqs), rows, cols)
             key_parts = parts(key)
             gram = mul_t(key_parts, key_parts) * decay_mat
             d_target = d_target_ref[chunk, seq]
@@ -319,7 +430,7 @@
             for tap in range(CONV):
                 start = HALO - (CONV - 1) + tap
                 grad_taps_ref[tap : tap + 1, :] += jnp.sum(
-                    d_conv * rows_ref[slot, start : start + size, :], axis=0, keepdims=True
+                    d_conv * rows_ref[unit, start : start + size, :], axis=0, keepdims=True
                 )
                 shift = CONV - 1 - tap
                 term = d_conv_ref[seq, shift : shift + size, :] * taps_ref[tap : tap + 1, :]
@@ -327,7 +438,6 @@
             d_conv_ref[seq, size:, :] = d_conv[:8, :]
             d_all_ref[chunk ^ head, seq, :, :WIDTH] = d_in.astype(bf16)
             d_logit = d_beta * beta * (1.0 - beta)
-            lane = lax.broadcasted_iota(jnp.int32, (size, 128), 1)
             d_all_ref[chunk ^ head, seq, :, WIDTH + DV :] = jnp.where(
                 lane == 0, d_logit, 0.0
             ).astype(bf16)
@@ -336,6 +446,9 @@
     lax.fori_loop(0, chunks // BACKWARD_CHUNKS, finish, 0)
     for seq in range(seqs):
         d_before_ref[seq] = d_conv_ref[seq, size:, :]
+    for chunk in range(BACKWARD_CHUNKS):
+        send(chunk)
+    pltpu.make_async_copy(d_all_ref, d_all_out, out_sem).wait()
 
 
 def whole(count):
@@ -349,45 +462,64 @@
 shaped = jax.ShapeDtypeStruct
 
 
+def cost(flops):
+    return pl.CostEstimate(flops=flops, bytes_accessed=0, transcendentals=0)
+
+
 def kernel_params():
     return pltpu.CompilerParams(vmem_limit_bytes=VMEM_LIMIT)
 
 
-def forward_rule(head, blocks, weight, beta_w, run, taps, gain, state, halo):
-    chunks, seqs, _, size = run.shape
-    lead = (chunks, seqs)
+def anywhere(count):
+    return [pl.BlockSpec(memory_space=pltpu.HBM)] * count
+
+
+def forward_rule(head, blocks, decay_blocks, weight, beta_w, taps, gain, state, halo):
+    rows, model = blocks[0].shape
+    seqs = state.shape[0]
+    size = rows // seqs
+    lead = (H, seqs)
+    held = [
+        (lead + (size, DV), bf16),
+        (lead + (size, WIDTH), bf16),
+        (lead + (size, DV + 128), f32),
+        (lead + (size, DV), f32),
+        (lead + (size, 2 * size), bf16),
+        (lead + (size, 2 * size), bf16),
+        (lead + (size, DV), f32),
+        (lead + (DK, DV), f32),
+    ]
     return pl.pallas_call(
         forward_kernel,
         name="mixer_forward",
-        out_shape=(
-            shaped(lead + (size, DV), bf16),
-            shaped(lead + (size, WIDTH), bf16),
-            shaped(lead + (size, DV + 128), f32),
-            shaped(lead + (size, DV), f32),
-            shaped(lead + (size, 2 * size), bf16),
-            shaped(lead + (size, 2 * size), bf16),
-            shaped(lead + (size, DV), f32),
-            shaped(lead + (DK, DV), f32),
-            shaped((seqs, DK, DV), f32),
-        ),
-        in_specs=scalar() + whole(H + 7),
-        out_specs=tuple(whole(9)),
-        scratch_shapes=[
+        out_shape=[shaped(*item) for item in held]
+        + [shaped((H * seqs, size), f32), shaped((seqs, DK, DV), f32)],
+        in_specs=scalar() + anywhere(H) + whole(H) + anywhere(1) + whole(5),
+        out_specs=anywhere(8) + whole(2),
+        scratch_shapes=[pltpu.VMEM(*item) for item in held]
+        + [
+            pltpu.VMEM((H, rows, model), bf16),
+            pltpu.VMEM((model, WIDTH + DV), bf16),
+            pltpu.VMEM((H * seqs, size), f32),
             pltpu.VMEM((FORWARD_CHUNKS * seqs, HALO + size, WIDTH), f32),
             pltpu.VMEM(lead + (size, 2 * DK), bf16),
             pltpu.VMEM(lead + (size, DV), f32),
             pltpu.VMEM(lead + (size, 2 * DK), bf16),
             pltpu.VMEM(lead + (DK, 2 * size), bf16),
             pltpu.VMEM(lead + (size, 2 * size), bf16),
+            pltpu.SemaphoreType.DMA((H,)),
+            pltpu.SemaphoreType.DMA,
+            pltpu.SemaphoreType.DMA((8,)),
         ],
         compiler_params=kernel_params(),
-    )(head, *blocks, weight, beta_w, run, taps, gain, state, halo)
-
-
-def backward_rule(head, branch, out_w, run, taps, gain, halo, saved, d_end, d_after):
-    chunks, seqs, _, size = run.shape
-    lead = (chunks, seqs)
-    conv_in, gate_beta, mixed, inverse, scores, delta, starts = saved
+    )(head, *blocks, *decay_blocks, weight, beta_w, taps, gain, state, halo)
+
+
+def backward_rule(head, branch, weight, saved, run, taps, gain, halo, d_end, d_after):
+    rows, model = branch[0].shape
+    seqs = d_end.shape[0]
+    size = rows // seqs
+    lead = (H, seqs)
     return pl.pallas_call(
         backward_kernel,
         name="mixer_backward",
@@ -398,10 +530,15 @@
             shaped((seqs, DK, DV), f32),
             shaped((seqs, 8, WIDTH), f32),
         ),
-        in_specs=scalar() + whole(15),
-        out_specs=tuple(whole(5)),
+        in_specs=scalar() + anywhere(H + 8) + whole(6),
+        out_specs=tuple(anywhere(1) + whole(4)),
         scratch_shapes=[
-            pltpu.VMEM((BACKWARD_CHUNKS * seqs, HALO + size, WIDTH), f32),
+            pltpu.VMEM((H, rows, model), bf16),
+            pltpu.VMEM((model, DV), bf16),
+        ]
+        + [pltpu.VMEM(item.shape, item.dtype) for item in saved]
+        + [
+            pltpu.VMEM((H * seqs, HALO + size, WIDTH), f32),
             pltpu.VMEM(lead + (size, DV), f32),
             pltpu.VMEM(lead + (size, 2 * DK), bf16),
             pltpu.VMEM(lead + (DK, 2 * size), bf16),
@@ -410,96 +547,235 @@
             pltpu.VMEM(lead + (size, DV), f32),
             pltpu.VMEM(lead + (DK, DV), f32),
             pltpu.VMEM((seqs, size + 8, WIDTH), f32),
+            pltpu.VMEM(lead + (size, WIDTH + DV + 128), bf16),
+            pltpu.VMEM((H * seqs, size, WIDTH), f32),
+            pltpu.VMEM((H * seqs, size, WIDTH), f32),
+            pltpu.VMEM((H * seqs, size, 128), f32),
+            pltpu.SemaphoreType.DMA((H,)),
+            pltpu.SemaphoreType.DMA,
+            pltpu.SemaphoreType.DMA((7,)),
+            pltpu.SemaphoreType.DMA,
         ],
         compiler_params=kernel_params(),
-    )(
-        head, branch, out_w, conv_in, gate_beta, run, taps, gain, halo, mixed, inverse, scores,
-        delta, starts, d_end, d_after,
-    )
-
-
-def out_kernel(head_ref, *refs):
-    block_refs, (headed_ref, inputs_ref, gain_ref, residual_ref, normed_ref) = refs[:H], refs[H:]
-    head = head_ref[0]
+    )(head, *branch, weight, *saved, run, taps, gain, halo, d_end, d_after)
+
+
+def out_kernel(
+    weight_in, headed_ref, inputs_ref, gain_ref, residual_ref, normed_ref, weight_ref, sems
+):
+    copies = [
+        pltpu.make_async_copy(weight_in.at[peer], weight_ref.at[peer], sems.at[peer])
+        for peer in range(H)
+    ]
+    for copy in copies:
+        copy.start()
     total = inputs_ref[...].astype(f32)
-    for slot in range(H):
-        total = total + contract_cols(headed_ref[slot ^ head], block_refs[slot][...])
+    for peer in range(H):
+        copies[peer].wait()
+        total = total + contract_cols(headed_ref[peer], weight_ref[peer])
     residual_ref[...] = total
     scale = lax.rsqrt(jnp.mean(total * total, axis=1, keepdims=True) + 1e-05)
     normed_ref[...] = (total * scale * gain_ref[...]).astype(bf16)
 
 
-def out_rule(head, blocks, headed, inputs, gain):
+def out_rule(weight, headed, inputs, gain):
     return pl.pallas_call(
         out_kernel,
         name="out_projection",
         out_shape=(shaped(inputs.shape, f32), shaped(inputs.shape, bf16)),
-        in_specs=scalar() + whole(H + 3),
+        in_specs=anywhere(1) + whole(3),
         out_specs=tuple(whole(2)),
+        scratch_shapes=[pltpu.VMEM(weight.shape, bf16), pltpu.SemaphoreType.DMA((H,))],
         compiler_params=kernel_params(),
-    )(head, *blocks, headed, inputs, gain)
-
-
-def ffn_kernel(head_ref, normed_ref, up_ref, weight_ref, d_both_ref, hidden_ref, d_in_ref, out_ref):
+    )(weight, headed, inputs, gain)
+
+
+def ffn_kernel(*refs):
+    normed_refs, up_refs, refs = refs[:H], refs[H : 2 * H], refs[2 * H :]
+    weight_in, d_both_ref, hidden_ref, d_even_ref, d_odd_ref, even_ref, odd_ref = refs[:7]
+    normed_all_ref, up_all_ref, weight_ref, normed_sems, up_sems, weight_sem = refs[7:]
     share = weight_ref.shape[1] // 3
-    both = product(normed_ref[0], weight_ref[:, : 2 * share])
-    d_hidden = product(up_ref[0], weight_ref[:, 2 * share :])
-    gate, up = both[:, :share], both[:, share:]
-    logistic = jax.nn.sigmoid(gate)
-    swish = gate * logistic
-    hidden = (swish * up).astype(bf16)
-    hidden_ref[0] = hidden
-    d_gate = (d_hidden * up * logistic * (1.0 + gate * (1.0 - logistic))).astype(bf16)
-    d_up = (d_hidden * swish).astype(bf16)
-    d_both = jnp.concatenate([d_gate, d_up], 1)
-    d_both_ref[0] = d_both
-    d_in_ref[0] = contract_cols(d_both, weight_ref[:, : 2 * share]).astype(bf16)
-    out_ref[0] = contract_cols(hidden, weight_ref[:, 2 * share :]).astype(bf16)
-
-
-def ffn_rule(head, normed, upstream, weight):
-    count, rows, model = normed.shape
+    step = pl.program_id(0)
+
+    def copy_of(source, target, sems, slot):
+        return pltpu.make_async_copy(source, target.at[slot], sems.at[slot])
+
+    def start_pair(pair):
+        for slot in (2 * pair, 2 * pair + 1):
+            copy_of(normed_refs[slot], normed_all_ref, normed_sems, slot).start()
+            copy_of(up_refs[slot], up_all_ref, up_sems, slot).start()
+
+    @pl.when(step == 0)
+    def _():
+        weight_copy = pltpu.make_async_copy(weight_in, weight_ref, weight_sem)
+        weight_copy.start()
+        start_pair(0)
+        weight_copy.wait()
+
+    for later in range(1, H // 2):
+
+        @pl.when(step == later - 1)
+        def _():
+            start_pair(later)
+
+    for side, d_in_ref, out_ref in ((0, d_even_ref, even_ref), (1, d_odd_ref, odd_ref)):
+        slot = 2 * step + side
+        copy_of(normed_refs[0], normed_all_ref, normed_sems, slot).wait()
+        copy_of(up_refs[0], up_all_ref, up_sems, slot).wait()
+        both = product(normed_all_ref[slot], weight_ref[:, : 2 * share])
+        d_hidden = product(up_all_ref[slot], weight_ref[:, 2 * share :])
+        gate, up = both[:, :share], both[:, share:]
+        logistic = jax.nn.sigmoid(gate)
+        swish = gate * logistic
+        hidden = (swish * up).astype(bf16)
+        hidden_ref[side] = hidden
+        d_gate = (d_hidden * up * logistic * (1.0 + gate * (1.0 - logistic))).astype(bf16)
+        d_up = (d_hidden * swish).astype(bf16)
+        d_both = jnp.concatenate([d_gate, d_up], 1)
+        d_both_ref[side] = d_both
+        d_in_ref[0] = contract_cols(d_both, weight_ref[:, : 2 * share]).astype(bf16)
+        out_ref[0] = contract_cols(hidden, weight_ref[:, 2 * share :]).astype(bf16)
+
+
+def ffn_rule(normed, upstream, weight):
+    rows, model = normed[0].shape
     share = weight.shape[1] // 3
 
-    def same(step, head_ref):
-        return (step, 0, 0)
-
-    def moved(step, head_ref):
-        return (step ^ head_ref[0], 0, 0)
+    def moving(count, width):
+        return pl.BlockSpec((count, rows, width), lambda step: (step, 0, 0))
 
     return pl.pallas_call(
         ffn_kernel,
         name="feed_forward",
-        grid_spec=pltpu.PrefetchScalarGridSpec(
-            num_scalar_prefetch=1,
-            grid=(count,),
-            in_specs=[
-                pl.BlockSpec((1, rows, model), same),
-                pl.BlockSpec((1, rows, model), moved),
-                pl.BlockSpec(weight.shape, lambda step, head_ref: (0, 0)),
-            ],
-            out_specs=[
-                pl.BlockSpec((1, rows, 2 * share), same),
-                pl.BlockSpec((1, rows, share), moved),
-                pl.BlockSpec((1, rows, model), moved),
-                pl.BlockSpec((1, rows, model), moved),
-            ],
-        ),
-        out_shape=(
-            shaped((count, rows, 2 * share), bf16),
-            shaped((count, rows, share), bf16),
-            shaped((count, rows, model), bf16),
-            shaped((count, rows, model), bf16),
-        ),
+        grid=(H // 2,),
+        in_specs=anywhere(2 * H + 1),
+        out_specs=[moving(2, 2 * share), moving(2, share)] + [moving(1, model)] * 4,
+        out_shape=[shaped((H, rows, 2 * share), bf16), shaped((H, rows, share), bf16)]
+        + [shaped((H // 2, rows, model), bf16)] * 4,
+        scratch_shapes=[pltpu.VMEM((H, rows, model), bf16)] * 2
+        + [
+            pltpu.VMEM(weight.shape, bf16),
+            pltpu.SemaphoreType.DMA((H,)),
+            pltpu.SemaphoreType.DMA((H,)),
+            pltpu.SemaphoreType.DMA,
+        ],
         compiler_params=kernel_params(),
-    )(head, normed, upstream, weight)
+    )(*normed, *upstream, weight)
+
+
+GRAD_TILE = 256
+
+
+def ffn_grads_kernel(*refs):
+    normed_refs, up_refs, (d_both_ref, hidden_ref, out_ref) = refs[:H], refs[H : 2 * H], refs[2 * H :]
+    wide = d_both_ref.shape[1]
+    normed = jnp.concatenate([ref[...] for ref in normed_refs], 0)
+    out_ref[:, :wide] = contract_rows(normed, d_both_ref[...]).astype(bf16)
+    upstream = jnp.concatenate([ref[...] for ref in up_refs], 0)
+    out_ref[:, wide:] = contract_rows(upstream, hidden_ref[...]).astype(bf16)
+
+
+def ffn_grads_rule(normed, upstream, d_both, hidden):
+    rows, model = normed[0].shape
+    width = d_both.shape[1] + hidden.shape[1]
+    columns = pl.BlockSpec((rows, GRAD_TILE), lambda step: (0, step))
+    return pl.pallas_call(
+        ffn_grads_kernel,
+        name="feed_forward_grads",
+        grid=(model // GRAD_TILE,),
+        in_specs=[columns] * (2 * H)
+        + [
+            pl.BlockSpec(d_both.shape, lambda step: (0, 0)),
+            pl.BlockSpec(hidden.shape, lambda step: (0, 0)),
+        ],
+        out_specs=pl.BlockSpec((GRAD_TILE, width), lambda step: (step, 0)),
+        out_shape=shaped((model, width), bf16),
+        cost_estimate=cost(4 * H * rows * model * width),
+        compiler_params=kernel_params(),
+    )(*normed, *upstream, d_both, hidden)
+
+
+def mixer_grads_kernel(head_ref, *refs):
+    normed_refs, branch_refs, refs = refs[:H], refs[H : 2 * H], refs[2 * H :]
+    d_all_ref, headed_ref, weight_ref, beta_ref, out_ref, small_ref = refs
+    head = head_ref[0]
+    width = WIDTH + DV
+    normed = jnp.concatenate([ref[...] for ref in normed_refs], 0)
+    partial = contract_rows(normed, d_all_ref[:, :width])
+    out_ref[:, :width] = partial.astype(bf16)
+    beta = contract_rows(normed, d_all_ref[:, width:])
+    branch = jnp.concatenate([ref[...] for ref in branch_refs], 0)
+    headed = jnp.concatenate([headed_ref[slot ^ head] for slot in range(H)], 0)
+    out_ref[:, width:] = contract_rows(branch, headed).astype(bf16)
+    weighed = jnp.sum(partial * weight_ref[:, :width].astype(f32), axis=1, keepdims=True)
+    weighed = weighed + beta[:, :1] * beta_ref[:, :1].astype(f32)
+    lane = lax.broadcasted_iota(jnp.int32, beta.shape, 1)
+    small_ref[...] = jnp.where(lane == 0, beta, jnp.where(lane == 1, weighed, 0.0))
+
+
+def mixer_grads_rule(head, normed, branch, d_all, headed, weight, beta_w):
+    rows, model = normed[0].shape
+    width = WIDTH + 2 * DV
+    columns = pl.BlockSpec((rows, GRAD_TILE), lambda step: (0, step))
+    return pl.pallas_call(
+        mixer_grads_kernel,
+        name="mixer_grads",
+        grid=(model // GRAD_TILE,),
+        in_specs=scalar()
+        + [columns] * (2 * H)
+        + [
+            pl.BlockSpec(d_all.shape, lambda step: (0, 0)),
+            pl.BlockSpec(headed.shape, lambda step: (0, 0, 0)),
+            pl.BlockSpec((GRAD_TILE, width), lambda step: (step, 0)),
+            pl.BlockSpec((GRAD_TILE, 128), lambda step: (step, 0)),
+        ],
+        out_specs=[
+            pl.BlockSpec((GRAD_TILE, width), lambda step: (step, 0)),
+            pl.BlockSpec((GRAD_TILE, 128), lambda step: (step, 0)),
+        ],
+        out_shape=[shaped((model, width), bf16), shaped((model, 128), f32)],
+        compiler_params=kernel_params(),
+    )(head, *normed, *branch, d_all, headed, weight, beta_w)
+
+
+def d_in_kernel(d_all_ref, weight_ref, beta_ref, even_ref, odd_ref):
+    width = WIDTH + DV
+    for side, out_ref in ((0, even_ref), (1, odd_ref)):
+        d_all = d_all_ref[side]
+        total = contract_cols(d_all[:, :width], weight_ref[:, :width])
+        total = total + contract_cols(d_all[:, width:], beta_ref[...])
+        out_ref[0] = total.astype(bf16)
+
+
+def d_in_rule(d_all, weight, beta_w):
+    _, rows, width = d_all.shape
+    model = weight.shape[0]
+    out = pl.BlockSpec((1, rows, model), lambda step: (step, 0, 0))
+    return pl.pallas_call(
+        d_in_kernel,
+        name="mixer_d_in",
+        grid=(H // 2,),
+        in_specs=[
+            pl.BlockSpec((2, rows, width), lambda step: (step, 0, 0)),
+            pl.BlockSpec(weight.shape, lambda step: (0, 0)),
+            pl.BlockSpec(beta_w.shape, lambda step: (0, 0)),
+        ],
+        out_specs=[out, out],
+        out_shape=[shaped((H // 2, rows, model), bf16)] * 2,
+        compiler_params=kernel_params(),
+    )(d_all, weight, beta_w)
+
+
+JOIN_ROWS = 32
 
 
 def join_kernel(spread_ref, *out_refs):
     start = 0
     for out_ref in out_refs:
-        width = out_ref.shape[1]
-        out_ref[...] = spread_ref[0, :, start : start + width].astype(f32)
+        width = out_ref.shape[1] // H
+        for peer in range(H):
+            piece = spread_ref[peer, :, start : start + width]
+            out_ref[:, peer * width : (peer + 1) * width] = piece.astype(f32)
         start += width
 
 
@@ -508,32 +784,34 @@
     return pl.pallas_call(
         join_kernel,
         name="join_heads",
-        grid=(count,),
-        in_specs=[pl.BlockSpec((1, rows, width), lambda step: (step, 0, 0))],
-        out_specs=[pl.BlockSpec((rows, width), lambda step: (0, step)) for width in widths],
+        grid=(rows // JOIN_ROWS,),
+        in_specs=[pl.BlockSpec((count, JOIN_ROWS, width), lambda step: (0, step, 0))],
+        out_specs=[pl.BlockSpec((JOIN_ROWS, count * width), lambda step: (step, 0)) for width in widths],
         out_shape=[shaped((rows, count * width), f32) for width in widths],
         compiler_params=kernel_params(),
     )(spread)
 
 
-def join_hidden_kernel(total, spread_ref, *out_refs):
+def join_hidden_kernel(spread_ref, *out_refs):
     count, _, width = spread_ref.shape
     share = width // len(out_refs)
+    total = out_refs[0].shape[1]
     for index, out_ref in enumerate(out_refs):
         for peer in range(count):
-            start = min(peer * share, total - share)
-            skip = peer * share - start
+            first = peer * share
+            skip = first - min(first, total - share)
             piece = spread_ref[peer, :, index * share + skip : (index + 1) * share]
-            out_ref[:, start + skip : start + share] = piece.astype(f32)
+            out_ref[:, first : first + share - skip] = piece.astype(f32)
 
 
 def join_hidden_rule(spread, total, pieces):
     count, rows, width = spread.shape
     return pl.pallas_call(
-        lambda *refs: join_hidden_kernel(total, *refs),
+        join_hidden_kernel,
         name="join_hidden",
-        in_specs=whole(1),
-        out_specs=whole(pieces),
+        grid=(rows // JOIN_ROWS,),
+        in_specs=[pl.BlockSpec((count, JOIN_ROWS, width), lambda step: (0, step, 0))],
+        out_specs=[pl.BlockSpec((JOIN_ROWS, total), lambda step: (step, 0))] * pieces,
         out_shape=[shaped((rows, total), f32)] * pieces,
         compiler_params=kernel_params(),
     )(spread)
@@ -549,21 +827,31 @@
     return lax.ppermute(array, axis, [(i, i ^ bits) for i in range(lax.axis_size(axis))])
 
 
+def neighbours(own):
+    return [own] + [swapped(own, "seq", bits) for bits in range(2, H, 2)]
+
+
+def with_siblings(blocks):
+    return [each for block in blocks for each in (block, swapped(block, "seq", 1))]
+
+
 def gather_blocks(own):
-    near, far, across = (swapped(own, "seq", bits) for bits in (2, 4, 6))
-    blocks = [own, None, near, None, far, None, across, None]
-    for slot in range(0, H, 2):
-        blocks[slot + 1] = swapped(blocks[slot], "seq", 1)
-    return blocks
-
-
-def scatter_blocks(partial):
-    handed = [swapped(partial[slot + 1], "seq", 1) for slot in range(0, H, 2)]
-    sums = [partial[2 * i].astype(f32) + handed[i].astype(f32) for i in range(H // 2)]
-    total = sums[0]
-    for i in range(H // 2 - 1, 0, -1):
-        total = total + swapped(sums[i].astype(bf16), "seq", 2 * i).astype(f32)
-    return total
+    return with_siblings(neighbours(own))
+
+
+def pair_sums(even, handed):
+    sums = [even[i].astype(f32) + handed[i].astype(f32) for i in range(H // 2)]
+    return sums[0], [each.astype(bf16) for each in sums[1:]]
+
+
+def exchanged(sums):
+    return [swapped(sums[i - 1], "seq", 2 * i) for i in range(1, H // 2)]
+
+
+def total_of(own, received):
+    for piece in received:
+        own = own + piece.astype(f32)
+    return own
 
 
 def rms_scale(values):
@@ -637,26 +925,38 @@
             axis=1,
         )
     )
-    ffn_w = gather_weight(
-        jnp.concatenate(
-            [own_hidden(w_ffn_gate), own_hidden(w_ffn_up), own_hidden(w_ffn_down)], axis=1
-        )
-    )
+    ffn_w_own = jnp.concatenate(
+        [own_hidden(w_ffn_gate), own_hidden(w_ffn_up), own_hidden(w_ffn_down)], axis=1
+    )
+
+    def reduce_weight(partial):
+        return lax.psum_scatter(partial, "wt", scatter_dimension=0, tiled=True)
+
+    def spread_grads(summed):
+        spread = lax.all_gather(summed, "seq")
+        if stages > 1:
+            spread = spread.reshape((stages, H) + summed.shape).astype(f32)
+            spread = jnp.sum(spread, axis=0)
+        return spread
+
     own_in = inputs.reshape(rows, model)
     flat_in = own_in.astype(f32)
     normed_own = (flat_in * rms_scale(flat_in) * norm_in).astype(bf16)
-    normed_in = gather_blocks(normed_own)
     upstream_own = cotangent.reshape(rows, model)
-    upstream = jnp.stack(gather_blocks(upstream_own))
+    decay_rows = decay.reshape(rows, H).T
+    near_in = neighbours(normed_own)
+    near_in, late_upstream, ffn_w_own = lax.optimization_barrier(
+        (near_in, upstream_own, ffn_w_own)
+    )
+    up_near = neighbours(late_upstream)
+    normed_in, decay_blocks, mixer_w = lax.optimization_barrier(
+        (with_siblings(near_in), gather_blocks(decay_rows), mixer_w)
+    )
+    ffn_w = gather_weight(ffn_w_own)
     beta_w = jnp.pad(own_columns(w_beta, 1), ((0, 0), (0, 127)))
     in_width = WIDTH + DV
-    out_w = mixer_w[:, in_width:]
-    out_blocks = gather_blocks(out_w)
-
-    own_decay = gather_rows(decay)
-    own_decay = lax.dynamic_index_in_dim(own_decay, head, axis=3, keepdims=False)
-    run = jnp.cumsum(jnp.log(own_decay), axis=-1)
-    run = jnp.broadcast_to(run[:, :, None, :], (H, seqs, 8, size))
+    out_w = gather_rows(mixer_w[:, in_width:])
+
     taps = jnp.concatenate(
         [
             own_columns(conv_weight[:, : H * DK], DK),
@@ -677,75 +977,75 @@
         halo = jnp.where(place >= H, rolled.reshape(halo.shape), halo)
     for stage in range(stages):
         headed, *saved, ending = forward_rule(
-            head_arg, normed_in, mixer_w, beta_w, run, taps, gain, state, halo
+            head_arg, normed_in, decay_blocks, mixer_w, beta_w, taps, gain, state, halo
         )
+        run = saved.pop()
         if stage < stages - 1:
             state = passed_along(ending, "seq", H)
 
     headed = headed.reshape(H, rows, DV)
+    headed, up_near = lax.optimization_barrier((headed, up_near))
+    upstream = with_siblings(up_near)
     own_headed = lax.all_to_all(headed, "seq", 0, 0, axis_index_groups=groups, tiled=True)
-    residual, normed_mid = out_rule(head_arg, out_blocks, own_headed, own_in, norm_mid[None, :])
-    normed_mid = gather_rows(normed_mid)
-
-    d_both, hidden, d_mid_blocks, ffn_blocks = ffn_rule(head_arg, normed_mid, upstream, ffn_w)
-    d_normed_mid = scatter_blocks(d_mid_blocks)
+    residual, normed_own = out_rule(out_w, own_headed, own_in, norm_mid[None, :])
+    normed_mid = gather_blocks(normed_own)
+
+    d_both, hidden, d_even, d_odd, even, odd = ffn_rule(normed_mid, upstream, ffn_w)
+    ffn_partial = ffn_grads_rule(
+        normed_mid, upstream, d_both.reshape(all_rows, -1), hidden.reshape(all_rows, -1)
+    )
+    ffn_summed = reduce_weight(ffn_partial)
+    handed, _ = lax.optimization_barrier((swapped(d_odd, "seq", 1), ffn_partial))
+    own_sum, sums = pair_sums(d_even, handed)
+    received = exchanged(sums)
+    ffn_own, ffn_sums = pair_sums(even, swapped(odd, "seq", 1))
+    received, ffn_own, ffn_sums = lax.optimization_barrier((received, ffn_own, ffn_sums))
+    d_normed_mid = total_of(own_sum, received)
     d_from_mid, grad_mid = rms_back(residual, norm_mid, d_normed_mid)
     d_residual = upstream_own.astype(f32) + d_from_mid
-    branch = gather_rows(d_residual.astype(bf16))
+    branch, ffn_sums, ffn_summed = lax.optimization_barrier(
+        (gather_blocks(d_residual.astype(bf16)), ffn_sums, ffn_summed)
+    )
+    ffn_spread = spread_grads(ffn_summed)
+    ffn_received = exchanged(ffn_sums)
 
     d_end = jnp.zeros((seqs, DK, DV), f32)
     d_after = jnp.zeros((seqs, 8, WIDTH), f32)
     for stage in range(stages):
         d_all, grad_taps, grad_gain, d_start, d_before = backward_rule(
-            head_arg, branch, out_w, run, taps, gain, halo, saved, d_end, d_after
+            head_arg, branch, mixer_w, saved, run, taps, gain, halo, d_end, d_after
         )
         if stage < stages - 1:
             d_end = passed_along(d_start, "seq", -H)
             d_after = passed_along(d_before, "seq", -H)
-    d_all = d_all.reshape(all_rows, -1)
-
-    layer_out = (residual + scatter_blocks(ffn_blocks)).astype(bf16).reshape(inputs.shape)
-
-    def reduce_grads(partial):
-        summed = lax.psum_scatter(partial.astype(bf16), "wt", scatter_dimension=0, tiled=True)
-        spread = lax.all_gather(summed, "seq")
-        if stages > 1:
-            spread = spread.reshape((stages, H) + summed.shape).astype(f32)
-            spread = jnp.sum(spread, axis=0)
-        return spread
-
-    def flat(blocks):
-        return blocks.reshape(all_rows, -1)
-
-    ffn_partial = jnp.concatenate(
-        [
-            contract_rows(flat(normed_mid), flat(d_both)),
-            contract_rows(flat(upstream), flat(hidden)),
-        ],
-        axis=1,
-    )
-    ffn_grads = join_hidden_rule(reduce_grads(ffn_partial), hidden_all, 3)
-
-    mixer_partial = contract_rows(jnp.concatenate(normed_in, axis=0), d_all)
-    out_partial = contract_rows(flat(branch), flat(headed))
-    mixer_grads = join_rule(
-        reduce_grads(jnp.concatenate([mixer_partial[:, :in_width], out_partial], axis=1)),
-        [DK, DK, DV, DV, DV],
-    )
-
-    in_w = jnp.concatenate([mixer_w[:, :in_width], beta_w], axis=1)
-    d_in_blocks = contract_cols(d_all, in_w).astype(bf16).reshape(H, rows, model)
-    d_from_in, _ = rms_back(flat_in, norm_in, scatter_blocks(d_in_blocks))
+    d_all = d_all.reshape(H, rows, -1)
+
+    layer_out = (residual + total_of(ffn_own, ffn_received)).astype(bf16).reshape(inputs.shape)
+
+    mixer_partial, narrow = mixer_grads_rule(
+        head_arg, normed_in, branch, d_all.reshape(all_rows, -1), headed, mixer_w, beta_w
+    )
+    mixer_partial, ffn_spread = lax.optimization_barrier((mixer_partial, ffn_spread))
+    mixer_summed = reduce_weight(mixer_partial)
+    ffn_grads = join_hidden_rule(ffn_spread, hidden_all, 3)
+
+    d_even, d_odd = d_in_rule(d_all, mixer_w, beta_w)
+    own_sum, sums = pair_sums(d_even, swapped(d_odd, "seq", 1))
+    received, mixer_summed, narrow, ffn_grads = lax.optimization_barrier(
+        (exchanged(sums), mixer_summed, narrow, ffn_grads)
+    )
+    mixer_grads = join_rule(spread_grads(mixer_summed), [DK, DK, DV, DV, DV])
+    d_normed_in = total_of(own_sum, received)
+    d_from_in, _ = rms_back(flat_in, norm_in, d_normed_in)
     grad_input = (d_residual + d_from_in).reshape(inputs.shape)
 
-    grad_in_part = jnp.sum(mixer_partial * in_w.astype(f32), axis=1) / norm_in
     small = jnp.concatenate(
         [
             grad_taps[:CONV].reshape(-1),
-            mixer_partial[:, in_width],
+            narrow[:, 0],
             grad_gain[0],
             grad_mid,
-            grad_in_part,
+            narrow[:, 1] / norm_in,
         ]
     ).reshape(-1, 128)
     step = 1

time: 504 us -> 421 us (0.84)
  local copies, waits for them, and re-layouts: 58.2 us -> 21 us
  waiting for transfers between devices: 214 us -> 180 us
  Pallas kernels: 102 us -> 133 us
  blocking collectives: 27.5 us -> 0 us
  matrix products: 21.5 us -> 0 us
    ppermute x47 -> x52, waiting for transfers between devices: 99.4 us -> 152 us  [swapped(): lax.ppermute(array, axis, [(i, i ^ bits) for i in range(lax.axis_size(axi...]
    reduce_scatter x2, waiting for transfers between devices: 48.3 us -> 0.01 us  [reduce_weight(): return lax.psum_scatter(partial, 'wt', scatter_dimension=0, tiled=True)]
    pallas_call x4 -> x7, Pallas kernels: 59.9 us -> 90.8 us  [the longest x1 30 us: forward_rule(): pl.pallas_call(forward_kernel, name='mixer_forward', out_shape=[shaped(*i...]
    all_gather x2 -> x1, waiting for transfers between devices: 27.5 us -> 0.01 us  [gather_rows(): return lax.all_gather(local, 'seq', axis_index_groups=groups)]
    all_gather x1 -> x0, blocking collectives: 27.5 us -> none  [gather_rows(): return lax.all_gather(local, 'seq', axis_index_groups=groups)]
    dot_general x5 -> x0, matrix products: 21.5 us -> none  [dot(): lax.dot_general(left, right, (dims, ((), ())), preferred_element_type=f32)]
    all_gather x2 -> x0, local copies, waits for them, and re-layouts: 13.1 us -> none  [reduce_grads(): spread = lax.all_gather(summed, 'seq')]
    unnamed x100 -> x115, local copies, waits for them, and re-layouts: 23.1 us -> 11.4 us
  transfers between devices with their start and end apart: 56 -> 60, of which waited for: 25 -> 26; matrix products, arithmetic and copies ran while one was open for 17% -> 7% of each run, Pallas kernels for 16% -> 26%
where the time goes in v3:
time: 421 us; the launch traced here: 413 us
  waiting for transfers between devices  180 us (43%)
  Pallas kernels  133 us (32%)
  starting transfers between devices  41.5 us (10%)
  other arithmetic  21.6 us (5%)
  local copies, waits for them, and re-layouts  21 us (5%)
  between operations  15.2 us (4%)
    ppermute x52, waiting for transfers between devices, swapped(): lax.ppermute(array, axis, [(i, i ^ bits) for i in range(lax.axis_size(axi...  152 us
    ppermute x52, starting transfers between devices, swapped(): lax.ppermute(array, axis, [(i, i ^ bits) for i in range(lax.axis_size(axi...  37.5 us
    pallas_call x1, Pallas kernels, backward_rule(): pl.pallas_call(backward_kernel, name='mixer_backward', out_shape=(shaped(...  36.4 us
    pallas_call x1, Pallas kernels, forward_rule(): pl.pallas_call(forward_kernel, name='mixer_forward', out_shape=[shaped(*i...  30 us
    pallas_call x1, Pallas kernels, ffn_rule(): pl.pallas_call(ffn_kernel, name='feed_forward', grid=(H // 2,), in_specs=...  16.3 us
    all_to_all x1, waiting for transfers between devices, shards(): lax.all_to_all(headed, 'seq', 0, 0, axis_index_groups=groups, tiled=True)  14.4 us
    unnamed x115, local copies, waits for them, and re-layouts  11.4 us
    pallas_call x1, Pallas kernels, mixer_grads_rule(): pl.pallas_call(mixer_grads_kernel, name='mixer_grads', grid=(model // GRA...  11 us
  transfers between devices with their start and end apart: 60, of which 26 were waited for; matrix products, arithmetic and copies ran while one was open for 7% of the time, Pallas kernels for 26%

profile of v3, /device:TPU:0, one launch (start us, length us, event | category | flops | bytes accessed | tf_op | source)
XLA Modules:
  0.0 412.6 jit_solution(11580490797533928368)
XLA Ops:
  14.2 3.0 collective-permute-start
  21.0 8.9 %collective-permute-done.refs_2_ = bf16[256,1024]{1,0:T(8,128)(2,1)S(1)} collective-permute-done((bf16[256,1024]{1,0:T(8,128)(2,1)S(1)}, bf16[256,1024]{1,0:T(8,128)(2,1)S(1)}, u32[]{:S(2)}, u32[]{:S(2)}) %collective-permute-start) | collective-permute-done | bytes 524320 | tf_op jit(solution)/shard_map/ppermute | solution.py:827
  29.9 11.9 %collective-permute-done.1.refs_4_ = bf16[256,1024]{1,0:T(8,128)(2,1)S(1)} collective-permute-done((bf16[256,1024]{1,0:T(8,128)(2,1)S(1)}, bf16[256,1024]{1,0:T(8,128)(2,1)S(1)}, u32[]{:S(2)}, u32[]{:S(2)}) %collective-permute-start.1) | collective-permute-done | bytes 524320 | tf_op jit(solution)/shard_map/ppermute | solution.py:827
  43.0 3.1 collective-permute-done.7.refs_9_
  54.8 3.1 collective-permute-done.12.refs_14_
  72.3 30.0 %mixer_forward.1 = (bf16[8,2,128,256]{3,2,1,0:T(8,128)(2,1)}, bf16[8,2,128,512]{3,2,1,0:T(8,128)(2,1)}, f32[8,2,128,384]{3,2,1,0:T(8,128)}, f32[8,2,128,256]{3,2...) custom-call(s32[1]{0:T(128)} %bitcast.7.head_ref, ...), custom_call_target="tpu_custom_call" | custom-call | tf_op jit(solution)/shard_map/mixer_forward/pallas_call | solution.py:492
  103.3 3.7 all-to-all-start
  107.9 14.4 %all-to-all-done.headed_ref = bf16[8,256,256]{2,1,0:T(8,128)(2,1)S(1)} async-done(((bf16[8,256,256]{2,1,0:T(8,128)(2,1)}), bf16[8,256,256]{2,1,0:T(8,128)(2,1)S(1)}, u32[]{:S(2)}, u32[]{:S(2)}) %all-to-all-start) | async-done | bytes 1048608 | tf_op jit(solution)/shard_map/all_to_all | solution.py:989
  123.3 5.6 %out_projection.1 = (f32[256,1024]{1,0:T(8,128)}, bf16[256,1024]{1,0:T(8,128)(2,1)}) custom-call(bf16[8,1024,256]{2,1,0:T(8,128)(2,1)} %bitcast.114, bf16[8,256,256]{2,1,0:T(8,128)(2,1)} %copy-done.9, bf16[256,1024]{1,0:T(8,128)(2,1)} %bitcast.104, f32[1,1024]{1,0:T(1,128)} %bitcast.128), custom_call_target="tpu_custom_call" | custom-call | tf_op jit(solution)/shard_map/out_projection/pallas_call | solution.py:582
  133.0 11.1 %collective-permute-done.18.refs_2_ = bf16[256,1024]{1,0:T(8,128)(2,1)S(1)} collective-permute-done((bf16[256,1024]{1,0:T(8,128)(2,1)}, bf16[256,1024]{1,0:T(8,128)(2,1)S(1)}, u32[]{:S(2)}, u32[]{:S(2)}) %collective-permute-start.18) | collective-permute-done | bytes 524320 | tf_op jit(solution)/shard_map/ppermute | solution.py:827
  144.1 10.6 %collective-permute-done.20.refs_4_ = bf16[256,1024]{1,0:T(8,128)(2,1)S(1)} collective-permute-done((bf16[256,1024]{1,0:T(8,128)(2,1)}, bf16[256,1024]{1,0:T(8,128)(2,1)S(1)}, u32[]{:S(2)}, u32[]{:S(2)}) %collective-permute-start.20) | collective-permute-done | bytes 524320 | tf_op jit(solution)/shard_map/ppermute | solution.py:827
  155.2 10.2 %all-gather.11.cloned.1.call-done.refs_16_ = bf16[1024,1152]{1,0:T(8,128)(2,1)} async-done(((bf16[256,1152]{1,0:T(8,128)(2,1)}), bf16[1024,1152]{1,0:T(8,128)(2,1)}) %all-gather.11.cloned.1.call-update) | async-done | bytes 2359312 | tf_op jit(solution)/shard_map/all_gather | solution.py:914
  166.1 16.3 %feed_forward.1 = (bf16[8,256,768]{2,1,0:T(8,128)(2,1)}, bf16[8,256,384]{2,1,0:T(8,128)(2,1)}, bf16[4,256,1024]{2,1,0:T(8,128)(2,1)}, bf16[4,256,1024]{2,1,0:T(8...) custom-call(bf16[256,1024]{1,0:T(8,128)(2,1)} %get-tuple-element.130.refs_0_, ...), custom_call_target="tpu_custom_call" | custom-call | tf_op jit(solution)/shard_map/feed_forward/pallas_call | solution.py:647
  182.6 10.5 %feed_forward_grads.1 = bf16[1024,1152]{1,0:T(8,128)(2,1)} custom-call(bf16[256,1024]{1,0:T(8,128)(2,1)} %get-tuple-element.130.refs_0_, bf16[256,1024]{1,0:T(8,128)(2,1)} %copy-done.35, bf16[256,1024]{1,0:T(8,128)(2,1)} %copy-done.32, bf16[256,1024]{1,0:T(8,128)(2,1)} %collective-permute-done.19.refs_3_, bf16[256,1024]{1,0:T(8,128)(2,1)} %copy-done.33, ...), custom_call_target="tpu_custom_call" | custom-call | flops 9663676416 | tf_op jit(solution)/shard_map/feed_forward_grads/pallas_call | solution.py:682
  203.0 9.0 %collective-permute-done.29 = bf16[256,1024]{1,0:T(8,128)(2,1)S(1)} collective-permute-done((bf16[256,1024]{1,0:T(8,128)(2,1)S(1)}, bf16[256,1024]{1,0:T(8,128)(2,1)S(1)}, u32[]{:S(2)}, u32[]{:S(2)}) %collective-permute-start.29) | collective-permute-done | bytes 524320 | tf_op jit(solution)/shard_map/ppermute | solution.py:827
  212.0 12.0 %collective-permute-done.30 = bf16[256,1024]{1,0:T(8,128)(2,1)S(1)} collective-permute-done((bf16[256,1024]{1,0:T(8,128)(2,1)S(1)}, bf16[256,1024]{1,0:T(8,128)(2,1)S(1)}, u32[]{:S(2)}, u32[]{:S(2)}) %collective-permute-start.30) | collective-permute-done | bytes 524320 | tf_op jit(solution)/shard_map/ppermute | solution.py:827
  229.9 11.4 %collective-permute-done.34.refs_2_.refs_10_ = bf16[256,1024]{1,0:T(8,128)(2,1)S(1)} collective-permute-done((bf16[256,1024]{1,0:T(8,128)(2,1)S(1)}, bf16[256,1024]{1,0:T(8,128)(2,1)S(1)}, u32[]{:S(2)}, u32[]{:S(2)}) %collective-permute-start.34) | collective-permute-done | bytes 524320 | tf_op jit(solution)/shard_map/ppermute | solution.py:827
  241.3 10.8 %collective-permute-done.36.refs_4_.refs_12_ = bf16[256,1024]{1,0:T(8,128)(2,1)S(1)} collective-permute-done((bf16[256,1024]{1,0:T(8,128)(2,1)S(1)}, bf16[256,1024]{1,0:T(8,128)(2,1)S(1)}, u32[]{:S(2)}, u32[]{:S(2)}) %collective-permute-start.36) | collective-permute-done | bytes 524320 | tf_op jit(solution)/shard_map/ppermute | solution.py:827
  255.5 36.4 %mixer_backward.1 = (bf16[8,2,128,896]{3,2,1,0:T(8,128)(2,1)}, f32[8,512]{1,0:T(8,128)}, f32[1,256]{1,0:T(1,128)}, f32[2,128,256]{2,1,0:T(8,128)}, f32[2,8,512]{2,1,0:T(8,128)}) custom-call(s32[1]{0:T(128)} %bitcast.7.head_ref, bf16[256,1024]{1,0:T(8,128)(2,1)} %copy-done.6, bf16[256,1024]{1,0:T(8,128)(2,1)} %copy-done.21, bf16[256,1024]{1,0:T(8,128)(2,1)} %copy-done.18, ...), custom_call_target="tpu_custom_call" | custom-call | tf_op jit(solution)/shard_map/mixer_backward/pallas_call | solution.py:523
  292.0 11.0 %mixer_grads.1 = (bf16[1024,1024]{1,0:T(8,128)(2,1)}, f32[1024,128]{1,0:T(8,128)}) custom-call(s32[1]{0:T(128)} %bitcast.7.head_ref, bf16[256,1024]{1,0:T(8,128)(2,1)} %copy-done.5, bf16[256,1024]{1,0:T(8,128)(2,1)} %copy-done.15, bf16[256,1024]{1,0:T(8,128)(2,1)} %copy-done.12, bf16[256,1024]{1,0:T(8,128)(2,1)} %copy-done.16, bf16[256,1024]{1,0:T(8,128)(2,1)} %copy-done.13, ...), custom_call_target="tpu_custom_call" | custom-call | tf_op jit(solution)/shard_map/mixer_grads/pallas_call | solution.py:720
  303.1 8.1 %mixer_d_in.1 = (bf16[4,256,1024]{2,1,0:T(8,128)(2,1)}, bf16[4,256,1024]{2,1,0:T(8,128)(2,1)}) custom-call(bf16[8,256,896]{2,1,0:T(8,128)(2,1)} %bitcast.103, bf16[1024,1024]{1,0:T(8,128)(2,1)} %all-gather.9.cloned.1.call-done.refs_16_.refs_8_.weight_ref.refs_18_, bf16[1024,128]{1,0:T(8,128)(2,1)} %pad.8.refs_17_.beta_ref.refs_19_), custom_call_target="tpu_custom_call" | custom-call | tf_op jit(solution)/shard_map/mixer_d_in/pallas_call | solution.py:754
  311.4 4.2 %collective-permute-done.43 = bf16[4,256,1024]{2,1,0:T(8,128)(2,1)S(1)} collective-permute-done((bf16[4,256,1024]{2,1,0:T(8,128)(2,1)}, bf16[4,256,1024]{2,1,0:T(8,128)(2,1)S(1)}, u32[]{:S(2)}, u32[]{:S(2)}) %collective-permute-start.43) | collective-permute-done | bytes 2097184 | tf_op jit(solution)/shard_map/ppermute | solution.py:827
  315.6 3.8 fusion.13
  322.9 7.5 %join_hidden.1 = (f32[256,2816]{1,0:T(8,128)}, f32[256,2816]{1,0:T(8,128)}, f32[256,2816]{1,0:T(8,128)}) custom-call(bf16[8,256,1152]{2,1,0:T(8,128)(2,1)} %bitcast.105), custom_call_target="tpu_custom_call" | custom-call | tf_op jit(solution)/shard_map/join_hidden/pallas_call | solution.py:809
  330.4 4.1 collective-permute-done.44
  334.5 10.7 %collective-permute-done.45 = bf16[256,1024]{1,0:T(8,128)(2,1)} collective-permute-done((bf16[256,1024]{1,0:T(8,128)(2,1)}, bf16[256,1024]{1,0:T(8,128)(2,1)}, u32[]{:S(2)}, u32[]{:S(2)}) %collective-permute-start.45) | collective-permute-done | bytes 524320 | tf_op jit(solution)/shard_map/ppermute | solution.py:827
  347.1 3.8 collective-permute-done.47
  359.6 25.4 %collective-permute-done.50 = f32[2,42,128]{2,1,0:T(8,128)S(1)} collective-permute-done((f32[2,42,128]{2,1,0:T(8,128)S(1)}, f32[2,42,128]{2,1,0:T(8,128)S(1)}, u32[]{:S(2)}, u32[]{:S(2)}) %collective-permute-start.50) | collective-permute-done | bytes 43040 | tf_op jit(solution)/shard_map/ppermute | solution.py:827
  385.1 3.8 multiply_add_fusion
  388.9 2.9 collective-permute-done.51
  395.0 3.3 all-gather.17.cloned.1.call-done
  398.3 7.2 %join_heads.1 = (f32[256,1024]{1,0:T(8,128)}, f32[256,1024]{1,0:T(8,128)}, f32[256,2048]{1,0:T(8,128)}, f32[256,2048]{1,0:T(8,128)}, f32[256,2048]{1,0:T(8,128)}) custom-call(bf16[8,256,1024]{2,1,0:T(8,128)(2,1)} %bitcast.115), custom_call_target="tpu_custom_call" | custom-call | tf_op jit(solution)/shard_map/join_heads/pallas_call | solution.py:784
  (265 shorter events, 79.7 us)
Async XLA Ops:
  7.2 55.9 %all-gather.9.cloned.1.call-start = ((), (), s32[]{:S(2)}) async-start(), calls=%async_computation.3 | async-start | bytes 2621440 | tf_op jit(solution)/shard_map/all_gather | solution.py:914
  12.7 109.7 %all-gather.13.cloned.1.call-start = ((), (), s32[]{:S(2)}) async-start(), calls=%async_computation.7 | async-start | bytes 4718592 | tf_op jit(solution)/shard_map/all_gather | solution.py:902
  17.2 24.6 %collective-permute-start.1 = (bf16[256,1024]{1,0:T(8,128)(2,1)S(1)}, bf16[256,1024]{1,0:T(8,128)(2,1)S(1)}, u32[]{:S(2)}, u32[]{:S(2)}) collective-permute-start(bf16[256,1024]{1,0:T(8,128)(2,1)S(1)} %multiply_convert_fusion.refs_0_), channel_id=1, source_target_pairs={{0,16},{4,20},{8,24},{12,28},{16,0},{20,4},{24,8},{28,12},{1,17},{... | collective-permute-start | bytes 1572872 | tf_op jit(solution)/shard_map/ppermute | solution.py:827
  18.7 23.1 %collective-permute-start.2 = (bf16[256,1024]{1,0:T(8,128)(2,1)S(1)}, bf16[256,1024]{1,0:T(8,128)(2,1)S(1)}, u32[]{:S(2)}, u32[]{:S(2)}) collective-permute-start(bf16[256,1024]{1,0:T(8,128)(2,1)S(1)} %multiply_convert_fusion.refs_0_), channel_id=1, source_target_pairs={{0,24},{4,28},{8,16},{12,20},{16,8},{20,12},{24,0},{28,4},{1,25},{... | collective-permute-start | bytes 1572872 | tf_op jit(solution)/shard_map/ppermute | solution.py:827
  42.5 20.6 %collective-permute-start.6 = (bf16[256,1024]{1,0:T(8,128)(2,1)S(1)}, bf16[256,1024]{1,0:T(8,128)(2,1)}, u32[]{:S(2)}, u32[]{:S(2)}) collective-permute-start(bf16[256,1024]{1,0:T(8,128)(2,1)S(1)} %collective-permute-done.2.refs_6_), channel_id=1, source_target_pairs={{0,4},{4,0},{8,12},{12,8},{16,20},{20,16},{24,28},{28,24},{1,5},{5... | collective-permute-start | bytes 1572872 | tf_op jit(solution)/shard_map/ppermute | solution.py:827
  65.0 100.3 %all-gather.11.cloned.1.call-start = ((), (), s32[]{:S(2)}) async-start(), calls=%async_computation.4 | async-start | bytes 2949120 | tf_op jit(solution)/shard_map/all_gather | solution.py:914
  66.7 35.6 %collective-permute-start.14 = (bf16[256,1024]{1,0:T(8,128)(2,1)S(1)}, bf16[256,1024]{1,0:T(8,128)(2,1)S(1)}, u32[]{:S(2)}, u32[]{:S(2)}) collective-permute-start(bf16[256,1024]{1,0:T(8,128)(2,1)S(1)} %bitcast.108), channel_id=1, source_target_pairs={{0,8},{4,12},{8,0},{12,4},{16,24},{20,28},{24,16},{28,20},{1,9},{5... | collective-permute-start | bytes 1572872 | tf_op jit(solution)/shard_map/ppermute | solution.py:827
  67.9 34.4 %collective-permute-start.15 = (bf16[256,1024]{1,0:T(8,128)(2,1)S(1)}, bf16[256,1024]{1,0:T(8,128)(2,1)S(1)}, u32[]{:S(2)}, u32[]{:S(2)}) collective-permute-start(bf16[256,1024]{1,0:T(8,128)(2,1)S(1)} %bitcast.109), channel_id=1, source_target_pairs={{0,16},{4,20},{8,24},{12,28},{16,0},{20,4},{24,8},{28,12},{1,17},{... | collective-permute-start | bytes 1572872 | tf_op jit(solution)/shard_map/ppermute | solution.py:827
  68.8 33.6 %collective-permute-start.16 = (bf16[256,1024]{1,0:T(8,128)(2,1)S(1)}, bf16[256,1024]{1,0:T(8,128)(2,1)}, u32[]{:S(2)}, u32[]{:S(2)}) collective-permute-start(bf16[256,1024]{1,0:T(8,128)(2,1)S(1)} %bitcast.110), channel_id=1, source_target_pairs={{0,24},{4,28},{8,16},{12,20},{16,8},{20,12},{24,0},{28,4},{1,25},{... | collective-permute-start | bytes 1572872 | tf_op jit(solution)/shard_map/ppermute | solution.py:827
  107.0 147.8 %reduce-scatter.3.cloned.1.call-start = ((), (), s32[]{:S(2)}) async-start(), calls=%async_computation.5 | async-start | bytes 2949120 | tf_op jit(solution)/shard_map/reduce_scatter | solution.py:933
  107.1 23.2 %collective-permute-start.24 = (bf16[256,1024]{1,0:T(8,128)(2,1)S(1)}, bf16[256,1024]{1,0:T(8,128)(2,1)S(1)}, u32[]{:S(2)}, u32[]{:S(2)}) collective-permute-start(bf16[256,1024]{1,0:T(8,128)(2,1)S(1)} %bitcast.111), channel_id=1, source_target_pairs={{0,4},{4,0},{8,12},{12,8},{16,20},{20,16},{24,28},{28,24},{1,5},{5... | collective-permute-start | bytes 1572872 | tf_op jit(solution)/shard_map/ppermute | solution.py:827
  107.4 25.1 %collective-permute-start.25 = (bf16[256,1024]{1,0:T(8,128)(2,1)}, bf16[256,1024]{1,0:T(8,128)(2,1)S(1)}, u32[]{:S(2)}, u32[]{:S(2)}) collective-permute-start(bf16[256,1024]{1,0:T(8,128)(2,1)} %copy-done.27), channel_id=1, source_target_pairs={{0,4},{4,0},{8,12},{12,8},{16,20},{20,16},{24,28},{28,24},{1,5},{5... | collective-permute-start | bytes 1572872 | tf_op jit(solution)/shard_map/ppermute | solution.py:827
  107.7 24.8 %collective-permute-start.26 = (bf16[256,1024]{1,0:T(8,128)(2,1)S(1)}, bf16[256,1024]{1,0:T(8,128)(2,1)}, u32[]{:S(2)}, u32[]{:S(2)}) collective-permute-start(bf16[256,1024]{1,0:T(8,128)(2,1)S(1)} %copy-done.29), channel_id=1, source_target_pairs={{0,4},{4,0},{8,12},{12,8},{16,20},{20,16},{24,28},{28,24},{1,5},{5... | collective-permute-start | bytes 1572872 | tf_op jit(solution)/shard_map/ppermute | solution.py:827
  129.6 25.1 %collective-permute-start.20 = (bf16[256,1024]{1,0:T(8,128)(2,1)}, bf16[256,1024]{1,0:T(8,128)(2,1)S(1)}, u32[]{:S(2)}, u32[]{:S(2)}) collective-permute-start(bf16[256,1024]{1,0:T(8,128)(2,1)} %get-tuple-element.130.refs_0_), channel_id=1, source_target_pairs={{0,16},{4,20},{8,24},{12,28},{16,0},{20,4},{24,8},{28,12},{1,17},{... | collective-permute-start | bytes 1572872 | tf_op jit(solution)/shard_map/ppermute | solution.py:827
  130.2 24.4 %collective-permute-start.22 = (bf16[256,1024]{1,0:T(8,128)(2,1)}, bf16[256,1024]{1,0:T(8,128)(2,1)S(1)}, u32[]{:S(2)}, u32[]{:S(2)}) collective-permute-start(bf16[256,1024]{1,0:T(8,128)(2,1)} %get-tuple-element.130.refs_0_), channel_id=1, source_target_pairs={{0,24},{4,28},{8,16},{12,20},{16,8},{20,12},{24,0},{28,4},{1,25},{... | collective-permute-start | bytes 1572872 | tf_op jit(solution)/shard_map/ppermute | solution.py:827
  132.5 22.7 %collective-permute-start.27 = (bf16[256,1024]{1,0:T(8,128)(2,1)}, bf16[256,1024]{1,0:T(8,128)(2,1)}, u32[]{:S(2)}, u32[]{:S(2)}) collective-permute-start(bf16[256,1024]{1,0:T(8,128)(2,1)} %collective-permute-done.16.refs_14_), channel_id=1, source_target_pairs={{0,4},{4,0},{8,12},{12,8},{16,20},{20,16},{24,28},{28,24},{1,5},{5... | collective-permute-start | bytes 1572872 | tf_op jit(solution)/shard_map/ppermute | solution.py:827
  132.5 32.8 %collective-permute-start.17 = (bf16[256,1024]{1,0:T(8,128)(2,1)}, bf16[256,1024]{1,0:T(8,128)(2,1)S(1)}, u32[]{:S(2)}, u32[]{:S(2)}) collective-permute-start(bf16[256,1024]{1,0:T(8,128)(2,1)} %get-tuple-element.130.refs_0_), channel_id=1, source_target_pairs={{0,4},{4,0},{8,12},{12,8},{16,20},{20,16},{24,28},{28,24},{1,5},{5... | collective-permute-start | bytes 1572872 | tf_op jit(solution)/shard_map/ppermute | solution.py:827
  144.1 21.3 %collective-permute-start.19 = (bf16[256,1024]{1,0:T(8,128)(2,1)S(1)}, bf16[256,1024]{1,0:T(8,128)(2,1)}, u32[]{:S(2)}, u32[]{:S(2)}) collective-permute-start(bf16[256,1024]{1,0:T(8,128)(2,1)S(1)} %collective-permute-done.18.refs_2_), channel_id=1, source_target_pairs={{0,4},{4,0},{8,12},{12,8},{16,20},{20,16},{24,28},{28,24},{1,5},{5... | collective-permute-start | bytes 1572872 | tf_op jit(solution)/shard_map/ppermute | solution.py:827
  193.2 109.8 %all-gather.15.cloned.1.call-start = ((), (), s32[]{:S(2)}) async-start(), calls=%async_computation.8 | async-start | bytes 5308416 | tf_op jit(solution)/shard_map/all_gather | solution.py:936
  198.8 25.3 %collective-permute-start.30 = (bf16[256,1024]{1,0:T(8,128)(2,1)S(1)}, bf16[256,1024]{1,0:T(8,128)(2,1)S(1)}, u32[]{:S(2)}, u32[]{:S(2)}) collective-permute-start(bf16[256,1024]{1,0:T(8,128)(2,1)S(1)} %get-tuple-element.208), channel_id=1, source_target_pairs={{0,16},{4,20},{8,24},{12,28},{16,0},{20,4},{24,8},{28,12},{1,17},{... | collective-permute-start | bytes 1572872 | tf_op jit(solution)/shard_map/ppermute | solution.py:827
  200.2 23.8 %collective-permute-start.31 = (bf16[256,1024]{1,0:T(8,128)(2,1)S(1)}, bf16[256,1024]{1,0:T(8,128)(2,1)S(1)}, u32[]{:S(2)}, u32[]{:S(2)}) collective-permute-start(bf16[256,1024]{1,0:T(8,128)(2,1)S(1)} %get-tuple-element.207), channel_id=1, source_target_pairs={{0,24},{4,28},{8,16},{12,20},{16,8},{20,12},{24,0},{28,4},{1,25},{... | collective-permute-start | bytes 1572872 | tf_op jit(solution)/shard_map/ppermute | solution.py:827
  227.6 24.5 %collective-permute-start.36 = (bf16[256,1024]{1,0:T(8,128)(2,1)S(1)}, bf16[256,1024]{1,0:T(8,128)(2,1)S(1)}, u32[]{:S(2)}, u32[]{:S(2)}) collective-permute-start(bf16[256,1024]{1,0:T(8,128)(2,1)S(1)} %fusion.15.refs_0_.refs_8_), channel_id=1, source_target_pairs={{0,16},{4,20},{8,24},{12,28},{16,0},{20,4},{24,8},{28,12},{1,17},{... | collective-permute-start | bytes 1572872 | tf_op jit(solution)/shard_map/ppermute | solution.py:827
  228.4 23.6 %collective-permute-start.38 = (bf16[256,1024]{1,0:T(8,128)(2,1)S(1)}, bf16[256,1024]{1,0:T(8,128)(2,1)S(1)}, u32[]{:S(2)}, u32[]{:S(2)}) collective-permute-start(bf16[256,1024]{1,0:T(8,128)(2,1)S(1)} %fusion.15.refs_0_.refs_8_), channel_id=1, source_target_pairs={{0,24},{4,28},{8,16},{12,20},{16,8},{20,12},{24,0},{28,4},{1,25},{... | collective-permute-start | bytes 1572872 | tf_op jit(solution)/shard_map/ppermute | solution.py:827
  229.9 22.7 %collective-permute-start.33 = (bf16[256,1024]{1,0:T(8,128)(2,1)S(1)}, bf16[256,1024]{1,0:T(8,128)(2,1)S(1)}, u32[]{:S(2)}, u32[]{:S(2)}) collective-permute-start(bf16[256,1024]{1,0:T(8,128)(2,1)S(1)} %fusion.15.refs_0_.refs_8_), channel_id=1, source_target_pairs={{0,4},{4,0},{8,12},{12,8},{16,20},{20,16},{24,28},{28,24},{1,5},{5... | collective-permute-start | bytes 1572872 | tf_op jit(solution)/shard_map/ppermute | solution.py:827
  254.9 90.2 %reduce-scatter.5.cloned.1.call-start = ((), (), s32[]{:S(2)}) async-start(), calls=%async_computation.6 | async-start | bytes 2621440 | tf_op jit(solution)/shard_map/reduce_scatter | solution.py:933
  303.0 95.2 %all-gather.17.cloned.1.call-start = ((), (), s32[]{:S(2)}) async-start(), calls=%async_computation.9 | async-start | bytes 4718592 | tf_op jit(solution)/shard_map/all_gather | solution.py:936
  319.9 25.2 %collective-permute-start.45 = (bf16[256,1024]{1,0:T(8,128)(2,1)}, bf16[256,1024]{1,0:T(8,128)(2,1)}, u32[]{:S(2)}, u32[]{:S(2)}) collective-permute-start(bf16[256,1024]{1,0:T(8,128)(2,1)} %get-tuple-element.201), channel_id=1, source_target_pairs={{0,16},{4,20},{8,24},{12,28},{16,0},{20,4},{24,8},{28,12},{1,17},{... | collective-permute-start | bytes 1572872 | tf_op jit(solution)/shard_map/ppermute | solution.py:827
  321.4 23.8 %collective-permute-start.46 = (bf16[256,1024]{1,0:T(8,128)(2,1)S(1)}, bf16[256,1024]{1,0:T(8,128)(2,1)}, u32[]{:S(2)}, u32[]{:S(2)}) collective-permute-start(bf16[256,1024]{1,0:T(8,128)(2,1)S(1)} %get-tuple-element.200), channel_id=1, source_target_pairs={{0,24},{4,28},{8,16},{12,20},{16,8},{20,12},{24,0},{28,4},{1,25},{... | collective-permute-start | bytes 1572872 | tf_op jit(solution)/shard_map/ppermute | solution.py:827
  352.2 32.9 %collective-permute-start.42 = (bf16[256,1024]{1,0:T(8,128)(2,1)}, bf16[256,1024]{1,0:T(8,128)(2,1)S(1)}, u32[]{:S(2)}, u32[]{:S(2)}) collective-permute-start(bf16[256,1024]{1,0:T(8,128)(2,1)} %get-tuple-element.152), channel_id=1, source_target_pairs={{0,24},{4,28},{8,16},{12,20},{16,8},{20,12},{24,0},{28,4},{1,25},{... | collective-permute-start | bytes 1572872 | tf_op jit(solution)/shard_map/ppermute | solution.py:827
  354.5 30.6 %collective-permute-start.41 = (bf16[256,1024]{1,0:T(8,128)(2,1)}, bf16[256,1024]{1,0:T(8,128)(2,1)S(1)}, u32[]{:S(2)}, u32[]{:S(2)}) collective-permute-start(bf16[256,1024]{1,0:T(8,128)(2,1)} %get-tuple-element.151), channel_id=1, source_target_pairs={{0,16},{4,20},{8,24},{12,28},{16,0},{20,4},{24,8},{28,12},{1,17},{... | collective-permute-start | bytes 1572872 | tf_op jit(solution)/shard_map/ppermute | solution.py:827
  355.1 30.0 %collective-permute-start.40 = (bf16[256,1024]{1,0:T(8,128)(2,1)}, bf16[256,1024]{1,0:T(8,128)(2,1)S(1)}, u32[]{:S(2)}, u32[]{:S(2)}) collective-permute-start(bf16[256,1024]{1,0:T(8,128)(2,1)} %get-tuple-element.150), channel_id=1, source_target_pairs={{0,8},{4,12},{8,0},{12,4},{16,24},{20,28},{24,16},{28,20},{1,9},{5... | collective-permute-start | bytes 1572872 | tf_op jit(solution)/shard_map/ppermute | solution.py:827
  358.0 27.0 %collective-permute-start.50 = (f32[2,42,128]{2,1,0:T(8,128)S(1)}, f32[2,42,128]{2,1,0:T(8,128)S(1)}, u32[]{:S(2)}, u32[]{:S(2)}) collective-permute-start(f32[2,42,128]{2,1,0:T(8,128)S(1)} %pad_maximum_fusion.4), channel_id=1, source_target_pairs={{0,8},{4,12},{8,0},{12,4},{16,24},{20,28},{24,16},{28,20},{1,9},{5... | collective-permute-start | bytes 129032 | tf_op jit(solution)/shard_map/ppermute | solution.py:827
  (78 other events, 1109.1 us)
Sparse Core Ops, SparseCore 0:
  12.8 48.6 all-gather.8
  65.1 46.3 all-gather.12
  113.7 51.6 all-gather.10
  193.3 46.9 reduce-scatter.2
  255.0 36.9 all-gather.14
  303.2 41.4 reduce-scatter.4
  346.7 51.5 all-gather.16

commit v4 on v3

--- a/solution.py
+++ b/solution.py
@@ -147,12 +147,11 @@
         weight_in.at[:, pl.ds(0, WIDTH + DV)], weight_ref, weight_sem
     )
     weight_copy.start()
-    block_copies = [
-        pltpu.make_async_copy(block_refs[slot], block_ref.at[slot], block_sems.at[slot])
-        for slot in range(H)
-    ]
-    for copy in block_copies[:2]:
-        copy.start()
+    def block_copy(source, slot):
+        return pltpu.make_async_copy(source, block_ref.at[slot], block_sems.at[slot])
+
+    for slot in range(H):
+        block_copy(block_refs[slot], slot).start()
     for slot in range(H):
         logs = jnp.log(decay_refs[slot][pl.ds(head, 1), :])
         for seq in range(seqs):
@@ -160,11 +159,10 @@
     run_ref[...] = running_sums(log_ref[...], rows, cols)
 
     weight_copy.wait()
-    for slot in range(H):
+
+    def project(slot, _):
         chunk = slot ^ head
-        if slot + 2 < H:
-            block_copies[slot + 2].start()
-        block_copies[slot].wait()
+        block_copy(block_refs[0], slot).wait()
         block = block_ref[slot]
         conv = product(block, weight_ref[:, :WIDTH]).astype(bf16)
         gate = product(block, weight_ref[:, WIDTH:])
@@ -174,6 +172,9 @@
             conv_ref[chunk, seq] = conv[span]
             gate_ref[chunk, seq, :, :DV] = gate[span]
             gate_ref[chunk, seq, :, DV:] = beta[span]
+        return 0
+
+    lax.fori_loop(0, H, project, 0)
 
     def send(index, first, count):
         span = pl.ds(first, count)
@@ -284,12 +285,12 @@
         weight_in.at[:, pl.ds(WIDTH + DV, DV)], weight_ref, weight_sem
     )
     weight_copy.start()
-    block_copies = [
-        pltpu.make_async_copy(branch_refs[slot], branch_ref.at[slot], block_sems.at[slot])
-        for slot in range(H)
-    ]
-    for copy in block_copies[:2]:
-        copy.start()
+
+    def block_copy(source, slot):
+        return pltpu.make_async_copy(source, branch_ref.at[slot], block_sems.at[slot])
+
+    for slot in range(H):
+        block_copy(branch_refs[slot], slot).start()
     saved_copies = [
         pltpu.make_async_copy(saved[index], held[index], saved_sems.at[index])
         for index in range(len(saved))
@@ -300,15 +301,20 @@
     grad_taps_ref[...] = jnp.zeros_like(grad_taps_ref)
 
     weight_copy.wait()
-    for slot in range(H):
-        if slot + 2 < H:
-            block_copies[slot + 2].start()
-        if 1 < slot < len(saved_copies):
-            saved_copies[slot - 2].start()
-        block_copies[slot].wait()
+
+    def project(slot, _):
+        @pl.when(slot == 1)
+        def _():
+            for copy in saved_copies[:5]:
+                copy.start()
+
+        block_copy(branch_refs[0], slot).wait()
         d_headed = product(branch_ref[slot], weight_ref[...])
         for seq in range(seqs):
             d_headed_ref[slot ^ head, seq] = d_headed[seq * size : (seq + 1) * size]
+        return 0
+
+    lax.fori_loop(0, H, project, 0)
     for copy in saved_copies[:5]:
         copy.wait()
     for copy in saved_copies[5:]:
@@ -560,38 +566,53 @@
     )(head, *branch, weight, *saved, run, taps, gain, halo, d_end, d_after)
 
 
-def out_kernel(
-    weight_in, headed_ref, inputs_ref, gain_ref, residual_ref, normed_ref, weight_ref, sems
-):
-    copies = [
-        pltpu.make_async_copy(weight_in.at[peer], weight_ref.at[peer], sems.at[peer])
-        for peer in range(H)
-    ]
-    for copy in copies:
-        copy.start()
-    total = inputs_ref[...].astype(f32)
-    for peer in range(H):
-        copies[peer].wait()
-        total = total + contract_cols(headed_ref[peer], weight_ref[peer])
-    residual_ref[...] = total
+def out_kernel(head_ref, *refs):
+    block_refs, refs = refs[:H], refs[H:]
+    headed_ref, inputs_ref, gain_ref, residual_ref, normed_ref, weight_ref, sems = refs
+    head = head_ref[0]
+
+    def block_copy(source, slot):
+        return pltpu.make_async_copy(source, weight_ref.at[slot], sems.at[slot])
+
+    for slot in range(H):
+        block_copy(block_refs[slot], slot).start()
+    residual_ref[...] = inputs_ref[...].astype(f32)
+
+    def add_heads(pair, _):
+        slots = (2 * pair, 2 * pair + 1)
+        for slot in slots:
+            block_copy(block_refs[0], slot).wait()
+        headed = jnp.concatenate([headed_ref[slot ^ head] for slot in slots], 1)
+        weight = jnp.concatenate([weight_ref[slot] for slot in slots], 1)
+        residual_ref[...] += contract_cols(headed, weight)
+        return 0
+
+    lax.fori_loop(0, H // 2, add_heads, 0)
+    total = residual_ref[...]
     scale = lax.rsqrt(jnp.mean(total * total, axis=1, keepdims=True) + 1e-05)
     normed_ref[...] = (total * scale * gain_ref[...]).astype(bf16)
 
 
-def out_rule(weight, headed, inputs, gain):
+def out_rule(head, blocks, headed, inputs, gain):
     return pl.pallas_call(
         out_kernel,
         name="out_projection",
         out_shape=(shaped(inputs.shape, f32), shaped(inputs.shape, bf16)),
-        in_specs=anywhere(1) + whole(3),
+        in_specs=scalar() + anywhere(H) + whole(3),
         out_specs=tuple(whole(2)),
-        scratch_shapes=[pltpu.VMEM(weight.shape, bf16), pltpu.SemaphoreType.DMA((H,))],
+        scratch_shapes=[
+            pltpu.VMEM((H,) + blocks[0].shape, bf16),
+            pltpu.SemaphoreType.DMA((H,)),
+        ],
         compiler_params=kernel_params(),
-    )(weight, headed, inputs, gain)
+    )(head, *blocks, headed, inputs, gain)
+
+
+PART = H // 2
 
 
 def ffn_kernel(*refs):
-    normed_refs, up_refs, refs = refs[:H], refs[H : 2 * H], refs[2 * H :]
+    normed_refs, up_refs, refs = refs[:PART], refs[PART : 2 * PART], refs[2 * PART :]
     weight_in, d_both_ref, hidden_ref, d_even_ref, d_odd_ref, even_ref, odd_ref = refs[:7]
     normed_all_ref, up_all_ref, weight_ref, normed_sems, up_sems, weight_sem = refs[7:]
     share = weight_ref.shape[1] // 3
@@ -600,63 +621,67 @@
     def copy_of(source, target, sems, slot):
         return pltpu.make_async_copy(source, target.at[slot], sems.at[slot])
 
-    def start_pair(pair):
-        for slot in (2 * pair, 2 * pair + 1):
-            copy_of(normed_refs[slot], normed_all_ref, normed_sems, slot).start()
-            copy_of(up_refs[slot], up_all_ref, up_sems, slot).start()
+    def start_slot(slot):
+        copy_of(normed_refs[slot], normed_all_ref, normed_sems, slot).start()
+        copy_of(up_refs[slot], up_all_ref, up_sems, slot).start()
 
     @pl.when(step == 0)
     def _():
         weight_copy = pltpu.make_async_copy(weight_in, weight_ref, weight_sem)
         weight_copy.start()
-        start_pair(0)
+        start_slot(0)
         weight_copy.wait()
 
-    for later in range(1, H // 2):
+    for later in range(1, PART):
 
         @pl.when(step == later - 1)
         def _():
-            start_pair(later)
-
+            start_slot(later)
+
+    slot = step
+    copy_of(normed_refs[0], normed_all_ref, normed_sems, slot).wait()
+    copy_of(up_refs[0], up_all_ref, up_sems, slot).wait()
+    both = product(normed_all_ref[slot], weight_ref[:, : 2 * share])
+    d_hidden = product(up_all_ref[slot], weight_ref[:, 2 * share :])
+    gate, up = both[:, :share], both[:, share:]
+    logistic = jax.nn.sigmoid(gate)
+    swish = gate * logistic
+    hidden = (swish * up).astype(bf16)
+    hidden_ref[0] = hidden
+    d_gate = (d_hidden * up * logistic * (1.0 + gate * (1.0 - logistic))).astype(bf16)
+    d_up = (d_hidden * swish).astype(bf16)
+    d_both = jnp.concatenate([d_gate, d_up], 1)
+    d_both_ref[0] = d_both
+    d_in = contract_cols(d_both, weight_ref[:, : 2 * share]).astype(bf16)
+    out = contract_cols(hidden, weight_ref[:, 2 * share :]).astype(bf16)
     for side, d_in_ref, out_ref in ((0, d_even_ref, even_ref), (1, d_odd_ref, odd_ref)):
-        slot = 2 * step + side
-        copy_of(normed_refs[0], normed_all_ref, normed_sems, slot).wait()
-        copy_of(up_refs[0], up_all_ref, up_sems, slot).wait()
-        both = product(normed_all_ref[slot], weight_ref[:, : 2 * share])
-        d_hidden = product(up_all_ref[slot], weight_ref[:, 2 * share :])
-        gate, up = both[:, :share], both[:, share:]
-        logistic = jax.nn.sigmoid(gate)
-        swish = gate * logistic
-        hidden = (swish * up).astype(bf16)
-        hidden_ref[side] = hidden
-        d_gate = (d_hidden * up * logistic * (1.0 + gate * (1.0 - logistic))).astype(bf16)
-        d_up = (d_hidden * swish).astype(bf16)
-        d_both = jnp.concatenate([d_gate, d_up], 1)
-        d_both_ref[side] = d_both
-        d_in_ref[0] = contract_cols(d_both, weight_ref[:, : 2 * share]).astype(bf16)
-        out_ref[0] = contract_cols(hidden, weight_ref[:, 2 * share :]).astype(bf16)
+
+        @pl.when(step % 2 == side)
+        def _():
+            d_in_ref[0] = d_in
+            out_ref[0] = out
 
 
 def ffn_rule(normed, upstream, weight):
     rows, model = normed[0].shape
     share = weight.shape[1] // 3
 
-    def moving(count, width):
-        return pl.BlockSpec((count, rows, width), lambda step: (step, 0, 0))
+    def moving(width, steps):
+        return pl.BlockSpec((1, rows, width), lambda step: (step // steps, 0, 0))
 
     return pl.pallas_call(
         ffn_kernel,
         name="feed_forward",
-        grid=(H // 2,),
-        in_specs=anywhere(2 * H + 1),
-        out_specs=[moving(2, 2 * share), moving(2, share)] + [moving(1, model)] * 4,
-        out_shape=[shaped((H, rows, 2 * share), bf16), shaped((H, rows, share), bf16)]
-        + [shaped((H // 2, rows, model), bf16)] * 4,
-        scratch_shapes=[pltpu.VMEM((H, rows, model), bf16)] * 2
+        grid=(PART,),
+        in_specs=anywhere(2 * PART + 1),
+        out_specs=[moving(2 * share, 1), moving(share, 1)] + [moving(model, 2)] * 4,
+        out_shape=[shaped((PART, rows, 2 * share), bf16), shaped((PART, rows, share), bf16)]
+        + [shaped((PART // 2, rows, model), bf16)] * 4,
+        scratch_shapes=[pltpu.VMEM((PART, rows, model), bf16)] * 2
         + [
             pltpu.VMEM(weight.shape, bf16),
-            pltpu.SemaphoreType.DMA((H,)),
-            pltpu.SemaphoreType.DMA((H,)),
+            pltpu.SemaphoreType.DMA((PART,)),
+            pltpu.SemaphoreType.DMA((PART,)),
             pltpu.SemaphoreType.DMA,
         ],
         compiler_params=kernel_params(),
@@ -667,32 +692,33 @@
 
 
 def ffn_grads_kernel(*refs):
-    normed_refs, up_refs, (d_both_ref, hidden_ref, out_ref) = refs[:H], refs[H : 2 * H], refs[2 * H :]
-    wide = d_both_ref.shape[1]
+    normed_refs, up_refs, refs = refs[:H], refs[H : 2 * H], refs[2 * H :]
+    both_refs, hidden_refs, out_ref = refs[:2], refs[2:4], refs[4]
+    wide = both_refs[0].shape[1]
     normed = jnp.concatenate([ref[...] for ref in normed_refs], 0)
-    out_ref[:, :wide] = contract_rows(normed, d_both_ref[...]).astype(bf16)
+    d_both = jnp.concatenate([ref[...] for ref in both_refs], 0)
+    out_ref[:, :wide] = contract_rows(normed, d_both).astype(bf16)
     upstream = jnp.concatenate([ref[...] for ref in up_refs], 0)
-    out_ref[:, wide:] = contract_rows(upstream, hidden_ref[...]).astype(bf16)
+    hidden = jnp.concatenate([ref[...] for ref in hidden_refs], 0)
+    out_ref[:, wide:] = contract_rows(upstream, hidden).astype(bf16)
 
 
 def ffn_grads_rule(normed, upstream, d_both, hidden):
     rows, model = normed[0].shape
-    width = d_both.shape[1] + hidden.shape[1]
+    d_both = [part.reshape(PART * rows, -1) for part in d_both]
+    hidden = [part.reshape(PART * rows, -1) for part in hidden]
+    width = d_both[0].shape[1] + hidden[0].shape[1]
     columns = pl.BlockSpec((rows, GRAD_TILE), lambda step: (0, step))
     return pl.pallas_call(
         ffn_grads_kernel,
         name="feed_forward_grads",
         grid=(model // GRAD_TILE,),
         in_specs=[columns] * (2 * H)
-        + [
-            pl.BlockSpec(d_both.shape, lambda step: (0, 0)),
-            pl.BlockSpec(hidden.shape, lambda step: (0, 0)),
-        ],
+        + [pl.BlockSpec(part.shape, lambda step: (0, 0)) for part in (*d_both, *hidden)],
         out_specs=pl.BlockSpec((GRAD_TILE, width), lambda step: (step, 0)),
         out_shape=shaped((model, width), bf16),
-        cost_estimate=cost(4 * H * rows * model * width),
         compiler_params=kernel_params(),
-    )(*normed, *upstream, d_both, hidden)
+    )(*normed, *upstream, *d_both, *hidden)
 
 
 def mixer_grads_kernel(head_ref, *refs):
@@ -714,7 +740,7 @@
 
 
 def mixer_grads_rule(head, normed, branch, d_all, headed, weight, beta_w):
-    rows, model = normed[0].shape
+    rows, model = branch[0].shape
     width = WIDTH + 2 * DV
     columns = pl.BlockSpec((rows, GRAD_TILE), lambda step: (0, step))
     return pl.pallas_call(
@@ -740,23 +766,25 @@
 
 def d_in_kernel(d_all_ref, weight_ref, beta_ref, even_ref, odd_ref):
     width = WIDTH + DV
+    total = contract_cols(d_all_ref[0, :, :width], weight_ref[:, :width])
+    total = (total + contract_cols(d_all_ref[0, :, width:], beta_ref[...])).astype(bf16)
     for side, out_ref in ((0, even_ref), (1, odd_ref)):
-        d_all = d_all_ref[side]
-        total = contract_cols(d_all[:, :width], weight_ref[:, :width])
-        total = total + contract_cols(d_all[:, width:], beta_ref[...])
-        out_ref[0] = total.astype(bf16)
+
+        @pl.when(pl.program_id(0) % 2 == side)
+        def _():
+            out_ref[0] = total
 
 
 def d_in_rule(d_all, weight, beta_w):
     _, rows, width = d_all.shape
     model = weight.shape[0]
-    out = pl.BlockSpec((1, rows, model), lambda step: (step, 0, 0))
+    out = pl.BlockSpec((1, rows, model), lambda step: (step // 2, 0, 0))
     return pl.pallas_call(
         d_in_kernel,
         name="mixer_d_in",
-        grid=(H // 2,),
+        grid=(H,),
         in_specs=[
-            pl.BlockSpec((2, rows, width), lambda step: (step, 0, 0)),
+            pl.BlockSpec((1, rows, width), lambda step: (step, 0, 0)),
             pl.BlockSpec(weight.shape, lambda step: (0, 0)),
             pl.BlockSpec(beta_w.shape, lambda step: (0, 0)),
         ],
@@ -840,7 +868,7 @@
 
 
 def pair_sums(even, handed):
-    sums = [even[i].astype(f32) + handed[i].astype(f32) for i in range(H // 2)]
+    sums = [even[i].astype(f32) + handed[i].astype(f32) for i in range(even.shape[0])]
     return sums[0], [each.astype(bf16) for each in sums[1:]]
 
 
@@ -949,14 +977,8 @@
         (near_in, upstream_own, ffn_w_own)
     )
     up_near = neighbours(late_upstream)
-    normed_in, decay_blocks, mixer_w = lax.optimization_barrier(
-        (with_siblings(near_in), gather_blocks(decay_rows), mixer_w)
-    )
-    ffn_w = gather_weight(ffn_w_own)
-    beta_w = jnp.pad(own_columns(w_beta, 1), ((0, 0), (0, 127)))
-    in_width = WIDTH + DV
-    out_w = gather_rows(mixer_w[:, in_width:])
-
+    decay_rows, up_sides = lax.optimization_barrier((decay_rows, up_near[:3]))
+    up_near = up_sides + up_near[3:]
     taps = jnp.concatenate(
         [
             own_columns(conv_weight[:, : H * DK], DK),
@@ -966,6 +988,15 @@
         axis=1,
     )
     taps = jnp.pad(taps, ((0, 8 - CONV), (0, 0)))
+    beta_w = jnp.pad(own_columns(w_beta, 1), ((0, 0), (0, 127)))
+    decay_rows, taps, beta_w = lax.optimization_barrier((decay_rows, taps, beta_w))
+    normed_in, decay_blocks, mixer_w = lax.optimization_barrier(
+        (with_siblings(near_in), gather_blocks(decay_rows), mixer_w)
+    )
+    ffn_w = gather_weight(ffn_w_own)
+    in_width = WIDTH + DV
+    out_near = neighbours(mixer_w[:, in_width:])
+
     gain = norm_head[None, :]
 
     state = jnp.zeros((seqs, DK, DV), f32)
@@ -984,21 +1015,42 @@
             state = passed_along(ending, "seq", H)
 
     headed = headed.reshape(H, rows, DV)
-    headed, up_near = lax.optimization_barrier((headed, up_near))
+    headed, up_near, out_near = lax.optimization_barrier((headed, up_near, out_near))
     upstream = with_siblings(up_near)
     own_headed = lax.all_to_all(headed, "seq", 0, 0, axis_index_groups=groups, tiled=True)
-    residual, normed_own = out_rule(out_w, own_headed, own_in, norm_mid[None, :])
-    normed_mid = gather_blocks(normed_own)
-
-    d_both, hidden, d_even, d_odd, even, odd = ffn_rule(normed_mid, upstream, ffn_w)
+    residual, normed_own = out_rule(
+        head_arg, with_siblings(out_near), own_headed, own_in, norm_mid[None, :]
+    )
+    across = swapped(normed_own, "seq", 6)
+    near, far = swapped(normed_own, "seq", 2), swapped(normed_own, "seq", 4)
+    mid_first = with_siblings([normed_own, across])
+    up_first, up_last = upstream[:2] + upstream[6:], upstream[2:6]
+    both_first, hidden_first, d_even, d_odd, even_first, odd_first = ffn_rule(
+        mid_first, up_first, ffn_w
+    )
+    d_odd, near, far = lax.optimization_barrier((d_odd, near, far))
+    own_sum, across_sum = pair_sums(d_even, swapped(d_odd, "seq", 1))
+    mid_last, across_sum = lax.optimization_barrier((with_siblings([near, far]), across_sum))
+    across_sum = swapped(across_sum[0], "seq", 6)
+    both_last, hidden_last, d_even, d_odd, even_last, odd_last = ffn_rule(
+        mid_last, up_last, ffn_w
+    )
+    both_last, d_odd, across_sum = lax.optimization_barrier((both_last, d_odd, across_sum))
     ffn_partial = ffn_grads_rule(
-        normed_mid, upstream, d_both.reshape(all_rows, -1), hidden.reshape(all_rows, -1)
-    )
+        mid_first + mid_last,
+        up_first + up_last,
+        (both_first, both_last),
+        (hidden_first, hidden_last),
+    )
+    handed, ffn_partial = lax.optimization_barrier((swapped(d_odd, "seq", 1), ffn_partial))
     ffn_summed = reduce_weight(ffn_partial)
-    handed, _ = lax.optimization_barrier((swapped(d_odd, "seq", 1), ffn_partial))
-    own_sum, sums = pair_sums(d_even, handed)
-    received = exchanged(sums)
-    ffn_own, ffn_sums = pair_sums(even, swapped(odd, "seq", 1))
+    near_sum, far_sum = ((d_even[i].astype(f32) + handed[i].astype(f32)).astype(bf16) for i in (0, 1))
+    received = [swapped(near_sum, "seq", 2), swapped(far_sum, "seq", 4), across_sum]
+    ffn_own, ffn_across = pair_sums(even_first, swapped(odd_first, "seq", 1))
+    ffn_handed = swapped(odd_last, "seq", 1)
+    ffn_sums = [
+        (even_last[i].astype(f32) + ffn_handed[i].astype(f32)).astype(bf16) for i in (0, 1)
+    ] + ffn_across
     received, ffn_own, ffn_sums = lax.optimization_barrier((received, ffn_own, ffn_sums))
     d_normed_mid = total_of(own_sum, received)
     d_from_mid, grad_mid = rms_back(residual, norm_mid, d_normed_mid)
@@ -1006,8 +1058,8 @@
     branch, ffn_sums, ffn_summed = lax.optimization_barrier(
         (gather_blocks(d_residual.astype(bf16)), ffn_sums, ffn_summed)
     )
+    ffn_received = exchanged(ffn_sums)
     ffn_spread = spread_grads(ffn_summed)
-    ffn_received = exchanged(ffn_sums)
 
     d_end = jnp.zeros((seqs, DK, DV), f32)
     d_after = jnp.zeros((seqs, 8, WIDTH), f32)
@@ -1020,12 +1072,12 @@
             d_after = passed_along(d_before, "seq", -H)
     d_all = d_all.reshape(H, rows, -1)
 
-    layer_out = (residual + total_of(ffn_own, ffn_received)).astype(bf16).reshape(inputs.shape)
-
     mixer_partial, narrow = mixer_grads_rule(
         head_arg, normed_in, branch, d_all.reshape(all_rows, -1), headed, mixer_w, beta_w
     )
-    mixer_partial, ffn_spread = lax.optimization_barrier((mixer_partial, ffn_spread))
+    mixer_partial, ffn_spread, ffn_received = lax.optimization_barrier(
+        (mixer_partial, ffn_spread, ffn_received)
+    )
     mixer_summed = reduce_weight(mixer_partial)
     ffn_grads = join_hidden_rule(ffn_spread, hidden_all, 3)
 
@@ -1034,6 +1086,7 @@
     received, mixer_summed, narrow, ffn_grads = lax.optimization_barrier(
         (exchanged(sums), mixer_summed, narrow, ffn_grads)
     )
+    layer_out = (residual + total_of(ffn_own, ffn_received)).astype(bf16).reshape(inputs.shape)
     mixer_grads = join_rule(spread_grads(mixer_summed), [DK, DK, DV, DV, DV])
     d_normed_in = total_of(own_sum, received)
     d_from_in, _ = rms_back(flat_in, norm_in, d_normed_in)

time: 421 us -> 394 us (0.936); the launches traced: 413 us -> 393 us
  waiting for transfers between devices: 180 us -> 143 us
  starting transfers between devices: 41.5 us -> 50.6 us
  Pallas kernels: 133 us -> 140 us
    ppermute x52 -> x61, waiting for transfers between devices: 152 us -> 116 us  [swapped(): lax.ppermute(array, axis, [(i, i ^ bits) for i in range(lax.axis_size(axi...]
    all_gather x2, waiting for transfers between devices: 3.33 us -> 13.8 us  [spread_grads(): spread = lax.all_gather(summed, 'seq')]
    all_gather x2, waiting for transfers between devices: 10.2 us -> 0.02 us  [gather_weight(): return lax.all_gather(local, 'wt', axis=0, tiled=True)]
    ppermute x52 -> x61, starting transfers between devices: 37.5 us -> 46.1 us  [swapped(): lax.ppermute(array, axis, [(i, i ^ bits) for i in range(lax.axis_size(axi...]
    pallas_call x2 -> x3, Pallas kernels: 24.5 us -> 32.1 us  [the longest x2 21.3 us: ffn_rule(): pl.pallas_call(ffn_kernel, name='feed_forward', grid=(PART,), in_specs=an...]
    all_to_all x1, waiting for transfers between devices: 14.4 us -> 9.85 us  [shards(): lax.all_to_all(headed, 'seq', 0, 0, axis_index_groups=groups, tiled=True)]
    unnamed x115 -> x145, local copies, waits for them, and re-layouts: 11.4 us -> 12.9 us
  transfers between devices with their start and end apart: 60 -> 68, of which waited for: 26 -> 32; matrix products, arithmetic and copies ran while one was open for 7% -> 8% of each run, Pallas kernels for 26% -> 34%
where the time goes in v4:
time: 394 us; the launch traced here: 393 us
  waiting for transfers between devices  143 us (36%)
  Pallas kernels  140 us (36%)
  starting transfers between devices  50.6 us (13%)
  other arithmetic  22.1 us (6%)
  local copies, waits for them, and re-layouts  21.7 us (6%)
  between operations  15.1 us (4%)
    ppermute x61, waiting for transfers between devices, swapped(): lax.ppermute(array, axis, [(i, i ^ bits) for i in range(lax.axis_size(axi...  116 us
    ppermute x61, starting transfers between devices, swapped(): lax.ppermute(array, axis, [(i, i ^ bits) for i in range(lax.axis_size(axi...  46.1 us
    pallas_call x1, Pallas kernels, backward_rule(): pl.pallas_call(backward_kernel, name='mixer_backward', out_shape=(shaped(...  36 us
    pallas_call x1, Pallas kernels, forward_rule(): pl.pallas_call(forward_kernel, name='mixer_forward', out_shape=[shaped(*i...  30.3 us
    pallas_call x2, Pallas kernels, ffn_rule(): pl.pallas_call(ffn_kernel, name='feed_forward', grid=(PART,), in_specs=an...  21.3 us
    all_gather x2, waiting for transfers between devices, spread_grads(): spread = lax.all_gather(summed, 'seq')  13.8 us
    unnamed x145, local copies, waits for them, and re-layouts  12.9 us
    pallas_call x1, Pallas kernels, mixer_grads_rule(): pl.pallas_call(mixer_grads_kernel, name='mixer_grads', grid=(model // GRA...  11.1 us
  transfers between devices with their start and end apart: 68, of which 32 were waited for; matrix products, arithmetic and copies ran while one was open for 8% of the time, Pallas kernels for 34%

profile of v4, /device:TPU:0, one launch (start us, length us, event | category | flops | bytes accessed | tf_op | source)
XLA Modules:
  0.0 392.9 jit_solution(13503654948177320711)
XLA Ops:
  14.3 4.0 %collective-permute-start.2 = (bf16[256,1024]{1,0:T(8,128)(2,1)S(1)}, bf16[256,1024]{1,0:T(8,128)(2,1)S(1)}, u32[]{:S(2)}, u32[]{:S(2)}) collective-permute-start(bf16[256,1024]{1,0:T(8,128)(2,1)S(1)} %multiply_convert_fusion.refs_0_), channel_id=1, source_target_pairs={{0,24},{4,28},{8,16},{12,20},{16,8},{20,12},{24,0},{28,4},{1,25},{... | collective-permute-start | bytes 1572872 | tf_op jit(solution)/shard_map/ppermute | solution.py:855
  21.1 9.9 %collective-permute-done.2.refs_6_ = bf16[256,1024]{1,0:T(8,128)(2,1)S(1)} collective-permute-done((bf16[256,1024]{1,0:T(8,128)(2,1)S(1)}, bf16[256,1024]{1,0:T(8,128)(2,1)S(1)}, u32[]{:S(2)}, u32[]{:S(2)}) %collective-permute-start.2) | collective-permute-done | bytes 524320 | tf_op jit(solution)/shard_map/ppermute | solution.py:855
  31.0 10.4 %collective-permute-done.1.refs_4_ = bf16[256,1024]{1,0:T(8,128)(2,1)S(1)} collective-permute-done((bf16[256,1024]{1,0:T(8,128)(2,1)S(1)}, bf16[256,1024]{1,0:T(8,128)(2,1)S(1)}, u32[]{:S(2)}, u32[]{:S(2)}) %collective-permute-start.1) | collective-permute-done | bytes 524320 | tf_op jit(solution)/shard_map/ppermute | solution.py:855
  45.4 10.1 %collective-permute-done.8.refs_6_.refs_14_ = bf16[256,1024]{1,0:T(8,128)(2,1)} collective-permute-done((bf16[256,1024]{1,0:T(8,128)(2,1)S(1)}, bf16[256,1024]{1,0:T(8,128)(2,1)}, u32[]{:S(2)}, u32[]{:S(2)}) %collective-permute-start.8) | collective-permute-done | bytes 524320 | tf_op jit(solution)/shard_map/ppermute | solution.py:855
  71.2 30.3 %mixer_forward.1 = (bf16[8,2,128,256]{3,2,1,0:T(8,128)(2,1)}, bf16[8,2,128,512]{3,2,1,0:T(8,128)(2,1)}, f32[8,2,128,384]{3,2,1,0:T(8,128)}, f32[8,2,128,256]{3,2...) custom-call(s32[1]{0:T(128)} %bitcast.head_ref, ...), custom_call_target="tpu_custom_call" | custom-call | tf_op jit(solution)/shard_map/mixer_forward/pallas_call | solution.py:498
  102.4 3.6 all-to-all-start
  111.5 9.9 %all-to-all-done.refs_8_ = bf16[8,256,256]{2,1,0:T(8,128)(2,1)S(1)} async-done(((bf16[8,256,256]{2,1,0:T(8,128)(2,1)}), bf16[8,256,256]{2,1,0:T(8,128)(2,1)S(1)}, u32[]{:S(2)}, u32[]{:S(2)}) %all-to-all-start) | async-done | bytes 1048608 | tf_op jit(solution)/shard_map/all_to_all | solution.py:1020
  122.3 5.7 %out_projection.1 = (f32[256,1024]{1,0:T(8,128)}, bf16[256,1024]{1,0:T(8,128)(2,1)}) custom-call(s32[1]{0:T(128)} %bitcast.head_ref, bf16[1024,256]{1,0:T(8,128)(2,1)} %copy-done.25, bf16[1024,256]{1,0:T(8,128)(2,1)} %copy-done.48, bf16[1024,256]{1,0:T(8,128)(2,1)} %collective-permute-done.17.refs_2_, bf16[1024,256]{1,0:T(8,128)(2,1)} %copy-done.49, ...), custom_call_target="tpu_custom_call" | custom-call | tf_op jit(solution)/shard_map/out_projection/pallas_call | solution.py:597
  129.2 11.5 %collective-permute-done.25.refs_2_ = bf16[256,1024]{1,0:T(8,128)(2,1)S(1)} collective-permute-done((bf16[256,1024]{1,0:T(8,128)(2,1)}, bf16[256,1024]{1,0:T(8,128)(2,1)S(1)}, u32[]{:S(2)}, u32[]{:S(2)}) %collective-permute-start.25) | collective-permute-done | bytes 524320 | tf_op jit(solution)/shard_map/ppermute | solution.py:855
  145.0 10.6 %feed_forward.2 = (bf16[4,256,768]{2,1,0:T(8,128)(2,1)}, bf16[4,256,384]{2,1,0:T(8,128)(2,1)}, bf16[2,256,1024]{2,1,0:T(8,128)(2,1)}, bf16[2,256,1024]{2,1,0:T(8...) custom-call(bf16[256,1024]{1,0:T(8,128)(2,1)} %get-tuple-element.173.refs_0_, ...), custom_call_target="tpu_custom_call" | custom-call | tf_op jit(solution)/shard_map/feed_forward/pallas_call | solution.py:672
  157.8 3.3 collective-permute-done.33
  163.5 2.7 collective-permute-start.36
  167.8 10.7 %feed_forward.3 = (bf16[4,256,768]{2,1,0:T(8,128)(2,1)}, bf16[4,256,384]{2,1,0:T(8,128)(2,1)}, bf16[2,256,1024]{2,1,0:T(8,128)(2,1)}, bf16[2,256,1024]{2,1,0:T(8...) custom-call(bf16[256,1024]{1,0:T(8,128)(2,1)} %copy-done.33, bf16[256,1024]{1,0:T(8,128)(2,1)} %copy-done.34, ...), custom_call_target="tpu_custom_call" | custom-call | tf_op jit(solution)/shard_map/feed_forward/pallas_call | solution.py:672
  179.4 10.5 %feed_forward_grads.1 = bf16[1024,1152]{1,0:T(8,128)(2,1)} custom-call(bf16[256,1024]{1,0:T(8,128)(2,1)} %get-tuple-element.173.refs_0_, bf16[256,1024]{1,0:T(8,128)(2,1)} %copy-done.32, bf16[256,1024]{1,0:T(8,128)(2,1)} %copy-done.29, bf16[256,1024]{1,0:T(8,128)(2,1)} %collective-permute-done.26.refs_3_, bf16[256,1024]{1,0:T(8,128)(2,1)} %copy-done.33, ...), custom_call_target="tpu_custom_call" | custom-call | tf_op jit(solution)/shard_map/feed_forward_grads/pallas_call | solution.py:712
  198.1 8.1 %collective-permute-done.39 = bf16[256,1024]{1,0:T(8,128)(2,1)S(1)} collective-permute-done((bf16[256,1024]{1,0:T(8,128)(2,1)S(1)}, bf16[256,1024]{1,0:T(8,128)(2,1)S(1)}, u32[]{:S(2)}, u32[]{:S(2)}) %collective-permute-start.39) | collective-permute-done | bytes 524320 | tf_op jit(solution)/shard_map/ppermute | solution.py:855
  212.4 12.3 %collective-permute-done.47.refs_6_.refs_14_ = bf16[256,1024]{1,0:T(8,128)(2,1)S(1)} collective-permute-done((bf16[256,1024]{1,0:T(8,128)(2,1)S(1)}, bf16[256,1024]{1,0:T(8,128)(2,1)S(1)}, u32[]{:S(2)}, u32[]{:S(2)}) %collective-permute-start.47) | collective-permute-done | bytes 524320 | tf_op jit(solution)/shard_map/ppermute | solution.py:855
  224.7 9.7 %collective-permute-done.45.refs_4_.refs_12_ = bf16[256,1024]{1,0:T(8,128)(2,1)S(1)} collective-permute-done((bf16[256,1024]{1,0:T(8,128)(2,1)S(1)}, bf16[256,1024]{1,0:T(8,128)(2,1)S(1)}, u32[]{:S(2)}, u32[]{:S(2)}) %collective-permute-start.45) | collective-permute-done | bytes 524320 | tf_op jit(solution)/shard_map/ppermute | solution.py:855
  237.2 2.6 reduce-scatter.3.cloned.1.call-done
  244.2 36.0 %mixer_backward.1 = (bf16[8,2,128,896]{3,2,1,0:T(8,128)(2,1)}, f32[8,512]{1,0:T(8,128)}, f32[1,256]{1,0:T(1,128)}, f32[2,128,256]{2,1,0:T(8,128)}, f32[2,8,512]{2,1,0:T(8,128)}) custom-call(s32[1]{0:T(128)} %bitcast.head_ref, bf16[256,1024]{1,0:T(8,128)(2,1)} %copy-done.8, bf16[256,1024]{1,0:T(8,128)(2,1)} %copy-done.22, bf16[256,1024]{1,0:T(8,128)(2,1)} %copy-done.21, ...), custom_call_target="tpu_custom_call" | custom-call | tf_op jit(solution)/shard_map/mixer_backward/pallas_call | solution.py:529
  280.2 11.1 %mixer_grads.1 = (bf16[1024,1024]{1,0:T(8,128)(2,1)}, f32[1024,128]{1,0:T(8,128)}) custom-call(s32[1]{0:T(128)} %bitcast.head_ref, bf16[256,1024]{1,0:T(8,128)(2,1)} %copy-done.7, bf16[256,1024]{1,0:T(8,128)(2,1)} %copy-done.15, bf16[256,1024]{1,0:T(8,128)(2,1)} %copy-done.14, bf16[256,1024]{1,0:T(8,128)(2,1)} %copy-done.16, bf16[256,1024]{1,0:T(8,128)(2,1)} %copy-done.13, ...), custom_call_target="tpu_custom_call" | custom-call | tf_op jit(solution)/shard_map/mixer_grads/pallas_call | solution.py:746
  293.8 10.8 %mixer_d_in.1 = (bf16[4,256,1024]{2,1,0:T(8,128)(2,1)}, bf16[4,256,1024]{2,1,0:T(8,128)(2,1)}) custom-call(bf16[8,256,896]{2,1,0:T(8,128)(2,1)} %bitcast.104, bf16[1024,1024]{1,0:T(8,128)(2,1)} %all-gather.7.cloned.1.call-done.refs_16_.refs_8_.refs_18_.weight_ref, bf16[1024,128]{1,0:T(8,128)(2,1)} %pad.9.refs_17_.refs_19_.beta_ref), custom_call_target="tpu_custom_call" | custom-call | tf_op jit(solution)/shard_map/mixer_d_in/pallas_call | solution.py:782
  304.9 4.1 %collective-permute-done.52 = bf16[4,256,1024]{2,1,0:T(8,128)(2,1)S(1)} collective-permute-done((bf16[4,256,1024]{2,1,0:T(8,128)(2,1)}, bf16[4,256,1024]{2,1,0:T(8,128)(2,1)S(1)}, u32[]{:S(2)}, u32[]{:S(2)}) %collective-permute-start.52) | collective-permute-done | bytes 2097184 | tf_op jit(solution)/shard_map/ppermute | solution.py:855
  309.0 3.8 fusion.13
  316.2 7.5 %join_hidden.1 = (f32[256,2816]{1,0:T(8,128)}, f32[256,2816]{1,0:T(8,128)}, f32[256,2816]{1,0:T(8,128)}) custom-call(bf16[8,256,1152]{2,1,0:T(8,128)(2,1)} %bitcast.112), custom_call_target="tpu_custom_call" | custom-call | tf_op jit(solution)/shard_map/join_hidden/pallas_call | solution.py:837
  323.7 5.0 %collective-permute-done.55 = bf16[256,1024]{1,0:T(8,128)(2,1)} collective-permute-done((bf16[256,1024]{1,0:T(8,128)(2,1)}, bf16[256,1024]{1,0:T(8,128)(2,1)}, u32[]{:S(2)}, u32[]{:S(2)}) %collective-permute-start.55) | collective-permute-done | bytes 524320 | tf_op jit(solution)/shard_map/ppermute | solution.py:855
  328.7 10.5 %collective-permute-done.54 = bf16[256,1024]{1,0:T(8,128)(2,1)} collective-permute-done((bf16[256,1024]{1,0:T(8,128)(2,1)}, bf16[256,1024]{1,0:T(8,128)(2,1)}, u32[]{:S(2)}, u32[]{:S(2)}) %collective-permute-start.54) | collective-permute-done | bytes 524320 | tf_op jit(solution)/shard_map/ppermute | solution.py:855
  342.7 3.2 collective-permute-done.56
  347.7 3.2 collective-permute-done.57
  354.7 3.5 collective-permute-done.59
  359.8 4.2 %multiply_add_fusion = (f32[256,1024]{1,0:T(8,128)}, bf16[256,1024]{1,0:T(8,128)(2,1)}) fusion(f32[256]{0:T(256)S(1)} %broadcast_multiply_fusion, f32[256]{0:T(256)S(1)} %rsqrt_bitcast_fusion, bf16[2,128,1024]{2,1,0:T(8,128)(2,1)S(1)} %copy-done.4, f32[1024]{0:T(1024)S(1)} %copy-done.51, bf16[256,1024]{1,0:T(8,128)(2,1)} %collective-permute-done.55, ...), kind=kLoop, calls=%fused_computation.9 | loop fusion | flops 8126464 | bytes 9973760 | tf_op jit(solution)/shard_map/add | solution.py:1093
  367.2 11.7 %all-gather.13.cloned.1.call-done = bf16[2048,1024]{1,0:T(8,128)(2,1)} async-done(((bf16[256,1024]{1,0:T(8,128)(2,1)}), bf16[2048,1024]{1,0:T(8,128)(2,1)}) %all-gather.13.cloned.1.call-update) | async-done | bytes 4194320 | tf_op jit(solution)/shard_map/all_gather | solution.py:964
  378.9 7.2 %join_heads.1 = (f32[256,1024]{1,0:T(8,128)}, f32[256,1024]{1,0:T(8,128)}, f32[256,2048]{1,0:T(8,128)}, f32[256,2048]{1,0:T(8,128)}, f32[256,2048]{1,0:T(8,128)}) custom-call(bf16[8,256,1024]{2,1,0:T(8,128)(2,1)} %bitcast.115), custom_call_target="tpu_custom_call" | custom-call | tf_op jit(solution)/shard_map/join_heads/pallas_call | solution.py:812
  (313 shorter events, 90.3 us)
Async XLA Ops:
  7.2 57.9 %all-gather.7.cloned.1.call-start = ((), (), s32[]{:S(2)}) async-start(), calls=%async_computation.3 | async-start | bytes 2621440 | tf_op jit(solution)/shard_map/all_gather | solution.py:942
  12.7 131.3 %all-gather.9.cloned.1.call-start = ((), (), s32[]{:S(2)}) async-start(), calls=%async_computation.4 | async-start | bytes 2949120 | tf_op jit(solution)/shard_map/all_gather | solution.py:942
  14.3 16.8 %collective-permute-start.2 = (bf16[256,1024]{1,0:T(8,128)(2,1)S(1)}, bf16[256,1024]{1,0:T(8,128)(2,1)S(1)}, u32[]{:S(2)}, u32[]{:S(2)}) collective-permute-start(bf16[256,1024]{1,0:T(8,128)(2,1)S(1)} %multiply_convert_fusion.refs_0_), channel_id=1, source_target_pairs={{0,24},{4,28},{8,16},{12,20},{16,8},{20,12},{24,0},{28,4},{1,25},{... | collective-permute-start | bytes 1572872 | tf_op jit(solution)/shard_map/ppermute | solution.py:855
  18.2 23.2 %collective-permute-start.1 = (bf16[256,1024]{1,0:T(8,128)(2,1)S(1)}, bf16[256,1024]{1,0:T(8,128)(2,1)S(1)}, u32[]{:S(2)}, u32[]{:S(2)}) collective-permute-start(bf16[256,1024]{1,0:T(8,128)(2,1)S(1)} %multiply_convert_fusion.refs_0_), channel_id=1, source_target_pairs={{0,16},{4,20},{8,24},{12,28},{16,0},{20,4},{24,8},{28,12},{1,17},{... | collective-permute-start | bytes 1572872 | tf_op jit(solution)/shard_map/ppermute | solution.py:855
  18.7 22.9 %collective-permute-start = (bf16[256,1024]{1,0:T(8,128)(2,1)S(1)}, bf16[256,1024]{1,0:T(8,128)(2,1)S(1)}, u32[]{:S(2)}, u32[]{:S(2)}) collective-permute-start(bf16[256,1024]{1,0:T(8,128)(2,1)S(1)} %multiply_convert_fusion.refs_0_), channel_id=1, source_target_pairs={{0,8},{4,12},{8,0},{12,4},{16,24},{20,28},{24,16},{28,20},{1,9},{5... | collective-permute-start | bytes 1572872 | tf_op jit(solution)/shard_map/ppermute | solution.py:855
  44.9 14.4 %collective-permute-start.3 = (bf16[256,1024]{1,0:T(8,128)(2,1)S(1)}, bf16[256,1024]{1,0:T(8,128)(2,1)S(1)}, u32[]{:S(2)}, u32[]{:S(2)}) collective-permute-start(bf16[256,1024]{1,0:T(8,128)(2,1)S(1)} %multiply_convert_fusion.refs_0_), channel_id=1, source_target_pairs={{0,4},{4,0},{8,12},{12,8},{16,20},{20,16},{24,28},{28,24},{1,5},{5... | collective-permute-start | bytes 1572872 | tf_op jit(solution)/shard_map/ppermute | solution.py:855
  44.9 14.8 %collective-permute-start.4 = (bf16[256,1024]{1,0:T(8,128)(2,1)S(1)}, bf16[256,1024]{1,0:T(8,128)(2,1)S(1)}, u32[]{:S(2)}, u32[]{:S(2)}) collective-permute-start(bf16[256,1024]{1,0:T(8,128)(2,1)S(1)} %collective-permute-done.refs_2_), channel_id=1, source_target_pairs={{0,4},{4,0},{8,12},{12,8},{16,20},{20,16},{24,28},{28,24},{1,5},{5... | collective-permute-start | bytes 1572872 | tf_op jit(solution)/shard_map/ppermute | solution.py:855
  45.4 16.0 %collective-permute-start.5 = (bf16[256,1024]{1,0:T(8,128)(2,1)S(1)}, bf16[256,1024]{1,0:T(8,128)(2,1)S(1)}, u32[]{:S(2)}, u32[]{:S(2)}) collective-permute-start(bf16[256,1024]{1,0:T(8,128)(2,1)S(1)} %collective-permute-done.1.refs_4_), channel_id=1, source_target_pairs={{0,4},{4,0},{8,12},{12,8},{16,20},{20,16},{24,28},{28,24},{1,5},{5... | collective-permute-start | bytes 1572872 | tf_op jit(solution)/shard_map/ppermute | solution.py:855
  63.5 38.1 %collective-permute-start.16 = (bf16[256,1024]{1,0:T(8,128)(2,1)S(1)}, bf16[256,1024]{1,0:T(8,128)(2,1)}, u32[]{:S(2)}, u32[]{:S(2)}) collective-permute-start(bf16[256,1024]{1,0:T(8,128)(2,1)S(1)} %bitcast.110), channel_id=1, source_target_pairs={{0,24},{4,28},{8,16},{12,20},{16,8},{20,12},{24,0},{28,4},{1,25},{... | collective-permute-start | bytes 1572872 | tf_op jit(solution)/shard_map/ppermute | solution.py:855
  66.3 35.4 %collective-permute-start.19 = (bf16[1024,256]{1,0:T(8,128)(2,1)S(1)}, bf16[1024,256]{1,0:T(8,128)(2,1)}, u32[]{:S(2)}, u32[]{:S(2)}) collective-permute-start(bf16[1024,256]{1,0:T(8,128)(2,1)S(1)} %slice.123.refs_0_), channel_id=1, source_target_pairs={{0,24},{4,28},{8,16},{12,20},{16,8},{20,12},{24,0},{28,4},{1,25},{... | collective-permute-start | bytes 1572872 | tf_op jit(solution)/shard_map/ppermute | solution.py:855
  67.8 33.9 %collective-permute-start.18 = (bf16[1024,256]{1,0:T(8,128)(2,1)S(1)}, bf16[1024,256]{1,0:T(8,128)(2,1)S(1)}, u32[]{:S(2)}, u32[]{:S(2)}) collective-permute-start(bf16[1024,256]{1,0:T(8,128)(2,1)S(1)} %slice.123.refs_0_), channel_id=1, source_target_pairs={{0,16},{4,20},{8,24},{12,28},{16,0},{20,4},{24,8},{28,12},{1,17},{... | collective-permute-start | bytes 1572872 | tf_op jit(solution)/shard_map/ppermute | solution.py:855
  69.3 32.3 %collective-permute-start.17 = (bf16[1024,256]{1,0:T(8,128)(2,1)S(1)}, bf16[1024,256]{1,0:T(8,128)(2,1)}, u32[]{:S(2)}, u32[]{:S(2)}) collective-permute-start(bf16[1024,256]{1,0:T(8,128)(2,1)S(1)} %slice.123.refs_0_), channel_id=1, source_target_pairs={{0,8},{4,12},{8,0},{12,4},{16,24},{20,28},{24,16},{28,20},{1,9},{5... | collective-permute-start | bytes 1572872 | tf_op jit(solution)/shard_map/ppermute | solution.py:855
  102.4 18.9 %all-to-all-start = ((bf16[8,256,256]{2,1,0:T(8,128)(2,1)}), bf16[8,256,256]{2,1,0:T(8,128)(2,1)S(1)}, u32[]{:S(2)}, u32[]{:S(2)}) async-start(bf16[8,256,256]{2,1,0:T(8,128)(2,1)} %bitcast.113), calls=%async_computation | async-start | bytes 2097152 | tf_op jit(solution)/shard_map/all_to_all | solution.py:1020
  106.0 133.8 %reduce-scatter.3.cloned.1.call-start = ((), (), s32[]{:S(2)}) async-start(), calls=%async_computation.5 | async-start | bytes 2949120 | tf_op jit(solution)/shard_map/reduce_scatter | solution.py:961
  128.7 15.3 %collective-permute-start.28 = (bf16[256,1024]{1,0:T(8,128)(2,1)}, bf16[256,1024]{1,0:T(8,128)(2,1)S(1)}, u32[]{:S(2)}, u32[]{:S(2)}) collective-permute-start(bf16[256,1024]{1,0:T(8,128)(2,1)} %collective-permute-done.16.refs_6_.refs_10_), channel_id=1, source_target_pairs={{0,4},{4,0},{8,12},{12,8},{16,20},{20,16},{24,28},{28,24},{1,5},{5... | collective-permute-start | bytes 1572872 | tf_op jit(solution)/shard_map/ppermute | solution.py:855
  129.2 14.8 %collective-permute-start.24 = (bf16[256,1024]{1,0:T(8,128)(2,1)}, bf16[256,1024]{1,0:T(8,128)(2,1)S(1)}, u32[]{:S(2)}, u32[]{:S(2)}) collective-permute-start(bf16[256,1024]{1,0:T(8,128)(2,1)} %get-tuple-element.173.refs_0_), channel_id=1, source_target_pairs={{0,4},{4,0},{8,12},{12,8},{16,20},{20,16},{24,28},{28,24},{1,5},{5... | collective-permute-start | bytes 1572872 | tf_op jit(solution)/shard_map/ppermute | solution.py:855
  140.8 14.8 %collective-permute-start.30 = (bf16[256,1024]{1,0:T(8,128)(2,1)}, bf16[256,1024]{1,0:T(8,128)(2,1)}, u32[]{:S(2)}, u32[]{:S(2)}) collective-permute-start(bf16[256,1024]{1,0:T(8,128)(2,1)} %get-tuple-element.173.refs_0_), channel_id=1, source_target_pairs={{0,16},{4,20},{8,24},{12,28},{16,0},{20,4},{24,8},{28,12},{1,17},{... | collective-permute-start | bytes 1572872 | tf_op jit(solution)/shard_map/ppermute | solution.py:855
  163.5 15.1 %collective-permute-start.36 = (bf16[256,1024]{1,0:T(8,128)(2,1)}, bf16[256,1024]{1,0:T(8,128)(2,1)S(1)}, u32[]{:S(2)}, u32[]{:S(2)}) collective-permute-start(bf16[256,1024]{1,0:T(8,128)(2,1)} %fusion.5), channel_id=1, source_target_pairs={{0,24},{4,28},{8,16},{12,20},{16,8},{20,12},{24,0},{28,4},{1,25},{... | collective-permute-start | bytes 1572872 | tf_op jit(solution)/shard_map/ppermute | solution.py:855
  190.0 103.5 %all-gather.11.cloned.1.call-start = ((), (), s32[]{:S(2)}) async-start(), calls=%async_computation.7 | async-start | bytes 5308416 | tf_op jit(solution)/shard_map/all_gather | solution.py:964
  191.9 14.4 %collective-permute-start.39 = (bf16[256,1024]{1,0:T(8,128)(2,1)S(1)}, bf16[256,1024]{1,0:T(8,128)(2,1)S(1)}, u32[]{:S(2)}, u32[]{:S(2)}) collective-permute-start(bf16[256,1024]{1,0:T(8,128)(2,1)S(1)} %get-tuple-element.271), channel_id=1, source_target_pairs={{0,16},{4,20},{8,24},{12,28},{16,0},{20,4},{24,8},{28,12},{1,17},{... | collective-permute-start | bytes 1572872 | tf_op jit(solution)/shard_map/ppermute | solution.py:855
  208.9 15.9 %collective-permute-start.47 = (bf16[256,1024]{1,0:T(8,128)(2,1)S(1)}, bf16[256,1024]{1,0:T(8,128)(2,1)S(1)}, u32[]{:S(2)}, u32[]{:S(2)}) collective-permute-start(bf16[256,1024]{1,0:T(8,128)(2,1)S(1)} %fusion.15.refs_0_.refs_8_), channel_id=1, source_target_pairs={{0,24},{4,28},{8,16},{12,20},{16,8},{20,12},{24,0},{28,4},{1,25},{... | collective-permute-start | bytes 1572872 | tf_op jit(solution)/shard_map/ppermute | solution.py:855
  210.4 24.0 %collective-permute-start.45 = (bf16[256,1024]{1,0:T(8,128)(2,1)S(1)}, bf16[256,1024]{1,0:T(8,128)(2,1)S(1)}, u32[]{:S(2)}, u32[]{:S(2)}) collective-permute-start(bf16[256,1024]{1,0:T(8,128)(2,1)S(1)} %fusion.15.refs_0_.refs_8_), channel_id=1, source_target_pairs={{0,16},{4,20},{8,24},{12,28},{16,0},{20,4},{24,8},{28,12},{1,17},{... | collective-permute-start | bytes 1572872 | tf_op jit(solution)/shard_map/ppermute | solution.py:855
  212.1 22.4 %collective-permute-start.43 = (bf16[256,1024]{1,0:T(8,128)(2,1)S(1)}, bf16[256,1024]{1,0:T(8,128)(2,1)S(1)}, u32[]{:S(2)}, u32[]{:S(2)}) collective-permute-start(bf16[256,1024]{1,0:T(8,128)(2,1)S(1)} %fusion.15.refs_0_.refs_8_), channel_id=1, source_target_pairs={{0,8},{4,12},{8,0},{12,4},{16,24},{20,28},{24,16},{28,20},{1,9},{5... | collective-permute-start | bytes 1572872 | tf_op jit(solution)/shard_map/ppermute | solution.py:855
  212.4 22.5 %collective-permute-start.42 = (bf16[256,1024]{1,0:T(8,128)(2,1)S(1)}, bf16[256,1024]{1,0:T(8,128)(2,1)S(1)}, u32[]{:S(2)}, u32[]{:S(2)}) collective-permute-start(bf16[256,1024]{1,0:T(8,128)(2,1)S(1)} %fusion.15.refs_0_.refs_8_), channel_id=1, source_target_pairs={{0,4},{4,0},{8,12},{12,8},{16,20},{20,16},{24,28},{28,24},{1,5},{5... | collective-permute-start | bytes 1572872 | tf_op jit(solution)/shard_map/ppermute | solution.py:855
  239.8 100.3 %reduce-scatter.5.cloned.1.call-start = ((), (), s32[]{:S(2)}) async-start(), calls=%async_computation.6 | async-start | bytes 2621440 | tf_op jit(solution)/shard_map/reduce_scatter | solution.py:961
  240.1 51.3 %collective-permute-start.49 = (bf16[256,1024]{1,0:T(8,128)(2,1)}, bf16[256,1024]{1,0:T(8,128)(2,1)}, u32[]{:S(2)}, u32[]{:S(2)}) collective-permute-start(bf16[256,1024]{1,0:T(8,128)(2,1)} %get-tuple-element.230), channel_id=1, source_target_pairs={{0,8},{4,12},{8,0},{12,4},{16,24},{20,28},{24,16},{28,20},{1,9},{5... | collective-permute-start | bytes 1572872 | tf_op jit(solution)/shard_map/ppermute | solution.py:855
  241.6 49.7 %collective-permute-start.50 = (bf16[256,1024]{1,0:T(8,128)(2,1)}, bf16[256,1024]{1,0:T(8,128)(2,1)}, u32[]{:S(2)}, u32[]{:S(2)}) collective-permute-start(bf16[256,1024]{1,0:T(8,128)(2,1)} %get-tuple-element.231), channel_id=1, source_target_pairs={{0,16},{4,20},{8,24},{12,28},{16,0},{20,4},{24,8},{28,12},{1,17},{... | collective-permute-start | bytes 1572872 | tf_op jit(solution)/shard_map/ppermute | solution.py:855
  243.1 48.3 %collective-permute-start.51 = (bf16[256,1024]{1,0:T(8,128)(2,1)}, bf16[256,1024]{1,0:T(8,128)(2,1)}, u32[]{:S(2)}, u32[]{:S(2)}) collective-permute-start(bf16[256,1024]{1,0:T(8,128)(2,1)} %get-tuple-element.232), channel_id=1, source_target_pairs={{0,24},{4,28},{8,16},{12,20},{16,8},{20,12},{24,0},{28,4},{1,25},{... | collective-permute-start | bytes 1572872 | tf_op jit(solution)/shard_map/ppermute | solution.py:855
  293.5 85.4 %all-gather.13.cloned.1.call-start = ((), (), s32[]{:S(2)}) async-start(), calls=%async_computation.8 | async-start | bytes 4718592 | tf_op jit(solution)/shard_map/all_gather | solution.py:964
  312.7 16.0 %collective-permute-start.55 = (bf16[256,1024]{1,0:T(8,128)(2,1)}, bf16[256,1024]{1,0:T(8,128)(2,1)}, u32[]{:S(2)}, u32[]{:S(2)}) collective-permute-start(bf16[256,1024]{1,0:T(8,128)(2,1)} %get-tuple-element.264), channel_id=1, source_target_pairs={{0,24},{4,28},{8,16},{12,20},{16,8},{20,12},{24,0},{28,4},{1,25},{... | collective-permute-start | bytes 1572872 | tf_op jit(solution)/shard_map/ppermute | solution.py:855
  314.2 25.1 %collective-permute-start.54 = (bf16[256,1024]{1,0:T(8,128)(2,1)}, bf16[256,1024]{1,0:T(8,128)(2,1)}, u32[]{:S(2)}, u32[]{:S(2)}) collective-permute-start(bf16[256,1024]{1,0:T(8,128)(2,1)} %get-tuple-element.265), channel_id=1, source_target_pairs={{0,16},{4,20},{8,24},{12,28},{16,0},{20,4},{24,8},{28,12},{1,17},{... | collective-permute-start | bytes 1572872 | tf_op jit(solution)/shard_map/ppermute | solution.py:855
  315.6 23.6 %collective-permute-start.53 = (bf16[256,1024]{1,0:T(8,128)(2,1)S(1)}, bf16[256,1024]{1,0:T(8,128)(2,1)}, u32[]{:S(2)}, u32[]{:S(2)}) collective-permute-start(bf16[256,1024]{1,0:T(8,128)(2,1)S(1)} %get-tuple-element.266), channel_id=1, source_target_pairs={{0,8},{4,12},{8,0},{12,4},{16,24},{20,28},{24,16},{28,20},{1,9},{5... | collective-permute-start | bytes 1572872 | tf_op jit(solution)/shard_map/ppermute | solution.py:855
  (101 other events, 1001.1 us)
Sparse Core Ops, SparseCore 0:
  12.8 48.6 all-gather.6
  63.6 49.1 all-gather.8
  190.1 49.6 reduce-scatter.2
  241.5 51.9 all-gather.10
  296.2 43.8 reduce-scatter.4
  342.0 36.7 all-gather.12

commit v5 on v4

--- a/solution.py
+++ b/solution.py
@@ -76,6 +76,38 @@
         blocks = [jnp.where(corner, lower, 0.0) for lower in lowers]
         if level == 0:
             inverses = [inverse - block for inverse, block in zip(inverses, blocks)]
+        elif (1 << level) >= 16:
+            half = 1 << level
+            starts = range(half, size, 2 * half)
+            below = [jnp.concatenate([i[at : at + half] for at in starts], 0) for i in inverses]
+            blocks = [jnp.concatenate([b[at : at + half] for at in starts], 0) for b in blocks]
+            steps = [mul(parts(b), parts(i)) for b, i in zip(blocks, inverses)]
+            gap = jnp.zeros((half, size), f32)
+            spread = [
+                jnp.concatenate(
+                    [
+                        piece
+                        for index in range(len(starts))
+                        for piece in (gap, step[index * half : (index + 1) * half])
+                    ],
+                    0,
+                )
+                for step in steps
+            ]
+            steps = [low - mul(parts(low), parts(wide)) for low, wide in zip(below, spread)]
+            inverses = [
+                jnp.concatenate(
+                    [
+                        piece
+                        for index, at in enumerate(starts)
+                        for piece in (
+                            inverse[at - half : at], step[index * half : (index + 1) * half]
+                        )
+                    ],
+                    0,
+                )
+                for inverse, step in zip(inverses, steps)
+            ]
         else:
             wholes = [parts(inverse) for inverse in inverses]
             steps = [mul(parts(block), whole) for block, whole in zip(blocks, wholes)]
@@ -131,7 +163,7 @@
 
 
 def forward_kernel(head_ref, *refs):
-    block_refs, decay_refs, refs = refs[:H], refs[H : 2 * H], refs[2 * H :]
+    block_refs, decay_ref, refs = refs[:H], refs[H], refs[H + 1 :]
     weight_in, beta_ref, taps_ref, gain_ref, state_ref, halo_ref = refs[:6]
     outs, (run_ref, end_ref), held, refs = refs[6:14], refs[14:16], refs[16:24], refs[24:]
     headed_ref, conv_ref, gate_ref, mixed_ref, inverse_ref, scores_ref, delta_ref, starts_ref = held
@@ -152,10 +184,11 @@
 
     for slot in range(H):
         block_copy(block_refs[slot], slot).start()
-    for slot in range(H):
-        logs = jnp.log(decay_refs[slot][pl.ds(head, 1), :])
+    logs = jnp.log(decay_ref[...])
+    for chunk in range(chunks):
         for seq in range(seqs):
-            log_ref[pl.ds((slot ^ head) * seqs + seq, 1), :] = logs[:, seq * size : (seq + 1) * size]
+            row = chunk * seqs + seq
+            log_ref[row : row + 1, :] = logs[chunk : chunk + 1, seq * size : (seq + 1) * size]
     run_ref[...] = running_sums(log_ref[...], rows, cols)
 
     weight_copy.wait()
@@ -480,7 +513,7 @@
     return [pl.BlockSpec(memory_space=pltpu.HBM)] * count
 
 
-def forward_rule(head, blocks, decay_blocks, weight, beta_w, taps, gain, state, halo):
+def forward_rule(head, blocks, own_decay, weight, beta_w, taps, gain, state, halo):
     rows, model = blocks[0].shape
     seqs = state.shape[0]
     size = rows // seqs
@@ -500,7 +533,7 @@
         name="mixer_forward",
         out_shape=[shaped(*item) for item in held]
         + [shaped((H * seqs, size), f32), shaped((seqs, DK, DV), f32)],
-        in_specs=scalar() + anywhere(H) + whole(H) + anywhere(1) + whole(5),
+        in_specs=scalar() + anywhere(H) + whole(1) + anywhere(1) + whole(5),
         out_specs=anywhere(8) + whole(2),
         scratch_shapes=[pltpu.VMEM(*item) for item in held]
         + [
@@ -518,7 +551,7 @@
             pltpu.SemaphoreType.DMA((8,)),
         ],
         compiler_params=kernel_params(),
-    )(head, *blocks, *decay_blocks, weight, beta_w, taps, gain, state, halo)
+    )(head, *blocks, own_decay, weight, beta_w, taps, gain, state, halo)
 
 
 def backward_rule(head, branch, weight, saved, run, taps, gain, halo, d_end, d_after):
@@ -977,8 +1010,6 @@
         (near_in, upstream_own, ffn_w_own)
     )
     up_near = neighbours(late_upstream)
-    decay_rows, up_sides = lax.optimization_barrier((decay_rows, up_near[:3]))
-    up_near = up_sides + up_near[3:]
     taps = jnp.concatenate(
         [
             own_columns(conv_weight[:, : H * DK], DK),
@@ -989,10 +1020,14 @@
     )
     taps = jnp.pad(taps, ((0, 8 - CONV), (0, 0)))
     beta_w = jnp.pad(own_columns(w_beta, 1), ((0, 0), (0, 127)))
-    decay_rows, taps, beta_w = lax.optimization_barrier((decay_rows, taps, beta_w))
-    normed_in, decay_blocks, mixer_w = lax.optimization_barrier(
-        (with_siblings(near_in), gather_blocks(decay_rows), mixer_w)
-    )
+    own_decay = lax.all_to_all(
+        decay_rows, "seq", 0, 0, axis_index_groups=groups, tiled=True
+    )
+    own_decay, taps, beta_w, near_in = lax.optimization_barrier((own_decay, taps, beta_w, near_in))
+    normed_in, mixer_w, up_sides = lax.optimization_barrier(
+        (with_siblings(near_in), mixer_w, up_near[:3])
+    )
+    up_near = up_sides + up_near[3:]
     ffn_w = gather_weight(ffn_w_own)
     in_width = WIDTH + DV
     out_near = neighbours(mixer_w[:, in_width:])
@@ -1008,7 +1043,7 @@
         halo = jnp.where(place >= H, rolled.reshape(halo.shape), halo)
     for stage in range(stages):
         headed, *saved, ending = forward_rule(
-            head_arg, normed_in, decay_blocks, mixer_w, beta_w, taps, gain, state, halo
+            head_arg, normed_in, own_decay, mixer_w, beta_w, taps, gain, state, halo
         )
         run = saved.pop()
         if stage < stages - 1:

time: 394 us -> 388 us (0.985)
  waiting for transfers between devices: 143 us -> 134 us
    ppermute x61 -> x54, waiting for transfers between devices: 116 us -> 93.2 us  [swapped(): lax.ppermute(array, axis, [(i, i ^ bits) for i in range(lax.axis_size(axi...]
    all_to_all x0 -> x1, waiting for transfers between devices: none -> 14.1 us  [shards(): lax.all_to_all(decay_rows, 'seq', 0, 0, axis_index_groups=groups, tiled=T...]
    all_to_all x0 -> x1, starting transfers between devices: none -> 4.12 us  [shards(): lax.all_to_all(decay_rows, 'seq', 0, 0, axis_index_groups=groups, tiled=T...]
    ppermute x61 -> x54, starting transfers between devices: 46.1 us -> 43.3 us  [swapped(): lax.ppermute(array, axis, [(i, i ^ bits) for i in range(lax.axis_size(axi...]
    unnamed x145 -> x132, local copies, waits for them, and re-layouts: 12.9 us -> 14.2 us
  transfers between devices with their start and end apart: 68 -> 62, of which waited for: 32 -> 28; matrix products, arithmetic and copies ran while one was open for 8% -> 8% of each run, Pallas kernels for 34% -> 34%
where the time goes in v5:
time: 388 us; the launch traced here: 387 us
  Pallas kernels  140 us (36%)
  waiting for transfers between devices  134 us (35%)
  starting transfers between devices  52 us (13%)
  local copies, waits for them, and re-layouts  23.7 us (6%)
  other arithmetic  22.2 us (6%)
  between operations  15 us (4%)
    ppermute x54, waiting for transfers between devices, swapped(): lax.ppermute(array, axis, [(i, i ^ bits) for i in range(lax.axis_size(axi...  93.2 us
    ppermute x54, starting transfers between devices, swapped(): lax.ppermute(array, axis, [(i, i ^ bits) for i in range(lax.axis_size(axi...  43.3 us
    pallas_call x1, Pallas kernels, backward_rule(): pl.pallas_call(backward_kernel, name='mixer_backward', out_shape=(shaped(...  36 us
    pallas_call x1, Pallas kernels, forward_rule(): pl.pallas_call(forward_kernel, name='mixer_forward', out_shape=[shaped(*i...  29.5 us
    pallas_call x2, Pallas kernels, ffn_rule(): pl.pallas_call(ffn_kernel, name='feed_forward', grid=(PART,), in_specs=an...  21.3 us
    unnamed x132, local copies, waits for them, and re-layouts  14.2 us
    all_to_all x1, waiting for transfers between devices, shards(): lax.all_to_all(decay_rows, 'seq', 0, 0, axis_index_groups=groups, tiled=T...  14.1 us
    all_gather x2, waiting for transfers between devices, spread_grads(): spread = lax.all_gather(summed, 'seq')  13.8 us
  transfers between devices with their start and end apart: 62, of which 28 were waited for; matrix products, arithmetic and copies ran while one was open for 8% of the time, Pallas kernels for 34%

profile of v5, /device:TPU:0, one launch (start us, length us, event | category | flops | bytes accessed | tf_op | source)
XLA Modules:
  0.0 386.6 jit_solution(17833792682689914541)
XLA Ops:
  14.2 4.0 %collective-permute-start.2 = (bf16[256,1024]{1,0:T(8,128)(2,1)S(1)}, bf16[256,1024]{1,0:T(8,128)(2,1)S(1)}, u32[]{:S(2)}, u32[]{:S(2)}) collective-permute-start(bf16[256,1024]{1,0:T(8,128)(2,1)S(1)} %multiply_convert_fusion.refs_0_), channel_id=1, source_target_pairs={{0,24},{4,28},{8,16},{12,20},{16,8},{20,12},{24,0},{28,4},{1,25},{... | collective-permute-start | bytes 1572872 | tf_op jit(solution)/shard_map/ppermute | solution.py:888
  19.4 4.1 %all-to-all-start = ((f32[8,1,256]{2,1,0:T(1,128)}), f32[8,1,256]{2,1,0:T(1,128)S(1)}, u32[]{:S(2)}, u32[]{:S(2)}) async-start(f32[8,1,256]{2,1,0:T(1,128)} %all_to_all.11), calls=%async_computation | async-start | bytes 16384 | tf_op jit(solution)/shard_map/all_to_all | solution.py:1023
  27.6 14.1 %all-to-all-done = f32[8,1,256]{2,1,0:T(1,128)S(1)} async-done(((f32[8,1,256]{2,1,0:T(1,128)}), f32[8,1,256]{2,1,0:T(1,128)S(1)}, u32[]{:S(2)}, u32[]{:S(2)}) %all-to-all-start) | async-done | bytes 8224 | tf_op jit(solution)/shard_map/all_to_all | solution.py:1023
  47.5 10.1 %collective-permute-done.8.refs_6_.refs_14_ = bf16[256,1024]{1,0:T(8,128)(2,1)S(1)} collective-permute-done((bf16[256,1024]{1,0:T(8,128)(2,1)S(1)}, bf16[256,1024]{1,0:T(8,128)(2,1)S(1)}, u32[]{:S(2)}, u32[]{:S(2)}) %collective-permute-start.8) | collective-permute-done | bytes 524320 | tf_op jit(solution)/shard_map/ppermute | solution.py:888
  62.6 2.4 collective-permute-start.12
  67.5 29.5 %mixer_forward.1 = (bf16[8,2,128,256]{3,2,1,0:T(8,128)(2,1)}, bf16[8,2,128,512]{3,2,1,0:T(8,128)(2,1)}, f32[8,2,128,384]{3,2,1,0:T(8,128)}, f32[8,2,128,256]{3,2...) custom-call(s32[1]{0:T(128)} %bitcast.head_ref, ...), custom_call_target="tpu_custom_call" | custom-call | tf_op jit(solution)/shard_map/mixer_forward/pallas_call | solution.py:531
  97.9 3.7 all-to-all-start.1
  107.1 9.9 %all-to-all-done.1.refs_8_ = bf16[8,256,256]{2,1,0:T(8,128)(2,1)S(1)} async-done(((bf16[8,256,256]{2,1,0:T(8,128)(2,1)}), bf16[8,256,256]{2,1,0:T(8,128)(2,1)S(1)}, u32[]{:S(2)}, u32[]{:S(2)}) %all-to-all-start.1) | async-done | bytes 1048608 | tf_op jit(solution)/shard_map/all_to_all | solution.py:1055
  118.0 5.7 %out_projection.1 = (f32[256,1024]{1,0:T(8,128)}, bf16[256,1024]{1,0:T(8,128)(2,1)}) custom-call(s32[1]{0:T(128)} %bitcast.head_ref, bf16[1024,256]{1,0:T(8,128)(2,1)} %copy-done.25, bf16[1024,256]{1,0:T(8,128)(2,1)} %copy-done.48, bf16[1024,256]{1,0:T(8,128)(2,1)} %collective-permute-done.10.refs_2_, bf16[1024,256]{1,0:T(8,128)(2,1)} %copy-done.49, ...), custom_call_target="tpu_custom_call" | custom-call | tf_op jit(solution)/shard_map/out_projection/pallas_call | solution.py:630
  124.9 11.6 %collective-permute-done.18.refs_2_ = bf16[256,1024]{1,0:T(8,128)(2,1)S(1)} collective-permute-done((bf16[256,1024]{1,0:T(8,128)(2,1)}, bf16[256,1024]{1,0:T(8,128)(2,1)S(1)}, u32[]{:S(2)}, u32[]{:S(2)}) %collective-permute-start.18) | collective-permute-done | bytes 524320 | tf_op jit(solution)/shard_map/ppermute | solution.py:888
  140.6 10.7 %feed_forward.2 = (bf16[4,256,768]{2,1,0:T(8,128)(2,1)}, bf16[4,256,384]{2,1,0:T(8,128)(2,1)}, bf16[2,256,1024]{2,1,0:T(8,128)(2,1)}, bf16[2,256,1024]{2,1,0:T(8...) custom-call(bf16[256,1024]{1,0:T(8,128)(2,1)} %get-tuple-element.163.refs_0_, ...), custom_call_target="tpu_custom_call" | custom-call | tf_op jit(solution)/shard_map/feed_forward/pallas_call | solution.py:705
  153.4 3.3 collective-permute-done.26
  159.1 2.7 collective-permute-start.29
  163.4 10.6 %feed_forward.3 = (bf16[4,256,768]{2,1,0:T(8,128)(2,1)}, bf16[4,256,384]{2,1,0:T(8,128)(2,1)}, bf16[2,256,1024]{2,1,0:T(8,128)(2,1)}, bf16[2,256,1024]{2,1,0:T(8...) custom-call(bf16[256,1024]{1,0:T(8,128)(2,1)} %copy-done.33, bf16[256,1024]{1,0:T(8,128)(2,1)} %copy-done.34, ...), custom_call_target="tpu_custom_call" | custom-call | tf_op jit(solution)/shard_map/feed_forward/pallas_call | solution.py:705
  175.1 10.5 %feed_forward_grads.1 = bf16[1024,1152]{1,0:T(8,128)(2,1)} custom-call(bf16[256,1024]{1,0:T(8,128)(2,1)} %get-tuple-element.163.refs_0_, bf16[256,1024]{1,0:T(8,128)(2,1)} %copy-done.32, bf16[256,1024]{1,0:T(8,128)(2,1)} %copy-done.29, bf16[256,1024]{1,0:T(8,128)(2,1)} %collective-permute-done.19.refs_3_, bf16[256,1024]{1,0:T(8,128)(2,1)} %copy-done.33, ...), custom_call_target="tpu_custom_call" | custom-call | tf_op jit(solution)/shard_map/feed_forward_grads/pallas_call | solution.py:745
  193.8 8.1 %collective-permute-done.32 = bf16[256,1024]{1,0:T(8,128)(2,1)S(1)} collective-permute-done((bf16[256,1024]{1,0:T(8,128)(2,1)S(1)}, bf16[256,1024]{1,0:T(8,128)(2,1)S(1)}, u32[]{:S(2)}, u32[]{:S(2)}) %collective-permute-start.32) | collective-permute-done | bytes 524320 | tf_op jit(solution)/shard_map/ppermute | solution.py:888
  208.1 12.3 %collective-permute-done.40.refs_6_.refs_14_ = bf16[256,1024]{1,0:T(8,128)(2,1)S(1)} collective-permute-done((bf16[256,1024]{1,0:T(8,128)(2,1)S(1)}, bf16[256,1024]{1,0:T(8,128)(2,1)S(1)}, u32[]{:S(2)}, u32[]{:S(2)}) %collective-permute-start.40) | collective-permute-done | bytes 524320 | tf_op jit(solution)/shard_map/ppermute | solution.py:888
  220.4 9.7 %collective-permute-done.38.refs_4_.refs_12_ = bf16[256,1024]{1,0:T(8,128)(2,1)S(1)} collective-permute-done((bf16[256,1024]{1,0:T(8,128)(2,1)S(1)}, bf16[256,1024]{1,0:T(8,128)(2,1)S(1)}, u32[]{:S(2)}, u32[]{:S(2)}) %collective-permute-start.38) | collective-permute-done | bytes 524320 | tf_op jit(solution)/shard_map/ppermute | solution.py:888
  237.9 36.0 %mixer_backward.1 = (bf16[8,2,128,896]{3,2,1,0:T(8,128)(2,1)}, f32[8,512]{1,0:T(8,128)}, f32[1,256]{1,0:T(1,128)}, f32[2,128,256]{2,1,0:T(8,128)}, f32[2,8,512]{2,1,0:T(8,128)}) custom-call(s32[1]{0:T(128)} %bitcast.head_ref, bf16[256,1024]{1,0:T(8,128)(2,1)} %copy-done.8, bf16[256,1024]{1,0:T(8,128)(2,1)} %copy-done.22, bf16[256,1024]{1,0:T(8,128)(2,1)} %copy-done.21, ...), custom_call_target="tpu_custom_call" | custom-call | tf_op jit(solution)/shard_map/mixer_backward/pallas_call | solution.py:562
  273.9 11.1 %mixer_grads.1 = (bf16[1024,1024]{1,0:T(8,128)(2,1)}, f32[1024,128]{1,0:T(8,128)}) custom-call(s32[1]{0:T(128)} %bitcast.head_ref, bf16[256,1024]{1,0:T(8,128)(2,1)} %copy-done.7, bf16[256,1024]{1,0:T(8,128)(2,1)} %copy-done.15, bf16[256,1024]{1,0:T(8,128)(2,1)} %copy-done.14, bf16[256,1024]{1,0:T(8,128)(2,1)} %copy-done.16, bf16[256,1024]{1,0:T(8,128)(2,1)} %copy-done.13, ...), custom_call_target="tpu_custom_call" | custom-call | tf_op jit(solution)/shard_map/mixer_grads/pallas_call | solution.py:779
  287.5 10.8 %mixer_d_in.1 = (bf16[4,256,1024]{2,1,0:T(8,128)(2,1)}, bf16[4,256,1024]{2,1,0:T(8,128)(2,1)}) custom-call(bf16[8,256,896]{2,1,0:T(8,128)(2,1)} %bitcast.107, bf16[1024,1024]{1,0:T(8,128)(2,1)} %all-gather.7.cloned.1.call-done.refs_9_.refs_8_.refs_18_.weight_ref, bf16[1024,128]{1,0:T(8,128)(2,1)} %pad.9.refs_10_.refs_19_.beta_ref), custom_call_target="tpu_custom_call" | custom-call | tf_op jit(solution)/shard_map/mixer_d_in/pallas_call | solution.py:815
  298.5 4.1 %collective-permute-done.45 = bf16[4,256,1024]{2,1,0:T(8,128)(2,1)S(1)} collective-permute-done((bf16[4,256,1024]{2,1,0:T(8,128)(2,1)}, bf16[4,256,1024]{2,1,0:T(8,128)(2,1)S(1)}, u32[]{:S(2)}, u32[]{:S(2)}) %collective-permute-start.45) | collective-permute-done | bytes 2097184 | tf_op jit(solution)/shard_map/ppermute | solution.py:888
  302.6 3.8 fusion.13
  309.9 7.5 %join_hidden.1 = (f32[256,2816]{1,0:T(8,128)}, f32[256,2816]{1,0:T(8,128)}, f32[256,2816]{1,0:T(8,128)}) custom-call(bf16[8,256,1152]{2,1,0:T(8,128)(2,1)} %bitcast.115), custom_call_target="tpu_custom_call" | custom-call | tf_op jit(solution)/shard_map/join_hidden/pallas_call | solution.py:870
  317.4 5.0 %collective-permute-done.48 = bf16[256,1024]{1,0:T(8,128)(2,1)} collective-permute-done((bf16[256,1024]{1,0:T(8,128)(2,1)}, bf16[256,1024]{1,0:T(8,128)(2,1)}, u32[]{:S(2)}, u32[]{:S(2)}) %collective-permute-start.48) | collective-permute-done | bytes 524320 | tf_op jit(solution)/shard_map/ppermute | solution.py:888
  322.4 10.5 %collective-permute-done.47 = bf16[256,1024]{1,0:T(8,128)(2,1)} collective-permute-done((bf16[256,1024]{1,0:T(8,128)(2,1)}, bf16[256,1024]{1,0:T(8,128)(2,1)}, u32[]{:S(2)}, u32[]{:S(2)}) %collective-permute-start.47) | collective-permute-done | bytes 524320 | tf_op jit(solution)/shard_map/ppermute | solution.py:888
  336.4 3.2 collective-permute-done.49
  341.3 3.2 collective-permute-done.50
  348.4 3.5 collective-permute-done.52
  353.4 4.2 %multiply_add_fusion = (f32[256,1024]{1,0:T(8,128)}, bf16[256,1024]{1,0:T(8,128)(2,1)}) fusion(f32[256]{0:T(256)S(1)} %broadcast_multiply_fusion, f32[256]{0:T(256)S(1)} %rsqrt_bitcast_fusion, bf16[2,128,1024]{2,1,0:T(8,128)(2,1)S(1)} %copy-done.4, f32[1024]{0:T(1024)S(1)} %copy-done.51, bf16[256,1024]{1,0:T(8,128)(2,1)} %collective-permute-done.48, ...), kind=kLoop, calls=%fused_computation.9 | loop fusion | flops 8126464 | bytes 9973760 | tf_op jit(solution)/shard_map/add | solution.py:1128
  360.8 11.7 %all-gather.13.cloned.1.call-done = bf16[2048,1024]{1,0:T(8,128)(2,1)} async-done(((bf16[256,1024]{1,0:T(8,128)(2,1)}), bf16[2048,1024]{1,0:T(8,128)(2,1)}) %all-gather.13.cloned.1.call-update) | async-done | bytes 4194320 | tf_op jit(solution)/shard_map/all_gather | solution.py:997
  372.5 7.2 %join_heads.1 = (f32[256,1024]{1,0:T(8,128)}, f32[256,1024]{1,0:T(8,128)}, f32[256,2048]{1,0:T(8,128)}, f32[256,2048]{1,0:T(8,128)}, f32[256,2048]{1,0:T(8,128)}) custom-call(bf16[8,256,1024]{2,1,0:T(8,128)(2,1)} %bitcast.118), custom_call_target="tpu_custom_call" | custom-call | tf_op jit(solution)/shard_map/join_heads/pallas_call | solution.py:845
  (289 shorter events, 86.8 us)
Async XLA Ops:
  7.3 54.3 %all-gather.7.cloned.1.call-start = ((), (), s32[]{:S(2)}) async-start(), calls=%async_computation.4 | async-start | bytes 2621440 | tf_op jit(solution)/shard_map/all_gather | solution.py:975
  14.2 28.1 %collective-permute-start.2 = (bf16[256,1024]{1,0:T(8,128)(2,1)S(1)}, bf16[256,1024]{1,0:T(8,128)(2,1)S(1)}, u32[]{:S(2)}, u32[]{:S(2)}) collective-permute-start(bf16[256,1024]{1,0:T(8,128)(2,1)S(1)} %multiply_convert_fusion.refs_0_), channel_id=1, source_target_pairs={{0,24},{4,28},{8,16},{12,20},{16,8},{20,12},{24,0},{28,4},{1,25},{... | collective-permute-start | bytes 1572872 | tf_op jit(solution)/shard_map/ppermute | solution.py:888
  18.2 24.2 %collective-permute-start.1 = (bf16[256,1024]{1,0:T(8,128)(2,1)S(1)}, bf16[256,1024]{1,0:T(8,128)(2,1)S(1)}, u32[]{:S(2)}, u32[]{:S(2)}) collective-permute-start(bf16[256,1024]{1,0:T(8,128)(2,1)S(1)} %multiply_convert_fusion.refs_0_), channel_id=1, source_target_pairs={{0,16},{4,20},{8,24},{12,28},{16,0},{20,4},{24,8},{28,12},{1,17},{... | collective-permute-start | bytes 1572872 | tf_op jit(solution)/shard_map/ppermute | solution.py:888
  18.7 23.7 %collective-permute-start = (bf16[256,1024]{1,0:T(8,128)(2,1)S(1)}, bf16[256,1024]{1,0:T(8,128)(2,1)S(1)}, u32[]{:S(2)}, u32[]{:S(2)}) collective-permute-start(bf16[256,1024]{1,0:T(8,128)(2,1)S(1)} %multiply_convert_fusion.refs_0_), channel_id=1, source_target_pairs={{0,8},{4,12},{8,0},{12,4},{16,24},{20,28},{24,16},{28,20},{1,9},{5... | collective-permute-start | bytes 1572872 | tf_op jit(solution)/shard_map/ppermute | solution.py:888
  19.4 22.3 %all-to-all-start = ((f32[8,1,256]{2,1,0:T(1,128)}), f32[8,1,256]{2,1,0:T(1,128)S(1)}, u32[]{:S(2)}, u32[]{:S(2)}) async-start(f32[8,1,256]{2,1,0:T(1,128)} %all_to_all.11), calls=%async_computation | async-start | bytes 16384 | tf_op jit(solution)/shard_map/all_to_all | solution.py:1023
  23.5 116.1 %all-gather.9.cloned.1.call-start = ((), (), s32[]{:S(2)}) async-start(), calls=%async_computation.5 | async-start | bytes 2949120 | tf_op jit(solution)/shard_map/all_gather | solution.py:975
  45.0 14.9 %collective-permute-start.7 = (bf16[256,1024]{1,0:T(8,128)(2,1)S(1)}, bf16[256,1024]{1,0:T(8,128)(2,1)}, u32[]{:S(2)}, u32[]{:S(2)}) collective-permute-start(bf16[256,1024]{1,0:T(8,128)(2,1)S(1)} %bitcast.112), channel_id=1, source_target_pairs={{0,8},{4,12},{8,0},{12,4},{16,24},{20,28},{24,16},{28,20},{1,9},{5... | collective-permute-start | bytes 1572872 | tf_op jit(solution)/shard_map/ppermute | solution.py:888
  46.5 50.6 %collective-permute-start.9 = (bf16[256,1024]{1,0:T(8,128)(2,1)S(1)}, bf16[256,1024]{1,0:T(8,128)(2,1)}, u32[]{:S(2)}, u32[]{:S(2)}) collective-permute-start(bf16[256,1024]{1,0:T(8,128)(2,1)S(1)} %bitcast.113), channel_id=1, source_target_pairs={{0,24},{4,28},{8,16},{12,20},{16,8},{20,12},{24,0},{28,4},{1,25},{... | collective-permute-start | bytes 1572872 | tf_op jit(solution)/shard_map/ppermute | solution.py:888
  62.6 34.5 %collective-permute-start.12 = (bf16[1024,256]{1,0:T(8,128)(2,1)S(1)}, bf16[1024,256]{1,0:T(8,128)(2,1)}, u32[]{:S(2)}, u32[]{:S(2)}) collective-permute-start(bf16[1024,256]{1,0:T(8,128)(2,1)S(1)} %slice.123.refs_0_), channel_id=1, source_target_pairs={{0,24},{4,28},{8,16},{12,20},{16,8},{20,12},{24,0},{28,4},{1,25},{... | collective-permute-start | bytes 1572872 | tf_op jit(solution)/shard_map/ppermute | solution.py:888
  65.0 32.1 %collective-permute-start.11 = (bf16[1024,256]{1,0:T(8,128)(2,1)S(1)}, bf16[1024,256]{1,0:T(8,128)(2,1)S(1)}, u32[]{:S(2)}, u32[]{:S(2)}) collective-permute-start(bf16[1024,256]{1,0:T(8,128)(2,1)S(1)} %slice.123.refs_0_), channel_id=1, source_target_pairs={{0,16},{4,20},{8,24},{12,28},{16,0},{20,4},{24,8},{28,12},{1,17},{... | collective-permute-start | bytes 1572872 | tf_op jit(solution)/shard_map/ppermute | solution.py:888
  65.6 31.5 %collective-permute-start.10 = (bf16[1024,256]{1,0:T(8,128)(2,1)S(1)}, bf16[1024,256]{1,0:T(8,128)(2,1)}, u32[]{:S(2)}, u32[]{:S(2)}) collective-permute-start(bf16[1024,256]{1,0:T(8,128)(2,1)S(1)} %slice.123.refs_0_), channel_id=1, source_target_pairs={{0,8},{4,12},{8,0},{12,4},{16,24},{20,28},{24,16},{28,20},{1,9},{5... | collective-permute-start | bytes 1572872 | tf_op jit(solution)/shard_map/ppermute | solution.py:888
  97.9 19.1 %all-to-all-start.1 = ((bf16[8,256,256]{2,1,0:T(8,128)(2,1)}), bf16[8,256,256]{2,1,0:T(8,128)(2,1)S(1)}, u32[]{:S(2)}, u32[]{:S(2)}) async-start(bf16[8,256,256]{2,1,0:T(8,128)(2,1)} %bitcast.116), calls=%async_computation.1 | async-start | bytes 2097152 | tf_op jit(solution)/shard_map/all_to_all | solution.py:1055
  101.6 131.8 %reduce-scatter.3.cloned.1.call-start = ((), (), s32[]{:S(2)}) async-start(), calls=%async_computation.6 | async-start | bytes 2949120 | tf_op jit(solution)/shard_map/reduce_scatter | solution.py:994
  124.4 15.3 %collective-permute-start.21 = (bf16[256,1024]{1,0:T(8,128)(2,1)}, bf16[256,1024]{1,0:T(8,128)(2,1)S(1)}, u32[]{:S(2)}, u32[]{:S(2)}) collective-permute-start(bf16[256,1024]{1,0:T(8,128)(2,1)} %collective-permute-done.9.refs_6_.refs_10_), channel_id=1, source_target_pairs={{0,4},{4,0},{8,12},{12,8},{16,20},{20,16},{24,28},{28,24},{1,5},{5... | collective-permute-start | bytes 1572872 | tf_op jit(solution)/shard_map/ppermute | solution.py:888
  124.9 14.8 %collective-permute-start.17 = (bf16[256,1024]{1,0:T(8,128)(2,1)}, bf16[256,1024]{1,0:T(8,128)(2,1)S(1)}, u32[]{:S(2)}, u32[]{:S(2)}) collective-permute-start(bf16[256,1024]{1,0:T(8,128)(2,1)} %get-tuple-element.163.refs_0_), channel_id=1, source_target_pairs={{0,4},{4,0},{8,12},{12,8},{16,20},{20,16},{24,28},{28,24},{1,5},{5... | collective-permute-start | bytes 1572872 | tf_op jit(solution)/shard_map/ppermute | solution.py:888
  136.4 14.8 %collective-permute-start.23 = (bf16[256,1024]{1,0:T(8,128)(2,1)}, bf16[256,1024]{1,0:T(8,128)(2,1)}, u32[]{:S(2)}, u32[]{:S(2)}) collective-permute-start(bf16[256,1024]{1,0:T(8,128)(2,1)} %get-tuple-element.163.refs_0_), channel_id=1, source_target_pairs={{0,16},{4,20},{8,24},{12,28},{16,0},{20,4},{24,8},{28,12},{1,17},{... | collective-permute-start | bytes 1572872 | tf_op jit(solution)/shard_map/ppermute | solution.py:888
  138.1 14.3 %collective-permute-start.22 = (bf16[256,1024]{1,0:T(8,128)(2,1)}, bf16[256,1024]{1,0:T(8,128)(2,1)S(1)}, u32[]{:S(2)}, u32[]{:S(2)}) collective-permute-start(bf16[256,1024]{1,0:T(8,128)(2,1)} %get-tuple-element.163.refs_0_), channel_id=1, source_target_pairs={{0,8},{4,12},{8,0},{12,4},{16,24},{20,28},{24,16},{28,20},{1,9},{5... | collective-permute-start | bytes 1572872 | tf_op jit(solution)/shard_map/ppermute | solution.py:888
  159.1 15.1 %collective-permute-start.29 = (bf16[256,1024]{1,0:T(8,128)(2,1)}, bf16[256,1024]{1,0:T(8,128)(2,1)S(1)}, u32[]{:S(2)}, u32[]{:S(2)}) collective-permute-start(bf16[256,1024]{1,0:T(8,128)(2,1)} %fusion.5), channel_id=1, source_target_pairs={{0,24},{4,28},{8,16},{12,20},{16,8},{20,12},{24,0},{28,4},{1,25},{... | collective-permute-start | bytes 1572872 | tf_op jit(solution)/shard_map/ppermute | solution.py:888
  185.6 101.5 %all-gather.11.cloned.1.call-start = ((), (), s32[]{:S(2)}) async-start(), calls=%async_computation.8 | async-start | bytes 5308416 | tf_op jit(solution)/shard_map/all_gather | solution.py:997
  187.5 14.4 %collective-permute-start.32 = (bf16[256,1024]{1,0:T(8,128)(2,1)S(1)}, bf16[256,1024]{1,0:T(8,128)(2,1)S(1)}, u32[]{:S(2)}, u32[]{:S(2)}) collective-permute-start(bf16[256,1024]{1,0:T(8,128)(2,1)S(1)} %get-tuple-element.261), channel_id=1, source_target_pairs={{0,16},{4,20},{8,24},{12,28},{16,0},{20,4},{24,8},{28,12},{1,17},{... | collective-permute-start | bytes 1572872 | tf_op jit(solution)/shard_map/ppermute | solution.py:888
  204.5 15.9 %collective-permute-start.40 = (bf16[256,1024]{1,0:T(8,128)(2,1)S(1)}, bf16[256,1024]{1,0:T(8,128)(2,1)S(1)}, u32[]{:S(2)}, u32[]{:S(2)}) collective-permute-start(bf16[256,1024]{1,0:T(8,128)(2,1)S(1)} %fusion.15.refs_0_.refs_8_), channel_id=1, source_target_pairs={{0,24},{4,28},{8,16},{12,20},{16,8},{20,12},{24,0},{28,4},{1,25},{... | collective-permute-start | bytes 1572872 | tf_op jit(solution)/shard_map/ppermute | solution.py:888
  206.1 24.0 %collective-permute-start.38 = (bf16[256,1024]{1,0:T(8,128)(2,1)S(1)}, bf16[256,1024]{1,0:T(8,128)(2,1)S(1)}, u32[]{:S(2)}, u32[]{:S(2)}) collective-permute-start(bf16[256,1024]{1,0:T(8,128)(2,1)S(1)} %fusion.15.refs_0_.refs_8_), channel_id=1, source_target_pairs={{0,16},{4,20},{8,24},{12,28},{16,0},{20,4},{24,8},{28,12},{1,17},{... | collective-permute-start | bytes 1572872 | tf_op jit(solution)/shard_map/ppermute | solution.py:888
  207.7 22.3 %collective-permute-start.36 = (bf16[256,1024]{1,0:T(8,128)(2,1)S(1)}, bf16[256,1024]{1,0:T(8,128)(2,1)S(1)}, u32[]{:S(2)}, u32[]{:S(2)}) collective-permute-start(bf16[256,1024]{1,0:T(8,128)(2,1)S(1)} %fusion.15.refs_0_.refs_8_), channel_id=1, source_target_pairs={{0,8},{4,12},{8,0},{12,4},{16,24},{20,28},{24,16},{28,20},{1,9},{5... | collective-permute-start | bytes 1572872 | tf_op jit(solution)/shard_map/ppermute | solution.py:888
  208.1 22.5 %collective-permute-start.35 = (bf16[256,1024]{1,0:T(8,128)(2,1)S(1)}, bf16[256,1024]{1,0:T(8,128)(2,1)S(1)}, u32[]{:S(2)}, u32[]{:S(2)}) collective-permute-start(bf16[256,1024]{1,0:T(8,128)(2,1)S(1)} %fusion.15.refs_0_.refs_8_), channel_id=1, source_target_pairs={{0,4},{4,0},{8,12},{12,8},{16,20},{20,16},{24,28},{28,24},{1,5},{5... | collective-permute-start | bytes 1572872 | tf_op jit(solution)/shard_map/ppermute | solution.py:888
  233.4 100.3 %reduce-scatter.5.cloned.1.call-start = ((), (), s32[]{:S(2)}) async-start(), calls=%async_computation.7 | async-start | bytes 2621440 | tf_op jit(solution)/shard_map/reduce_scatter | solution.py:994
  233.7 51.3 %collective-permute-start.42 = (bf16[256,1024]{1,0:T(8,128)(2,1)}, bf16[256,1024]{1,0:T(8,128)(2,1)}, u32[]{:S(2)}, u32[]{:S(2)}) collective-permute-start(bf16[256,1024]{1,0:T(8,128)(2,1)} %get-tuple-element.220), channel_id=1, source_target_pairs={{0,8},{4,12},{8,0},{12,4},{16,24},{20,28},{24,16},{28,20},{1,9},{5... | collective-permute-start | bytes 1572872 | tf_op jit(solution)/shard_map/ppermute | solution.py:888
  235.3 49.7 %collective-permute-start.43 = (bf16[256,1024]{1,0:T(8,128)(2,1)}, bf16[256,1024]{1,0:T(8,128)(2,1)}, u32[]{:S(2)}, u32[]{:S(2)}) collective-permute-start(bf16[256,1024]{1,0:T(8,128)(2,1)} %get-tuple-element.221), channel_id=1, source_target_pairs={{0,16},{4,20},{8,24},{12,28},{16,0},{20,4},{24,8},{28,12},{1,17},{... | collective-permute-start | bytes 1572872 | tf_op jit(solution)/shard_map/ppermute | solution.py:888
  236.7 48.3 %collective-permute-start.44 = (bf16[256,1024]{1,0:T(8,128)(2,1)}, bf16[256,1024]{1,0:T(8,128)(2,1)}, u32[]{:S(2)}, u32[]{:S(2)}) collective-permute-start(bf16[256,1024]{1,0:T(8,128)(2,1)} %get-tuple-element.222), channel_id=1, source_target_pairs={{0,24},{4,28},{8,16},{12,20},{16,8},{20,12},{24,0},{28,4},{1,25},{... | collective-permute-start | bytes 1572872 | tf_op jit(solution)/shard_map/ppermute | solution.py:888
  287.1 85.4 %all-gather.13.cloned.1.call-start = ((), (), s32[]{:S(2)}) async-start(), calls=%async_computation.9 | async-start | bytes 4718592 | tf_op jit(solution)/shard_map/all_gather | solution.py:997
  306.4 16.0 %collective-permute-start.48 = (bf16[256,1024]{1,0:T(8,128)(2,1)}, bf16[256,1024]{1,0:T(8,128)(2,1)}, u32[]{:S(2)}, u32[]{:S(2)}) collective-permute-start(bf16[256,1024]{1,0:T(8,128)(2,1)} %get-tuple-element.254), channel_id=1, source_target_pairs={{0,24},{4,28},{8,16},{12,20},{16,8},{20,12},{24,0},{28,4},{1,25},{... | collective-permute-start | bytes 1572872 | tf_op jit(solution)/shard_map/ppermute | solution.py:888
  307.8 25.1 %collective-permute-start.47 = (bf16[256,1024]{1,0:T(8,128)(2,1)}, bf16[256,1024]{1,0:T(8,128)(2,1)}, u32[]{:S(2)}, u32[]{:S(2)}) collective-permute-start(bf16[256,1024]{1,0:T(8,128)(2,1)} %get-tuple-element.255), channel_id=1, source_target_pairs={{0,16},{4,20},{8,24},{12,28},{16,0},{20,4},{24,8},{28,12},{1,17},{... | collective-permute-start | bytes 1572872 | tf_op jit(solution)/shard_map/ppermute | solution.py:888
  309.3 23.6 %collective-permute-start.46 = (bf16[256,1024]{1,0:T(8,128)(2,1)S(1)}, bf16[256,1024]{1,0:T(8,128)(2,1)}, u32[]{:S(2)}, u32[]{:S(2)}) collective-permute-start(bf16[256,1024]{1,0:T(8,128)(2,1)S(1)} %get-tuple-element.256), channel_id=1, source_target_pairs={{0,8},{4,12},{8,0},{12,4},{16,24},{20,28},{24,16},{28,20},{1,9},{5... | collective-permute-start | bytes 1572872 | tf_op jit(solution)/shard_map/ppermute | solution.py:888
  (88 other events, 807.6 us)
Sparse Core Ops, SparseCore 0:
  12.8 48.6 all-gather.6
  63.7 49.1 all-gather.8
  185.7 47.6 reduce-scatter.2
  235.2 51.9 all-gather.10
  289.8 43.8 reduce-scatter.4
  335.7 36.7 all-gather.12

commit v6 on v5

--- a/solution.py
+++ b/solution.py
@@ -509,6 +509,35 @@
     return pltpu.CompilerParams(vmem_limit_bytes=VMEM_LIMIT)
 
 
+def own_columns_kernel(head_ref, *refs):
+    out_ref = refs[-1]
+    start = 0
+    for ref in refs[:-1]:
+        width = ref.shape[1]
+        out_ref[:, start : start + width] = ref[...]
+        start += width
+
+
+def own_columns_rule(head, weights, widths):
+    rows = weights[0].shape[0]
+    total = sum(widths)
+    return pl.pallas_call(
+        own_columns_kernel,
+        name="own_columns",
+        grid_spec=pltpu.PrefetchScalarGridSpec(
+            num_scalar_prefetch=1,
+            grid=(1,),
+            in_specs=[
+                pl.BlockSpec((rows, width), lambda step, head_ref: (0, head_ref[0]))
+                for width in widths
+            ],
+            out_specs=pl.BlockSpec((rows, total), lambda step, head_ref: (0, 0)),
+        ),
+        out_shape=shaped((rows, total), bf16),
+        compiler_params=kernel_params(),
+    )(head, *weights)
+
+
 def anywhere(count):
     return [pl.BlockSpec(memory_space=pltpu.HBM)] * count
 
@@ -975,15 +1004,8 @@
         return lax.all_gather(local, "wt", axis=0, tiled=True)
 
     mixer_w = gather_weight(
-        jnp.concatenate(
-            [
-                own_columns(w_query, DK),
-                own_columns(w_key, DK),
-                own_columns(w_value, DV),
-                own_columns(w_gate_out, DV),
-                own_columns(w_out, DV),
-            ],
-            axis=1,
+        own_columns_rule(
+            head_arg, (w_query, w_key, w_value, w_gate_out, w_out), (DK, DK, DV, DV, DV)
         )
     )
     ffn_w_own = jnp.concatenate(
@@ -1064,9 +1086,10 @@
         mid_first, up_first, ffn_w
     )
     d_odd, near, far = lax.optimization_barrier((d_odd, near, far))
-    own_sum, across_sum = pair_sums(d_even, swapped(d_odd, "seq", 1))
+    own_pair = (d_even, swapped(d_odd, "seq", 1))
+    across_sum = sum(each[1].astype(f32) for each in own_pair).astype(bf16)
     mid_last, across_sum = lax.optimization_barrier((with_siblings([near, far]), across_sum))
-    across_sum = swapped(across_sum[0], "seq", 6)
+    across_sum = swapped(across_sum, "seq", 6)
     both_last, hidden_last, d_even, d_odd, even_last, odd_last = ffn_rule(
         mid_last, up_last, ffn_w
     )
@@ -1086,7 +1109,10 @@
     ffn_sums = [
         (even_last[i].astype(f32) + ffn_handed[i].astype(f32)).astype(bf16) for i in (0, 1)
     ] + ffn_across
-    received, ffn_own, ffn_sums = lax.optimization_barrier((received, ffn_own, ffn_sums))
+    received, ffn_own, ffn_sums, own_pair = lax.optimization_barrier(
+        (received, ffn_own, ffn_sums, own_pair)
+    )
+    own_sum = sum(each[0].astype(f32) for each in own_pair)
     d_normed_mid = total_of(own_sum, received)
     d_from_mid, grad_mid = rms_back(residual, norm_mid, d_normed_mid)
     d_residual = upstream_own.astype(f32) + d_from_mid

time: 388 us -> 384 us (0.990)
  local copies, waits for them, and re-layouts: 23.7 us -> 18.3 us
    unnamed x132 -> x126, local copies, waits for them, and re-layouts: 14.2 us -> 9.8 us
  transfers between devices with their start and end apart: 62 -> 62, of which waited for: 28 -> 27; matrix products, arithmetic and copies ran while one was open for 8% -> 8% of each run, Pallas kernels for 34% -> 35%
where the time goes in v6:
time: 384 us; the launch traced here: 383 us
  Pallas kernels  142 us (37%)
  waiting for transfers between devices  135 us (35%)
  starting transfers between devices  51.9 us (14%)
  other arithmetic  21.1 us (5%)
  local copies, waits for them, and re-layouts  18.3 us (5%)
  between operations  14.9 us (4%)
    ppermute x54, waiting for transfers between devices, swapped(): lax.ppermute(array, axis, [(i, i ^ bits) for i in range(lax.axis_size(axi...  93.2 us
    ppermute x54, starting transfers between devices, swapped(): lax.ppermute(array, axis, [(i, i ^ bits) for i in range(lax.axis_size(axi...  43.3 us
    pallas_call x1, Pallas kernels, backward_rule(): pl.pallas_call(backward_kernel, name='mixer_backward', out_shape=(shaped(...  36 us
    pallas_call x1, Pallas kernels, forward_rule(): pl.pallas_call(forward_kernel, name='mixer_forward', out_shape=[shaped(*i...  29.5 us
    pallas_call x2, Pallas kernels, ffn_rule(): pl.pallas_call(ffn_kernel, name='feed_forward', grid=(PART,), in_specs=an...  21.3 us
    all_to_all x1, waiting for transfers between devices, shards(): lax.all_to_all(decay_rows, 'seq', 0, 0, axis_index_groups=groups, tiled=T...  14.2 us
    all_gather x2, waiting for transfers between devices, spread_grads(): spread = lax.all_gather(summed, 'seq')  13.6 us
    pallas_call x1, Pallas kernels, mixer_grads_rule(): pl.pallas_call(mixer_grads_kernel, name='mixer_grads', grid=(model // GRA...  11.1 us
  transfers between devices with their start and end apart: 62, of which 27 were waited for; matrix products, arithmetic and copies ran while one was open for 8% of the time, Pallas kernels for 35%

profile of v6, /device:TPU:0, one launch (start us, length us, event | category | flops | bytes accessed | tf_op | source)
XLA Modules:
  0.0 383.2 jit_solution(17205398293592812903)
XLA Ops:
  9.8 4.0 %collective-permute-start.2 = (bf16[256,1024]{1,0:T(8,128)(2,1)S(1)}, bf16[256,1024]{1,0:T(8,128)(2,1)S(1)}, u32[]{:S(2)}, u32[]{:S(2)}) collective-permute-start(bf16[256,1024]{1,0:T(8,128)(2,1)S(1)} %multiply_convert_fusion.refs_0_), channel_id=1, source_target_pairs={{0,24},{4,28},{8,16},{12,20},{16,8},{20,12},{24,0},{28,4},{1,25},{... | collective-permute-start | bytes 1572872 | tf_op jit(solution)/shard_map/ppermute | solution.py:917
  15.0 4.1 %all-to-all-start = ((f32[8,1,256]{2,1,0:T(1,128)}), f32[8,1,256]{2,1,0:T(1,128)S(1)}, u32[]{:S(2)}, u32[]{:S(2)}) async-start(f32[8,1,256]{2,1,0:T(1,128)} %all_to_all.11), calls=%async_computation | async-start | bytes 16384 | tf_op jit(solution)/shard_map/all_to_all | solution.py:1045
  23.1 14.2 %all-to-all-done = f32[8,1,256]{2,1,0:T(1,128)S(1)} async-done(((f32[8,1,256]{2,1,0:T(1,128)}), f32[8,1,256]{2,1,0:T(1,128)S(1)}, u32[]{:S(2)}, u32[]{:S(2)}) %all-to-all-start) | async-done | bytes 8224 | tf_op jit(solution)/shard_map/all_to_all | solution.py:1045
  43.0 10.1 %collective-permute-done.8.refs_6_.refs_14_ = bf16[256,1024]{1,0:T(8,128)(2,1)S(1)} collective-permute-done((bf16[256,1024]{1,0:T(8,128)(2,1)S(1)}, bf16[256,1024]{1,0:T(8,128)(2,1)S(1)}, u32[]{:S(2)}, u32[]{:S(2)}) %collective-permute-start.8) | collective-permute-done | bytes 524320 | tf_op jit(solution)/shard_map/ppermute | solution.py:917
  55.5 3.4 all-gather.7.cloned.1.call-done.refs_9_.refs_8_.refs_18_.weight_ref
  64.9 29.5 %mixer_forward.1 = (bf16[8,2,128,256]{3,2,1,0:T(8,128)(2,1)}, bf16[8,2,128,512]{3,2,1,0:T(8,128)(2,1)}, f32[8,2,128,384]{3,2,1,0:T(8,128)}, f32[8,2,128,256]{3,2...) custom-call(s32[1]{0:T(128)} %bitcast.head_ref, ...), custom_call_target="tpu_custom_call" | custom-call | tf_op jit(solution)/shard_map/mixer_forward/pallas_call | solution.py:560
  95.3 3.7 all-to-all-start.1
  104.4 9.9 %all-to-all-done.1.refs_8_ = bf16[8,256,256]{2,1,0:T(8,128)(2,1)S(1)} async-done(((bf16[8,256,256]{2,1,0:T(8,128)(2,1)}), bf16[8,256,256]{2,1,0:T(8,128)(2,1)S(1)}, u32[]{:S(2)}, u32[]{:S(2)}) %all-to-all-start.1) | async-done | bytes 1048608 | tf_op jit(solution)/shard_map/all_to_all | solution.py:1077
  115.3 5.7 %out_projection.1 = (f32[256,1024]{1,0:T(8,128)}, bf16[256,1024]{1,0:T(8,128)(2,1)}) custom-call(s32[1]{0:T(128)} %bitcast.head_ref, bf16[1024,256]{1,0:T(8,128)(2,1)} %copy-done.25, bf16[1024,256]{1,0:T(8,128)(2,1)} %copy-done.47, bf16[1024,256]{1,0:T(8,128)(2,1)} %collective-permute-done.10.refs_2_, bf16[1024,256]{1,0:T(8,128)(2,1)} %copy-done.48, ...), custom_call_target="tpu_custom_call" | custom-call | tf_op jit(solution)/shard_map/out_projection/pallas_call | solution.py:659
  122.2 11.6 %collective-permute-done.18.refs_2_ = bf16[256,1024]{1,0:T(8,128)(2,1)S(1)} collective-permute-done((bf16[256,1024]{1,0:T(8,128)(2,1)}, bf16[256,1024]{1,0:T(8,128)(2,1)S(1)}, u32[]{:S(2)}, u32[]{:S(2)}) %collective-permute-start.18) | collective-permute-done | bytes 524320 | tf_op jit(solution)/shard_map/ppermute | solution.py:917
  138.0 10.6 %feed_forward.2 = (bf16[4,256,768]{2,1,0:T(8,128)(2,1)}, bf16[4,256,384]{2,1,0:T(8,128)(2,1)}, bf16[2,256,1024]{2,1,0:T(8,128)(2,1)}, bf16[2,256,1024]{2,1,0:T(8...) custom-call(bf16[256,1024]{1,0:T(8,128)(2,1)} %get-tuple-element.165.refs_0_, ...), custom_call_target="tpu_custom_call" | custom-call | tf_op jit(solution)/shard_map/feed_forward/pallas_call | solution.py:734
  150.7 3.3 collective-permute-done.26
  156.5 2.7 collective-permute-start.29
  160.8 10.7 %feed_forward.3 = (bf16[4,256,768]{2,1,0:T(8,128)(2,1)}, bf16[4,256,384]{2,1,0:T(8,128)(2,1)}, bf16[2,256,1024]{2,1,0:T(8,128)(2,1)}, bf16[2,256,1024]{2,1,0:T(8...) custom-call(bf16[256,1024]{1,0:T(8,128)(2,1)} %copy-done.33, bf16[256,1024]{1,0:T(8,128)(2,1)} %copy-done.34, ...), custom_call_target="tpu_custom_call" | custom-call | tf_op jit(solution)/shard_map/feed_forward/pallas_call | solution.py:734
  172.4 10.5 %feed_forward_grads.1 = bf16[1024,1152]{1,0:T(8,128)(2,1)} custom-call(bf16[256,1024]{1,0:T(8,128)(2,1)} %get-tuple-element.165.refs_0_, bf16[256,1024]{1,0:T(8,128)(2,1)} %copy-done.32, bf16[256,1024]{1,0:T(8,128)(2,1)} %copy-done.29, bf16[256,1024]{1,0:T(8,128)(2,1)} %collective-permute-done.19.refs_3_, bf16[256,1024]{1,0:T(8,128)(2,1)} %copy-done.33, ...), custom_call_target="tpu_custom_call" | custom-call | tf_op jit(solution)/shard_map/feed_forward_grads/pallas_call | solution.py:774
  191.1 8.1 %collective-permute-done.32 = bf16[256,1024]{1,0:T(8,128)(2,1)S(1)} collective-permute-done((bf16[256,1024]{1,0:T(8,128)(2,1)S(1)}, bf16[256,1024]{1,0:T(8,128)(2,1)S(1)}, u32[]{:S(2)}, u32[]{:S(2)}) %collective-permute-start.32) | collective-permute-done | bytes 524320 | tf_op jit(solution)/shard_map/ppermute | solution.py:917
  205.4 12.3 %collective-permute-done.40.refs_6_.refs_14_ = bf16[256,1024]{1,0:T(8,128)(2,1)S(1)} collective-permute-done((bf16[256,1024]{1,0:T(8,128)(2,1)S(1)}, bf16[256,1024]{1,0:T(8,128)(2,1)S(1)}, u32[]{:S(2)}, u32[]{:S(2)}) %collective-permute-start.40) | collective-permute-done | bytes 524320 | tf_op jit(solution)/shard_map/ppermute | solution.py:917
  217.7 9.7 %collective-permute-done.38.refs_4_.refs_12_ = bf16[256,1024]{1,0:T(8,128)(2,1)S(1)} collective-permute-done((bf16[256,1024]{1,0:T(8,128)(2,1)S(1)}, bf16[256,1024]{1,0:T(8,128)(2,1)S(1)}, u32[]{:S(2)}, u32[]{:S(2)}) %collective-permute-start.38) | collective-permute-done | bytes 524320 | tf_op jit(solution)/shard_map/ppermute | solution.py:917
  234.6 36.0 %mixer_backward.1 = (bf16[8,2,128,896]{3,2,1,0:T(8,128)(2,1)}, f32[8,512]{1,0:T(8,128)}, f32[1,256]{1,0:T(1,128)}, f32[2,128,256]{2,1,0:T(8,128)}, f32[2,8,512]{2,1,0:T(8,128)}) custom-call(s32[1]{0:T(128)} %bitcast.head_ref, bf16[256,1024]{1,0:T(8,128)(2,1)} %copy-done.8, bf16[256,1024]{1,0:T(8,128)(2,1)} %copy-done.22, bf16[256,1024]{1,0:T(8,128)(2,1)} %copy-done.21, ...), custom_call_target="tpu_custom_call" | custom-call | tf_op jit(solution)/shard_map/mixer_backward/pallas_call | solution.py:591
  270.6 11.1 %mixer_grads.1 = (bf16[1024,1024]{1,0:T(8,128)(2,1)}, f32[1024,128]{1,0:T(8,128)}) custom-call(s32[1]{0:T(128)} %bitcast.head_ref, bf16[256,1024]{1,0:T(8,128)(2,1)} %copy-done.7, bf16[256,1024]{1,0:T(8,128)(2,1)} %copy-done.15, bf16[256,1024]{1,0:T(8,128)(2,1)} %copy-done.14, bf16[256,1024]{1,0:T(8,128)(2,1)} %copy-done.16, bf16[256,1024]{1,0:T(8,128)(2,1)} %copy-done.13, ...), custom_call_target="tpu_custom_call" | custom-call | tf_op jit(solution)/shard_map/mixer_grads/pallas_call | solution.py:808
  284.0 10.8 %mixer_d_in.1 = (bf16[4,256,1024]{2,1,0:T(8,128)(2,1)}, bf16[4,256,1024]{2,1,0:T(8,128)(2,1)}) custom-call(bf16[8,256,896]{2,1,0:T(8,128)(2,1)} %bitcast.107, bf16[1024,1024]{1,0:T(8,128)(2,1)} %all-gather.7.cloned.1.call-done.refs_9_.refs_8_.refs_18_.weight_ref, bf16[1024,128]{1,0:T(8,128)(2,1)} %pad.9.refs_10_.refs_19_.beta_ref), custom_call_target="tpu_custom_call" | custom-call | tf_op jit(solution)/shard_map/mixer_d_in/pallas_call | solution.py:844
  295.1 4.1 %collective-permute-done.45 = bf16[4,256,1024]{2,1,0:T(8,128)(2,1)S(1)} collective-permute-done((bf16[4,256,1024]{2,1,0:T(8,128)(2,1)}, bf16[4,256,1024]{2,1,0:T(8,128)(2,1)S(1)}, u32[]{:S(2)}, u32[]{:S(2)}) %collective-permute-start.45) | collective-permute-done | bytes 2097184 | tf_op jit(solution)/shard_map/ppermute | solution.py:917
  299.2 3.8 fusion.13
  306.4 7.5 %join_hidden.1 = (f32[256,2816]{1,0:T(8,128)}, f32[256,2816]{1,0:T(8,128)}, f32[256,2816]{1,0:T(8,128)}) custom-call(bf16[8,256,1152]{2,1,0:T(8,128)(2,1)} %bitcast.115), custom_call_target="tpu_custom_call" | custom-call | tf_op jit(solution)/shard_map/join_hidden/pallas_call | solution.py:899
  313.9 5.0 %collective-permute-done.48 = bf16[256,1024]{1,0:T(8,128)(2,1)} collective-permute-done((bf16[256,1024]{1,0:T(8,128)(2,1)}, bf16[256,1024]{1,0:T(8,128)(2,1)}, u32[]{:S(2)}, u32[]{:S(2)}) %collective-permute-start.48) | collective-permute-done | bytes 524320 | tf_op jit(solution)/shard_map/ppermute | solution.py:917
  319.0 10.5 %collective-permute-done.47 = bf16[256,1024]{1,0:T(8,128)(2,1)} collective-permute-done((bf16[256,1024]{1,0:T(8,128)(2,1)}, bf16[256,1024]{1,0:T(8,128)(2,1)}, u32[]{:S(2)}, u32[]{:S(2)}) %collective-permute-start.47) | collective-permute-done | bytes 524320 | tf_op jit(solution)/shard_map/ppermute | solution.py:917
  332.9 3.2 collective-permute-done.49
  337.9 3.2 collective-permute-done.50
  344.9 3.5 collective-permute-done.52
  350.0 4.2 %multiply_add_fusion = (f32[256,1024]{1,0:T(8,128)}, bf16[256,1024]{1,0:T(8,128)(2,1)}) fusion(f32[256]{0:T(256)S(1)} %broadcast_multiply_fusion, f32[256]{0:T(256)S(1)} %rsqrt_bitcast_fusion, bf16[2,128,1024]{2,1,0:T(8,128)(2,1)S(1)} %copy-done.4, f32[1024]{0:T(1024)S(1)} %copy-done.50, bf16[256,1024]{1,0:T(8,128)(2,1)} %collective-permute-done.48, ...), kind=kLoop, calls=%fused_computation.9 | loop fusion | flops 8126464 | bytes 9973760 | tf_op jit(solution)/shard_map/add | solution.py:1154
  357.4 11.7 %all-gather.13.cloned.1.call-done = bf16[2048,1024]{1,0:T(8,128)(2,1)} async-done(((bf16[256,1024]{1,0:T(8,128)(2,1)}), bf16[2048,1024]{1,0:T(8,128)(2,1)}) %all-gather.13.cloned.1.call-update) | async-done | bytes 4194320 | tf_op jit(solution)/shard_map/all_gather | solution.py:1019
  369.1 7.2 %join_heads.1 = (f32[256,1024]{1,0:T(8,128)}, f32[256,1024]{1,0:T(8,128)}, f32[256,2048]{1,0:T(8,128)}, f32[256,2048]{1,0:T(8,128)}, f32[256,2048]{1,0:T(8,128)}) custom-call(bf16[8,256,1024]{2,1,0:T(8,128)(2,1)} %bitcast.118), custom_call_target="tpu_custom_call" | custom-call | tf_op jit(solution)/shard_map/join_heads/pallas_call | solution.py:874
  (283 shorter events, 82.5 us)
Async XLA Ops:
  7.2 51.6 %all-gather.7.cloned.1.call-start = ((), (), s32[]{:S(2)}) async-start(), calls=%async_computation.4 | async-start | bytes 2621440 | tf_op jit(solution)/shard_map/all_gather | solution.py:1004
  9.8 28.1 %collective-permute-start.2 = (bf16[256,1024]{1,0:T(8,128)(2,1)S(1)}, bf16[256,1024]{1,0:T(8,128)(2,1)S(1)}, u32[]{:S(2)}, u32[]{:S(2)}) collective-permute-start(bf16[256,1024]{1,0:T(8,128)(2,1)S(1)} %multiply_convert_fusion.refs_0_), channel_id=1, source_target_pairs={{0,24},{4,28},{8,16},{12,20},{16,8},{20,12},{24,0},{28,4},{1,25},{... | collective-permute-start | bytes 1572872 | tf_op jit(solution)/shard_map/ppermute | solution.py:917
  13.7 24.2 %collective-permute-start.1 = (bf16[256,1024]{1,0:T(8,128)(2,1)S(1)}, bf16[256,1024]{1,0:T(8,128)(2,1)S(1)}, u32[]{:S(2)}, u32[]{:S(2)}) collective-permute-start(bf16[256,1024]{1,0:T(8,128)(2,1)S(1)} %multiply_convert_fusion.refs_0_), channel_id=1, source_target_pairs={{0,16},{4,20},{8,24},{12,28},{16,0},{20,4},{24,8},{28,12},{1,17},{... | collective-permute-start | bytes 1572872 | tf_op jit(solution)/shard_map/ppermute | solution.py:917
  14.2 23.7 %collective-permute-start = (bf16[256,1024]{1,0:T(8,128)(2,1)S(1)}, bf16[256,1024]{1,0:T(8,128)(2,1)S(1)}, u32[]{:S(2)}, u32[]{:S(2)}) collective-permute-start(bf16[256,1024]{1,0:T(8,128)(2,1)S(1)} %multiply_convert_fusion.refs_0_), channel_id=1, source_target_pairs={{0,8},{4,12},{8,0},{12,4},{16,24},{20,28},{24,16},{28,20},{1,9},{5... | collective-permute-start | bytes 1572872 | tf_op jit(solution)/shard_map/ppermute | solution.py:917
  15.0 22.3 %all-to-all-start = ((f32[8,1,256]{2,1,0:T(1,128)}), f32[8,1,256]{2,1,0:T(1,128)S(1)}, u32[]{:S(2)}, u32[]{:S(2)}) async-start(f32[8,1,256]{2,1,0:T(1,128)} %all_to_all.11), calls=%async_computation | async-start | bytes 16384 | tf_op jit(solution)/shard_map/all_to_all | solution.py:1045
  19.1 117.9 %all-gather.9.cloned.1.call-start = ((), (), s32[]{:S(2)}) async-start(), calls=%async_computation.5 | async-start | bytes 2949120 | tf_op jit(solution)/shard_map/all_gather | solution.py:1004
  40.6 14.9 %collective-permute-start.7 = (bf16[256,1024]{1,0:T(8,128)(2,1)S(1)}, bf16[256,1024]{1,0:T(8,128)(2,1)}, u32[]{:S(2)}, u32[]{:S(2)}) collective-permute-start(bf16[256,1024]{1,0:T(8,128)(2,1)S(1)} %bitcast.112), channel_id=1, source_target_pairs={{0,8},{4,12},{8,0},{12,4},{16,24},{20,28},{24,16},{28,20},{1,9},{5... | collective-permute-start | bytes 1572872 | tf_op jit(solution)/shard_map/ppermute | solution.py:917
  42.0 52.4 %collective-permute-start.9 = (bf16[256,1024]{1,0:T(8,128)(2,1)S(1)}, bf16[256,1024]{1,0:T(8,128)(2,1)}, u32[]{:S(2)}, u32[]{:S(2)}) collective-permute-start(bf16[256,1024]{1,0:T(8,128)(2,1)S(1)} %bitcast.113), channel_id=1, source_target_pairs={{0,24},{4,28},{8,16},{12,20},{16,8},{20,12},{24,0},{28,4},{1,25},{... | collective-permute-start | bytes 1572872 | tf_op jit(solution)/shard_map/ppermute | solution.py:917
  59.9 34.5 %collective-permute-start.12 = (bf16[1024,256]{1,0:T(8,128)(2,1)S(1)}, bf16[1024,256]{1,0:T(8,128)(2,1)}, u32[]{:S(2)}, u32[]{:S(2)}) collective-permute-start(bf16[1024,256]{1,0:T(8,128)(2,1)S(1)} %slice.123.refs_0_), channel_id=1, source_target_pairs={{0,24},{4,28},{8,16},{12,20},{16,8},{20,12},{24,0},{28,4},{1,25},{... | collective-permute-start | bytes 1572872 | tf_op jit(solution)/shard_map/ppermute | solution.py:917
  62.4 32.1 %collective-permute-start.11 = (bf16[1024,256]{1,0:T(8,128)(2,1)S(1)}, bf16[1024,256]{1,0:T(8,128)(2,1)S(1)}, u32[]{:S(2)}, u32[]{:S(2)}) collective-permute-start(bf16[1024,256]{1,0:T(8,128)(2,1)S(1)} %slice.123.refs_0_), channel_id=1, source_target_pairs={{0,16},{4,20},{8,24},{12,28},{16,0},{20,4},{24,8},{28,12},{1,17},{... | collective-permute-start | bytes 1572872 | tf_op jit(solution)/shard_map/ppermute | solution.py:917
  62.9 31.5 %collective-permute-start.10 = (bf16[1024,256]{1,0:T(8,128)(2,1)S(1)}, bf16[1024,256]{1,0:T(8,128)(2,1)}, u32[]{:S(2)}, u32[]{:S(2)}) collective-permute-start(bf16[1024,256]{1,0:T(8,128)(2,1)S(1)} %slice.123.refs_0_), channel_id=1, source_target_pairs={{0,8},{4,12},{8,0},{12,4},{16,24},{20,28},{24,16},{28,20},{1,9},{5... | collective-permute-start | bytes 1572872 | tf_op jit(solution)/shard_map/ppermute | solution.py:917
  95.3 19.1 %all-to-all-start.1 = ((bf16[8,256,256]{2,1,0:T(8,128)(2,1)}), bf16[8,256,256]{2,1,0:T(8,128)(2,1)S(1)}, u32[]{:S(2)}, u32[]{:S(2)}) async-start(bf16[8,256,256]{2,1,0:T(8,128)(2,1)} %bitcast.116), calls=%async_computation.1 | async-start | bytes 2097152 | tf_op jit(solution)/shard_map/all_to_all | solution.py:1077
  98.9 131.2 %reduce-scatter.3.cloned.1.call-start = ((), (), s32[]{:S(2)}) async-start(), calls=%async_computation.6 | async-start | bytes 2949120 | tf_op jit(solution)/shard_map/reduce_scatter | solution.py:1016
  121.7 15.3 %collective-permute-start.21 = (bf16[256,1024]{1,0:T(8,128)(2,1)}, bf16[256,1024]{1,0:T(8,128)(2,1)S(1)}, u32[]{:S(2)}, u32[]{:S(2)}) collective-permute-start(bf16[256,1024]{1,0:T(8,128)(2,1)} %collective-permute-done.9.refs_6_.refs_10_), channel_id=1, source_target_pairs={{0,4},{4,0},{8,12},{12,8},{16,20},{20,16},{24,28},{28,24},{1,5},{5... | collective-permute-start | bytes 1572872 | tf_op jit(solution)/shard_map/ppermute | solution.py:917
  122.2 14.8 %collective-permute-start.17 = (bf16[256,1024]{1,0:T(8,128)(2,1)}, bf16[256,1024]{1,0:T(8,128)(2,1)S(1)}, u32[]{:S(2)}, u32[]{:S(2)}) collective-permute-start(bf16[256,1024]{1,0:T(8,128)(2,1)} %get-tuple-element.165.refs_0_), channel_id=1, source_target_pairs={{0,4},{4,0},{8,12},{12,8},{16,20},{20,16},{24,28},{28,24},{1,5},{5... | collective-permute-start | bytes 1572872 | tf_op jit(solution)/shard_map/ppermute | solution.py:917
  133.8 14.8 %collective-permute-start.23 = (bf16[256,1024]{1,0:T(8,128)(2,1)}, bf16[256,1024]{1,0:T(8,128)(2,1)}, u32[]{:S(2)}, u32[]{:S(2)}) collective-permute-start(bf16[256,1024]{1,0:T(8,128)(2,1)} %get-tuple-element.165.refs_0_), channel_id=1, source_target_pairs={{0,16},{4,20},{8,24},{12,28},{16,0},{20,4},{24,8},{28,12},{1,17},{... | collective-permute-start | bytes 1572872 | tf_op jit(solution)/shard_map/ppermute | solution.py:917
  135.4 14.3 %collective-permute-start.22 = (bf16[256,1024]{1,0:T(8,128)(2,1)}, bf16[256,1024]{1,0:T(8,128)(2,1)S(1)}, u32[]{:S(2)}, u32[]{:S(2)}) collective-permute-start(bf16[256,1024]{1,0:T(8,128)(2,1)} %get-tuple-element.165.refs_0_), channel_id=1, source_target_pairs={{0,8},{4,12},{8,0},{12,4},{16,24},{20,28},{24,16},{28,20},{1,9},{5... | collective-permute-start | bytes 1572872 | tf_op jit(solution)/shard_map/ppermute | solution.py:917
  156.5 15.1 %collective-permute-start.29 = (bf16[256,1024]{1,0:T(8,128)(2,1)}, bf16[256,1024]{1,0:T(8,128)(2,1)S(1)}, u32[]{:S(2)}, u32[]{:S(2)}) collective-permute-start(bf16[256,1024]{1,0:T(8,128)(2,1)} %fusion.5), channel_id=1, source_target_pairs={{0,24},{4,28},{8,16},{12,20},{16,8},{20,12},{24,0},{28,4},{1,25},{... | collective-permute-start | bytes 1572872 | tf_op jit(solution)/shard_map/ppermute | solution.py:917
  182.9 100.8 %all-gather.11.cloned.1.call-start = ((), (), s32[]{:S(2)}) async-start(), calls=%async_computation.8 | async-start | bytes 5308416 | tf_op jit(solution)/shard_map/all_gather | solution.py:1019
  184.8 14.4 %collective-permute-start.32 = (bf16[256,1024]{1,0:T(8,128)(2,1)S(1)}, bf16[256,1024]{1,0:T(8,128)(2,1)S(1)}, u32[]{:S(2)}, u32[]{:S(2)}) collective-permute-start(bf16[256,1024]{1,0:T(8,128)(2,1)S(1)} %get-tuple-element.265), channel_id=1, source_target_pairs={{0,16},{4,20},{8,24},{12,28},{16,0},{20,4},{24,8},{28,12},{1,17},{... | collective-permute-start | bytes 1572872 | tf_op jit(solution)/shard_map/ppermute | solution.py:917
  201.8 15.9 %collective-permute-start.40 = (bf16[256,1024]{1,0:T(8,128)(2,1)S(1)}, bf16[256,1024]{1,0:T(8,128)(2,1)S(1)}, u32[]{:S(2)}, u32[]{:S(2)}) collective-permute-start(bf16[256,1024]{1,0:T(8,128)(2,1)S(1)} %fusion.15.refs_0_.refs_8_), channel_id=1, source_target_pairs={{0,24},{4,28},{8,16},{12,20},{16,8},{20,12},{24,0},{28,4},{1,25},{... | collective-permute-start | bytes 1572872 | tf_op jit(solution)/shard_map/ppermute | solution.py:917
  203.4 24.0 %collective-permute-start.38 = (bf16[256,1024]{1,0:T(8,128)(2,1)S(1)}, bf16[256,1024]{1,0:T(8,128)(2,1)S(1)}, u32[]{:S(2)}, u32[]{:S(2)}) collective-permute-start(bf16[256,1024]{1,0:T(8,128)(2,1)S(1)} %fusion.15.refs_0_.refs_8_), channel_id=1, source_target_pairs={{0,16},{4,20},{8,24},{12,28},{16,0},{20,4},{24,8},{28,12},{1,17},{... | collective-permute-start | bytes 1572872 | tf_op jit(solution)/shard_map/ppermute | solution.py:917
  205.1 22.4 %collective-permute-start.36 = (bf16[256,1024]{1,0:T(8,128)(2,1)S(1)}, bf16[256,1024]{1,0:T(8,128)(2,1)S(1)}, u32[]{:S(2)}, u32[]{:S(2)}) collective-permute-start(bf16[256,1024]{1,0:T(8,128)(2,1)S(1)} %fusion.15.refs_0_.refs_8_), channel_id=1, source_target_pairs={{0,8},{4,12},{8,0},{12,4},{16,24},{20,28},{24,16},{28,20},{1,9},{5... | collective-permute-start | bytes 1572872 | tf_op jit(solution)/shard_map/ppermute | solution.py:917
  205.4 22.5 %collective-permute-start.35 = (bf16[256,1024]{1,0:T(8,128)(2,1)S(1)}, bf16[256,1024]{1,0:T(8,128)(2,1)S(1)}, u32[]{:S(2)}, u32[]{:S(2)}) collective-permute-start(bf16[256,1024]{1,0:T(8,128)(2,1)S(1)} %fusion.15.refs_0_.refs_8_), channel_id=1, source_target_pairs={{0,4},{4,0},{8,12},{12,8},{16,20},{20,16},{24,28},{28,24},{1,5},{5... | collective-permute-start | bytes 1572872 | tf_op jit(solution)/shard_map/ppermute | solution.py:917
  230.2 100.2 %reduce-scatter.5.cloned.1.call-start = ((), (), s32[]{:S(2)}) async-start(), calls=%async_computation.7 | async-start | bytes 2621440 | tf_op jit(solution)/shard_map/reduce_scatter | solution.py:1016
  230.5 51.3 %collective-permute-start.42 = (bf16[256,1024]{1,0:T(8,128)(2,1)}, bf16[256,1024]{1,0:T(8,128)(2,1)}, u32[]{:S(2)}, u32[]{:S(2)}) collective-permute-start(bf16[256,1024]{1,0:T(8,128)(2,1)} %get-tuple-element.224), channel_id=1, source_target_pairs={{0,8},{4,12},{8,0},{12,4},{16,24},{20,28},{24,16},{28,20},{1,9},{5... | collective-permute-start | bytes 1572872 | tf_op jit(solution)/shard_map/ppermute | solution.py:917
  231.8 49.9 %collective-permute-start.43 = (bf16[256,1024]{1,0:T(8,128)(2,1)}, bf16[256,1024]{1,0:T(8,128)(2,1)}, u32[]{:S(2)}, u32[]{:S(2)}) collective-permute-start(bf16[256,1024]{1,0:T(8,128)(2,1)} %get-tuple-element.225), channel_id=1, source_target_pairs={{0,16},{4,20},{8,24},{12,28},{16,0},{20,4},{24,8},{28,12},{1,17},{... | collective-permute-start | bytes 1572872 | tf_op jit(solution)/shard_map/ppermute | solution.py:917
  233.3 48.5 %collective-permute-start.44 = (bf16[256,1024]{1,0:T(8,128)(2,1)}, bf16[256,1024]{1,0:T(8,128)(2,1)}, u32[]{:S(2)}, u32[]{:S(2)}) collective-permute-start(bf16[256,1024]{1,0:T(8,128)(2,1)} %get-tuple-element.226), channel_id=1, source_target_pairs={{0,24},{4,28},{8,16},{12,20},{16,8},{20,12},{24,0},{28,4},{1,25},{... | collective-permute-start | bytes 1572872 | tf_op jit(solution)/shard_map/ppermute | solution.py:917
  283.7 85.4 %all-gather.13.cloned.1.call-start = ((), (), s32[]{:S(2)}) async-start(), calls=%async_computation.9 | async-start | bytes 4718592 | tf_op jit(solution)/shard_map/all_gather | solution.py:1019
  303.0 16.0 %collective-permute-start.48 = (bf16[256,1024]{1,0:T(8,128)(2,1)}, bf16[256,1024]{1,0:T(8,128)(2,1)}, u32[]{:S(2)}, u32[]{:S(2)}) collective-permute-start(bf16[256,1024]{1,0:T(8,128)(2,1)} %get-tuple-element.258), channel_id=1, source_target_pairs={{0,24},{4,28},{8,16},{12,20},{16,8},{20,12},{24,0},{28,4},{1,25},{... | collective-permute-start | bytes 1572872 | tf_op jit(solution)/shard_map/ppermute | solution.py:917
  304.4 25.1 %collective-permute-start.47 = (bf16[256,1024]{1,0:T(8,128)(2,1)}, bf16[256,1024]{1,0:T(8,128)(2,1)}, u32[]{:S(2)}, u32[]{:S(2)}) collective-permute-start(bf16[256,1024]{1,0:T(8,128)(2,1)} %get-tuple-element.259), channel_id=1, source_target_pairs={{0,16},{4,20},{8,24},{12,28},{16,0},{20,4},{24,8},{28,12},{1,17},{... | collective-permute-start | bytes 1572872 | tf_op jit(solution)/shard_map/ppermute | solution.py:917
  305.9 23.6 %collective-permute-start.46 = (bf16[256,1024]{1,0:T(8,128)(2,1)S(1)}, bf16[256,1024]{1,0:T(8,128)(2,1)}, u32[]{:S(2)}, u32[]{:S(2)}) collective-permute-start(bf16[256,1024]{1,0:T(8,128)(2,1)S(1)} %get-tuple-element.260), channel_id=1, source_target_pairs={{0,8},{4,12},{8,0},{12,4},{16,24},{20,28},{24,16},{28,20},{1,9},{5... | collective-permute-start | bytes 1572872 | tf_op jit(solution)/shard_map/ppermute | solution.py:917
  (87 other events, 781.7 us)
Sparse Core Ops, SparseCore 0:
  10.2 48.6 all-gather.6
  61.0 49.1 all-gather.8
  183.0 46.9 reduce-scatter.2
  231.7 51.9 all-gather.10
  286.4 43.8 reduce-scatter.4
  332.2 36.7 all-gather.12

commit v7 on v6

--- a/solution.py
+++ b/solution.py
@@ -324,10 +324,18 @@
 
     for slot in range(H):
         block_copy(branch_refs[slot], slot).start()
-    saved_copies = [
-        pltpu.make_async_copy(saved[index], held[index], saved_sems.at[index])
-        for index in range(len(saved))
-    ]
+
+    def saved_copy(index, first, count, turn):
+        span = pl.ds(first, count)
+        return pltpu.make_async_copy(
+            saved[index].at[span], held[index].at[span], saved_sems.at[index, turn]
+        )
+
+    early = len(saved) - 2
+
+    def turn_copy(index, turn):
+        return saved_copy(index, turn * BACKWARD_CHUNKS, BACKWARD_CHUNKS, turn)
+
 
     lane = lax.broadcasted_iota(jnp.int32, (size, 128), 1)
     grad_gain_ref[...] = jnp.zeros_like(grad_gain_ref)
@@ -338,8 +346,9 @@
     def project(slot, _):
         @pl.when(slot == 1)
         def _():
-            for copy in saved_copies[:5]:
-                copy.start()
+            for turn in range(chunks // BACKWARD_CHUNKS):
+                for index in range(early):
+                    turn_copy(index, turn).start()
 
         block_copy(branch_refs[0], slot).wait()
         d_headed = product(branch_ref[slot], weight_ref[...])
@@ -348,13 +357,13 @@
         return 0
 
     lax.fori_loop(0, H, project, 0)
-    for copy in saved_copies[:5]:
-        copy.wait()
-    for copy in saved_copies[5:]:
-        copy.start()
+    for index in range(early, len(saved)):
+        saved_copy(index, 0, chunks, 0).start()
 
     def prepare(turn, _):
         units = units_of(turn * BACKWARD_CHUNKS, BACKWARD_CHUNKS, seqs)
+        for index in range(early):
+            turn_copy(index, turn).wait()
         for chunk, seq in units:
             unit = chunk * seqs + seq
             summed = conv_rows(conv_ref, halo_ref, rows_ref, taps_ref, chunk, seq, unit)
@@ -412,8 +421,8 @@
     for seq in range(seqs):
         d_start_ref[seq] = first[seq]
         d_conv_ref[seq, size:, :] = d_after_ref[seq]
-    for copy in saved_copies[5:]:
-        copy.wait()
+    for index in range(early, len(saved)):
+        saved_copy(index, 0, chunks, 0).wait()
 
     def send(chunk):
         slot = chunk ^ head
@@ -621,7 +630,7 @@
             pltpu.VMEM((H * seqs, size, 128), f32),
             pltpu.SemaphoreType.DMA((H,)),
             pltpu.SemaphoreType.DMA,
-            pltpu.SemaphoreType.DMA((7,)),
+            pltpu.SemaphoreType.DMA((7, H // BACKWARD_CHUNKS)),
             pltpu.SemaphoreType.DMA,
         ],
         compiler_params=kernel_params(),

time: 384 us -> 384 us (level)
  transfers between devices with their start and end apart: 62 -> 62, of which waited for: 27 -> 27; matrix products, arithmetic and copies ran while one was open for 8% -> 8% of each run, Pallas kernels for 35% -> 34%
where the time goes in v7:
time: 384 us; the launch traced here: 383 us
  Pallas kernels  140 us (36%)
  waiting for transfers between devices  137 us (36%)
  starting transfers between devices  51.9 us (14%)
  other arithmetic  21.1 us (5%)
  local copies, waits for them, and re-layouts  18.3 us (5%)
  between operations  14.9 us (4%)
    ppermute x54, waiting for transfers between devices, swapped(): lax.ppermute(array, axis, [(i, i ^ bits) for i in range(lax.axis_size(axi...  93.3 us
    ppermute x54, starting transfers between devices, swapped(): lax.ppermute(array, axis, [(i, i ^ bits) for i in range(lax.axis_size(axi...  43.2 us
    pallas_call x1, Pallas kernels, backward_rule(): pl.pallas_call(backward_kernel, name='mixer_backward', out_shape=(shaped(...  34.5 us
    pallas_call x1, Pallas kernels, forward_rule(): pl.pallas_call(forward_kernel, name='mixer_forward', out_shape=[shaped(*i...  29.5 us
    pallas_call x2, Pallas kernels, ffn_rule(): pl.pallas_call(ffn_kernel, name='feed_forward', grid=(PART,), in_specs=an...  21.3 us
    all_gather x2, waiting for transfers between devices, spread_grads(): spread = lax.all_gather(summed, 'seq')  15.1 us
    all_to_all x1, waiting for transfers between devices, shards(): lax.all_to_all(decay_rows, 'seq', 0, 0, axis_index_groups=groups, tiled=T...  14.2 us
    pallas_call x1, Pallas kernels, mixer_grads_rule(): pl.pallas_call(mixer_grads_kernel, name='mixer_grads', grid=(model // GRA...  11.1 us
  transfers between devices with their start and end apart: 62, of which 27 were waited for; matrix products, arithmetic and copies ran while one was open for 8% of the time, Pallas kernels for 34%

profile of v7, /device:TPU:0, one launch (start us, length us, event | category | flops | bytes accessed | tf_op | source)
XLA Modules:
  0.0 383.2 jit_solution(16633705388889310405)
XLA Ops:
  9.8 4.0 %collective-permute-start.2 = (bf16[256,1024]{1,0:T(8,128)(2,1)S(1)}, bf16[256,1024]{1,0:T(8,128)(2,1)S(1)}, u32[]{:S(2)}, u32[]{:S(2)}) collective-permute-start(bf16[256,1024]{1,0:T(8,128)(2,1)S(1)} %multiply_convert_fusion.refs_0_), channel_id=1, source_target_pairs={{0,24},{4,28},{8,16},{12,20},{16,8},{20,12},{24,0},{28,4},{1,25},{... | collective-permute-start | bytes 1572872 | tf_op jit(solution)/shard_map/ppermute | solution.py:926
  15.0 4.1 %all-to-all-start = ((f32[8,1,256]{2,1,0:T(1,128)}), f32[8,1,256]{2,1,0:T(1,128)S(1)}, u32[]{:S(2)}, u32[]{:S(2)}) async-start(f32[8,1,256]{2,1,0:T(1,128)} %all_to_all.11), calls=%async_computation | async-start | bytes 16384 | tf_op jit(solution)/shard_map/all_to_all | solution.py:1054
  23.1 14.2 %all-to-all-done = f32[8,1,256]{2,1,0:T(1,128)S(1)} async-done(((f32[8,1,256]{2,1,0:T(1,128)}), f32[8,1,256]{2,1,0:T(1,128)S(1)}, u32[]{:S(2)}, u32[]{:S(2)}) %all-to-all-start) | async-done | bytes 8224 | tf_op jit(solution)/shard_map/all_to_all | solution.py:1054
  43.0 10.1 %collective-permute-done.8.refs_6_.refs_14_ = bf16[256,1024]{1,0:T(8,128)(2,1)S(1)} collective-permute-done((bf16[256,1024]{1,0:T(8,128)(2,1)S(1)}, bf16[256,1024]{1,0:T(8,128)(2,1)S(1)}, u32[]{:S(2)}, u32[]{:S(2)}) %collective-permute-start.8) | collective-permute-done | bytes 524320 | tf_op jit(solution)/shard_map/ppermute | solution.py:926
  55.5 3.4 all-gather.7.cloned.1.call-done.refs_9_.refs_8_.refs_18_.weight_ref
  64.9 29.5 %mixer_forward.1 = (bf16[8,2,128,256]{3,2,1,0:T(8,128)(2,1)}, bf16[8,2,128,512]{3,2,1,0:T(8,128)(2,1)}, f32[8,2,128,384]{3,2,1,0:T(8,128)}, f32[8,2,128,256]{3,2...) custom-call(s32[1]{0:T(128)} %bitcast.head_ref, ...), custom_call_target="tpu_custom_call" | custom-call | tf_op jit(solution)/shard_map/mixer_forward/pallas_call | solution.py:569
  95.3 3.7 all-to-all-start.1
  104.4 9.9 %all-to-all-done.1.refs_8_ = bf16[8,256,256]{2,1,0:T(8,128)(2,1)S(1)} async-done(((bf16[8,256,256]{2,1,0:T(8,128)(2,1)}), bf16[8,256,256]{2,1,0:T(8,128)(2,1)S(1)}, u32[]{:S(2)}, u32[]{:S(2)}) %all-to-all-start.1) | async-done | bytes 1048608 | tf_op jit(solution)/shard_map/all_to_all | solution.py:1086
  115.3 5.7 %out_projection.1 = (f32[256,1024]{1,0:T(8,128)}, bf16[256,1024]{1,0:T(8,128)(2,1)}) custom-call(s32[1]{0:T(128)} %bitcast.head_ref, bf16[1024,256]{1,0:T(8,128)(2,1)} %copy-done.25, bf16[1024,256]{1,0:T(8,128)(2,1)} %copy-done.47, bf16[1024,256]{1,0:T(8,128)(2,1)} %collective-permute-done.10.refs_2_, bf16[1024,256]{1,0:T(8,128)(2,1)} %copy-done.48, ...), custom_call_target="tpu_custom_call" | custom-call | tf_op jit(solution)/shard_map/out_projection/pallas_call | solution.py:668
  122.2 11.6 %collective-permute-done.18.refs_2_ = bf16[256,1024]{1,0:T(8,128)(2,1)S(1)} collective-permute-done((bf16[256,1024]{1,0:T(8,128)(2,1)}, bf16[256,1024]{1,0:T(8,128)(2,1)S(1)}, u32[]{:S(2)}, u32[]{:S(2)}) %collective-permute-start.18) | collective-permute-done | bytes 524320 | tf_op jit(solution)/shard_map/ppermute | solution.py:926
  138.0 10.6 %feed_forward.2 = (bf16[4,256,768]{2,1,0:T(8,128)(2,1)}, bf16[4,256,384]{2,1,0:T(8,128)(2,1)}, bf16[2,256,1024]{2,1,0:T(8,128)(2,1)}, bf16[2,256,1024]{2,1,0:T(8...) custom-call(bf16[256,1024]{1,0:T(8,128)(2,1)} %get-tuple-element.165.refs_0_, ...), custom_call_target="tpu_custom_call" | custom-call | tf_op jit(solution)/shard_map/feed_forward/pallas_call | solution.py:743
  150.7 3.3 collective-permute-done.26
  160.8 10.7 %feed_forward.3 = (bf16[4,256,768]{2,1,0:T(8,128)(2,1)}, bf16[4,256,384]{2,1,0:T(8,128)(2,1)}, bf16[2,256,1024]{2,1,0:T(8,128)(2,1)}, bf16[2,256,1024]{2,1,0:T(8...) custom-call(bf16[256,1024]{1,0:T(8,128)(2,1)} %copy-done.33, bf16[256,1024]{1,0:T(8,128)(2,1)} %copy-done.34, ...), custom_call_target="tpu_custom_call" | custom-call | tf_op jit(solution)/shard_map/feed_forward/pallas_call | solution.py:743
  172.4 10.5 %feed_forward_grads.1 = bf16[1024,1152]{1,0:T(8,128)(2,1)} custom-call(bf16[256,1024]{1,0:T(8,128)(2,1)} %get-tuple-element.165.refs_0_, bf16[256,1024]{1,0:T(8,128)(2,1)} %copy-done.32, bf16[256,1024]{1,0:T(8,128)(2,1)} %copy-done.29, bf16[256,1024]{1,0:T(8,128)(2,1)} %collective-permute-done.19.refs_3_, bf16[256,1024]{1,0:T(8,128)(2,1)} %copy-done.33, ...), custom_call_target="tpu_custom_call" | custom-call | tf_op jit(solution)/shard_map/feed_forward_grads/pallas_call | solution.py:783
  191.1 8.1 %collective-permute-done.32 = bf16[256,1024]{1,0:T(8,128)(2,1)S(1)} collective-permute-done((bf16[256,1024]{1,0:T(8,128)(2,1)S(1)}, bf16[256,1024]{1,0:T(8,128)(2,1)S(1)}, u32[]{:S(2)}, u32[]{:S(2)}) %collective-permute-start.32) | collective-permute-done | bytes 524320 | tf_op jit(solution)/shard_map/ppermute | solution.py:926
  205.4 12.3 %collective-permute-done.40.refs_6_.refs_14_ = bf16[256,1024]{1,0:T(8,128)(2,1)S(1)} collective-permute-done((bf16[256,1024]{1,0:T(8,128)(2,1)S(1)}, bf16[256,1024]{1,0:T(8,128)(2,1)S(1)}, u32[]{:S(2)}, u32[]{:S(2)}) %collective-permute-start.40) | collective-permute-done | bytes 524320 | tf_op jit(solution)/shard_map/ppermute | solution.py:926
  217.7 9.7 %collective-permute-done.38.refs_4_.refs_12_ = bf16[256,1024]{1,0:T(8,128)(2,1)S(1)} collective-permute-done((bf16[256,1024]{1,0:T(8,128)(2,1)S(1)}, bf16[256,1024]{1,0:T(8,128)(2,1)S(1)}, u32[]{:S(2)}, u32[]{:S(2)}) %collective-permute-start.38) | collective-permute-done | bytes 524320 | tf_op jit(solution)/shard_map/ppermute | solution.py:926
  234.6 34.5 %mixer_backward.1 = (bf16[8,2,128,896]{3,2,1,0:T(8,128)(2,1)}, f32[8,512]{1,0:T(8,128)}, f32[1,256]{1,0:T(1,128)}, f32[2,128,256]{2,1,0:T(8,128)}, f32[2,8,512]{2,1,0:T(8,128)}) custom-call(s32[1]{0:T(128)} %bitcast.head_ref, bf16[256,1024]{1,0:T(8,128)(2,1)} %copy-done.8, bf16[256,1024]{1,0:T(8,128)(2,1)} %copy-done.22, bf16[256,1024]{1,0:T(8,128)(2,1)} %copy-done.21, ...), custom_call_target="tpu_custom_call" | custom-call | tf_op jit(solution)/shard_map/mixer_backward/pallas_call | solution.py:600
  269.1 11.1 %mixer_grads.1 = (bf16[1024,1024]{1,0:T(8,128)(2,1)}, f32[1024,128]{1,0:T(8,128)}) custom-call(s32[1]{0:T(128)} %bitcast.head_ref, bf16[256,1024]{1,0:T(8,128)(2,1)} %copy-done.7, bf16[256,1024]{1,0:T(8,128)(2,1)} %copy-done.15, bf16[256,1024]{1,0:T(8,128)(2,1)} %copy-done.14, bf16[256,1024]{1,0:T(8,128)(2,1)} %copy-done.16, bf16[256,1024]{1,0:T(8,128)(2,1)} %copy-done.13, ...), custom_call_target="tpu_custom_call" | custom-call | tf_op jit(solution)/shard_map/mixer_grads/pallas_call | solution.py:817
  280.3 3.4 all-gather.11.cloned.1.call-done
  284.0 10.8 %mixer_d_in.1 = (bf16[4,256,1024]{2,1,0:T(8,128)(2,1)}, bf16[4,256,1024]{2,1,0:T(8,128)(2,1)}) custom-call(bf16[8,256,896]{2,1,0:T(8,128)(2,1)} %bitcast.107, bf16[1024,1024]{1,0:T(8,128)(2,1)} %all-gather.7.cloned.1.call-done.refs_9_.refs_8_.refs_18_.weight_ref, bf16[1024,128]{1,0:T(8,128)(2,1)} %pad.9.refs_10_.refs_19_.beta_ref), custom_call_target="tpu_custom_call" | custom-call | tf_op jit(solution)/shard_map/mixer_d_in/pallas_call | solution.py:853
  295.1 4.1 %collective-permute-done.45 = bf16[4,256,1024]{2,1,0:T(8,128)(2,1)S(1)} collective-permute-done((bf16[4,256,1024]{2,1,0:T(8,128)(2,1)}, bf16[4,256,1024]{2,1,0:T(8,128)(2,1)S(1)}, u32[]{:S(2)}, u32[]{:S(2)}) %collective-permute-start.45) | collective-permute-done | bytes 2097184 | tf_op jit(solution)/shard_map/ppermute | solution.py:926
  299.2 3.8 fusion.13
  306.4 7.5 %join_hidden.1 = (f32[256,2816]{1,0:T(8,128)}, f32[256,2816]{1,0:T(8,128)}, f32[256,2816]{1,0:T(8,128)}) custom-call(bf16[8,256,1152]{2,1,0:T(8,128)(2,1)} %bitcast.115), custom_call_target="tpu_custom_call" | custom-call | tf_op jit(solution)/shard_map/join_hidden/pallas_call | solution.py:908
  313.9 5.0 %collective-permute-done.48 = bf16[256,1024]{1,0:T(8,128)(2,1)} collective-permute-done((bf16[256,1024]{1,0:T(8,128)(2,1)}, bf16[256,1024]{1,0:T(8,128)(2,1)}, u32[]{:S(2)}, u32[]{:S(2)}) %collective-permute-start.48) | collective-permute-done | bytes 524320 | tf_op jit(solution)/shard_map/ppermute | solution.py:926
  319.0 10.5 %collective-permute-done.47 = bf16[256,1024]{1,0:T(8,128)(2,1)} collective-permute-done((bf16[256,1024]{1,0:T(8,128)(2,1)}, bf16[256,1024]{1,0:T(8,128)(2,1)}, u32[]{:S(2)}, u32[]{:S(2)}) %collective-permute-start.47) | collective-permute-done | bytes 524320 | tf_op jit(solution)/shard_map/ppermute | solution.py:926
  332.9 3.2 collective-permute-done.49
  337.9 3.2 collective-permute-done.50
  345.0 3.5 collective-permute-done.52
  350.0 4.2 %multiply_add_fusion = (f32[256,1024]{1,0:T(8,128)}, bf16[256,1024]{1,0:T(8,128)(2,1)}) fusion(f32[256]{0:T(256)S(1)} %broadcast_multiply_fusion, f32[256]{0:T(256)S(1)} %rsqrt_bitcast_fusion, bf16[2,128,1024]{2,1,0:T(8,128)(2,1)S(1)} %copy-done.4, f32[1024]{0:T(1024)S(1)} %copy-done.50, bf16[256,1024]{1,0:T(8,128)(2,1)} %collective-permute-done.48, ...), kind=kLoop, calls=%fused_computation.9 | loop fusion | flops 8126464 | bytes 9973760 | tf_op jit(solution)/shard_map/add | solution.py:1163
  357.4 11.7 %all-gather.13.cloned.1.call-done = bf16[2048,1024]{1,0:T(8,128)(2,1)} async-done(((bf16[256,1024]{1,0:T(8,128)(2,1)}), bf16[2048,1024]{1,0:T(8,128)(2,1)}) %all-gather.13.cloned.1.call-update) | async-done | bytes 4194320 | tf_op jit(solution)/shard_map/all_gather | solution.py:1028
  369.1 7.2 %join_heads.1 = (f32[256,1024]{1,0:T(8,128)}, f32[256,1024]{1,0:T(8,128)}, f32[256,2048]{1,0:T(8,128)}, f32[256,2048]{1,0:T(8,128)}, f32[256,2048]{1,0:T(8,128)}) custom-call(bf16[8,256,1024]{2,1,0:T(8,128)(2,1)} %bitcast.118), custom_call_target="tpu_custom_call" | custom-call | tf_op jit(solution)/shard_map/join_heads/pallas_call | solution.py:883
  (283 shorter events, 83.2 us)
Async XLA Ops:
  7.2 51.6 %all-gather.7.cloned.1.call-start = ((), (), s32[]{:S(2)}) async-start(), calls=%async_computation.4 | async-start | bytes 2621440 | tf_op jit(solution)/shard_map/all_gather | solution.py:1013
  9.8 28.1 %collective-permute-start.2 = (bf16[256,1024]{1,0:T(8,128)(2,1)S(1)}, bf16[256,1024]{1,0:T(8,128)(2,1)S(1)}, u32[]{:S(2)}, u32[]{:S(2)}) collective-permute-start(bf16[256,1024]{1,0:T(8,128)(2,1)S(1)} %multiply_convert_fusion.refs_0_), channel_id=1, source_target_pairs={{0,24},{4,28},{8,16},{12,20},{16,8},{20,12},{24,0},{28,4},{1,25},{... | collective-permute-start | bytes 1572872 | tf_op jit(solution)/shard_map/ppermute | solution.py:926
  13.7 24.2 %collective-permute-start.1 = (bf16[256,1024]{1,0:T(8,128)(2,1)S(1)}, bf16[256,1024]{1,0:T(8,128)(2,1)S(1)}, u32[]{:S(2)}, u32[]{:S(2)}) collective-permute-start(bf16[256,1024]{1,0:T(8,128)(2,1)S(1)} %multiply_convert_fusion.refs_0_), channel_id=1, source_target_pairs={{0,16},{4,20},{8,24},{12,28},{16,0},{20,4},{24,8},{28,12},{1,17},{... | collective-permute-start | bytes 1572872 | tf_op jit(solution)/shard_map/ppermute | solution.py:926
  14.2 23.7 %collective-permute-start = (bf16[256,1024]{1,0:T(8,128)(2,1)S(1)}, bf16[256,1024]{1,0:T(8,128)(2,1)S(1)}, u32[]{:S(2)}, u32[]{:S(2)}) collective-permute-start(bf16[256,1024]{1,0:T(8,128)(2,1)S(1)} %multiply_convert_fusion.refs_0_), channel_id=1, source_target_pairs={{0,8},{4,12},{8,0},{12,4},{16,24},{20,28},{24,16},{28,20},{1,9},{5... | collective-permute-start | bytes 1572872 | tf_op jit(solution)/shard_map/ppermute | solution.py:926
  15.0 22.3 %all-to-all-start = ((f32[8,1,256]{2,1,0:T(1,128)}), f32[8,1,256]{2,1,0:T(1,128)S(1)}, u32[]{:S(2)}, u32[]{:S(2)}) async-start(f32[8,1,256]{2,1,0:T(1,128)} %all_to_all.11), calls=%async_computation | async-start | bytes 16384 | tf_op jit(solution)/shard_map/all_to_all | solution.py:1054
  19.1 117.9 %all-gather.9.cloned.1.call-start = ((), (), s32[]{:S(2)}) async-start(), calls=%async_computation.5 | async-start | bytes 2949120 | tf_op jit(solution)/shard_map/all_gather | solution.py:1013
  40.6 14.9 %collective-permute-start.7 = (bf16[256,1024]{1,0:T(8,128)(2,1)S(1)}, bf16[256,1024]{1,0:T(8,128)(2,1)}, u32[]{:S(2)}, u32[]{:S(2)}) collective-permute-start(bf16[256,1024]{1,0:T(8,128)(2,1)S(1)} %bitcast.112), channel_id=1, source_target_pairs={{0,8},{4,12},{8,0},{12,4},{16,24},{20,28},{24,16},{28,20},{1,9},{5... | collective-permute-start | bytes 1572872 | tf_op jit(solution)/shard_map/ppermute | solution.py:926
  42.0 52.4 %collective-permute-start.9 = (bf16[256,1024]{1,0:T(8,128)(2,1)S(1)}, bf16[256,1024]{1,0:T(8,128)(2,1)}, u32[]{:S(2)}, u32[]{:S(2)}) collective-permute-start(bf16[256,1024]{1,0:T(8,128)(2,1)S(1)} %bitcast.113), channel_id=1, source_target_pairs={{0,24},{4,28},{8,16},{12,20},{16,8},{20,12},{24,0},{28,4},{1,25},{... | collective-permute-start | bytes 1572872 | tf_op jit(solution)/shard_map/ppermute | solution.py:926
  59.9 34.5 %collective-permute-start.12 = (bf16[1024,256]{1,0:T(8,128)(2,1)S(1)}, bf16[1024,256]{1,0:T(8,128)(2,1)}, u32[]{:S(2)}, u32[]{:S(2)}) collective-permute-start(bf16[1024,256]{1,0:T(8,128)(2,1)S(1)} %slice.123.refs_0_), channel_id=1, source_target_pairs={{0,24},{4,28},{8,16},{12,20},{16,8},{20,12},{24,0},{28,4},{1,25},{... | collective-permute-start | bytes 1572872 | tf_op jit(solution)/shard_map/ppermute | solution.py:926
  62.4 32.1 %collective-permute-start.11 = (bf16[1024,256]{1,0:T(8,128)(2,1)S(1)}, bf16[1024,256]{1,0:T(8,128)(2,1)S(1)}, u32[]{:S(2)}, u32[]{:S(2)}) collective-permute-start(bf16[1024,256]{1,0:T(8,128)(2,1)S(1)} %slice.123.refs_0_), channel_id=1, source_target_pairs={{0,16},{4,20},{8,24},{12,28},{16,0},{20,4},{24,8},{28,12},{1,17},{... | collective-permute-start | bytes 1572872 | tf_op jit(solution)/shard_map/ppermute | solution.py:926
  62.9 31.5 %collective-permute-start.10 = (bf16[1024,256]{1,0:T(8,128)(2,1)S(1)}, bf16[1024,256]{1,0:T(8,128)(2,1)}, u32[]{:S(2)}, u32[]{:S(2)}) collective-permute-start(bf16[1024,256]{1,0:T(8,128)(2,1)S(1)} %slice.123.refs_0_), channel_id=1, source_target_pairs={{0,8},{4,12},{8,0},{12,4},{16,24},{20,28},{24,16},{28,20},{1,9},{5... | collective-permute-start | bytes 1572872 | tf_op jit(solution)/shard_map/ppermute | solution.py:926
  95.3 19.1 %all-to-all-start.1 = ((bf16[8,256,256]{2,1,0:T(8,128)(2,1)}), bf16[8,256,256]{2,1,0:T(8,128)(2,1)S(1)}, u32[]{:S(2)}, u32[]{:S(2)}) async-start(bf16[8,256,256]{2,1,0:T(8,128)(2,1)} %bitcast.116), calls=%async_computation.1 | async-start | bytes 2097152 | tf_op jit(solution)/shard_map/all_to_all | solution.py:1086
  98.9 131.2 %reduce-scatter.3.cloned.1.call-start = ((), (), s32[]{:S(2)}) async-start(), calls=%async_computation.6 | async-start | bytes 2949120 | tf_op jit(solution)/shard_map/reduce_scatter | solution.py:1025
  121.7 15.3 %collective-permute-start.21 = (bf16[256,1024]{1,0:T(8,128)(2,1)}, bf16[256,1024]{1,0:T(8,128)(2,1)S(1)}, u32[]{:S(2)}, u32[]{:S(2)}) collective-permute-start(bf16[256,1024]{1,0:T(8,128)(2,1)} %collective-permute-done.9.refs_6_.refs_10_), channel_id=1, source_target_pairs={{0,4},{4,0},{8,12},{12,8},{16,20},{20,16},{24,28},{28,24},{1,5},{5... | collective-permute-start | bytes 1572872 | tf_op jit(solution)/shard_map/ppermute | solution.py:926
  122.2 14.8 %collective-permute-start.17 = (bf16[256,1024]{1,0:T(8,128)(2,1)}, bf16[256,1024]{1,0:T(8,128)(2,1)S(1)}, u32[]{:S(2)}, u32[]{:S(2)}) collective-permute-start(bf16[256,1024]{1,0:T(8,128)(2,1)} %get-tuple-element.165.refs_0_), channel_id=1, source_target_pairs={{0,4},{4,0},{8,12},{12,8},{16,20},{20,16},{24,28},{28,24},{1,5},{5... | collective-permute-start | bytes 1572872 | tf_op jit(solution)/shard_map/ppermute | solution.py:926
  133.8 14.8 %collective-permute-start.23 = (bf16[256,1024]{1,0:T(8,128)(2,1)}, bf16[256,1024]{1,0:T(8,128)(2,1)}, u32[]{:S(2)}, u32[]{:S(2)}) collective-permute-start(bf16[256,1024]{1,0:T(8,128)(2,1)} %get-tuple-element.165.refs_0_), channel_id=1, source_target_pairs={{0,16},{4,20},{8,24},{12,28},{16,0},{20,4},{24,8},{28,12},{1,17},{... | collective-permute-start | bytes 1572872 | tf_op jit(solution)/shard_map/ppermute | solution.py:926
  135.4 14.3 %collective-permute-start.22 = (bf16[256,1024]{1,0:T(8,128)(2,1)}, bf16[256,1024]{1,0:T(8,128)(2,1)S(1)}, u32[]{:S(2)}, u32[]{:S(2)}) collective-permute-start(bf16[256,1024]{1,0:T(8,128)(2,1)} %get-tuple-element.165.refs_0_), channel_id=1, source_target_pairs={{0,8},{4,12},{8,0},{12,4},{16,24},{20,28},{24,16},{28,20},{1,9},{5... | collective-permute-start | bytes 1572872 | tf_op jit(solution)/shard_map/ppermute | solution.py:926
  156.5 15.1 %collective-permute-start.29 = (bf16[256,1024]{1,0:T(8,128)(2,1)}, bf16[256,1024]{1,0:T(8,128)(2,1)S(1)}, u32[]{:S(2)}, u32[]{:S(2)}) collective-permute-start(bf16[256,1024]{1,0:T(8,128)(2,1)} %fusion.5), channel_id=1, source_target_pairs={{0,24},{4,28},{8,16},{12,20},{16,8},{20,12},{24,0},{28,4},{1,25},{... | collective-permute-start | bytes 1572872 | tf_op jit(solution)/shard_map/ppermute | solution.py:926
  182.9 100.8 %all-gather.11.cloned.1.call-start = ((), (), s32[]{:S(2)}) async-start(), calls=%async_computation.8 | async-start | bytes 5308416 | tf_op jit(solution)/shard_map/all_gather | solution.py:1028
  184.8 14.4 %collective-permute-start.32 = (bf16[256,1024]{1,0:T(8,128)(2,1)S(1)}, bf16[256,1024]{1,0:T(8,128)(2,1)S(1)}, u32[]{:S(2)}, u32[]{:S(2)}) collective-permute-start(bf16[256,1024]{1,0:T(8,128)(2,1)S(1)} %get-tuple-element.265), channel_id=1, source_target_pairs={{0,16},{4,20},{8,24},{12,28},{16,0},{20,4},{24,8},{28,12},{1,17},{... | collective-permute-start | bytes 1572872 | tf_op jit(solution)/shard_map/ppermute | solution.py:926
  201.8 15.9 %collective-permute-start.40 = (bf16[256,1024]{1,0:T(8,128)(2,1)S(1)}, bf16[256,1024]{1,0:T(8,128)(2,1)S(1)}, u32[]{:S(2)}, u32[]{:S(2)}) collective-permute-start(bf16[256,1024]{1,0:T(8,128)(2,1)S(1)} %fusion.15.refs_0_.refs_8_), channel_id=1, source_target_pairs={{0,24},{4,28},{8,16},{12,20},{16,8},{20,12},{24,0},{28,4},{1,25},{... | collective-permute-start | bytes 1572872 | tf_op jit(solution)/shard_map/ppermute | solution.py:926
  203.4 24.0 %collective-permute-start.38 = (bf16[256,1024]{1,0:T(8,128)(2,1)S(1)}, bf16[256,1024]{1,0:T(8,128)(2,1)S(1)}, u32[]{:S(2)}, u32[]{:S(2)}) collective-permute-start(bf16[256,1024]{1,0:T(8,128)(2,1)S(1)} %fusion.15.refs_0_.refs_8_), channel_id=1, source_target_pairs={{0,16},{4,20},{8,24},{12,28},{16,0},{20,4},{24,8},{28,12},{1,17},{... | collective-permute-start | bytes 1572872 | tf_op jit(solution)/shard_map/ppermute | solution.py:926
  205.1 22.4 %collective-permute-start.36 = (bf16[256,1024]{1,0:T(8,128)(2,1)S(1)}, bf16[256,1024]{1,0:T(8,128)(2,1)S(1)}, u32[]{:S(2)}, u32[]{:S(2)}) collective-permute-start(bf16[256,1024]{1,0:T(8,128)(2,1)S(1)} %fusion.15.refs_0_.refs_8_), channel_id=1, source_target_pairs={{0,8},{4,12},{8,0},{12,4},{16,24},{20,28},{24,16},{28,20},{1,9},{5... | collective-permute-start | bytes 1572872 | tf_op jit(solution)/shard_map/ppermute | solution.py:926
  205.4 22.5 %collective-permute-start.35 = (bf16[256,1024]{1,0:T(8,128)(2,1)S(1)}, bf16[256,1024]{1,0:T(8,128)(2,1)S(1)}, u32[]{:S(2)}, u32[]{:S(2)}) collective-permute-start(bf16[256,1024]{1,0:T(8,128)(2,1)S(1)} %fusion.15.refs_0_.refs_8_), channel_id=1, source_target_pairs={{0,4},{4,0},{8,12},{12,8},{16,20},{20,16},{24,28},{28,24},{1,5},{5... | collective-permute-start | bytes 1572872 | tf_op jit(solution)/shard_map/ppermute | solution.py:926
  230.2 100.2 %reduce-scatter.5.cloned.1.call-start = ((), (), s32[]{:S(2)}) async-start(), calls=%async_computation.7 | async-start | bytes 2621440 | tf_op jit(solution)/shard_map/reduce_scatter | solution.py:1025
  230.5 49.8 %collective-permute-start.42 = (bf16[256,1024]{1,0:T(8,128)(2,1)}, bf16[256,1024]{1,0:T(8,128)(2,1)}, u32[]{:S(2)}, u32[]{:S(2)}) collective-permute-start(bf16[256,1024]{1,0:T(8,128)(2,1)} %get-tuple-element.224), channel_id=1, source_target_pairs={{0,8},{4,12},{8,0},{12,4},{16,24},{20,28},{24,16},{28,20},{1,9},{5... | collective-permute-start | bytes 1572872 | tf_op jit(solution)/shard_map/ppermute | solution.py:926
  231.8 48.4 %collective-permute-start.43 = (bf16[256,1024]{1,0:T(8,128)(2,1)}, bf16[256,1024]{1,0:T(8,128)(2,1)}, u32[]{:S(2)}, u32[]{:S(2)}) collective-permute-start(bf16[256,1024]{1,0:T(8,128)(2,1)} %get-tuple-element.225), channel_id=1, source_target_pairs={{0,16},{4,20},{8,24},{12,28},{16,0},{20,4},{24,8},{28,12},{1,17},{... | collective-permute-start | bytes 1572872 | tf_op jit(solution)/shard_map/ppermute | solution.py:926
  233.3 47.0 %collective-permute-start.44 = (bf16[256,1024]{1,0:T(8,128)(2,1)}, bf16[256,1024]{1,0:T(8,128)(2,1)}, u32[]{:S(2)}, u32[]{:S(2)}) collective-permute-start(bf16[256,1024]{1,0:T(8,128)(2,1)} %get-tuple-element.226), channel_id=1, source_target_pairs={{0,24},{4,28},{8,16},{12,20},{16,8},{20,12},{24,0},{28,4},{1,25},{... | collective-permute-start | bytes 1572872 | tf_op jit(solution)/shard_map/ppermute | solution.py:926
  283.7 85.4 %all-gather.13.cloned.1.call-start = ((), (), s32[]{:S(2)}) async-start(), calls=%async_computation.9 | async-start | bytes 4718592 | tf_op jit(solution)/shard_map/all_gather | solution.py:1028
  302.9 16.0 %collective-permute-start.48 = (bf16[256,1024]{1,0:T(8,128)(2,1)}, bf16[256,1024]{1,0:T(8,128)(2,1)}, u32[]{:S(2)}, u32[]{:S(2)}) collective-permute-start(bf16[256,1024]{1,0:T(8,128)(2,1)} %get-tuple-element.258), channel_id=1, source_target_pairs={{0,24},{4,28},{8,16},{12,20},{16,8},{20,12},{24,0},{28,4},{1,25},{... | collective-permute-start | bytes 1572872 | tf_op jit(solution)/shard_map/ppermute | solution.py:926
  304.4 25.1 %collective-permute-start.47 = (bf16[256,1024]{1,0:T(8,128)(2,1)}, bf16[256,1024]{1,0:T(8,128)(2,1)}, u32[]{:S(2)}, u32[]{:S(2)}) collective-permute-start(bf16[256,1024]{1,0:T(8,128)(2,1)} %get-tuple-element.259), channel_id=1, source_target_pairs={{0,16},{4,20},{8,24},{12,28},{16,0},{20,4},{24,8},{28,12},{1,17},{... | collective-permute-start | bytes 1572872 | tf_op jit(solution)/shard_map/ppermute | solution.py:926
  305.9 23.6 %collective-permute-start.46 = (bf16[256,1024]{1,0:T(8,128)(2,1)S(1)}, bf16[256,1024]{1,0:T(8,128)(2,1)}, u32[]{:S(2)}, u32[]{:S(2)}) collective-permute-start(bf16[256,1024]{1,0:T(8,128)(2,1)S(1)} %get-tuple-element.260), channel_id=1, source_target_pairs={{0,8},{4,12},{8,0},{12,4},{16,24},{20,28},{24,16},{28,20},{1,9},{5... | collective-permute-start | bytes 1572872 | tf_op jit(solution)/shard_map/ppermute | solution.py:926
  (87 other events, 781.7 us)
Sparse Core Ops, SparseCore 0:
  10.2 48.6 all-gather.6
  61.0 49.1 all-gather.8
  183.0 46.9 reduce-scatter.2
  231.7 51.9 all-gather.10
  286.4 43.9 reduce-scatter.4
  332.3 36.7 all-gather.12
